TPU v7x, 32 devices: a whole 2x2x4 slice. The times are simulated.
32 devices in a mesh: seq: 2 (over x), mp: 16 (over z, y, core).
Axes of the slice: x: 2, y: 2, z: 4, core: 2. Of those that a mesh axis runs over, the one named last changes fastest.
Arguments:
- tokens: bfloat16 [512, 4, 1536], P('seq'), may hold values from -6 to 6
- target: bfloat16 [512, 4, 1536], P(('seq', 'mp')), may hold values from -6 to 6
- lengths: int32 [4], replicated, may hold values from 128 to 512, as said below
- routes: int32 [512, 4, 6], P(('seq', 'mp')), may hold values from 0 to 15, all different within a row; in each aligned block of 64 rows (0 to 63, 64 to 127, ..., all dimensions but the last counted through in order) at most 48 rows name the same one
- route_weight: float32 [512, 4, 6], P(('seq', 'mp')), may hold values from 0.1 to 0.4
- in_gain: bfloat16 [1536], P(('seq', 'mp')), may hold values from 0.5 to 1.5
- gate_proj: bfloat16 [1536, 3072], P(None, 'mp'), may hold values from -0.15625 to 0.15625
- value_proj: bfloat16 [1536, 3072], P(None, 'mp'), may hold values from -0.15625 to 0.15625
- state_proj: bfloat16 [1536, 256], P(('seq', 'mp')), may hold values from -0.078125 to 0.078125
- step_proj: bfloat16 [1536, 48], P(None, 'mp'), may hold values from -0.15625 to 0.15625
- conv_value: float32 [4, 3072], P(None, 'mp'), may hold values from -3 to 3
- conv_value_bias: float32 [3072], P('mp'), may hold values from -3 to 3
- conv_state: bfloat16 [256, 4], P(('seq', 'mp')), may hold values from -3 to 3
- conv_state_bias: bfloat16 [256], P(('seq', 'mp')), may hold values from -3 to 3
- step_bias: float32 [48], P('mp'), may hold values from -4 to -1
- decay_log: float32 [48], P('mp'), may hold values from -8 to -1
- skip_gain: float32 [48], P('mp'), may hold values from 0.5 to 2
- mixer_gain: float32 [3072], P('mp'), may hold values from 0.5 to 1.5
- out_proj: bfloat16 [3072, 1536], P('mp'), may hold values from -0.109375 to 0.109375
- ffn_gain: bfloat16 [1536], P(('seq', 'mp')), may hold values from 0.5 to 1.5
- shared_gate: bfloat16 [1536, 1024], P(('seq', 'mp')), may hold values from -0.15625 to 0.15625
- shared_up: bfloat16 [1536, 1024], P(('seq', 'mp')), may hold values from -0.15625 to 0.15625
- shared_down: bfloat16 [1024, 1536], P(('seq', 'mp')), may hold values from -0.1875 to 0.1875
- expert_gate: bfloat16 [16, 1536, 512], P('mp'), may hold values from -0.15625 to 0.15625
- routed_up_weights: bfloat16 [16, 1536, 512], P('mp'), may hold values from -0.15625 to 0.15625
- expert_down: bfloat16 [16, 512, 1536], P('mp'), may hold values from -0.25 to 0.25
Outputs:
- block_out: bfloat16 [512, 4, 1536], P(('seq', 'mp'))
- tokens_grad: float32 [512, 4, 1536], P(('seq', 'mp'))
- in_gain_grad: float32 [1536], P(('seq', 'mp'))
- gate_proj_grad: float32 [1536, 3072], P(None, 'mp')
- value_proj_grad: float32 [1536, 3072], P(None, 'mp')
- state_proj_grad: float32 [1536, 256], P(('seq', 'mp'))
- step_proj_grad: float32 [1536, 48], P(None, 'mp')
- conv_value_grad: float32 [4, 3072], P(None, 'mp')
- conv_value_bias_grad: float32 [3072], P('mp')
- conv_state_grad: float32 [256, 4], P(('seq', 'mp'))
- conv_state_bias_grad: float32 [256], P(('seq', 'mp'))
- step_bias_grad: float32 [48], P('mp')
- decay_log_grad: float32 [48], P('mp')
- skip_gain_grad: float32 [48], P('mp')
- mixer_gain_grad: float32 [3072], P('mp')
- out_proj_grad: float32 [3072, 1536], P('mp')
- ffn_gain_grad: float32 [1536], P(('seq', 'mp'))
- shared_gate_grad: float32 [1536, 1024], P(('seq', 'mp'))
- shared_up_grad: float32 [1536, 1024], P(('seq', 'mp'))
- shared_down_grad: float32 [1024, 1536], P(('seq', 'mp'))
- expert_gate_grad: float32 [16, 1536, 512], P('mp')
- expert_up_grad: float32 [16, 1536, 512], P('mp')
- expert_down_grad: float32 [16, 512, 1536], P('mp')
Inputs may be any that keep to these rules, and one draw needn't show every extreme that they name: `routes`: each row names 6 different experts. In each aligned block of 64 rows (the rows of one device), no expert is named by more than 48 rows, a bound that some block reaches. `lengths`: some sequence has all 512 slots true.
All inputs are finite; a program needn't handle non-finite values.
Results may differ from a plain program's by a relative error of at most 0.018.
The roundings to bfloat16 on the way count: a program that leaves them out, or rounds other values in their place, can miss the bound.
Values may be sent and summed in bfloat16 or wider, within the bound.
No kernel may reach another device: no remote copies, remote signals or barrier semaphores. Data moves between devices by JAX's collectives and lax.ppermute only.
A program may use at most 192 MiB of HBM per device.

v0:
```python
import jax
import jax.numpy as jnp
from jax import lax
from jax.sharding import PartitionSpec as P

STATE = 128
INNER = 3072


epsilon = 1e-05
highest = lax.Precision.HIGHEST


def shifted(block, axis, distance):
    devices = range(lax.axis_size(axis))
    route = [(i - distance, i) for i in devices if i - distance in devices]
    return lax.ppermute(block, axis, route)


def entering_2(value, axis, join, neutral, backward):
    count, mine = (lax.axis_size(axis), lax.axis_index(axis))
    pieces = jax.tree.map(lambda part: lax.all_gather(part, axis), value)
    if backward:
        pieces = jax.tree.map(lambda part: part[::-1], pieces)
        mine = count - 1 - mine
    running = jax.tree.map(
        lambda part, zero: jnp.full_like(part, 0) + jnp.asarray(zero, part.dtype), value, neutral
    )

    def hop(position, running):
        longer = join(running, jax.tree.map(lambda part: part[position], pieces))
        return jax.tree.map(lambda new, old: jnp.where(position < mine, new, old), longer, running)

    return lax.fori_loop(0, count - 1, hop, running)


def rms_scale(values, gain):
    return values * lax.rsqrt(jnp.mean(values * values, axis=-1, keepdims=True) + epsilon) * gain


def silu_slope(values):
    sigmoid_val = jax.nn.sigmoid(values)
    return sigmoid_val * (1.0 + values * (1.0 - sigmoid_val))


def conv_decay(
    extended, conv_weight, conv_bias, step_raw, step_bias, decay_log, inner_width, state_width
):
    length = step_raw.shape[0]
    preact = conv_bias + conv_weight[0] * extended[0:length]
    for offset in range(1, conv_weight.shape[0]):
        preact = preact + conv_weight[offset] * extended[offset : offset + length]
    activated = jax.nn.silu(preact)
    head_count = step_raw.shape[-1]
    values = activated[..., :inner_width].reshape(
        length, activated.shape[1], head_count, inner_width // head_count
    )
    input_matrix_b = activated[..., inner_width : inner_width + state_width]
    c_matrix = activated[..., inner_width + state_width :]
    step_size = jax.nn.softplus(step_raw + step_bias)
    log_decay = -jnp.exp(decay_log) * step_size
    return (values, input_matrix_b, c_matrix, step_size, log_decay)


def ssd_output(values, input_matrix_b, c_matrix, step_size, log_decay, entering, skip_gain):
    cumulative = jnp.cumsum(log_decay, axis=0)
    length = cumulative.shape[0]
    causal = (jnp.arange(length)[:, None] >= jnp.arange(length)[None, :])[:, :, None, None]
    log_gap = jnp.where(causal, cumulative[:, None] - cumulative[None, :], 0.0)
    decay_mask = jnp.where(causal, jnp.exp(log_gap), 0.0)
    intersection = jnp.einsum("tbn,sbn->tsb", c_matrix, input_matrix_b, precision=highest)
    weighted = decay_mask * intersection[..., None]
    scaled = values * step_size[..., None]
    within = jnp.einsum("tsbh,sbhp->tbhp", weighted, scaled, precision=highest)
    carried = jnp.exp(cumulative)[..., None] * jnp.einsum(
        "tbn,bhpn->tbhp", c_matrix, entering, precision=highest
    )
    return within + carried + skip_gain[:, None] * values


def state_update(values, input_matrix_b, step_size, log_decay):
    cumulative = jnp.cumsum(log_decay, axis=0)
    decay_total = jnp.exp(cumulative[-1])
    tail_weight = jnp.exp(cumulative[-1] - cumulative) * step_size
    local_state = jnp.einsum(
        "sbh,sbhp,sbn->bhpn", tail_weight, values, input_matrix_b, precision=highest
    )
    return (decay_total, local_state)


def chain_combine(earlier, latter):
    return (earlier[0] * latter[0], latter[0][..., None, None] * earlier[1] + latter[1])


def gather_shared(
    in_gain, state_proj, conv_state, conv_state_bias, ffn_gain, shared_gate, shared_up, shared_down
):
    return (
        lax.all_gather(in_gain, ("seq", "mp"), axis=0, tiled=True),
        lax.all_gather(state_proj, ("seq", "mp"), axis=0, tiled=True),
        lax.all_gather(conv_state, ("seq", "mp"), axis=0, tiled=True),
        lax.all_gather(conv_state_bias, ("seq", "mp"), axis=0, tiled=True),
        lax.all_gather(ffn_gain, ("seq", "mp"), axis=0, tiled=True),
        lax.all_gather(shared_gate, ("seq", "mp"), axis=0, tiled=True),
        lax.all_gather(shared_up, ("seq", "mp"), axis=0, tiled=True),
        lax.all_gather(shared_down, ("seq", "mp"), axis=0, tiled=True),
    )


def body(
    tokens,
    target,
    lengths,
    routes,
    route_weight,
    in_gain,
    gate_proj,
    value_proj,
    state_proj,
    step_proj,
    conv_value,
    conv_value_bias,
    conv_state,
    conv_state_bias,
    step_bias,
    decay_log,
    skip_gain,
    mixer_gain,
    out_proj,
    ffn_gain,
    shared_gate,
    shared_up,
    shared_down,
    expert_gate,
    routed_up_weights,
    expert_down,
):
    mp_count = lax.axis_size("mp")
    slot_count, seq_count, model_width = tokens.shape
    shared_expert_rows = slot_count // mp_count
    inner_width = gate_proj.shape[1]
    route_count = routes.shape[-1]
    local_experts = expert_gate.shape[0]
    expert_count = local_experts * mp_count
    row_count = shared_expert_rows * seq_count
    capacity = min(row_count, 2 * row_count * route_count // expert_count)
    window = conv_value.shape[0]
    gathered = gather_shared(
        in_gain,
        state_proj,
        conv_state,
        conv_state_bias,
        ffn_gain,
        shared_gate,
        shared_up,
        shared_down,
    )
    (
        gain_first,
        state_whole,
        conv_state_whole,
        conv_bias_whole,
        gain_second,
        gate_complete,
        up_whole,
        down_whole,
    ) = gathered
    inputs = tokens.astype(jnp.float32)
    normed = rms_scale(inputs, gain_first.astype(jnp.float32)).astype(jnp.bfloat16)
    gate_raw = jnp.dot(normed, gate_proj, preferred_element_type=jnp.float32)
    value_raw = jnp.dot(normed, value_proj, preferred_element_type=jnp.float32)
    state_raw = jnp.dot(normed, state_whole, preferred_element_type=jnp.float32)
    step_raw = jnp.dot(normed, step_proj, preferred_element_type=jnp.float32)
    conv_input = jnp.concatenate([value_raw, state_raw], axis=-1)
    edge_rows = shifted(conv_input[slot_count - window + 1 :], "seq", 1)
    extended = jnp.concatenate([edge_rows, conv_input], axis=0)
    conv_weight = jnp.concatenate([conv_value, conv_state_whole.astype(jnp.float32).T], axis=1)
    conv_bias = jnp.concatenate([conv_value_bias, conv_bias_whole.astype(jnp.float32)])

    def first_piece(ext_values, weight_values, bias_values, step_values, bias_step, decay_values):
        return conv_decay(
            ext_values,
            weight_values,
            bias_values,
            step_values,
            bias_step,
            decay_values,
            inner_width,
            STATE,
        )

    mixer_inputs, first_back = jax.vjp(
        first_piece, extended, conv_weight, conv_bias, step_raw, step_bias, decay_log
    )
    values, input_matrix_b, c_matrix, step_size, log_decay = mixer_inputs
    local_out, state_back = jax.vjp(state_update, values, input_matrix_b, step_size, log_decay)
    decay_total, local_state = local_out
    prefix = entering_2(
        (decay_total, local_state),
        "seq",
        chain_combine,
        (jnp.ones_like(decay_total), jnp.zeros_like(local_state)),
        False,
    )
    entering = prefix[1]

    def second_piece(
        in_values,
        in_bmatrix,
        in_cmatrix,
        in_step,
        in_decay,
        in_state,
        in_skip,
        in_gate,
        in_gain_mix,
    ):
        result = ssd_output(in_values, in_bmatrix, in_cmatrix, in_step, in_decay, in_state, in_skip)
        gated_part = result.reshape(in_gate.shape) * jax.nn.silu(in_gate)
        return (gated_part, gated_part * in_gain_mix)

    gated_pair, second_back = jax.vjp(
        second_piece,
        values,
        input_matrix_b,
        c_matrix,
        step_size,
        log_decay,
        entering,
        skip_gain,
        gate_raw,
        mixer_gain,
    )
    gated_out, scaled = gated_pair
    scaled_low = scaled.astype(jnp.bfloat16)
    mix_part = jnp.dot(scaled_low, out_proj, preferred_element_type=jnp.float32)
    pre_mix, square_sum = (
        lax.psum_scatter(mix_part, "mp", scatter_dimension=0, tiled=True),
        lax.psum_scatter(
            jnp.sum(gated_out * gated_out, axis=-1), "mp", scatter_dimension=0, tiled=True
        ),
    )
    inv_norm = lax.rsqrt(square_sum / INNER + epsilon)
    start_row = lax.axis_index("mp") * shared_expert_rows
    own_inputs = lax.dynamic_slice_in_dim(inputs, start_row, shared_expert_rows, 0)
    hidden = own_inputs + pre_mix * inv_norm[..., None]
    hidden_rows = hidden.reshape(row_count, model_width)
    ffn_input = rms_scale(hidden_rows, gain_second.astype(jnp.float32)).astype(jnp.bfloat16)
    shared_gate_val = jnp.dot(ffn_input, gate_complete, preferred_element_type=jnp.float32)
    shared_up_val = jnp.dot(ffn_input, up_whole, preferred_element_type=jnp.float32)
    shared_act = (jax.nn.silu(shared_gate_val) * shared_up_val).astype(jnp.bfloat16)
    shared_out = jnp.dot(shared_act, down_whole, preferred_element_type=jnp.float32)
    route_flat = routes.reshape(row_count * route_count)
    onehot = (route_flat[:, None] == jnp.arange(expert_count, dtype=jnp.int32)[None, :]).astype(
        jnp.int32
    )
    slot_rank = jnp.sum((jnp.cumsum(onehot, axis=0) - 1) * onehot, axis=1)
    slot_of = route_flat * capacity + slot_rank
    pair_of = (
        jnp.full((expert_count * capacity,), row_count * route_count, jnp.int32)
        .at[slot_of]
        .set(jnp.arange(row_count * route_count, dtype=jnp.int32))
    )
    padded_rows = jnp.concatenate([ffn_input, jnp.zeros((1, model_width), jnp.bfloat16)], axis=0)
    send_rows = padded_rows[pair_of // route_count].reshape(
        mp_count, local_experts, capacity, model_width
    )
    received_rows = lax.all_to_all(send_rows, "mp", split_axis=0, concat_axis=0, tiled=True)
    gate_activation = jnp.einsum(
        "mecd,edf->mecf", received_rows, expert_gate, preferred_element_type=jnp.float32
    )
    up_val = jnp.einsum(
        "mecd,edf->mecf", received_rows, routed_up_weights, preferred_element_type=jnp.float32
    )
    act_val = (jax.nn.silu(gate_activation) * up_val).astype(jnp.bfloat16)
    result = jnp.einsum(
        "mecf,efd->mecd", act_val, expert_down, preferred_element_type=jnp.float32
    ).astype(jnp.bfloat16)
    returned = lax.all_to_all(result, "mp", split_axis=0, concat_axis=0, tiled=True)
    returned, received_rows, gate_activation, up_val, act_val = (
        returned,
        received_rows,
        gate_activation,
        up_val,
        act_val,
    )
    route_rows = route_weight.reshape(row_count, route_count)
    picked = returned.reshape(expert_count * capacity, model_width)[slot_of].reshape(
        row_count, route_count, model_width
    )
    routed = jnp.sum(route_rows[:, :, None] * picked.astype(jnp.float32), axis=1)
    output = hidden_rows + shared_out + routed
    block_out = output.astype(jnp.bfloat16).reshape(shared_expert_rows, seq_count, model_width)
    position = (
        lax.axis_index("seq") * slot_count
        + start_row
        + jnp.arange(shared_expert_rows, dtype=jnp.int32)
    )
    valid_mask = (position[:, None] < lengths[None, :]).astype(jnp.float32).reshape(row_count, 1)
    grad_out = (output - target.astype(jnp.float32).reshape(row_count, model_width)) * valid_mask
    pair_grads = (
        (route_rows[:, :, None] * grad_out[:, None, :])
        .astype(jnp.bfloat16)
        .reshape(row_count * route_count, model_width)
    )
    pair_padded = jnp.concatenate([pair_grads, jnp.zeros((1, model_width), jnp.bfloat16)], axis=0)
    grad_send = pair_padded[pair_of].reshape(mp_count, local_experts, capacity, model_width)
    grad_arrived = lax.all_to_all(grad_send, "mp", split_axis=0, concat_axis=0, tiled=True)
    activation_gradient = jnp.einsum(
        "mecd,efd->mecf", grad_arrived, expert_down, preferred_element_type=jnp.float32
    )
    expert_down_grad = jnp.einsum(
        "mecf,mecd->efd", act_val, grad_arrived, preferred_element_type=jnp.float32
    )
    egate_grad = (activation_gradient * up_val * silu_slope(gate_activation)).astype(jnp.bfloat16)
    expert_up_gradient = (activation_gradient * jax.nn.silu(gate_activation)).astype(jnp.bfloat16)
    expert_gate_grad = jnp.einsum(
        "lqsb,lqsn->qbn", received_rows, egate_grad, preferred_element_type=jnp.float32
    )
    expert_up_grad = jnp.einsum(
        "lqsb,lqsn->qbn", received_rows, expert_up_gradient, preferred_element_type=jnp.float32
    )
    rows_grad = (
        jnp.einsum("kvsg,vog->kvso", egate_grad, expert_gate, preferred_element_type=jnp.float32)
        + jnp.einsum(
            "kvsg,vog->kvso",
            expert_up_gradient,
            routed_up_weights,
            preferred_element_type=jnp.float32,
        )
    ).astype(jnp.bfloat16)
    returned_grad = lax.all_to_all(rows_grad, "mp", split_axis=0, concat_axis=0, tiled=True)
    routed_grad = jnp.sum(
        returned_grad.reshape(expert_count * capacity, model_width)[slot_of]
        .reshape(row_count, route_count, model_width)
        .astype(jnp.float32),
        axis=1,
    )
    weights_back = gather_shared(
        in_gain,
        state_proj,
        conv_state,
        conv_state_bias,
        ffn_gain,
        shared_gate,
        shared_up,
        shared_down,
    )
    (
        gain_first_back,
        state_whole_back,
        _,
        _,
        gain_second_back,
        gate_whole_back,
        up_whole_back,
        down_whole_back,
    ) = weights_back
    out_grad_low = grad_out.astype(jnp.bfloat16)
    shared_down_grad = jnp.einsum(
        "rf,rd->fd", shared_act, out_grad_low, preferred_element_type=jnp.float32
    )
    shact_grad = jnp.einsum(
        "rd,fd->rf", out_grad_low, down_whole_back, preferred_element_type=jnp.float32
    )
    sgate_grad = (shact_grad * shared_up_val * silu_slope(shared_gate_val)).astype(jnp.bfloat16)
    sup_grad = (shact_grad * jax.nn.silu(shared_gate_val)).astype(jnp.bfloat16)
    shared_gate_grad = jnp.einsum(
        "rd,rf->df", ffn_input, sgate_grad, preferred_element_type=jnp.float32
    )
    shared_up_grad = jnp.einsum(
        "rd,rf->df", ffn_input, sup_grad, preferred_element_type=jnp.float32
    )
    ffn_input_grad = (
        routed_grad
        + jnp.einsum("rf,df->rd", sgate_grad, gate_whole_back, preferred_element_type=jnp.float32)
        + jnp.einsum("rf,df->rd", sup_grad, up_whole_back, preferred_element_type=jnp.float32)
    )
    _, second_norm_back = jax.vjp(rms_scale, hidden_rows, gain_second_back.astype(jnp.float32))
    hidden_part, ffn_gain_grad = second_norm_back(ffn_input_grad)
    hidden_grad_share = (grad_out + hidden_part).reshape(shared_expert_rows, seq_count, model_width)
    mix_grad_low = (hidden_grad_share * inv_norm[..., None]).astype(jnp.bfloat16)
    sum_grad_share = (
        jnp.sum(hidden_grad_share * pre_mix, axis=-1)
        * -0.5
        * inv_norm
        * inv_norm
        * inv_norm
        / INNER
    )
    mix_grad_wide, sum_grad = (
        lax.all_gather(mix_grad_low.astype(jnp.float32), "mp", axis=0, tiled=True),
        lax.all_gather(sum_grad_share, "mp", axis=0, tiled=True),
    )
    mix_grad_all = mix_grad_wide.astype(jnp.bfloat16)
    out_proj_grad = jnp.einsum(
        "sbc,sbd->cd", scaled_low, mix_grad_all, preferred_element_type=jnp.float32
    )
    scaled_grad = jnp.einsum(
        "sbd,cd->sbc", mix_grad_all, out_proj, preferred_element_type=jnp.float32
    )
    gated_grad = 2.0 * gated_out * sum_grad[..., None]
    (
        out_values_grad,
        out_bmatrix_grad,
        out_cmatrix_grad,
        out_step_grad,
        out_decay_grad,
        entering_grad,
        skip_gain_grad,
        gate_raw_grad,
        mixer_gain_grad,
    ) = second_back((gated_grad, scaled_grad))
    suffix = entering_2(
        (decay_total, entering_grad),
        "seq",
        chain_combine,
        (jnp.ones_like(decay_total), jnp.zeros_like(entering_grad)),
        True,
    )
    exit_grad = suffix[1]
    total_grad = jnp.sum(entering * exit_grad, axis=(-2, -1))
    tail_values_grad, tail_bmatrix_grad, tail_step_grad, tail_decay_grad = state_back(
        (total_grad, exit_grad)
    )
    ext_grad, conv_weight_grad, conv_bias_grad, step_raw_grad, step_bias_grad, decay_log_grad = (
        first_back(
            (
                out_values_grad + tail_values_grad,
                out_bmatrix_grad + tail_bmatrix_grad,
                out_cmatrix_grad,
                out_step_grad + tail_step_grad,
                out_decay_grad + tail_decay_grad,
            )
        )
    )
    edge_grad = shifted(ext_grad[: window - 1], "seq", -1)
    conv_grad = ext_grad[window - 1 :] + jnp.concatenate(
        [jnp.zeros((slot_count - window + 1,) + ext_grad.shape[1:], jnp.float32), edge_grad], axis=0
    )
    conv_grad_low = conv_grad.astype(jnp.bfloat16)
    value_grad = conv_grad_low[..., :inner_width]
    state_grad = conv_grad_low[..., inner_width:]
    gate_grad = gate_raw_grad.astype(jnp.bfloat16)
    step_grad = step_raw_grad.astype(jnp.bfloat16)
    partial_value = jnp.einsum(
        "sbc,dc->sbd", gate_grad, gate_proj, preferred_element_type=jnp.float32
    )
    partial_value = partial_value + jnp.einsum(
        "sbc,dc->sbd", value_grad, value_proj, preferred_element_type=jnp.float32
    )
    partial_value = partial_value + jnp.einsum(
        "sbc,dc->sbd", state_grad, state_whole_back, preferred_element_type=jnp.float32
    )
    partial_value = partial_value + jnp.einsum(
        "sbh,dh->sbd", step_grad, step_proj, preferred_element_type=jnp.float32
    )
    normed_grad = lax.psum_scatter(partial_value, "mp", scatter_dimension=0, tiled=True)
    gate_proj_grad = jnp.einsum(
        "sbd,sbc->dc", normed, gate_grad, preferred_element_type=jnp.float32
    )
    value_proj_grad = jnp.einsum(
        "sbd,sbc->dc", normed, value_grad, preferred_element_type=jnp.float32
    )
    state_proj_grad = jnp.einsum(
        "sbd,sbc->dc", normed, state_grad, preferred_element_type=jnp.float32
    )
    step_proj_grad = jnp.einsum(
        "sbd,sbh->dh", normed, step_grad, preferred_element_type=jnp.float32
    )
    _, first_norm_back = jax.vjp(rms_scale, own_inputs, gain_first_back.astype(jnp.float32))
    input_part, in_gain_grad = first_norm_back(normed_grad)
    tokens_grad = input_part + hidden_grad_share
    conv_value_grad = conv_weight_grad[:, :inner_width]
    conv_state_grad = conv_weight_grad[:, inner_width:].T
    conv_value_bias_grad = conv_bias_grad[:inner_width]
    conv_state_bias_grad = conv_bias_grad[inner_width:]
    summed = lax.psum(
        (
            gate_proj_grad,
            value_proj_grad,
            step_proj_grad,
            conv_value_grad,
            conv_value_bias_grad,
            step_bias_grad,
            decay_log_grad,
            skip_gain_grad,
            mixer_gain_grad,
            out_proj_grad,
            expert_gate_grad,
            expert_up_grad,
            expert_down_grad,
        ),
        "seq",
    )
    scattered = (
        lax.psum_scatter(in_gain_grad, ("seq", "mp"), scatter_dimension=0, tiled=True),
        lax.psum_scatter(state_proj_grad, ("seq", "mp"), scatter_dimension=0, tiled=True),
        lax.psum_scatter(conv_state_grad, ("seq", "mp"), scatter_dimension=0, tiled=True),
        lax.psum_scatter(conv_state_bias_grad, ("seq", "mp"), scatter_dimension=0, tiled=True),
        lax.psum_scatter(ffn_gain_grad, ("seq", "mp"), scatter_dimension=0, tiled=True),
        lax.psum_scatter(shared_gate_grad, ("seq", "mp"), scatter_dimension=0, tiled=True),
        lax.psum_scatter(shared_up_grad, ("seq", "mp"), scatter_dimension=0, tiled=True),
        lax.psum_scatter(shared_down_grad, ("seq", "mp"), scatter_dimension=0, tiled=True),
    )
    return (
        block_out,
        tokens_grad,
        scattered[0],
        summed[0],
        summed[1],
        scattered[1],
        summed[2],
        summed[3],
        summed[4],
        scattered[2],
        scattered[3],
        summed[5],
        summed[6],
        summed[7],
        summed[8],
        summed[9],
        scattered[4],
        scattered[5],
        scattered[6],
        scattered[7],
        summed[10],
        summed[11],
        summed[12],
    )


def solution(mesh):
    placed = (
        P("seq", None, None),
        P(("seq", "mp"), None, None),
        P(),
        P(("seq", "mp"), None, None),
        P(("seq", "mp"), None, None),
        P(("seq", "mp")),
        P(None, "mp"),
        P(None, "mp"),
        P(("seq", "mp"), None),
        P(None, "mp"),
        P(None, "mp"),
        P("mp"),
        P(("seq", "mp"), None),
        P(("seq", "mp")),
        P("mp"),
        P("mp"),
        P("mp"),
        P("mp"),
        P("mp", None),
        P(("seq", "mp")),
        P(("seq", "mp"), None),
        P(("seq", "mp"), None),
        P(("seq", "mp"), None),
        P("mp", None, None),
        P("mp", None, None),
        P("mp", None, None),
    )
    return jax.shard_map(
        body,
        mesh=mesh,
        in_specs=placed,
        out_specs=(
            P(("seq", "mp"), None, None),
            P(("seq", "mp"), None, None),
            P(("seq", "mp")),
            P(None, "mp"),
            P(None, "mp"),
            P(("seq", "mp"), None),
            P(None, "mp"),
            P(None, "mp"),
            P("mp"),
            P(("seq", "mp"), None),
            P(("seq", "mp")),
            P("mp"),
            P("mp"),
            P("mp"),
            P("mp"),
            P("mp", None),
            P(("seq", "mp")),
            P(("seq", "mp"), None),
            P(("seq", "mp"), None),
            P(("seq", "mp"), None),
            P("mp", None, None),
            P("mp", None, None),
            P("mp", None, None),
        ),
        check_vma=False,
    )
```

profile of v0, /device:TPU:0, one launch (start us, length us, event | category | flops | bytes accessed | tf_op | source)
XLA Modules:
  0.0 1481.0 jit_solution(1309344460942513882)
XLA Ops:
  10.8 42.2 %all-reduce.26 = (bf16[1536]{0:T(1024)(128)(2,1)S(1)}, bf16[256]{0:T(256)(128)(2,1)S(1)}, bf16[1536]{0:T(1024)(128)(2,1)}) all-reduce(bf16[1536]{0:T(1024)(128)(2,1)S(1)} %dynamic-update-slice.1, bf16[256]{0:T(256)(128)(2,1)S(1)} %dynamic-update-slice, ...), channel_id=1, replica_groups=mesh['seq'=2,'mp'=16] {'seq','mp'}, use_global_device_ids=true, to_apply=%add.17 | all-reduce | flops 3328 | bytes 13312
  55.9 42.6 %all_gather.57 = bf16[1536,256]{1,0:T(8,128)(2,1)S(1)} all-gather(bf16[48,256]{1,0:T(8,128)(2,1)S(1)} %copy-done.98), channel_id=1, replica_groups=mesh['seq'=2,'mp'=16] {'seq','mp'}, dimensions={0}, use_global_device_ids=true | all-gather | bytes 811008 | tf_op jit(solution)/shard_map/all_gather | solution.py:100
  104.6 4.0 collective-permute-start
  109.8 36.4 %all-gather.2 = bf16[32,8,4]{1,2,0:T(4,128)(2,1)S(1)} all-gather(bf16[1,8,4]{1,2,0:T(4,128)(2,1)S(1)} %bitcast.432), channel_id=1, replica_groups=mesh['seq'=2,'mp'=16] {'seq','mp'}, dimensions={0}, use_global_device_ids=true | all-gather | bytes 2112 | tf_op jit(solution)/shard_map/all_gather | solution.py:101
  155.2 4.3 all_gather.58
  167.2 4.4 fusion.27
  174.5 11.1 all-gather
  190.1 5.8 fusion.66
  200.5 4.5 fusion.98
  211.1 5.5 copy_convert_fusion
  216.7 39.2 %reduce-scatter.23.cloned.1.call-done = f32[16,4]{1,0:T(8,128)} async-done(((f32[256,4]{1,0:T(8,128)}), f32[16,4]{1,0:T(8,128)}) %reduce-scatter.23.cloned.1.call-update) | async-done | bytes 272
  256.6 97.7 %reduce-scatter.11.cloned.1.call-done = f32[16,4,1536]{2,0,1:T(8,128)} async-done(((f32[256,4,1536]{2,0,1:T(8,128)}), f32[16,4,1536]{2,0,1:T(8,128)}) %reduce-scatter.11.cloned.1.call-update) | async-done | bytes 393232 | tf_op jit(solution)/shard_map/reduce_scatter | solution.py:238
  357.0 3.8 gather_fusion
  360.8 4.7 all-to-all-start
  366.1 47.3 %all-to-all-done = bf16[16,1,48,1536]{3,2,1,0:T(8,128)(2,1)} async-done(((bf16[16,1,48,1536]{3,2,1,0:T(8,128)(2,1)}), bf16[16,1,48,1536]{3,2,1,0:T(8,128)(2,1)}, u32[]{:S(2)}, u32[]{:S(2)}) %all-to-all-start) | async-done | bytes 2359328 | tf_op jit(solution)/shard_map/all_to_all | solution.py:268
  425.5 16.7 %all-to-all-start.1 = ((bf16[16,1,48,1536]{3,2,1,0:T(8,128)(2,1)}), bf16[16,1,48,1536]{3,2,1,0:T(8,128)(2,1)}, u32[]{:S(2)}, u32[]{:S(2)}) async-start(bf16[16,1,48,1536]{3,2,1,0:T(8,128)(2,1)} %fusion.10), calls=%async_computation.2 | async-start | bytes 4718592 | tf_op jit(solution)/shard_map/all_to_all | solution.py:279
  449.5 38.3 %all-to-all-done.1 = bf16[16,1,48,1536]{3,2,1,0:T(8,128)(2,1)} async-done(((bf16[16,1,48,1536]{3,2,1,0:T(8,128)(2,1)}), bf16[16,1,48,1536]{3,2,1,0:T(8,128)(2,1)}, u32[]{:S(2)}, u32[]{:S(2)}) %all-to-all-start.1) | async-done | bytes 2359328 | tf_op jit(solution)/shard_map/all_to_all | solution.py:279
  487.8 6.2 gather_fusion.1
  511.1 3.8 gather_fusion.2
  515.0 67.3 %all_to_all.20 = bf16[16,1,48,1536]{3,2,1,0:T(8,128)(2,1)S(1)} all-to-all(bf16[16,1,48,1536]{3,2,1,0:T(8,128)(2,1)} %bitcast.399), channel_id=1, replica_groups=mesh['seq'=2,'mp'=16] {'mp'}, dimensions={0} | all-to-all | bytes 4718592 | tf_op jit(solution)/shard_map/all_to_all | solution.py:308
  589.1 4.2 all-to-all-start.3
  597.0 42.0 %all-to-all-done.3 = bf16[16,1,48,1536]{3,2,1,0:T(8,128)(2,1)S(1)} async-done(((bf16[16,1,48,1536]{3,2,1,0:T(8,128)(2,1)}), bf16[16,1,48,1536]{3,2,1,0:T(8,128)(2,1)S(1)}, u32[]{:S(2)}, u32[]{:S(2)}) %all-to-all-start.3) | async-done | bytes 2359328 | tf_op jit(solution)/shard_map/all_to_all | solution.py:332
  644.8 3.7 reduce_sum.281
  656.8 28.3 %all-gather.3 = f32[16,16,4]{1,2,0:T(4,128)S(1)} all-gather(f32[1,16,4]{1,2,0:T(4,128)S(1)} %fusion.179), channel_id=1, replica_groups=mesh['seq'=2,'mp'=16] {'mp'}, dimensions={0}, use_global_device_ids=true | all-gather | bytes 4352 | tf_op jit(solution)/shard_map/all_gather | solution.py:393
  685.3 24.3 %all-gather.15.cloned.1.call-done = bf16[256,4,1536]{2,0,1:T(8,128)(2,1)} async-done(((bf16[16,4,1536]{2,0,1:T(8,128)(2,1)}), bf16[256,4,1536]{2,0,1:T(8,128)(2,1)}) %all-gather.15.cloned.1.call-update) | async-done | bytes 3145744 | tf_op jit(solution)/shard_map/all_gather | solution.py:392
  709.6 5.4 multiply_reduce_fusion.8
  717.1 4.8 fusion.23
  724.8 12.2 all-gather.1
  742.5 3.8 multiply_reduce_fusion.10
  746.9 16.3 %reduce-window.34 = f32[3,4,2,128]{3,2,1,0:T(2,128)} reduce-window(f32[3,4,2,128]{3,2,1,0:T(2,128)} %copy.334, f32[]{:T(128)} %constant.56.clone.1), window={size=1x1x1x128 pad=0_0x0_0x0_0x0_127}, to_apply=%region_20.21 | reduce-window | flops 390144 | bytes 24580 | tf_op jit(solution)/shard_map/reduce-window.4
  771.7 16.3 %reduce-window.36 = f32[3,4,2,128]{3,2,1,0:T(2,128)} reduce-window(f32[3,4,2,128]{3,2,1,0:T(2,128)} %copy.340, f32[]{:T(128)} %constant.56.clone.1), window={size=1x1x1x128 pad=0_0x0_0x0_0x0_127}, to_apply=%region_24.25 | reduce-window | flops 390144 | bytes 24580 | tf_op jit(solution)/shard_map/reduce-window.6
  793.6 4.2 multiply_reduce_fusion.4
  804.3 3.7 fusion.170
  808.1 3.8 fusion.100
  812.1 3.8 pad_add_fusion
  821.5 7.0 add_add_fusion
  829.5 3.7 fusion.206
  838.9 3.7 fusion.152
  842.9 5.4 convolution_bitcast_fusion
  851.5 5.0 convolution_bitcast_fusion.1
  856.5 4.9 convolution_bitcast_fusion.2
  876.7 11.5 all-reduce.24
  889.0 25.0 %reduce-scatter.13.cloned.1.call-done = f32[16,4,1536]{2,0,1:T(8,128)} async-done(((f32[256,4,1536]{2,0,1:T(8,128)}), f32[16,4,1536]{2,0,1:T(8,128)}) %reduce-scatter.13.cloned.1.call-update) | async-done | bytes 393232 | tf_op jit(solution)/shard_map/reduce_scatter | solution.py:458
  915.4 40.6 %all-reduce.23 = (f32[1536]{0:T(1024)S(1)}, f32[256,4]{0,1:T(4,128)S(1)}, f32[256]{0:T(256)S(1)}, f32[1536]{0:T(1024)S(1)}) all-reduce(f32[1536]{0:T(1024)S(1)} %get-tuple-element.197, f32[256,4]{0,1:T(4,128)S(1)} %slice_bitcast_fusion, f32[256]{0:T(256)} %slice.123, ...), channel_id=7, replica_groups=mesh['seq'=2,'mp'=16] {'seq','mp'}, use_global_device_ids=true, to_apply=%region_30.31.clone | all-reduce | flops 4352 | bytes 34816
  961.4 127.1 %reduce-scatter.17.cloned.1.call-done = f32[48,1024]{1,0:T(8,128)} async-done(((f32[1536,1024]{1,0:T(8,128)}), f32[48,1024]{1,0:T(8,128)}) %reduce-scatter.17.cloned.1.call-update) | async-done | bytes 196624 | tf_op jit(solution)/shard_map/reduce_scatter | solution.py:502
  1088.5 148.8 %reduce-scatter.19.cloned.1.call-done = f32[48,1024]{1,0:T(8,128)} async-done(((f32[1536,1024]{1,0:T(8,128)}), f32[48,1024]{1,0:T(8,128)}) %reduce-scatter.19.cloned.1.call-update) | async-done | bytes 196624 | tf_op jit(solution)/shard_map/reduce_scatter | solution.py:503
  1237.3 120.9 %reduce-scatter.21.cloned.1.call-done = f32[32,1536]{1,0:T(8,128)} async-done(((f32[1024,1536]{1,0:T(8,128)}), f32[32,1536]{1,0:T(8,128)}) %reduce-scatter.21.cloned.1.call-update) | async-done | bytes 196624 | tf_op jit(solution)/shard_map/reduce_scatter | solution.py:504
  1358.2 102.1 %reduce-scatter.15.cloned.1.call-done = f32[48,256]{1,0:T(8,128)} async-done(((f32[1536,256]{1,0:T(8,128)}), f32[48,256]{1,0:T(8,128)}) %reduce-scatter.15.cloned.1.call-update) | async-done | bytes 49168 | tf_op jit(solution)/shard_map/reduce_scatter | solution.py:498
  (499 shorter events, 195.2 us)
Async XLA Ops:
  8.0 414.6 %copy-start = (bf16[1,512,1536]{2,1,0:T(8,128)(2,1)S(1)}, bf16[1,512,1536]{2,1,0:T(8,128)(2,1)}, u32[]{:S(2)}) copy-start(bf16[1,512,1536]{2,1,0:T(8,128)(2,1)} %param.51) | copy-start | bytes 4718596
  8.0 47.9 %copy-start.98 = (bf16[48,256]{1,0:T(8,128)(2,1)S(1)}, bf16[48,256]{1,0:T(8,128)(2,1)}, u32[]{:S(2)}) copy-start(bf16[48,256]{1,0:T(8,128)(2,1)} %param.34) | copy-start | bytes 73732
  8.1 247.8 %reduce-scatter.23.cloned.1.call-start = ((), (), s32[]{:S(2)}) async-start(), calls=%async_computation.21 | async-start | bytes 139264
  52.9 45.6 %copy-start.16 = (bf16[256,4,1536]{2,1,0:T(4,128)(2,1)S(1)}, bf16[256,4,1536]{2,1,0:T(4,128)(2,1)}, u32[]{:S(2)}) copy-start(bf16[256,4,1536]{2,1,0:T(4,128)(2,1)} %param.26) | copy-start | bytes 9437188
  52.9 93.4 %copy-start.83 = (f32[1536]{0:T(1024)}, f32[1536]{0:T(1024)S(1)}, u32[]{:S(2)}) copy-start(f32[1536]{0:T(1024)S(1)} %convert_element_type.124) | copy-start | bytes 18436
  55.9 90.5 %copy-start.126 = (f32[256,4]{0,1:T(4,128)}, f32[256,4]{0,1:T(4,128)S(1)}, u32[]{:S(2)}) copy-start(f32[256,4]{0,1:T(4,128)S(1)} %add_rsqrt_fusion) | copy-start | bytes 12292
  99.9 65.2 %copy-start.6 = (f32[256,4,256]{0,2,1:T(8,128)}, f32[256,4,256]{0,2,1:T(8,128)S(1)}, u32[]{:S(2)}) copy-start(f32[256,4,256]{0,2,1:T(8,128)S(1)} %fusion.86) | copy-start | bytes 3145732
  101.2 63.9 %copy-start.20 = (f32[256,4,192]{0,2,1:T(8,128)}, f32[256,4,192]{0,2,1:T(8,128)S(1)}, u32[]{:S(2)}) copy-start(f32[256,4,192]{0,2,1:T(8,128)S(1)} %fusion.105) | copy-start | bytes 2359300
  101.3 45.1 %copy-start.114 = (bf16[1536,3]{0,1:T(4,128)(2,1)S(1)}, bf16[1536,3]{0,1:T(4,128)(2,1)}, u32[]{:S(2)}) copy-start(bf16[1536,3]{0,1:T(4,128)(2,1)} %param.35) | copy-start | bytes 27652
  104.6 58.5 %collective-permute-start = (f32[3,4,448]{2,1,0:T(4,128)}, f32[3,4,448]{2,1,0:T(4,128)}, u32[]{:S(2)}, u32[]{:S(2)}) collective-permute-start(f32[3,4,448]{2,1,0:T(4,128)} %copy.289), channel_id=1, source_target_pairs={{0,16},{1,17},{2,18},{3,19},{4,20},{5,21},{6,22},{7,23},{8,24},{9,... | collective-permute-start | bytes 64520 | tf_op jit(solution)/shard_map/ppermute | solution.py:17
  149.3 17.8 %copy-start.79 = (f32[256,4,3]{0,2,1:T(4,128)}, f32[256,4,3]{0,2,1:T(4,128)S(1)}, u32[]{:S(2)}) copy-start(f32[256,4,3]{0,2,1:T(4,128)S(1)} %fusion.172) | copy-start | bytes 36868
  154.4 12.7 copy-start.74
  159.5 28.7 %copy-start.93 = (f32[4,3]{1,0:T(4,128)}, f32[4,3]{1,0:T(4,128)S(1)}, u32[]{:S(2)}) copy-start(f32[4,3]{1,0:T(4,128)S(1)} %get-tuple-element.271) | copy-start | bytes 148
  171.6 16.6 %copy-start.4 = (f32[256,4,448]{0,2,1:T(8,128)}, f32[256,4,448]{0,2,1:T(8,128)S(1)}, u32[]{:S(2)}) copy-start(f32[256,4,448]{0,2,1:T(8,128)S(1)} %get-tuple-element.244) | copy-start | bytes 5505028
  200.4 153.9 %reduce-scatter.11.cloned.1.call-start = ((), (), s32[]{:S(2)}) async-start(), calls=%async_computation.11 | async-start | bytes 6684672 | tf_op jit(solution)/shard_map/reduce_scatter | solution.py:238
  205.0 238.4 %all-gather.9.cloned.1.call-start = ((), (), s32[]{:S(2)}) async-start(), calls=%async_computation.12 | async-start | bytes 3244032 | tf_op jit(solution)/shard_map/all_gather | solution.py:104
  205.6 240.5 %all-gather.11.cloned.1.call-start = ((), (), s32[]{:S(2)}) async-start(), calls=%async_computation.13 | async-start | bytes 3244032 | tf_op jit(solution)/shard_map/all_gather | solution.py:105
  206.6 150.2 %copy-start.81 = (f32[1536]{0:T(1024)}, f32[1536]{0:T(1024)S(1)}, u32[]{:S(2)}) copy-start(f32[1536]{0:T(1024)S(1)} %convert_element_type.127) | copy-start | bytes 18436
  256.6 99.6 %copy-start.102 = (f32[16,4]{0,1:T(4,128)}, f32[16,4]{0,1:T(4,128)S(1)}, u32[]{:S(2)}) copy-start(f32[16,4]{0,1:T(4,128)S(1)} %copy.380) | copy-start | bytes 772
  256.6 99.6 %copy-start.99 = (f32[16,4]{0,1:T(4,128)}, f32[16,4]{0,1:T(4,128)S(1)}, u32[]{:S(2)}) copy-start(f32[16,4]{0,1:T(4,128)S(1)} %add_rsqrt_fusion.1) | copy-start | bytes 772
  356.6 143.6 %copy-start.26 = (f32[64,1536]{1,0:T(8,128)}, f32[64,1536]{1,0:T(8,128)S(1)}, u32[]{:S(2)}) copy-start(f32[64,1536]{1,0:T(8,128)S(1)} %reshape.399) | copy-start | bytes 1179652
  357.0 89.2 %copy-start.22 = (bf16[64,1536]{1,0:T(8,128)(2,1)}, bf16[64,1536]{1,0:T(8,128)(2,1)S(1)}, u32[]{:S(2)}) copy-start(bf16[64,1536]{1,0:T(8,128)(2,1)S(1)} %multiply_convert_fusion.4) | copy-start | bytes 589828
  360.8 52.6 %all-to-all-start = ((bf16[16,1,48,1536]{3,2,1,0:T(8,128)(2,1)}), bf16[16,1,48,1536]{3,2,1,0:T(8,128)(2,1)}, u32[]{:S(2)}, u32[]{:S(2)}) async-start(bf16[16,1,48,1536]{3,2,1,0:T(8,128)(2,1)} %bitcast.398), calls=%async_computation.1 | async-start | bytes 4718592 | tf_op jit(solution)/shard_map/all_to_all | solution.py:268
  365.5 134.7 %all-gather.13.cloned.1.call-start = ((), (), s32[]{:S(2)}) async-start(), calls=%async_computation.14 | async-start | bytes 3244032 | tf_op jit(solution)/shard_map/all_gather | solution.py:106
  425.5 16.7 %copy-start.113 = (f32[16,4,6]{0,1,2:T(4,128)S(1)}, f32[16,4,6]{0,1,2:T(4,128)}, u32[]{:S(2)}) copy-start(f32[16,4,6]{0,1,2:T(4,128)} %param.30) | copy-start | bytes 4612
  425.5 16.8 %copy-start.137 = (s32[4]{0:T(128)S(1)}, s32[4]{0:T(128)}, u32[]{:S(2)}) copy-start(s32[4]{0:T(128)} %param.28) | copy-start | bytes 52
  425.5 17.0 %copy-start.76 = (bf16[16,4,1536]{2,1,0:T(4,128)(2,1)S(1)}, bf16[16,4,1536]{2,1,0:T(4,128)(2,1)}, u32[]{:S(2)}) copy-start(bf16[16,4,1536]{2,1,0:T(4,128)(2,1)} %param.27) | copy-start | bytes 589828
  425.5 62.3 %all-to-all-start.1 = ((bf16[16,1,48,1536]{3,2,1,0:T(8,128)(2,1)}), bf16[16,1,48,1536]{3,2,1,0:T(8,128)(2,1)}, u32[]{:S(2)}, u32[]{:S(2)}) async-start(bf16[16,1,48,1536]{3,2,1,0:T(8,128)(2,1)} %fusion.10), calls=%async_computation.2 | async-start | bytes 4718592 | tf_op jit(solution)/shard_map/all_to_all | solution.py:279
  449.5 50.7 %copy-start.46 = (bf16[64,1024]{1,0:T(8,128)(2,1)}, bf16[64,1024]{1,0:T(8,128)(2,1)S(1)}, u32[]{:S(2)}) copy-start(bf16[64,1024]{1,0:T(8,128)(2,1)S(1)} %get-tuple-element.275) | copy-start | bytes 393220
  503.5 149.1 %copy-start.24 = (f32[64,1536]{1,0:T(8,128)}, f32[64,1536]{1,0:T(8,128)S(1)}, u32[]{:S(2)}) copy-start(f32[64,1536]{1,0:T(8,128)S(1)} %get-tuple-element.260) | copy-start | bytes 1179652
  514.9 67.3 %copy-start.52 = (f32[16,48,512]{2,1,0:T(8,128)S(1)}, f32[16,48,512]{2,1,0:T(8,128)}, u32[]{:S(2)}) copy-start(f32[16,48,512]{2,1,0:T(8,128)} %copy-done.51) | copy-start | bytes 4718596
  514.9 67.3 %copy-start.54 = (f32[16,48,512]{2,1,0:T(8,128)S(1)}, f32[16,48,512]{2,1,0:T(8,128)}, u32[]{:S(2)}) copy-start(f32[16,48,512]{2,1,0:T(8,128)} %copy-done.53) | copy-start | bytes 4718596
  589.1 49.8 %all-to-all-start.3 = ((bf16[16,1,48,1536]{3,2,1,0:T(8,128)(2,1)}), bf16[16,1,48,1536]{3,2,1,0:T(8,128)(2,1)S(1)}, u32[]{:S(2)}, u32[]{:S(2)}) async-start(bf16[16,1,48,1536]{3,2,1,0:T(8,128)(2,1)} %fusion.11), calls=%async_computation.4 | async-start | bytes 4718592 | tf_op jit(solution)/shard_map/all_to_all | solution.py:332
  593.2 116.4 %all-gather.15.cloned.1.call-start = ((), (), s32[]{:S(2)}) async-start(), calls=%async_computation.15 | async-start | bytes 3342336 | tf_op jit(solution)/shard_map/all_gather | solution.py:392
  652.6 57.0 %copy-start.5 = (f32[256,4,448]{0,2,1:T(8,128)S(1)}, f32[256,4,448]{0,2,1:T(8,128)}, u32[]{:S(2)}) copy-start(f32[256,4,448]{0,2,1:T(8,128)} %copy-done.4) | copy-start | bytes 5505028
  652.6 57.0 %copy-start.43 = (f32[256,4,192]{0,2,1:T(8,128)S(1)}, f32[256,4,192]{0,2,1:T(8,128)}, u32[]{:S(2)}) copy-start(f32[256,4,192]{0,2,1:T(8,128)} %copy-done.42) | copy-start | bytes 2359300
  652.6 57.0 %copy-start.129 = (f32[192]{0:T(256)S(1)}, f32[192]{0:T(256)}, u32[]{:S(2)}) copy-start(f32[192]{0:T(256)} %param.43) | copy-start | bytes 2308
  654.7 60.3 %copy-start.32 = (f32[16,4,1536]{2,1,0:T(4,128)}, f32[16,4,1536]{2,1,0:T(4,128)S(1)}, u32[]{:S(2)}) copy-start(f32[16,4,1536]{2,1,0:T(4,128)S(1)} %reshape.416) | copy-start | bytes 1179652
  656.8 257.2 %reduce-scatter.13.cloned.1.call-start = ((), (), s32[]{:S(2)}) async-start(), calls=%async_computation.16 | async-start | bytes 6684672 | tf_op jit(solution)/shard_map/reduce_scatter | solution.py:458
  742.5 51.1 %copy-start.3 = (f32[259,4,448]{0,2,1:T(8,128)S(1)}, f32[259,4,448]{0,2,1:T(8,128)}, u32[]{:S(2)}) copy-start(f32[259,4,448]{0,2,1:T(8,128)} %copy-done.2) | copy-start | bytes 5569540
  742.5 51.1 %copy-start.21 = (f32[256,4,192]{0,2,1:T(8,128)S(1)}, f32[256,4,192]{0,2,1:T(8,128)}, u32[]{:S(2)}) copy-start(f32[256,4,192]{0,2,1:T(8,128)} %copy-done.20) | copy-start | bytes 2359300
  801.8 14.0 collective-permute-start.1
  828.6 260.0 %reduce-scatter.17.cloned.1.call-start = ((), (), s32[]{:S(2)}) async-start(), calls=%async_computation.18 | async-start | bytes 6488064 | tf_op jit(solution)/shard_map/reduce_scatter | solution.py:502
  833.3 404.0 %reduce-scatter.19.cloned.1.call-start = ((), (), s32[]{:S(2)}) async-start(), calls=%async_computation.19 | async-start | bytes 6488064 | tf_op jit(solution)/shard_map/reduce_scatter | solution.py:503
  837.9 520.3 %reduce-scatter.21.cloned.1.call-start = ((), (), s32[]{:S(2)}) async-start(), calls=%async_computation.20 | async-start | bytes 6488064 | tf_op jit(solution)/shard_map/reduce_scatter | solution.py:504
  842.7 617.6 %reduce-scatter.15.cloned.1.call-start = ((), (), s32[]{:S(2)}) async-start(), calls=%async_computation.17 | async-start | bytes 1622016 | tf_op jit(solution)/shard_map/reduce_scatter | solution.py:498
  851.4 608.9 %all-reduce.29.cloned.1.call-start = ((), (), s32[]{:S(2)}) async-start(), calls=%async_computation.22 | async-start | bytes 25952256 | tf_op jit(solution)/shard_map/psum | solution.py:478
  874.3 83.6 %copy-start.33 = (f32[16,4,1536]{2,1,0:T(4,128)S(1)}, f32[16,4,1536]{2,1,0:T(4,128)}, u32[]{:S(2)}) copy-start(f32[16,4,1536]{2,1,0:T(4,128)} %copy-done.32) | copy-start | bytes 1179652
  (114 other events, 393.9 us)
Sparse Core Ops, SparseCore 0:
  200.6 55.2 reduce-scatter.22
  259.8 94.4 reduce-scatter.10
  656.9 52.6 all-gather.14
  828.7 85.2 reduce-scatter.12
  921.0 167.5 reduce-scatter.16
  1094.6 142.6 reduce-scatter.18
  1244.4 113.6 reduce-scatter.20
  1364.0 96.2 reduce-scatter.14
Sparse Core Ops, SparseCore 1:
  208.8 57.1 all-gather.8
  269.2 86.0 all-gather.10
  369.3 78.4 all-gather.12
  869.3 325.8 all-reduce.28
where the time goes:
time: 1490 us; the launch traced here: 1480 us
  waiting for transfers between devices  814 us (55%)
  blocking collectives  297 us (20%)
  matrix products  135 us (9%)
  other arithmetic  95.1 us (6%)
  local copies, waits for them, and re-layouts  90.3 us (6%)
  starting transfers between devices  32.1 us (2%)
  between operations  17.7 us (1%)
    reduce_scatter x1, waiting for transfers between devices, body(): lax.psum_scatter(shared_up_grad, ('seq', 'mp'), scatter_dimension=0, tile...  149 us
    reduce_scatter x1, waiting for transfers between devices, body(): lax.psum_scatter(shared_gate_grad, ('seq', 'mp'), scatter_dimension=0, ti...  127 us
    reduce_scatter x1, waiting for transfers between devices, body(): lax.psum_scatter(shared_down_grad, ('seq', 'mp'), scatter_dimension=0, ti...  121 us
    reduce_scatter x1, waiting for transfers between devices, body(): lax.psum_scatter(state_proj_grad, ('seq', 'mp'), scatter_dimension=0, til...  102 us
    reduce_scatter x1, waiting for transfers between devices, body(): lax.psum_scatter(mix_part, 'mp', scatter_dimension=0, tiled=True)  97.7 us
    unnamed x2, blocking collectives  82.8 us
    all_to_all x1, blocking collectives, body(): lax.all_to_all(grad_send, 'mp', split_axis=0, concat_axis=0, tiled=True)  67.3 us
    all_to_all x1, waiting for transfers between devices, body(): lax.all_to_all(send_rows, 'mp', split_axis=0, concat_axis=0, tiled=True)  47.3 us
  transfers between devices with their start and end apart: 17, of which 11 were waited for; matrix products, arithmetic and copies ran while one was open for 9% of the time, Pallas kernels for 0%

commit v1 on v0

v1 whole, which is shorter than its diff:
```python
import jax
import jax.numpy as jnp
from jax import lax
from jax.sharding import PartitionSpec as P

STATE = 128
INNER = 3072


epsilon = 1e-05
highest = lax.Precision.HIGHEST


def shifted(block, axis, distance):
    devices = range(lax.axis_size(axis))
    route = [(i - distance, i) for i in devices if i - distance in devices]
    return lax.ppermute(block, axis, route)


def entering_2(value, axis, join, neutral, backward):
    count, mine = (lax.axis_size(axis), lax.axis_index(axis))
    pieces = jax.tree.map(lambda part: lax.all_gather(part, axis), value)
    if backward:
        pieces = jax.tree.map(lambda part: part[::-1], pieces)
        mine = count - 1 - mine
    running = jax.tree.map(
        lambda part, zero: jnp.full_like(part, 0) + jnp.asarray(zero, part.dtype), value, neutral
    )

    def hop(position, running):
        longer = join(running, jax.tree.map(lambda part: part[position], pieces))
        return jax.tree.map(lambda new, old: jnp.where(position < mine, new, old), longer, running)

    return lax.fori_loop(0, count - 1, hop, running)


def rms_scale(values, gain):
    return values * lax.rsqrt(jnp.mean(values * values, axis=-1, keepdims=True) + epsilon) * gain


def silu_slope(values):
    sigmoid_val = jax.nn.sigmoid(values)
    return sigmoid_val * (1.0 + values * (1.0 - sigmoid_val))


def conv_decay(
    extended, conv_weight, conv_bias, step_raw, step_bias, decay_log, inner_width, state_width
):
    length = step_raw.shape[0]
    preact = conv_bias + conv_weight[0] * extended[0:length]
    for offset in range(1, conv_weight.shape[0]):
        preact = preact + conv_weight[offset] * extended[offset : offset + length]
    activated = jax.nn.silu(preact)
    head_count = step_raw.shape[-1]
    values = activated[..., :inner_width].reshape(
        length, activated.shape[1], head_count, inner_width // head_count
    )
    input_matrix_b = activated[..., inner_width : inner_width + state_width]
    c_matrix = activated[..., inner_width + state_width :]
    step_size = jax.nn.softplus(step_raw + step_bias)
    log_decay = -jnp.exp(decay_log) * step_size
    return (values, input_matrix_b, c_matrix, step_size, log_decay)


def ssd_output(values, input_matrix_b, c_matrix, step_size, log_decay, entering, skip_gain):
    cumulative = jnp.cumsum(log_decay, axis=0)
    length = cumulative.shape[0]
    causal = (jnp.arange(length)[:, None] >= jnp.arange(length)[None, :])[:, :, None, None]
    log_gap = jnp.where(causal, cumulative[:, None] - cumulative[None, :], 0.0)
    decay_mask = jnp.where(causal, jnp.exp(log_gap), 0.0)
    intersection = jnp.einsum("tbn,sbn->tsb", c_matrix, input_matrix_b, precision=highest)
    weighted = decay_mask * intersection[..., None]
    scaled = values * step_size[..., None]
    within = jnp.einsum("tsbh,sbhp->tbhp", weighted, scaled, precision=highest)
    carried = jnp.exp(cumulative)[..., None] * jnp.einsum(
        "tbn,bhpn->tbhp", c_matrix, entering, precision=highest
    )
    return within + carried + skip_gain[:, None] * values


def state_update(values, input_matrix_b, step_size, log_decay):
    cumulative = jnp.cumsum(log_decay, axis=0)
    decay_total = jnp.exp(cumulative[-1])
    tail_weight = jnp.exp(cumulative[-1] - cumulative) * step_size
    local_state = jnp.einsum(
        "sbh,sbhp,sbn->bhpn", tail_weight, values, input_matrix_b, precision=highest
    )
    return (decay_total, local_state)


def chain_combine(earlier, latter):
    return (earlier[0] * latter[0], latter[0][..., None, None] * earlier[1] + latter[1])


def bits(value):
    return value.astype(jnp.bfloat16)


def wide(value):
    return value.astype(jnp.float32)


def rounded(value):
    return lax.reduce_precision(value, 8, 7)


def mp_permute(value, target):
    count = lax.axis_size("mp")
    return lax.ppermute(value, "mp", [(i, target(i)) for i in range(count)])


def across_core(value):
    return mp_permute(value, lambda i: i ^ 1)


def across_pair(value):
    return mp_permute(value, lambda i: i ^ 2)


def ring_step(value, distance=1):
    count = lax.axis_size("mp")
    return mp_permute(value, lambda i: (i + 4 * distance) % count)


def coordinates():
    mine = lax.axis_index("mp")
    return mine // 4, (mine // 2) % 2, mine % 2


def pick(value, index, axis=0):
    return lax.dynamic_index_in_dim(value, index, axis, keepdims=False)


def gather_relative(block):
    ring = lax.axis_size("mp") // 4
    held, pairs = block, []
    for step in range(ring):
        pairs.append(jnp.stack([held, across_pair(held)]))
        if step < ring - 1:
            held = ring_step(held)
    own = jnp.stack(pairs)
    return own, across_core(own)


def relative_owner():
    ring = lax.axis_size("mp") // 4
    deep, pair, core = coordinates()
    cores = jnp.arange(2)[:, None, None]
    steps = jnp.arange(ring)[None, :, None]
    pairs = jnp.arange(2)[None, None, :]
    return ((deep - steps) % ring) * 4 + (pair ^ pairs) * 2 + (core ^ cores)


def scatter_relative(own, partner, kept=jnp.bfloat16):
    ring = lax.axis_size("mp") // 4
    half = (wide(own) + wide(across_core(partner))).astype(kept)
    order = list(range(1, ring)) + [0]
    received = {step: across_pair(half[step, 1]) for step in order}
    moving = None
    for step in range(1, ring):
        total = wide(half[step, 0]) + wide(received[step])
        if moving is not None:
            total = total + wide(moving)
        moving = ring_step(total.astype(kept))
    return wide(half[0, 0]) + wide(received[0]) + wide(moving)


def to_relative(value):
    ring = lax.axis_size("mp") // 4
    order = relative_owner()
    both = value[order.reshape(-1)].reshape((2, ring, 2) + value.shape[1:])
    return both[0], both[1]


def from_relative(own, partner):
    count = lax.axis_size("mp")
    order = relative_owner().reshape(-1)
    place = jnp.zeros((count,), jnp.int32).at[order].set(jnp.arange(count, dtype=jnp.int32))
    both = jnp.stack([own, partner])
    return both.reshape((count,) + both.shape[3:])[place]


def gather_small(block):
    ring = lax.axis_size("mp") // 4
    deep, pair, core = coordinates()
    both = [block, across_core(block)]
    rows = jnp.stack(both)
    rows = jnp.stack([rows, across_pair(rows)])
    turned = [rows] + [ring_step(rows, step) for step in range(1, ring)]
    every = jnp.stack(turned)
    count = lax.axis_size("mp")
    flat = every.reshape((count,) + block.shape)
    position = jnp.arange(count)
    steps = (deep - position // 4) % ring
    place = steps * 4 + (pair ^ ((position // 2) % 2)) * 2 + (core ^ (position % 2))
    return flat[place]


def seq_gather(value):
    if lax.axis_size("seq") != 2:
        return lax.all_gather(value, "seq")
    other = lax.ppermute(value, "seq", [(0, 1), (1, 0)])
    first = lax.axis_index("seq") == 0
    return jnp.stack([jnp.where(first, value, other), jnp.where(first, other, value)])


def seq_scatter(value):
    if lax.axis_size("seq") != 2:
        return lax.psum_scatter(wide(value), "seq", scatter_dimension=0, tiled=False)
    mine = lax.axis_index("seq")
    other = lax.ppermute(bits(pick(value, 1 - mine)), "seq", [(0, 1), (1, 0)])
    return wide(pick(value, mine)) + wide(other)


def seq_sum(value):
    if lax.axis_size("seq") != 2:
        return lax.psum(wide(value), "seq")
    low = bits(value)
    return wide(low) + wide(lax.ppermute(low, "seq", [(0, 1), (1, 0)]))


def seq_entering(decay, state, backward):
    if lax.axis_size("seq") == 2:
        route = [(1, 0)] if backward else [(0, 1)]
        return lax.ppermute(state, "seq", route)
    return entering_2(
        (decay, state),
        "seq",
        chain_combine,
        (jnp.ones_like(decay), jnp.zeros_like(state)),
        backward,
    )[1]


def mp_exchange(value):
    return lax.all_to_all(value, "mp", split_axis=0, concat_axis=0, tiled=True)


def body(
    tokens,
    target,
    lengths,
    routes,
    route_weight,
    in_gain,
    gate_proj,
    value_proj,
    state_proj,
    step_proj,
    conv_value,
    conv_value_bias,
    conv_state,
    conv_state_bias,
    step_bias,
    decay_log,
    skip_gain,
    mixer_gain,
    out_proj,
    ffn_gain,
    shared_gate,
    shared_up,
    shared_down,
    expert_gate,
    routed_up_weights,
    expert_down,
):
    mp_count = lax.axis_size("mp")
    slot_count, seq_count, model_width = tokens.shape
    seq_devices = lax.axis_size("seq")
    shared_expert_rows = slot_count // mp_count
    inner_width = gate_proj.shape[1]
    row_count = shared_expert_rows * seq_count
    window = conv_value.shape[0]
    gain_rows = in_gain.shape[0]
    state_rows = conv_state.shape[0]
    state_width = state_proj.shape[1]
    expert_count = expert_gate.shape[0] * mp_count

    packed = jnp.concatenate(
        [
            state_proj.reshape(-1),
            in_gain,
            ffn_gain,
            conv_state.reshape(-1),
            conv_state_bias,
        ]
    )
    route_rows = route_weight.reshape(row_count, -1)
    chosen = routes.reshape(row_count, -1, 1) == jnp.arange(expert_count, dtype=jnp.int32)
    coefficient = jnp.sum(jnp.where(chosen, route_rows[..., None], 0.0), axis=1)
    coefficient_high = rounded(coefficient)
    coefficient_low = coefficient - coefficient_high
    both_packed = seq_gather(packed)
    small = gather_small(
        jnp.concatenate(
            [
                both_packed.reshape(-1),
                bits(coefficient_high).reshape(-1),
                bits(coefficient_low).reshape(-1),
            ]
        )
    )
    width = packed.shape[0]
    weights_small = small[:, : seq_devices * width].reshape(mp_count, seq_devices, width)
    weights_small = jnp.moveaxis(weights_small, 1, 0).reshape(seq_devices * mp_count, width)
    cut = [gain_rows * state_width]
    for part in (gain_rows, gain_rows, conv_state.size):
        cut.append(cut[-1] + part)
    state_whole = weights_small[:, : cut[0]].reshape(-1, state_width)
    gain_first = weights_small[:, cut[0] : cut[1]].reshape(-1)
    gain_second = weights_small[:, cut[1] : cut[2]].reshape(-1)
    conv_state_whole = weights_small[:, cut[2] : cut[3]].reshape(-1, window)
    conv_bias_whole = weights_small[:, cut[3] :].reshape(-1)
    share = small[:, seq_devices * width :].reshape(mp_count, 2, row_count, expert_count)
    share = lax.dynamic_index_in_dim(share, lax.axis_index("mp"), 3, keepdims=False)
    share = wide(share[:, 0]) + wide(share[:, 1])
    share_own, share_partner = to_relative(share)

    columns = shared_gate.shape[1] // (seq_devices * mp_count)
    hidden_own = seq_devices * columns
    pair_cut = jnp.stack([shared_gate, shared_up]).reshape(2, gain_rows, seq_devices, mp_count, columns)
    pair_moved = mp_exchange(pair_cut.transpose(3, 0, 1, 2, 4).reshape(mp_count, -1))
    pair_all = seq_gather(pair_moved).reshape(
        seq_devices, mp_count, 2, gain_rows, hidden_own
    )
    pair_all = pair_all.transpose(2, 0, 1, 3, 4).reshape(2, model_width, hidden_own)
    gate_shared, up_shared = pair_all[0], pair_all[1]
    down_shared = seq_gather(shared_down).reshape(hidden_own, model_width)
    gate_weight, up_weight, down_weight = expert_gate[0], routed_up_weights[0], expert_down[0]

    inputs = tokens.astype(jnp.float32)
    normed = rms_scale(inputs, gain_first.astype(jnp.float32)).astype(jnp.bfloat16)
    gate_raw = jnp.dot(normed, gate_proj, preferred_element_type=jnp.float32)
    value_raw = jnp.dot(normed, value_proj, preferred_element_type=jnp.float32)
    state_raw = jnp.dot(normed, state_whole, preferred_element_type=jnp.float32)
    step_raw = jnp.dot(normed, step_proj, preferred_element_type=jnp.float32)
    conv_input = jnp.concatenate([value_raw, state_raw], axis=-1)
    edge_rows = shifted(conv_input[slot_count - window + 1 :], "seq", 1)
    extended = jnp.concatenate([edge_rows, conv_input], axis=0)
    conv_weight = jnp.concatenate([conv_value, conv_state_whole.astype(jnp.float32).T], axis=1)
    conv_bias = jnp.concatenate([conv_value_bias, conv_bias_whole.astype(jnp.float32)])

    def first_piece(ext_values, weight_values, bias_values, step_values, bias_step, decay_values):
        return conv_decay(
            ext_values,
            weight_values,
            bias_values,
            step_values,
            bias_step,
            decay_values,
            inner_width,
            STATE,
        )

    mixer_inputs, first_back = jax.vjp(
        first_piece, extended, conv_weight, conv_bias, step_raw, step_bias, decay_log
    )
    values, input_matrix_b, c_matrix, step_size, log_decay = mixer_inputs
    local_out, state_back = jax.vjp(state_update, values, input_matrix_b, step_size, log_decay)
    decay_total, local_state = local_out
    entering = seq_entering(decay_total, local_state, False)

    def second_piece(
        in_values,
        in_bmatrix,
        in_cmatrix,
        in_step,
        in_decay,
        in_state,
        in_skip,
        in_gate,
        in_gain_mix,
    ):
        result = ssd_output(in_values, in_bmatrix, in_cmatrix, in_step, in_decay, in_state, in_skip)
        gated_part = result.reshape(in_gate.shape) * jax.nn.silu(in_gate)
        return (gated_part, gated_part * in_gain_mix)

    gated_pair, second_back = jax.vjp(
        second_piece,
        values,
        input_matrix_b,
        c_matrix,
        step_size,
        log_decay,
        entering,
        skip_gain,
        gate_raw,
        mixer_gain,
    )
    gated_out, scaled = gated_pair
    scaled_low = scaled.astype(jnp.bfloat16)
    mix_part = jnp.dot(scaled_low, out_proj, preferred_element_type=jnp.float32)
    squares = jnp.sum(gated_out * gated_out, axis=-1)
    square_sum = jnp.sum(mp_exchange(squares.reshape(mp_count, row_count)), axis=0)
    mix_send = bits(mix_part).reshape(mp_count, row_count, model_width)
    pre_mix = scatter_relative(*to_relative(mix_send))
    inv_norm = lax.rsqrt(square_sum / INNER + epsilon)[:, None]
    start_row = lax.axis_index("mp") * shared_expert_rows
    own_inputs = lax.dynamic_slice_in_dim(inputs, start_row, shared_expert_rows, 0).reshape(
        row_count, model_width
    )
    hidden = own_inputs + pre_mix * inv_norm
    ffn_input = rms_scale(hidden, wide(gain_second)).astype(jnp.bfloat16)

    def dot(left, right):
        return jnp.dot(left, right, preferred_element_type=jnp.float32)

    def dot_t(left, right):
        return lax.dot_general(
            left, right, (((1,), (1,)), ((), ())), preferred_element_type=jnp.float32
        )

    def t_dot(left, right):
        return lax.dot_general(
            left, right, (((0,), (0,)), ((), ())), preferred_element_type=jnp.float32
        )

    rows_own, rows_partner = gather_relative(ffn_input)
    all_rows = jnp.stack([rows_own, rows_partner]).reshape(-1, model_width)
    shares = jnp.stack([share_own, share_partner]).reshape(-1, 1)
    gate_activation = dot(all_rows, gate_weight)
    up_val = dot(all_rows, up_weight)
    act_val = bits(jax.nn.silu(gate_activation) * up_val)
    shared_gate_val = dot(all_rows, gate_shared)
    shared_up_val = dot(all_rows, up_shared)
    shared_act = bits(jax.nn.silu(shared_gate_val) * shared_up_val)
    partial_out = shares * wide(bits(dot(act_val, down_weight))) + dot(shared_act, down_shared)

    def halves(value):
        cut_value = bits(value).reshape((2,) + rows_own.shape)
        return cut_value[0], cut_value[1]

    output = hidden + scatter_relative(*halves(partial_out))
    block_out = output.astype(jnp.bfloat16).reshape(shared_expert_rows, seq_count, model_width)
    position = (
        lax.axis_index("seq") * slot_count
        + start_row
        + jnp.arange(shared_expert_rows, dtype=jnp.int32)
    )
    valid_mask = (position[:, None] < lengths[None, :]).astype(jnp.float32).reshape(row_count, 1)
    grad_out = (output - target.astype(jnp.float32).reshape(row_count, model_width)) * valid_mask
    grad_own, grad_partner = gather_relative(bits(grad_out))
    all_grads = jnp.stack([grad_own, grad_partner]).reshape(-1, model_width)
    route_grads = bits(shares * wide(all_grads))
    activation_gradient = dot_t(route_grads, down_weight)
    egate_grad = bits(activation_gradient * up_val * silu_slope(gate_activation))
    expert_up_gradient = bits(activation_gradient * jax.nn.silu(gate_activation))
    shact_grad = dot_t(all_grads, down_shared)
    sgate_grad = bits(shact_grad * shared_up_val * silu_slope(shared_gate_val))
    sup_grad = bits(shact_grad * jax.nn.silu(shared_gate_val))
    partial_rows = (
        dot_t(egate_grad, gate_weight)
        + dot_t(expert_up_gradient, up_weight)
        + dot_t(sgate_grad, gate_shared)
        + dot_t(sup_grad, up_shared)
    )
    ffn_input_grad = scatter_relative(*halves(partial_rows))
    expert_down_grad = seq_sum(t_dot(act_val, route_grads))[None]
    expert_gate_grad = seq_sum(t_dot(all_rows, egate_grad))[None]
    expert_up_grad = seq_sum(t_dot(all_rows, expert_up_gradient))[None]
    shared_down_grad = seq_scatter(
        t_dot(shared_act, all_grads).reshape(seq_devices, columns, model_width)
    )
    pair_grad = jnp.stack([t_dot(all_rows, sgate_grad), t_dot(all_rows, sup_grad)])
    pair_grad = pair_grad.reshape(2, seq_devices, mp_count, gain_rows, hidden_own)
    pair_grad = seq_scatter(pair_grad.transpose(1, 2, 0, 3, 4))
    pair_grad = wide(mp_exchange(bits(pair_grad).reshape(mp_count, -1)))
    pair_grad = pair_grad.reshape(mp_count, 2, gain_rows, seq_devices, columns)
    pair_grad = pair_grad.transpose(1, 2, 3, 0, 4).reshape(2, gain_rows, -1)
    shared_gate_grad, shared_up_grad = pair_grad[0], pair_grad[1]

    _, second_norm_back = jax.vjp(rms_scale, hidden, wide(gain_second))
    hidden_part, ffn_gain_grad = second_norm_back(ffn_input_grad)
    hidden_grad_share = grad_out + hidden_part
    sum_grad_share = (
        jnp.sum(hidden_grad_share * pre_mix, axis=-1, keepdims=True)
        * (-0.5 / INNER)
        * inv_norm
        * inv_norm
        * inv_norm
    )
    sum_high = rounded(sum_grad_share)
    sum_low = sum_grad_share - sum_high
    mix_grad_send = jnp.concatenate(
        [
            bits(hidden_grad_share * inv_norm),
            bits(sum_high),
            bits(sum_low),
            jnp.zeros((row_count, 126), jnp.bfloat16),
        ],
        axis=-1,
    )
    mix_all = from_relative(*gather_relative(mix_grad_send))
    mix_all = mix_all.reshape(slot_count, seq_count, -1)
    mix_grad_all = mix_all[..., :model_width]
    sum_grad = wide(mix_all[..., model_width]) + wide(mix_all[..., model_width + 1])
    out_proj_grad = jnp.einsum(
        "sbc,sbd->cd", scaled_low, mix_grad_all, preferred_element_type=jnp.float32
    )
    scaled_grad = jnp.einsum(
        "sbd,cd->sbc", mix_grad_all, out_proj, preferred_element_type=jnp.float32
    )
    gated_grad = 2.0 * gated_out * sum_grad[..., None]
    (
        out_values_grad,
        out_bmatrix_grad,
        out_cmatrix_grad,
        out_step_grad,
        out_decay_grad,
        entering_grad,
        skip_gain_grad,
        gate_raw_grad,
        mixer_gain_grad,
    ) = second_back((gated_grad, scaled_grad))
    exit_grad = seq_entering(decay_total, entering_grad, True)
    total_grad = jnp.sum(entering * exit_grad, axis=(-2, -1))
    tail_values_grad, tail_bmatrix_grad, tail_step_grad, tail_decay_grad = state_back(
        (total_grad, exit_grad)
    )
    ext_grad, conv_weight_grad, conv_bias_grad, step_raw_grad, step_bias_grad, decay_log_grad = (
        first_back(
            (
                out_values_grad + tail_values_grad,
                out_bmatrix_grad + tail_bmatrix_grad,
                out_cmatrix_grad,
                out_step_grad + tail_step_grad,
                out_decay_grad + tail_decay_grad,
            )
        )
    )
    edge_grad = shifted(ext_grad[: window - 1], "seq", -1)
    conv_grad = ext_grad[window - 1 :] + jnp.concatenate(
        [jnp.zeros((slot_count - window + 1,) + ext_grad.shape[1:], jnp.float32), edge_grad], axis=0
    )
    conv_grad_low = conv_grad.astype(jnp.bfloat16)
    value_grad = conv_grad_low[..., :inner_width]
    state_grad = conv_grad_low[..., inner_width:]
    gate_grad = gate_raw_grad.astype(jnp.bfloat16)
    step_grad = step_raw_grad.astype(jnp.bfloat16)
    partial_value = jnp.einsum(
        "sbc,dc->sbd", gate_grad, gate_proj, preferred_element_type=jnp.float32
    )
    partial_value = partial_value + jnp.einsum(
        "sbc,dc->sbd", value_grad, value_proj, preferred_element_type=jnp.float32
    )
    partial_value = partial_value + jnp.einsum(
        "sbc,dc->sbd", state_grad, state_whole, preferred_element_type=jnp.float32
    )
    partial_value = partial_value + jnp.einsum(
        "sbh,dh->sbd", step_grad, step_proj, preferred_element_type=jnp.float32
    )
    gate_proj_grad = jnp.einsum(
        "sbd,sbc->dc", normed, gate_grad, preferred_element_type=jnp.float32
    )
    value_proj_grad = jnp.einsum(
        "sbd,sbc->dc", normed, value_grad, preferred_element_type=jnp.float32
    )
    state_proj_grad = jnp.einsum(
        "sbd,sbc->dc", normed, state_grad, preferred_element_type=jnp.float32
    )
    step_proj_grad = jnp.einsum(
        "sbd,sbh->dh", normed, step_grad, preferred_element_type=jnp.float32
    )
    conv_value_grad = conv_weight_grad[:, :inner_width]
    conv_state_grad = conv_weight_grad[:, inner_width:].T
    conv_value_bias_grad = conv_bias_grad[:inner_width]
    conv_state_bias_grad = conv_bias_grad[inner_width:]
    whole_width = lax.rsqrt(jnp.mean(inputs * inputs, axis=-1, keepdims=True) + epsilon)
    in_gain_grad = jnp.sum(partial_value * inputs * whole_width, axis=(0, 1))

    def by_owner(value):
        parts = value.reshape((seq_devices, mp_count, -1))
        return jnp.moveaxis(parts, 1, 0).reshape(mp_count, -1)

    extra = jnp.concatenate(
        [
            by_owner(state_proj_grad),
            by_owner(in_gain_grad),
            by_owner(ffn_gain_grad),
        ],
        axis=-1,
    )
    extra_rows = -(-extra.shape[1] // (8 * model_width)) * 8
    extra_size = extra.shape[1]
    extra = jnp.pad(extra, ((0, 0), (0, extra_rows * model_width - extra_size)))
    last_send = jnp.concatenate(
        [
            bits(partial_value).reshape(mp_count, row_count, model_width),
            bits(extra).reshape(mp_count, extra_rows, model_width),
        ],
        axis=1,
    )
    last_sum = scatter_relative(*to_relative(last_send))
    normed_grad = last_sum[:row_count]
    extra_sum = last_sum[row_count:].reshape(-1)[:extra_size]
    _, first_norm_back = jax.vjp(rms_scale, own_inputs, wide(gain_first))
    tokens_grad = (first_norm_back(normed_grad)[0] + hidden_grad_share).reshape(
        shared_expert_rows, seq_count, model_width
    )
    sizes = [gain_rows * state_width, gain_rows, gain_rows]
    parts, at = [], 0
    for size in sizes:
        parts.append(extra_sum[at : at + seq_devices * size].reshape(seq_devices, size))
        at += seq_devices * size
    extra_own = seq_scatter(jnp.concatenate(parts, axis=-1))
    state_proj_out = extra_own[: sizes[0]].reshape(gain_rows, state_width)
    at = sizes[0]
    in_gain_out = extra_own[at : at + gain_rows]
    at += gain_rows
    ffn_gain_out = extra_own[at : at + gain_rows]
    conv_small = jnp.concatenate(
        [
            conv_state_grad.reshape(seq_devices, mp_count, -1),
            conv_state_bias_grad.reshape(seq_devices, mp_count, -1),
        ],
        axis=-1,
    )
    conv_small = jnp.moveaxis(conv_small, 1, 0).reshape(mp_count, -1)
    conv_small = jnp.sum(mp_exchange(conv_small), axis=0)
    exact = (
        step_proj_grad,
        conv_value_grad,
        conv_value_bias_grad,
        step_bias_grad,
        decay_log_grad,
        skip_gain_grad,
        mixer_gain_grad,
        conv_small.reshape(seq_devices, -1),
    )
    flat = jnp.concatenate([part.reshape(-1) for part in exact])
    if seq_devices == 2:
        flat = flat + lax.ppermute(flat, "seq", [(0, 1), (1, 0)])
    else:
        flat = lax.psum(flat, "seq")
    exact_out, at = [], 0
    for part in exact:
        exact_out.append(flat[at : at + part.size].reshape(part.shape))
        at += part.size
    conv_own = pick(exact_out[7], lax.axis_index("seq"))
    conv_state_out = conv_own[: state_rows * window].reshape(state_rows, window)
    conv_state_bias_out = conv_own[state_rows * window :]
    return (
        block_out,
        tokens_grad,
        in_gain_out,
        seq_sum(gate_proj_grad),
        seq_sum(value_proj_grad),
        state_proj_out,
        exact_out[0],
        exact_out[1],
        exact_out[2],
        conv_state_out,
        conv_state_bias_out,
        exact_out[3],
        exact_out[4],
        exact_out[5],
        exact_out[6],
        seq_sum(out_proj_grad),
        ffn_gain_out,
        shared_gate_grad,
        shared_up_grad,
        shared_down_grad,
        expert_gate_grad,
        expert_up_grad,
        expert_down_grad,
    )


def solution(mesh):
    placed = (
        P("seq", None, None),
        P(("seq", "mp"), None, None),
        P(),
        P(("seq", "mp"), None, None),
        P(("seq", "mp"), None, None),
        P(("seq", "mp")),
        P(None, "mp"),
        P(None, "mp"),
        P(("seq", "mp"), None),
        P(None, "mp"),
        P(None, "mp"),
        P("mp"),
        P(("seq", "mp"), None),
        P(("seq", "mp")),
        P("mp"),
        P("mp"),
        P("mp"),
        P("mp"),
        P("mp", None),
        P(("seq", "mp")),
        P(("seq", "mp"), None),
        P(("seq", "mp"), None),
        P(("seq", "mp"), None),
        P("mp", None, None),
        P("mp", None, None),
        P("mp", None, None),
    )
    return jax.shard_map(
        body,
        mesh=mesh,
        in_specs=placed,
        out_specs=(
            P(("seq", "mp"), None, None),
            P(("seq", "mp"), None, None),
            P(("seq", "mp")),
            P(None, "mp"),
            P(None, "mp"),
            P(("seq", "mp"), None),
            P(None, "mp"),
            P(None, "mp"),
            P("mp"),
            P(("seq", "mp"), None),
            P(("seq", "mp")),
            P("mp"),
            P("mp"),
            P("mp"),
            P("mp"),
            P("mp", None),
            P(("seq", "mp")),
            P(("seq", "mp"), None),
            P(("seq", "mp"), None),
            P(("seq", "mp"), None),
            P("mp", None, None),
            P("mp", None, None),
            P("mp", None, None),
        ),
        check_vma=False,
    )
```

time: 1490 us -> 743 us (0.50)
  waiting for transfers between devices: 814 us -> 197 us
  blocking collectives: 297 us -> 0 us
  local copies, waits for them, and re-layouts: 90.3 us -> 168 us
  starting transfers between devices: 32.1 us -> 95.7 us
  other arithmetic: 95.1 us -> 156 us
  matrix products: 135 us -> 112 us
    reduce_scatter x6 -> x0, waiting for transfers between devices: 622 us -> none  [the longest x1 149 us: body(): lax.psum_scatter(shared_up_grad, ('seq', 'mp'), scatter_dimension=0, tile...]
    ppermute x0 -> x76, waiting for transfers between devices: none -> 190 us  [the longest x61 155 us: mp_permute(): return lax.ppermute(value, 'mp', [(i, target(i)) for i in range(count)])]
    all_gather x6 -> x0, blocking collectives: 135 us -> none  [the longest x1 42.6 us: gather_shared(): lax.all_gather(state_proj, ('seq', 'mp'), axis=0, tiled=True)]
    all_to_all x3 -> x4, waiting for transfers between devices: 128 us -> 7.22 us  [mp_exchange(): return lax.all_to_all(value, 'mp', split_axis=0, concat_axis=0, tiled=True)]
    unnamed x2 -> x0, blocking collectives: 82.8 us -> none
    ppermute x0 -> x76, starting transfers between devices: none -> 68.5 us  [the longest x61 46.7 us: mp_permute(): return lax.ppermute(value, 'mp', [(i, target(i)) for i in range(count)])]
    all_to_all x1 -> x0, blocking collectives: 67.3 us -> none  [body(): lax.all_to_all(grad_send, 'mp', split_axis=0, concat_axis=0, tiled=True)]
    unnamed x13 -> x0, waiting for transfers between devices: 40.7 us -> none
  transfers between devices with their start and end apart: 17 -> 82, of which waited for: 11 -> 43; matrix products, arithmetic and copies ran while one was open for 9% -> 31% of each run, Pallas kernels for 0% -> 0%
where the time goes in v1:
time: 743 us; the launch traced here: 732 us
  waiting for transfers between devices  197 us (27%)
  local copies, waits for them, and re-layouts  168 us (23%)
  other arithmetic  156 us (21%)
  matrix products  112 us (15%)
  starting transfers between devices  95.7 us (13%)
    ppermute x61, waiting for transfers between devices, mp_permute(): return lax.ppermute(value, 'mp', [(i, target(i)) for i in range(count)])  155 us
    ppermute x61, starting transfers between devices, mp_permute(): return lax.ppermute(value, 'mp', [(i, target(i)) for i in range(count)])  46.7 us
    another operation x8, other arithmetic  34.1 us
    unnamed x313, local copies, waits for them, and re-layouts  26.6 us
    ppermute x6, waiting for transfers between devices, seq_sum(): return wide(low) + wide(lax.ppermute(low, 'seq', [(0, 1), (1, 0)]))  24.3 us
    all_to_all x4, starting transfers between devices, mp_exchange(): return lax.all_to_all(value, 'mp', split_axis=0, concat_axis=0, tiled=True)  23 us
  transfers between devices with their start and end apart: 82, of which 43 were waited for; matrix products, arithmetic and copies ran while one was open for 31% of the time, Pallas kernels for 0%

profile of v1, /device:TPU:0, one launch (start us, length us, event | category | flops | bytes accessed | tf_op | source)
XLA Modules:
  0.0 732.3 jit_solution(17451883932742116036)
XLA Ops:
  26.1 4.5 collective-permute-done.5
  30.6 12.0 %collective-permute-done.4 = bf16[2,2,26896]{2,1,0:T(2,128)(2,1)S(1)} collective-permute-done((bf16[2,2,26896]{2,1,0:T(2,128)(2,1)S(1)}, bf16[2,2,26896]{2,1,0:T(2,128)(2,1)S(1)}, u32[]{:S(2)}, u32[]{:S(2)}) %collective-permute-start.4) | collective-permute-done | bytes 215200 | tf_op jit(solution)/shard_map/ppermute | solution.py:109
  77.8 4.4 fusion.36
  95.6 5.7 multiply_add_fusion.3
  106.3 4.1 copy.515
  110.4 6.1 reshape.921
  116.5 4.4 gather_fusion.1
  138.6 5.8 all-to-all-start.1
  185.1 6.3 all-to-all-start
  193.6 4.1 all-to-all-done
  200.2 4.5 collective-permute-done.9
  211.0 5.8 collective-permute-done.17
  218.3 6.0 collective-permute-done.19
  226.3 5.9 collective-permute-done.21
  233.7 4.2 collective-permute-done.22
  269.2 5.7 collective-permute-done.30
  284.8 6.3 collective-permute-done.32
  303.8 6.9 collective-permute-done.35
  312.2 8.1 %collective-permute-done.37 = bf16[64,1536]{1,0:T(8,128)(2,1)S(1)} collective-permute-done((bf16[64,1536]{1,0:T(8,128)(2,1)S(1)}, bf16[64,1536]{1,0:T(8,128)(2,1)S(1)}, u32[]{:S(2)}, u32[]{:S(2)}) %collective-permute-start.37) | collective-permute-done | bytes 196640 | tf_op jit(solution)/shard_map/ppermute | solution.py:109
  321.8 6.0 collective-permute-done.39
  329.2 4.2 collective-permute-done.40
  344.6 4.8 copy.558
  361.6 4.4 fusion.40
  389.3 5.0 collective-permute-done.46
  407.1 5.2 all-to-all-start.3
  442.1 5.7 collective-permute-done.53
  449.2 8.0 %collective-permute-done.55 = bf16[64,1664]{1,0:T(8,128)(2,1)S(1)} collective-permute-done((bf16[64,1664]{1,0:T(8,128)(2,1)S(1)}, bf16[64,1664]{1,0:T(8,128)(2,1)S(1)}, u32[]{:S(2)}, u32[]{:S(2)}) %collective-permute-start.55) | collective-permute-done | bytes 213024 | tf_op jit(solution)/shard_map/ppermute | solution.py:109
  457.3 7.5 %collective-permute-done.56 = bf16[64,1664]{1,0:T(8,128)(2,1)S(1)} collective-permute-done((bf16[64,1664]{1,0:T(8,128)(2,1)S(1)}, bf16[64,1664]{1,0:T(8,128)(2,1)S(1)}, u32[]{:S(2)}, u32[]{:S(2)}) %collective-permute-start.56) | collective-permute-done | bytes 213024 | tf_op jit(solution)/shard_map/ppermute | solution.py:109
  470.9 4.1 add_bitcast_fusion.1
  475.0 24.3 %collective-permute-done.77 = bf16[512,1536]{1,0:T(8,128)(2,1)} collective-permute-done((bf16[512,1536]{1,0:T(8,128)(2,1)}, bf16[512,1536]{1,0:T(8,128)(2,1)}, u32[]{:S(2)}, u32[]{:S(2)}) %collective-permute-start.77) | collective-permute-done | bytes 1572896 | tf_op jit(solution)/shard_map/ppermute | solution.py:219
  508.7 4.7 gather_fusion.3
  513.4 6.8 reshape.930
  521.5 4.7 slice.526
  526.6 4.9 multiply_reduce_fusion.8
  534.3 5.3 fusion.32
  565.3 15.1 %reduce-window.26 = f32[3,4,2,128]{3,2,1,0:T(2,128)S(1)} reduce-window(f32[3,4,2,128]{3,2,1,0:T(2,128)S(1)} %copy.542, f32[]{:T(128)} %constant.220.clone.1), window={size=1x1x1x128 pad=0_0x0_0x0_0x0_127}, to_apply=%region_19.20 | reduce-window | flops 390144 | bytes 24580 | tf_op jit(solution)/shard_map/reduce-window.4
  580.5 15.1 %reduce-window.24 = f32[3,4,2,128]{3,2,1,0:T(2,128)S(1)} reduce-window(f32[3,4,2,128]{3,2,1,0:T(2,128)S(1)} %copy.536, f32[]{:T(128)} %constant.220.clone.1), window={size=1x1x1x128 pad=0_0x0_0x0_0x0_127}, to_apply=%region_15.16 | reduce-window | flops 390144 | bytes 24580 | tf_op jit(solution)/shard_map/reduce-window.2
  607.1 4.1 fusion.24
  615.7 7.5 %fusion.221 = (bf16[256,4,1536]{2,0,1:T(8,128)(2,1)}, bf16[1536]{0:T(1024)(128)(2,1)S(1)}) fusion(f32[256,4]{0,1:T(4,128)S(1)} %copy-done.108, bf16[256,4,1536]{2,1,0:T(4,128)(2,1)S(1)} %copy-done.9, f32[256,4,1536]{2,0,1:T(8,128)} %fusion.180, f32[256,4,1536]{2,0,1:T(8,128)S(1)} %fusion.118, f32[256,4,1536]{2,0,1:T(8,128)} %fusion.100, ...), kind=kOutput, calls=%fused_computation.484 | convolution fusion | flops 616561152 | bytes 26156032 | tf_op jit(solution)/shard_map/sbc,dc->sbd/dot_general | solution.py:543
  628.2 4.1 copy.546
  632.3 4.5 reshape.938
  640.5 5.1 gather_fusion.4
  645.6 4.8 fusion.222
  656.7 5.7 all-to-all-start.2
  670.9 4.3 fusion.26
  675.2 7.5 %collective-permute-done.71 = f32[5849]{0:T(1024)S(1)} collective-permute-done((f32[5849]{0:T(1024)S(1)}, f32[5849]{0:T(1024)S(1)}, u32[]{:S(2)}, u32[]{:S(2)}) %collective-permute-start.71) | collective-permute-done | bytes 23428 | tf_op jit(solution)/shard_map/ppermute | solution.py:632
  711.1 4.1 collective-permute-done.66
  717.9 5.7 collective-permute-done.67
  (772 shorter events, 424.9 us)
Async XLA Ops:
  4.5 9.1 %collective-permute-start = (bf16[12424]{0:T(1024)(128)(2,1)S(1)}, bf16[12424]{0:T(1024)(128)(2,1)S(1)}, u32[]{:S(2)}, u32[]{:S(2)}) collective-permute-start(bf16[12424]{0:T(1024)(128)(2,1)S(1)} %concatenate.43), channel_id=1, source_target_pairs={{0,16},{16,0},{1,17},{17,1},{2,18},{18,2},{3,19},{19,3},{4,20},{20... | collective-permute-start | bytes 74552 | tf_op jit(solution)/shard_map/ppermute | solution.py:202
  21.2 9.5 %collective-permute-start.5 = (bf16[2,2,26896]{2,1,0:T(2,128)(2,1)S(1)}, bf16[2,2,26896]{2,1,0:T(2,128)(2,1)S(1)}, u32[]{:S(2)}, u32[]{:S(2)}) collective-permute-start(bf16[2,2,26896]{2,1,0:T(2,128)(2,1)S(1)} %pad_maximum_fusion.9), channel_id=1, source_target_pairs={{0,12},{1,13},{2,14},{3,15},{4,0},{5,1},{6,2},{7,3},{8,4},{9,5},{1... | collective-permute-start | bytes 645512 | tf_op jit(solution)/shard_map/ppermute | solution.py:109
  24.8 17.9 %collective-permute-start.4 = (bf16[2,2,26896]{2,1,0:T(2,128)(2,1)S(1)}, bf16[2,2,26896]{2,1,0:T(2,128)(2,1)S(1)}, u32[]{:S(2)}, u32[]{:S(2)}) collective-permute-start(bf16[2,2,26896]{2,1,0:T(2,128)(2,1)S(1)} %pad_maximum_fusion.9), channel_id=1, source_target_pairs={{0,8},{1,9},{2,10},{3,11},{4,12},{5,13},{6,14},{7,15},{8,0},{9,1},... | collective-permute-start | bytes 645512 | tf_op jit(solution)/shard_map/ppermute | solution.py:109
  24.8 17.9 %collective-permute-start.3 = (bf16[2,2,26896]{2,1,0:T(2,128)(2,1)S(1)}, bf16[2,2,26896]{2,1,0:T(2,128)(2,1)S(1)}, u32[]{:S(2)}, u32[]{:S(2)}) collective-permute-start(bf16[2,2,26896]{2,1,0:T(2,128)(2,1)S(1)} %pad_maximum_fusion.9), channel_id=1, source_target_pairs={{0,4},{1,5},{2,6},{3,7},{4,8},{5,9},{6,10},{7,11},{8,12},{9,13},{1... | collective-permute-start | bytes 645512 | tf_op jit(solution)/shard_map/ppermute | solution.py:109
  60.2 14.3 %collective-permute-start.6 = (f32[3,4,448]{2,1,0:T(4,128)S(1)}, f32[3,4,448]{2,1,0:T(4,128)S(1)}, u32[]{:S(2)}, u32[]{:S(2)}) collective-permute-start(f32[3,4,448]{2,1,0:T(4,128)S(1)} %copy.497), channel_id=1, source_target_pairs={{0,16},{1,17},{2,18},{3,19},{4,20},{5,21},{6,22},{7,23},{8,24},{9,... | collective-permute-start | bytes 64520 | tf_op jit(solution)/shard_map/ppermute | solution.py:17
  124.8 29.5 %collective-permute-start.8 = (bf16[4,2,64,1536]{3,2,1,0:T(8,128)(2,1)}, bf16[4,2,64,1536]{3,2,1,0:T(8,128)(2,1)}, u32[]{:S(2)}, u32[]{:S(2)}) collective-permute-start(bf16[4,2,64,1536]{3,2,1,0:T(8,128)(2,1)} %bitcast.35), channel_id=1, source_target_pairs={{0,1},{1,0},{2,3},{3,2},{4,5},{5,4},{6,7},{7,6},{8,9},{9,8},{10,11... | collective-permute-start | bytes 4718600 | tf_op jit(solution)/shard_map/ppermute | solution.py:109
  138.6 22.7 %all-to-all-start.1 = ((bf16[16,2,3072]{2,1,0:T(2,128)(2,1)}), bf16[16,2,3072]{2,1,0:T(2,128)(2,1)}, u32[]{:S(2)}, u32[]{:S(2)}) async-start(bf16[16,2,3072]{2,1,0:T(2,128)(2,1)} %reshape.1071), calls=%async_computation.1 | async-start | bytes 393216 | tf_op jit(solution)/shard_map/all_to_all | solution.py:236
  144.3 9.0 %collective-permute-start.25 = (bf16[32,1536]{1,0:T(8,128)(2,1)S(1)}, bf16[32,1536]{1,0:T(8,128)(2,1)}, u32[]{:S(2)}, u32[]{:S(2)}) collective-permute-start(bf16[32,1536]{1,0:T(8,128)(2,1)S(1)} %copy-done.82), channel_id=1, source_target_pairs={{0,16},{16,0},{1,17},{17,1},{2,18},{18,2},{3,19},{19,3},{4,20},{20... | collective-permute-start | bytes 294920 | tf_op jit(solution)/shard_map/ppermute | solution.py:202
  158.6 12.3 %collective-permute-start.12 = (bf16[64,1536]{1,0:T(8,128)(2,1)}, bf16[64,1536]{1,0:T(8,128)(2,1)}, u32[]{:S(2)}, u32[]{:S(2)}) collective-permute-start(bf16[64,1536]{1,0:T(8,128)(2,1)} %get-tuple-element.281), channel_id=1, source_target_pairs={{0,2},{1,3},{2,0},{3,1},{4,6},{5,7},{6,4},{7,5},{8,10},{9,11},{10,... | collective-permute-start | bytes 589832 | tf_op jit(solution)/shard_map/ppermute | solution.py:109
  165.2 74.6 %collective-permute-start.24 = (bf16[16,6144]{1,0:T(8,128)(2,1)}, bf16[16,6144]{1,0:T(8,128)(2,1)}, u32[]{:S(2)}, u32[]{:S(2)}) collective-permute-start(bf16[16,6144]{1,0:T(8,128)(2,1)} %bitcast.595), channel_id=1, source_target_pairs={{0,16},{16,0},{1,17},{17,1},{2,18},{18,2},{3,19},{19,3},{4,20},{20... | collective-permute-start | bytes 589832 | tf_op jit(solution)/shard_map/ppermute | solution.py:202
  175.3 23.1 %collective-permute-start.10 = (bf16[64,1536]{1,0:T(8,128)(2,1)}, bf16[64,1536]{1,0:T(8,128)(2,1)}, u32[]{:S(2)}, u32[]{:S(2)}) collective-permute-start(bf16[64,1536]{1,0:T(8,128)(2,1)} %get-tuple-element.283), channel_id=1, source_target_pairs={{0,2},{1,3},{2,0},{3,1},{4,6},{5,7},{6,4},{7,5},{8,10},{9,11},{10,... | collective-permute-start | bytes 589832 | tf_op jit(solution)/shard_map/ppermute | solution.py:109
  183.0 15.4 %collective-permute-start.14 = (bf16[64,1536]{1,0:T(8,128)(2,1)}, bf16[64,1536]{1,0:T(8,128)(2,1)}, u32[]{:S(2)}, u32[]{:S(2)}) collective-permute-start(bf16[64,1536]{1,0:T(8,128)(2,1)} %fusion.146), channel_id=1, source_target_pairs={{0,4},{1,5},{2,6},{3,7},{4,8},{5,9},{6,10},{7,11},{8,12},{9,13},{1... | collective-permute-start | bytes 589832 | tf_op jit(solution)/shard_map/ppermute | solution.py:109
  185.1 12.6 %all-to-all-start = ((f32[16,1,64]{2,1,0:T(1,128)}), f32[16,1,64]{2,1,0:T(1,128)S(1)}, u32[]{:S(2)}, u32[]{:S(2)}) async-start(f32[16,1,64]{2,1,0:T(1,128)} %bitcast.680), calls=%async_computation | async-start | bytes 16384 | tf_op jit(solution)/shard_map/all_to_all | solution.py:236
  209.4 8.9 %collective-permute-start.16 = (bf16[64,1536]{1,0:T(8,128)(2,1)S(1)}, bf16[64,1536]{1,0:T(8,128)(2,1)S(1)}, u32[]{:S(2)}, u32[]{:S(2)}) collective-permute-start(bf16[64,1536]{1,0:T(8,128)(2,1)S(1)} %multiply_convert_fusion.11), channel_id=1, source_target_pairs={{0,2},{1,3},{2,0},{3,1},{4,6},{5,7},{6,4},{7,5},{8,10},{9,11},{10,... | collective-permute-start | bytes 589832 | tf_op jit(solution)/shard_map/ppermute | solution.py:109
  216.8 9.4 %collective-permute-start.18 = (bf16[64,1536]{1,0:T(8,128)(2,1)S(1)}, bf16[64,1536]{1,0:T(8,128)(2,1)S(1)}, u32[]{:S(2)}, u32[]{:S(2)}) collective-permute-start(bf16[64,1536]{1,0:T(8,128)(2,1)S(1)} %collective-permute-done.17), channel_id=1, source_target_pairs={{0,2},{1,3},{2,0},{3,1},{4,6},{5,7},{6,4},{7,5},{8,10},{9,11},{10,... | collective-permute-start | bytes 589832 | tf_op jit(solution)/shard_map/ppermute | solution.py:109
  268.6 10.5 %collective-permute-start.29 = (bf16[64,1536]{1,0:T(8,128)(2,1)S(1)}, bf16[64,1536]{1,0:T(8,128)(2,1)S(1)}, u32[]{:S(2)}, u32[]{:S(2)}) collective-permute-start(bf16[64,1536]{1,0:T(8,128)(2,1)S(1)} %get-tuple-element.276), channel_id=1, source_target_pairs={{0,2},{1,3},{2,0},{3,1},{4,6},{5,7},{6,4},{7,5},{8,10},{9,11},{10,... | collective-permute-start | bytes 589832 | tf_op jit(solution)/shard_map/ppermute | solution.py:109
  275.0 9.8 %collective-permute-start.28 = (bf16[64,1536]{1,0:T(8,128)(2,1)}, bf16[64,1536]{1,0:T(8,128)(2,1)}, u32[]{:S(2)}, u32[]{:S(2)}) collective-permute-start(bf16[64,1536]{1,0:T(8,128)(2,1)} %get-tuple-element.277), channel_id=1, source_target_pairs={{0,2},{1,3},{2,0},{3,1},{4,6},{5,7},{6,4},{7,5},{8,10},{9,11},{10,... | collective-permute-start | bytes 589832 | tf_op jit(solution)/shard_map/ppermute | solution.py:109
  283.3 14.0 %collective-permute-start.27 = (bf16[64,1536]{1,0:T(8,128)(2,1)}, bf16[64,1536]{1,0:T(8,128)(2,1)}, u32[]{:S(2)}, u32[]{:S(2)}) collective-permute-start(bf16[64,1536]{1,0:T(8,128)(2,1)} %get-tuple-element.274), channel_id=1, source_target_pairs={{0,2},{1,3},{2,0},{3,1},{4,6},{5,7},{6,4},{7,5},{8,10},{9,11},{10,... | collective-permute-start | bytes 589832 | tf_op jit(solution)/shard_map/ppermute | solution.py:109
  302.3 9.9 %collective-permute-start.34 = (bf16[64,1536]{1,0:T(8,128)(2,1)S(1)}, bf16[64,1536]{1,0:T(8,128)(2,1)S(1)}, u32[]{:S(2)}, u32[]{:S(2)}) collective-permute-start(bf16[64,1536]{1,0:T(8,128)(2,1)S(1)} %fusion.167), channel_id=1, source_target_pairs={{0,2},{1,3},{2,0},{3,1},{4,6},{5,7},{6,4},{7,5},{8,10},{9,11},{10,... | collective-permute-start | bytes 589832 | tf_op jit(solution)/shard_map/ppermute | solution.py:109
  310.7 9.6 %collective-permute-start.37 = (bf16[64,1536]{1,0:T(8,128)(2,1)S(1)}, bf16[64,1536]{1,0:T(8,128)(2,1)S(1)}, u32[]{:S(2)}, u32[]{:S(2)}) collective-permute-start(bf16[64,1536]{1,0:T(8,128)(2,1)S(1)} %collective-permute-done.35), channel_id=1, source_target_pairs={{0,4},{1,5},{2,6},{3,7},{4,8},{5,9},{6,10},{7,11},{8,12},{9,13},{1... | collective-permute-start | bytes 589832 | tf_op jit(solution)/shard_map/ppermute | solution.py:109
  310.7 11.0 %collective-permute-start.36 = (bf16[64,1536]{1,0:T(8,128)(2,1)S(1)}, bf16[64,1536]{1,0:T(8,128)(2,1)S(1)}, u32[]{:S(2)}, u32[]{:S(2)}) collective-permute-start(bf16[64,1536]{1,0:T(8,128)(2,1)S(1)} %collective-permute-done.35), channel_id=1, source_target_pairs={{0,2},{1,3},{2,0},{3,1},{4,6},{5,7},{6,4},{7,5},{8,10},{9,11},{10,... | collective-permute-start | bytes 589832 | tf_op jit(solution)/shard_map/ppermute | solution.py:109
  320.3 8.9 %collective-permute-start.38 = (bf16[64,1536]{1,0:T(8,128)(2,1)S(1)}, bf16[64,1536]{1,0:T(8,128)(2,1)S(1)}, u32[]{:S(2)}, u32[]{:S(2)}) collective-permute-start(bf16[64,1536]{1,0:T(8,128)(2,1)S(1)} %collective-permute-done.37), channel_id=1, source_target_pairs={{0,2},{1,3},{2,0},{3,1},{4,6},{5,7},{6,4},{7,5},{8,10},{9,11},{10,... | collective-permute-start | bytes 589832 | tf_op jit(solution)/shard_map/ppermute | solution.py:109
  335.4 14.0 %collective-permute-start.41 = (bf16[4,2,64,1536]{3,2,1,0:T(8,128)(2,1)}, bf16[4,2,64,1536]{3,2,1,0:T(8,128)(2,1)}, u32[]{:S(2)}, u32[]{:S(2)}) collective-permute-start(bf16[4,2,64,1536]{3,2,1,0:T(8,128)(2,1)} %get-tuple-element.273), channel_id=1, source_target_pairs={{0,1},{1,0},{2,3},{3,2},{4,5},{5,4},{6,7},{7,6},{8,9},{9,8},{10,11... | collective-permute-start | bytes 4718600 | tf_op jit(solution)/shard_map/ppermute | solution.py:109
  370.1 15.0 %collective-permute-start.42 = (bf16[4,2,64,1536]{3,2,1,0:T(8,128)(2,1)S(1)}, bf16[4,2,64,1536]{3,2,1,0:T(8,128)(2,1)S(1)}, u32[]{:S(2)}, u32[]{:S(2)}) collective-permute-start(bf16[4,2,64,1536]{3,2,1,0:T(8,128)(2,1)S(1)} %bitcast.641), channel_id=1, source_target_pairs={{0,1},{1,0},{2,3},{3,2},{4,5},{5,4},{6,7},{7,6},{8,9},{9,8},{10,11... | collective-permute-start | bytes 4718600 | tf_op jit(solution)/shard_map/ppermute | solution.py:109
  373.8 30.2 %collective-permute-start.73 = (bf16[16,2,48,64]{3,2,0,1:T(8,128)(2,1)S(1)}, bf16[16,2,48,64]{3,2,0,1:T(8,128)(2,1)S(1)}, u32[]{:S(2)}, u32[]{:S(2)}) collective-permute-start(bf16[16,2,48,64]{3,2,0,1:T(8,128)(2,1)S(1)} %fusion.130), channel_id=1, source_target_pairs={{0,16},{16,0},{1,17},{17,1},{2,18},{18,2},{3,19},{19,3},{4,20},{20... | collective-permute-start | bytes 589832 | tf_op jit(solution)/shard_map/ppermute | solution.py:211
  388.6 9.1 %collective-permute-start.45 = (bf16[64,1536]{1,0:T(8,128)(2,1)S(1)}, bf16[64,1536]{1,0:T(8,128)(2,1)S(1)}, u32[]{:S(2)}, u32[]{:S(2)}) collective-permute-start(bf16[64,1536]{1,0:T(8,128)(2,1)S(1)} %get-tuple-element.270), channel_id=1, source_target_pairs={{0,2},{1,3},{2,0},{3,1},{4,6},{5,7},{6,4},{7,5},{8,10},{9,11},{10,... | collective-permute-start | bytes 589832 | tf_op jit(solution)/shard_map/ppermute | solution.py:109
  394.4 22.9 %collective-permute-start.74 = (bf16[32,1536]{1,0:T(8,128)(2,1)S(1)}, bf16[32,1536]{1,0:T(8,128)(2,1)}, u32[]{:S(2)}, u32[]{:S(2)}) collective-permute-start(bf16[32,1536]{1,0:T(8,128)(2,1)S(1)} %fusion.166), channel_id=1, source_target_pairs={{0,16},{16,0},{1,17},{17,1},{2,18},{18,2},{3,19},{19,3},{4,20},{20... | collective-permute-start | bytes 294920 | tf_op jit(solution)/shard_map/ppermute | solution.py:211
  395.1 71.7 %collective-permute-start.75 = (bf16[1536,512]{1,0:T(8,128)(2,1)}, bf16[1536,512]{1,0:T(8,128)(2,1)}, u32[]{:S(2)}, u32[]{:S(2)}) collective-permute-start(bf16[1536,512]{1,0:T(8,128)(2,1)} %convolution_convert_fusion.3), channel_id=1, source_target_pairs={{0,16},{16,0},{1,17},{17,1},{2,18},{18,2},{3,19},{19,3},{4,20},{20... | collective-permute-start | bytes 4718600 | tf_op jit(solution)/shard_map/ppermute | solution.py:219
  397.7 73.2 %collective-permute-start.76 = (bf16[1536,512]{1,0:T(8,128)(2,1)}, bf16[1536,512]{1,0:T(8,128)(2,1)}, u32[]{:S(2)}, u32[]{:S(2)}) collective-permute-start(bf16[1536,512]{1,0:T(8,128)(2,1)} %convolution_convert_fusion.2), channel_id=1, source_target_pairs={{0,16},{16,0},{1,17},{17,1},{2,18},{18,2},{3,19},{19,3},{4,20},{20... | collective-permute-start | bytes 4718600 | tf_op jit(solution)/shard_map/ppermute | solution.py:219
  401.8 10.5 %collective-permute-start.44 = (bf16[64,1536]{1,0:T(8,128)(2,1)}, bf16[64,1536]{1,0:T(8,128)(2,1)}, u32[]{:S(2)}, u32[]{:S(2)}) collective-permute-start(bf16[64,1536]{1,0:T(8,128)(2,1)} %get-tuple-element.271), channel_id=1, source_target_pairs={{0,2},{1,3},{2,0},{3,1},{4,6},{5,7},{6,4},{7,5},{8,10},{9,11},{10,... | collective-permute-start | bytes 589832 | tf_op jit(solution)/shard_map/ppermute | solution.py:109
  404.0 9.5 %collective-permute-start.48 = (bf16[64,1536]{1,0:T(8,128)(2,1)}, bf16[64,1536]{1,0:T(8,128)(2,1)S(1)}, u32[]{:S(2)}, u32[]{:S(2)}) collective-permute-start(bf16[64,1536]{1,0:T(8,128)(2,1)} %fusion.133), channel_id=1, source_target_pairs={{0,4},{1,5},{2,6},{3,7},{4,8},{5,9},{6,10},{7,11},{8,12},{9,13},{1... | collective-permute-start | bytes 589832 | tf_op jit(solution)/shard_map/ppermute | solution.py:109
  407.1 14.2 %all-to-all-start.3 = ((bf16[16,2,3072]{2,1,0:T(2,128)(2,1)}), bf16[16,2,3072]{2,1,0:T(2,128)(2,1)S(1)}, u32[]{:S(2)}, u32[]{:S(2)}) async-start(bf16[16,2,3072]{2,1,0:T(2,128)(2,1)} %reshape.1073), calls=%async_computation.3 | async-start | bytes 393216 | tf_op jit(solution)/shard_map/all_to_all | solution.py:236
  412.3 87.0 %collective-permute-start.77 = (bf16[512,1536]{1,0:T(8,128)(2,1)}, bf16[512,1536]{1,0:T(8,128)(2,1)}, u32[]{:S(2)}, u32[]{:S(2)}) collective-permute-start(bf16[512,1536]{1,0:T(8,128)(2,1)} %fusion.16), channel_id=1, source_target_pairs={{0,16},{16,0},{1,17},{17,1},{2,18},{18,2},{3,19},{19,3},{4,20},{20... | collective-permute-start | bytes 4718600 | tf_op jit(solution)/shard_map/ppermute | solution.py:219
  413.5 11.5 %collective-permute-start.43 = (bf16[64,1536]{1,0:T(8,128)(2,1)}, bf16[64,1536]{1,0:T(8,128)(2,1)}, u32[]{:S(2)}, u32[]{:S(2)}) collective-permute-start(bf16[64,1536]{1,0:T(8,128)(2,1)} %get-tuple-element.268), channel_id=1, source_target_pairs={{0,2},{1,3},{2,0},{3,1},{4,6},{5,7},{6,4},{7,5},{8,10},{9,11},{10,... | collective-permute-start | bytes 589832 | tf_op jit(solution)/shard_map/ppermute | solution.py:109
  447.8 9.4 %collective-permute-start.55 = (bf16[64,1664]{1,0:T(8,128)(2,1)S(1)}, bf16[64,1664]{1,0:T(8,128)(2,1)S(1)}, u32[]{:S(2)}, u32[]{:S(2)}) collective-permute-start(bf16[64,1664]{1,0:T(8,128)(2,1)S(1)} %collective-permute-done.53), channel_id=1, source_target_pairs={{0,4},{1,5},{2,6},{3,7},{4,8},{5,9},{6,10},{7,11},{8,12},{9,13},{1... | collective-permute-start | bytes 638984 | tf_op jit(solution)/shard_map/ppermute | solution.py:109
  447.9 9.4 %collective-permute-start.54 = (bf16[64,1664]{1,0:T(8,128)(2,1)S(1)}, bf16[64,1664]{1,0:T(8,128)(2,1)S(1)}, u32[]{:S(2)}, u32[]{:S(2)}) collective-permute-start(bf16[64,1664]{1,0:T(8,128)(2,1)S(1)} %collective-permute-done.53), channel_id=1, source_target_pairs={{0,2},{1,3},{2,0},{3,1},{4,6},{5,7},{6,4},{7,5},{8,10},{9,11},{10,... | collective-permute-start | bytes 638984 | tf_op jit(solution)/shard_map/ppermute | solution.py:109
  466.9 37.8 %collective-permute-start.57 = (bf16[4,2,64,1664]{3,2,1,0:T(8,128)(2,1)}, bf16[4,2,64,1664]{3,2,1,0:T(8,128)(2,1)}, u32[]{:S(2)}, u32[]{:S(2)}) collective-permute-start(bf16[4,2,64,1664]{3,2,1,0:T(8,128)(2,1)} %get-tuple-element.263), channel_id=1, source_target_pairs={{0,1},{1,0},{2,3},{3,2},{4,5},{5,4},{6,7},{7,6},{8,9},{9,8},{10,11... | collective-permute-start | bytes 5111816 | tf_op jit(solution)/shard_map/ppermute | solution.py:109
  542.5 11.0 %collective-permute-start.58 = (f32[4,3,64,128]{3,2,1,0:T(8,128)S(1)}, f32[4,3,64,128]{3,2,1,0:T(8,128)S(1)}, u32[]{:S(2)}, u32[]{:S(2)}) collective-permute-start(f32[4,3,64,128]{3,2,1,0:T(8,128)S(1)} %fusion.80), channel_id=1, source_target_pairs={{16,0},{17,1},{18,2},{19,3},{20,4},{21,5},{22,6},{23,7},{24,8},{25... | collective-permute-start | bytes 1179656 | tf_op jit(solution)/shard_map/ppermute | solution.py:225
  561.9 42.4 %collective-permute-start.59 = (f32[3,4,448]{2,1,0:T(4,128)S(1)}, f32[3,4,448]{2,1,0:T(4,128)S(1)}, u32[]{:S(2)}, u32[]{:S(2)}) collective-permute-start(f32[3,4,448]{2,1,0:T(4,128)S(1)} %copy.530), channel_id=1, source_target_pairs={{16,0},{17,1},{18,2},{19,3},{20,4},{21,5},{22,6},{23,7},{24,8},{25... | collective-permute-start | bytes 64520 | tf_op jit(solution)/shard_map/ppermute | solution.py:17
  650.4 33.7 %collective-permute-start.60 = (bf16[4,2,88,1536]{3,2,1,0:T(8,128)(2,1)}, bf16[4,2,88,1536]{3,2,1,0:T(8,128)(2,1)}, u32[]{:S(2)}, u32[]{:S(2)}) collective-permute-start(bf16[4,2,88,1536]{3,2,1,0:T(8,128)(2,1)} %bitcast.162), channel_id=1, source_target_pairs={{0,1},{1,0},{2,3},{3,2},{4,5},{5,4},{6,7},{7,6},{8,9},{9,8},{10,11... | collective-permute-start | bytes 6488072 | tf_op jit(solution)/shard_map/ppermute | solution.py:109
  652.5 46.0 %collective-permute-start.69 = (bf16[1536,192]{0,1:T(8,128)(2,1)}, bf16[1536,192]{0,1:T(8,128)(2,1)}, u32[]{:S(2)}, u32[]{:S(2)}) collective-permute-start(bf16[1536,192]{0,1:T(8,128)(2,1)} %fusion.25), channel_id=1, source_target_pairs={{0,16},{16,0},{1,17},{17,1},{2,18},{18,2},{3,19},{19,3},{4,20},{20... | collective-permute-start | bytes 1769480 | tf_op jit(solution)/shard_map/ppermute | solution.py:219
  655.4 51.6 %collective-permute-start.72 = (bf16[192,1536]{1,0:T(8,128)(2,1)}, bf16[192,1536]{1,0:T(8,128)(2,1)}, u32[]{:S(2)}, u32[]{:S(2)}) collective-permute-start(bf16[192,1536]{1,0:T(8,128)(2,1)} %fusion.27), channel_id=1, source_target_pairs={{0,16},{16,0},{1,17},{17,1},{2,18},{18,2},{3,19},{19,3},{4,20},{20... | collective-permute-start | bytes 1769480 | tf_op jit(solution)/shard_map/ppermute | solution.py:219
  656.7 12.0 %all-to-all-start.2 = ((f32[16,1,80]{2,1,0:T(1,128)}), f32[16,1,80]{2,1,0:T(1,128)S(1)}, u32[]{:S(2)}, u32[]{:S(2)}) async-start(f32[16,1,80]{2,1,0:T(1,128)} %bitcast.182), calls=%async_computation.2 | async-start | bytes 16384 | tf_op jit(solution)/shard_map/all_to_all | solution.py:236
  668.9 13.8 %collective-permute-start.71 = (f32[5849]{0:T(1024)S(1)}, f32[5849]{0:T(1024)S(1)}, u32[]{:S(2)}, u32[]{:S(2)}) collective-permute-start(f32[5849]{0:T(1024)S(1)} %concatenate.55), channel_id=1, source_target_pairs={{0,16},{16,0},{1,17},{17,1},{2,18},{18,2},{3,19},{19,3},{4,20},{20... | collective-permute-start | bytes 70196 | tf_op jit(solution)/shard_map/ppermute | solution.py:632
  675.2 40.2 %collective-permute-start.70 = (bf16[1536,192]{0,1:T(8,128)(2,1)}, bf16[1536,192]{0,1:T(8,128)(2,1)}, u32[]{:S(2)}, u32[]{:S(2)}) collective-permute-start(bf16[1536,192]{0,1:T(8,128)(2,1)} %fusion.26), channel_id=1, source_target_pairs={{0,16},{16,0},{1,17},{17,1},{2,18},{18,2},{3,19},{19,3},{4,20},{20... | collective-permute-start | bytes 1769480 | tf_op jit(solution)/shard_map/ppermute | solution.py:219
  687.9 9.4 %collective-permute-start.64 = (bf16[88,1536]{1,0:T(8,128)(2,1)}, bf16[88,1536]{1,0:T(8,128)(2,1)}, u32[]{:S(2)}, u32[]{:S(2)}) collective-permute-start(bf16[88,1536]{1,0:T(8,128)(2,1)} %get-tuple-element.255), channel_id=1, source_target_pairs={{0,2},{1,3},{2,0},{3,1},{4,6},{5,7},{6,4},{7,5},{8,10},{9,11},{10,... | collective-permute-start | bytes 811016 | tf_op jit(solution)/shard_map/ppermute | solution.py:109
  692.9 9.8 %collective-permute-start.63 = (bf16[88,1536]{1,0:T(8,128)(2,1)}, bf16[88,1536]{1,0:T(8,128)(2,1)S(1)}, u32[]{:S(2)}, u32[]{:S(2)}) collective-permute-start(bf16[88,1536]{1,0:T(8,128)(2,1)} %get-tuple-element.256), channel_id=1, source_target_pairs={{0,2},{1,3},{2,0},{3,1},{4,6},{5,7},{6,4},{7,5},{8,10},{9,11},{10,... | collective-permute-start | bytes 811016 | tf_op jit(solution)/shard_map/ppermute | solution.py:109
  700.9 10.2 %collective-permute-start.62 = (bf16[88,1536]{1,0:T(8,128)(2,1)S(1)}, bf16[88,1536]{1,0:T(8,128)(2,1)S(1)}, u32[]{:S(2)}, u32[]{:S(2)}) collective-permute-start(bf16[88,1536]{1,0:T(8,128)(2,1)S(1)} %copy-done.73), channel_id=1, source_target_pairs={{0,2},{1,3},{2,0},{3,1},{4,6},{5,7},{6,4},{7,5},{8,10},{9,11},{10,... | collective-permute-start | bytes 811016 | tf_op jit(solution)/shard_map/ppermute | solution.py:109
  (183 other events, 1868.2 us)

commit v2 on v1

--- a/solution.py
+++ b/solution.py
@@ -1,6 +1,8 @@
 import jax
 import jax.numpy as jnp
 from jax import lax
+from jax.experimental import pallas as pl
+from jax.experimental.pallas import tpu as pltpu
 from jax.sharding import PartitionSpec as P
 
 STATE = 128
@@ -41,51 +43,6 @@
 def silu_slope(values):
     sigmoid_val = jax.nn.sigmoid(values)
     return sigmoid_val * (1.0 + values * (1.0 - sigmoid_val))
-
-
-def conv_decay(
-    extended, conv_weight, conv_bias, step_raw, step_bias, decay_log, inner_width, state_width
-):
-    length = step_raw.shape[0]
-    preact = conv_bias + conv_weight[0] * extended[0:length]
-    for offset in range(1, conv_weight.shape[0]):
-        preact = preact + conv_weight[offset] * extended[offset : offset + length]
-    activated = jax.nn.silu(preact)
-    head_count = step_raw.shape[-1]
-    values = activated[..., :inner_width].reshape(
-        length, activated.shape[1], head_count, inner_width // head_count
-    )
-    input_matrix_b = activated[..., inner_width : inner_width + state_width]
-    c_matrix = activated[..., inner_width + state_width :]
-    step_size = jax.nn.softplus(step_raw + step_bias)
-    log_decay = -jnp.exp(decay_log) * step_size
-    return (values, input_matrix_b, c_matrix, step_size, log_decay)
-
-
-def ssd_output(values, input_matrix_b, c_matrix, step_size, log_decay, entering, skip_gain):
-    cumulative = jnp.cumsum(log_decay, axis=0)
-    length = cumulative.shape[0]
-    causal = (jnp.arange(length)[:, None] >= jnp.arange(length)[None, :])[:, :, None, None]
-    log_gap = jnp.where(causal, cumulative[:, None] - cumulative[None, :], 0.0)
-    decay_mask = jnp.where(causal, jnp.exp(log_gap), 0.0)
-    intersection = jnp.einsum("tbn,sbn->tsb", c_matrix, input_matrix_b, precision=highest)
-    weighted = decay_mask * intersection[..., None]
-    scaled = values * step_size[..., None]
-    within = jnp.einsum("tsbh,sbhp->tbhp", weighted, scaled, precision=highest)
-    carried = jnp.exp(cumulative)[..., None] * jnp.einsum(
-        "tbn,bhpn->tbhp", c_matrix, entering, precision=highest
-    )
-    return within + carried + skip_gain[:, None] * values
-
-
-def state_update(values, input_matrix_b, step_size, log_decay):
-    cumulative = jnp.cumsum(log_decay, axis=0)
-    decay_total = jnp.exp(cumulative[-1])
-    tail_weight = jnp.exp(cumulative[-1] - cumulative) * step_size
-    local_state = jnp.einsum(
-        "sbh,sbhp,sbn->bhpn", tail_weight, values, input_matrix_b, precision=highest
-    )
-    return (decay_total, local_state)
 
 
 def chain_combine(earlier, latter):
@@ -234,6 +191,518 @@
 
 def mp_exchange(value):
     return lax.all_to_all(value, "mp", split_axis=0, concat_axis=0, tiled=True)
+
+
+EDGE = 16
+TRANSPOSED = (((1,), (1,)), ((), ()))
+ROWS_SUMMED = (((0,), (0,)), ((), ()))
+PLAIN = (((1,), (0,)), ((), ()))
+
+
+def product(left, right, dims=PLAIN):
+    return lax.dot_general(left, right, dims, preferred_element_type=jnp.float32)
+
+
+def halves_of(value):
+    high = value.astype(jnp.bfloat16)
+    return high, (value - high.astype(jnp.float32)).astype(jnp.bfloat16)
+
+
+def fine(left, right, dims=PLAIN):
+    left_high, left_low = halves_of(left)
+    right_high, right_low = halves_of(right)
+    small = product(left_high, right_low, dims) + product(left_low, right_high, dims)
+    return product(left_high, right_high, dims) + small
+
+
+def exact_right(left, right, dims=PLAIN):
+    high, low = halves_of(left)
+    return product(high, right, dims) + product(low, right, dims)
+
+
+def exact_left(left, right, dims=PLAIN):
+    high = right.astype(jnp.bfloat16)
+    rest = right - high.astype(jnp.float32)
+    middle = rest.astype(jnp.bfloat16)
+    last = (rest - middle.astype(jnp.float32)).astype(jnp.bfloat16)
+    return product(left, high, dims) + (product(left, middle, dims) + product(left, last, dims))
+
+
+def softplus(value):
+    return jnp.maximum(value, 0.0) + jnp.log1p(jnp.exp(-jnp.abs(value)))
+
+
+def spread(value, heads, width):
+    channel = width // heads
+    lane = lax.broadcasted_iota(jnp.int32, (value.shape[0], width), 1)
+    result = jnp.broadcast_to(value[:, heads - 1 : heads], (value.shape[0], width))
+    for head in range(heads - 2, -1, -1):
+        result = jnp.where(lane < (head + 1) * channel, value[:, head : head + 1], result)
+    return result
+
+
+def only_head(value, head, heads):
+    channel = value.shape[1] // heads
+    lane = lax.broadcasted_iota(jnp.int32, value.shape, 1)
+    inside = (lane >= head * channel) & (lane < (head + 1) * channel)
+    return jnp.where(inside, value, 0.0)
+
+
+def head_sum_matrix(width, heads):
+    channel = width // heads
+    row = lax.broadcasted_iota(jnp.int32, (width, 128), 0) // channel
+    lane = lax.broadcasted_iota(jnp.int32, (width, 128), 1)
+    return (row == lane).astype(jnp.float32).astype(jnp.bfloat16)
+
+
+def not_before(length, reverse=False):
+    row = lax.broadcasted_iota(jnp.int32, (length, length), 0)
+    lane = lax.broadcasted_iota(jnp.int32, (length, length), 1)
+    return (row <= lane) if reverse else (row >= lane)
+
+
+def ones_of(mask):
+    return mask.astype(jnp.float32).astype(jnp.bfloat16)
+
+
+def whole(shape):
+    return pl.BlockSpec(shape, lambda b, *_: (0,) * len(shape))
+
+
+def each(shape):
+    return pl.BlockSpec((1,) + shape, lambda b, *_: (b,) + (0,) * len(shape))
+
+
+def f32(*shape):
+    return jax.ShapeDtypeStruct(shape, jnp.float32)
+
+
+def bf16(*shape):
+    return jax.ShapeDtypeStruct(shape, jnp.bfloat16)
+
+
+def call(kernel, grid, in_specs, out_specs, out_shape, scratch=(), prefetch=0):
+    return pl.pallas_call(
+        kernel,
+        grid_spec=pltpu.PrefetchScalarGridSpec(
+            num_scalar_prefetch=prefetch,
+            grid=grid,
+            in_specs=in_specs,
+            out_specs=out_specs,
+            scratch_shapes=list(scratch),
+        ),
+        out_shape=out_shape,
+        compiler_params=pltpu.CompilerParams(vmem_limit_bytes=56 * 1024 * 1024),
+    )
+
+
+def mixer_input(
+    x, edge, gain, gate_w, value_w, state_w, step_w, value_taps, state_taps,
+    value_bias, state_bias, step_shift, decay_rate, heads,
+):
+    count, length, model = x.shape
+    inner, double = value_w.shape[1], state_w.shape[1]
+    window = value_taps.shape[0]
+
+    def kernel(
+        x_ref, edge_ref, gain_ref, gate_ref, value_ref, state_ref, step_ref, vt_ref, st_ref,
+        vb_ref, sb_ref, shift_ref, rate_ref,
+        normed_out, gate_out, ev_out, es_out, pv_out, ps_out, step_out, decay_out, local_out,
+    ):
+        def norm(value):
+            value = value.astype(jnp.float32)
+            scale = lax.rsqrt(jnp.mean(value * value, axis=-1, keepdims=True) + epsilon)
+            return (value * scale * gain_ref[...]).astype(jnp.bfloat16)
+
+        normed = norm(x_ref[0])
+        normed_out[0] = normed
+        ev_out[0, EDGE:] = product(normed, value_ref[...])
+        es_out[0, EDGE:] = product(normed, state_ref[...])
+        step_raw = product(normed, step_ref[...])
+        step_out[0] = step_raw
+        gate_out[0] = product(normed, gate_ref[...])
+        edge_normed = norm(edge_ref[0])
+        ev_out[0, :EDGE] = product(edge_normed, value_ref[...])
+        es_out[0, :EDGE] = product(edge_normed, state_ref[...])
+        first = EDGE - window + 1
+        pre_value = jnp.broadcast_to(vb_ref[...], (length, inner))
+        pre_state = jnp.broadcast_to(sb_ref[...], (length, double))
+        for tap in range(window):
+            pre_value = pre_value + vt_ref[tap : tap + 1] * ev_out[0, first + tap : first + tap + length]
+            pre_state = pre_state + st_ref[tap : tap + 1] * es_out[0, first + tap : first + tap + length]
+        pv_out[0] = pre_value
+        ps_out[0] = pre_state
+        values = jax.nn.silu(pre_value)
+        b_matrix = jax.nn.silu(pre_state[:, : double // 2])
+        step = softplus(step_raw + shift_ref[...])
+        decay = exact_left(ones_of(not_before(length)), -jnp.exp(rate_ref[...]) * step)
+        decay_out[0] = decay
+        tail = jnp.exp(decay[length - 1 : length] - decay) * step
+        local_out[0] = fine(values * spread(tail, heads, inner), b_matrix, ROWS_SUMMED)
+
+    return call(
+        kernel,
+        (count,),
+        [
+            each((length, model)), each((EDGE, model)), whole(gain.shape), whole(gate_w.shape),
+            whole(value_w.shape), whole(state_w.shape), whole(step_w.shape), whole(value_taps.shape),
+            whole(state_taps.shape), whole(value_bias.shape), whole(state_bias.shape),
+            whole(step_shift.shape), whole(decay_rate.shape),
+        ],
+        [
+            each((length, model)), each((length, inner)), each((length + EDGE, inner)),
+            each((length + EDGE, double)), each((length, inner)), each((length, double)),
+            each((length, 128)), each((length, 128)), each((inner, double // 2)),
+        ],
+        [
+            bf16(count, length, model), f32(count, length, inner), f32(count, length + EDGE, inner),
+            f32(count, length + EDGE, double), f32(count, length, inner), f32(count, length, double),
+            f32(count, length, 128), f32(count, length, 128), f32(count, inner, double // 2),
+        ],
+    )(
+        x, edge, gain, gate_w, value_w, state_w, step_w, value_taps, state_taps,
+        value_bias, state_bias, step_shift, decay_rate,
+    )
+
+
+def decay_masks(decay, heads):
+    length = decay.shape[0]
+    causal = not_before(length)
+    turned = decay.T
+    return [
+        jnp.exp(jnp.where(causal, decay[:, head : head + 1] - turned[head : head + 1], -1e30))
+        for head in range(heads)
+    ]
+
+
+def mixer_within(pre_value, pre_state, step_raw, decay_sum, step_shift, skip, heads):
+    count, length, inner = pre_value.shape
+    double = pre_state.shape[2]
+
+    def kernel(pv_ref, ps_ref, step_ref, decay_ref, shift_ref, skip_ref, within_out):
+        values = jax.nn.silu(pv_ref[0])
+        both = jax.nn.silu(ps_ref[0])
+        b_matrix, c_matrix = both[:, : double // 2], both[:, double // 2 :]
+        scaled = values * spread(softplus(step_ref[0] + shift_ref[...]), heads, inner)
+        crossed = fine(c_matrix, b_matrix, TRANSPOSED)
+        result = spread(skip_ref[...], heads, inner) * values
+        for head, mask in enumerate(decay_masks(decay_ref[0], heads)):
+            result = result + fine(crossed * mask, only_head(scaled, head, heads))
+        within_out[0] = result
+
+    return call(
+        kernel,
+        (count,),
+        [
+            each((length, inner)), each((length, double)), each((length, 128)), each((length, 128)),
+            whole(step_shift.shape), whole(skip.shape),
+        ],
+        each((length, inner)),
+        f32(count, length, inner),
+    )(pre_value, pre_state, step_raw, decay_sum, step_shift, skip)
+
+
+def mixer_output(order, within, pre_state, decay_sum, entering, gate_raw, gain, out_w, heads, owners):
+    count, length, inner = within.shape
+    double, model = pre_state.shape[2], out_w.shape[1]
+    rows = length // owners
+    half = owners // 2
+
+    def kernel(
+        order_ref, within_ref, ps_ref, decay_ref, state_ref, gate_ref, gain_ref, out_ref,
+        ssm_out, scaled_out, square_out, own_out, partner_out, mixed,
+    ):
+        c_matrix = jax.nn.silu(ps_ref[0, :, double // 2 :])
+        carried = fine(c_matrix, state_ref[0], TRANSPOSED)
+        ssm = within_ref[0] + spread(jnp.exp(decay_ref[0]), heads, inner) * carried
+        ssm_out[0] = ssm
+        gated = ssm * jax.nn.silu(gate_ref[0])
+        scaled = (gated * gain_ref[...]).astype(jnp.bfloat16)
+        scaled_out[0] = scaled
+        square_out[0] = exact_left(jnp.ones((8, inner), jnp.bfloat16), gated * gated, TRANSPOSED)
+        mixed[...] = product(scaled, out_ref[...]).astype(jnp.bfloat16)
+        for place in range(owners):
+            start = pl.multiple_of(order_ref[place] * rows, rows)
+            target = own_out if place < half else partner_out
+            target[place % half] = mixed[pl.ds(start, rows)]
+
+    blocks = pl.BlockSpec((half, rows, model), lambda b, *_: (0, b, 0))
+    return call(
+        kernel,
+        (count,),
+        [
+            each((length, inner)), each((length, double)), each((length, 128)),
+            each((inner, double // 2)), each((length, inner)), whole(gain.shape), whole(out_w.shape),
+        ],
+        [each((length, inner)), each((length, inner)), each((8, length)), blocks, blocks],
+        [
+            f32(count, length, inner), bf16(count, length, inner), f32(count, 8, length),
+            bf16(half, count * rows, model), bf16(half, count * rows, model),
+        ],
+        [pltpu.VMEM((length, model), jnp.bfloat16)],
+        1,
+    )(order, within, pre_state, decay_sum, entering, gate_raw, gain, out_w)
+
+
+def mixer_output_back(order, blocks, gate_raw, ssm, pre_state, decay_sum, gain, out_w, heads):
+    count, length, inner = ssm.shape
+    double, model = pre_state.shape[2], out_w.shape[1]
+    owners, _, wide_model = blocks.shape
+    rows = length // owners
+
+    def kernel(
+        order_ref, blocks_ref, gate_ref, ssm_ref, ps_ref, decay_ref, gain_ref, out_ref,
+        mix_out, ssm_grad_out, gate_grad_out, state_out, gain_out, sums,
+    ):
+        for place in range(owners):
+            start = pl.multiple_of(order_ref[place] * rows, rows)
+            mix_out[0, pl.ds(start, rows)] = blocks_ref[place, :, :model]
+            sums[pl.ds(start, rows)] = blocks_ref[place, :, model:].astype(jnp.float32)
+        sum_grad = sums[:, 0:1] + sums[:, 1:2]
+        scaled_grad = product(mix_out[0], out_ref[...], TRANSPOSED)
+        gate, value = gate_ref[0], ssm_ref[0]
+        opened = jax.nn.silu(gate)
+        gated = value * opened
+
+        @pl.when(pl.program_id(0) == 0)
+        def _():
+            gain_out[...] = jnp.zeros_like(gain_out)
+
+        gain_out[...] += jnp.sum(scaled_grad * gated, axis=0, keepdims=True)
+        gated_grad = scaled_grad * gain_ref[...] + 2.0 * gated * sum_grad
+        ssm_grad = gated_grad * opened
+        ssm_grad_out[0] = ssm_grad
+        gate_grad_out[0] = (gated_grad * value * silu_slope(gate)).astype(jnp.bfloat16)
+        c_matrix = jax.nn.silu(ps_ref[0, :, double // 2 :])
+        carried_grad = spread(jnp.exp(decay_ref[0]), heads, inner) * ssm_grad
+        state_out[0] = fine(carried_grad, c_matrix, ROWS_SUMMED)
+
+    return call(
+        kernel,
+        (count,),
+        [
+            pl.BlockSpec((owners, rows, wide_model), lambda b, *_: (0, b, 0)),
+            each((length, inner)), each((length, inner)), each((length, double)), each((length, 128)),
+            whole(gain.shape), whole(out_w.shape),
+        ],
+        [
+            each((length, model)), each((length, inner)), each((length, inner)),
+            each((inner, double // 2)), whole((8, inner)),
+        ],
+        [
+            bf16(count, length, model), f32(count, length, inner), bf16(count, length, inner),
+            f32(count, inner, double // 2), f32(8, inner),
+        ],
+        [pltpu.VMEM((length, wide_model - model), jnp.float32)],
+        1,
+    )(order, blocks, gate_raw, ssm, pre_state, decay_sum, gain, out_w)
+
+
+def mixer_within_back(pre_value, pre_state, step_raw, decay_sum, step_shift, ssm_grad, entering, heads):
+    count, length, inner = pre_value.shape
+    double = pre_state.shape[2]
+
+    def kernel(pv_ref, ps_ref, step_ref, decay_ref, shift_ref, grad_ref, state_ref, scaled_out, both_out):
+        values = jax.nn.silu(pv_ref[0])
+        both = jax.nn.silu(ps_ref[0])
+        b_matrix, c_matrix = both[:, : double // 2], both[:, double // 2 :]
+        scaled = values * spread(softplus(step_ref[0] + shift_ref[...]), heads, inner)
+        crossed = fine(c_matrix, b_matrix, TRANSPOSED)
+        grad = grad_ref[0]
+        decay = decay_ref[0]
+        scaled_grad = jnp.zeros((length, inner), jnp.float32)
+        crossed_grad = jnp.zeros((length, length), jnp.float32)
+        for head, mask in enumerate(decay_masks(decay, heads)):
+            head_grad = only_head(grad, head, heads)
+            scaled_grad = scaled_grad + fine(crossed * mask, head_grad, ROWS_SUMMED)
+            crossed_grad = crossed_grad + fine(head_grad, scaled, TRANSPOSED) * mask
+        scaled_out[0] = scaled_grad
+        both_out[0, :, : double // 2] = fine(crossed_grad, c_matrix, ROWS_SUMMED)
+        carried_grad = spread(jnp.exp(decay), heads, inner) * grad
+        both_out[0, :, double // 2 :] = fine(crossed_grad, b_matrix) + fine(carried_grad, state_ref[0])
+
+    return call(
+        kernel,
+        (count,),
+        [
+            each((length, inner)), each((length, double)), each((length, 128)), each((length, 128)),
+            whole(step_shift.shape), each((length, inner)), each((inner, double // 2)),
+        ],
+        [each((length, inner)), each((length, double))],
+        [f32(count, length, inner), f32(count, length, double)],
+    )(pre_value, pre_state, step_raw, decay_sum, step_shift, ssm_grad, entering)
+
+
+def mixer_input_back(
+    pre_value, pre_state, ext_value, ext_state, step_raw, decay_sum, ssm, ssm_grad, scaled_grad,
+    state_part, entering, exit_grad, value_taps, state_taps, step_shift, decay_rate, skip, heads,
+):
+    count, length, inner = pre_value.shape
+    double = pre_state.shape[2]
+    window = value_taps.shape[0]
+
+    def kernel(
+        pv_ref, ps_ref, ev_ref, es_ref, step_ref, decay_ref, ssm_ref, grad_ref, scaled_ref, part_ref,
+        state_ref, exit_ref, vt_ref, st_ref, shift_ref, rate_ref, skip_ref,
+        value_out, state_out, edge_v_out, edge_s_out, step_out, taps_v_out, taps_s_out, head_out,
+        room_v, room_s,
+    ):
+        pre_v, pre_s = pv_ref[0], ps_ref[0]
+        values = jax.nn.silu(pre_v)
+        b_matrix = jax.nn.silu(pre_s[:, : double // 2])
+        grad, scaled = grad_ref[0], scaled_ref[0]
+        step_pre = step_ref[0] + shift_ref[...]
+        step = softplus(step_pre)
+        rate = jnp.exp(rate_ref[...])
+        decay = decay_ref[0]
+        last = decay[length - 1 : length]
+        remain = jnp.exp(last - decay)
+        remain_wide = spread(remain, heads, inner)
+        step_wide = spread(step, heads, inner)
+        tail_wide = remain_wide * step_wide
+        skip_wide = spread(skip_ref[...], heads, inner)
+        leaving = exit_ref[0]
+        passed = fine(b_matrix, leaving, TRANSPOSED)
+        value_grad = scaled * step_wide + tail_wide * passed + skip_wide * grad
+        b_grad = part_ref[0, :, : double // 2] + fine(tail_wide * values, leaving)
+        summing = head_sum_matrix(inner, heads)
+        crossing = values * passed
+        left_part = exact_right(crossing * tail_wide, summing)
+        decay_grad = (
+            exact_right(grad * (ssm_ref[0] - skip_wide * values) - values * step_wide * scaled, summing)
+            - left_part
+        )
+        total_grad = jnp.sum(left_part, axis=0, keepdims=True)
+        state_dot = exact_left(jnp.ones((8, double // 2), jnp.bfloat16), leaving * state_ref[0], TRANSPOSED)
+        total_grad = total_grad + jnp.exp(last) * exact_right(state_dot, summing)[:1]
+        row = lax.broadcasted_iota(jnp.int32, decay_grad.shape, 0)
+        decay_grad = decay_grad + jnp.where(row == length - 1, total_grad, 0.0)
+        log_grad = exact_left(ones_of(not_before(length, True)), decay_grad)
+        step_size_grad = exact_right(scaled * values + crossing * remain_wide, summing) - rate * log_grad
+        step_raw_grad = step_size_grad * jax.nn.sigmoid(step_pre)
+        step_out[0] = step_raw_grad.astype(jnp.bfloat16)
+        skip_grad = exact_right(grad * values, summing)
+
+        @pl.when(pl.program_id(0) == 0)
+        def _():
+            taps_v_out[...] = jnp.zeros_like(taps_v_out)
+            taps_s_out[...] = jnp.zeros_like(taps_s_out)
+            head_out[...] = jnp.zeros_like(head_out)
+            for room in (room_v, room_s):
+                room[:EDGE] = jnp.zeros((EDGE, room.shape[1]), jnp.float32)
+                room[EDGE + length :] = jnp.zeros((EDGE, room.shape[1]), jnp.float32)
+
+        head_out[0:1] += jnp.sum(step_raw_grad, axis=0, keepdims=True)
+        head_out[1:2] += jnp.sum(-rate * step * log_grad, axis=0, keepdims=True)
+        head_out[2:3] += jnp.sum(skip_grad, axis=0, keepdims=True)
+        room_v[EDGE : EDGE + length] = value_grad * silu_slope(pre_v)
+        room_s[EDGE : EDGE + length, : double // 2] = b_grad * silu_slope(pre_s[:, : double // 2])
+        room_s[EDGE : EDGE + length, double // 2 :] = part_ref[0, :, double // 2 :] * silu_slope(
+            pre_s[:, double // 2 :]
+        )
+        first = EDGE - window + 1
+        for room, ext, taps, taps_out, out, edge_out in (
+            (room_v, ev_ref, vt_ref, taps_v_out, value_out, edge_v_out),
+            (room_s, es_ref, st_ref, taps_s_out, state_out, edge_s_out),
+        ):
+            pre_grad = room[EDGE : EDGE + length]
+            taps_out[window : window + 1] += jnp.sum(pre_grad, axis=0, keepdims=True)
+            inside = jnp.zeros(pre_grad.shape, jnp.float32)
+            before = jnp.zeros((EDGE, pre_grad.shape[1]), jnp.float32)
+            for tap in range(window):
+                moved = ext[0, first + tap : first + tap + length]
+                taps_out[tap : tap + 1] += jnp.sum(pre_grad * moved, axis=0, keepdims=True)
+                ahead = window - 1 - tap
+                weight = taps[tap : tap + 1]
+                inside = inside + weight * room[EDGE + ahead : EDGE + ahead + length]
+                before = before + weight * room[ahead : ahead + EDGE]
+            out[0] = inside
+            edge_out[0] = before
+
+    return call(
+        kernel,
+        (count,),
+        [
+            each((length, inner)), each((length, double)), each((length + EDGE, inner)),
+            each((length + EDGE, double)), each((length, 128)), each((length, 128)),
+            each((length, inner)), each((length, inner)), each((length, inner)), each((length, double)),
+            each((inner, double // 2)), each((inner, double // 2)), whole(value_taps.shape),
+            whole(state_taps.shape), whole(step_shift.shape), whole(decay_rate.shape), whole(skip.shape),
+        ],
+        [
+            each((length, inner)), each((length, double)), each((EDGE, inner)), each((EDGE, double)),
+            each((length, 128)), whole((8, inner)), whole((8, double)), whole((8, 128)),
+        ],
+        [
+            f32(count, length, inner), f32(count, length, double), f32(count, EDGE, inner),
+            f32(count, EDGE, double), bf16(count, length, 128), f32(8, inner), f32(8, double), f32(8, 128),
+        ],
+        [
+            pltpu.VMEM((length + 2 * EDGE, inner), jnp.float32),
+            pltpu.VMEM((length + 2 * EDGE, double), jnp.float32),
+        ],
+    )(
+        pre_value, pre_state, ext_value, ext_state, step_raw, decay_sum, ssm, ssm_grad, scaled_grad,
+        state_part, entering, exit_grad, value_taps, state_taps, step_shift, decay_rate, skip,
+    )
+
+
+def mixer_project_back(
+    order, value_local, state_local, edge_value, edge_state, gate_grad, step_grad, x,
+    gate_w, value_w, state_w, step_w, owners,
+):
+    count, length, inner = value_local.shape
+    double, model = state_local.shape[2], x.shape[2]
+    rows = length // owners
+    half = owners // 2
+
+    def kernel(
+        order_ref, value_ref, state_ref, ev_ref, es_ref, gate_grad_ref, step_grad_ref, x_ref,
+        gate_ref, vw_ref, sw_ref, step_ref,
+        own_out, partner_out, value_out, state_out, gain_out, mixed,
+    ):
+        body_rows = length - EDGE
+        for part, edge, out in ((value_ref, ev_ref, value_out), (state_ref, es_ref, state_out)):
+            out[0, :body_rows] = part[0, :body_rows].astype(jnp.bfloat16)
+            out[0, body_rows:] = (part[0, body_rows:] + edge[0]).astype(jnp.bfloat16)
+        grad = product(gate_grad_ref[0], gate_ref[...], TRANSPOSED)
+        grad = grad + product(value_out[0], vw_ref[...], TRANSPOSED)
+        grad = grad + product(state_out[0], sw_ref[...], TRANSPOSED)
+        grad = grad + product(step_grad_ref[0], step_ref[...], TRANSPOSED)
+        value = x_ref[0].astype(jnp.float32)
+        scale = lax.rsqrt(jnp.mean(value * value, axis=-1, keepdims=True) + epsilon)
+
+        @pl.when(pl.program_id(0) == 0)
+        def _():
+            gain_out[...] = jnp.zeros_like(gain_out)
+
+        gain_out[...] += jnp.sum(grad * value * scale, axis=0, keepdims=True)
+        mixed[...] = grad.astype(jnp.bfloat16)
+        for place in range(owners):
+            start = pl.multiple_of(order_ref[place] * rows, rows)
+            target = own_out if place < half else partner_out
+            target[place % half] = mixed[pl.ds(start, rows)]
+
+    blocks = pl.BlockSpec((half, rows, model), lambda b, *_: (0, b, 0))
+    return call(
+        kernel,
+        (count,),
+        [
+            each((length, inner)), each((length, double)), each((EDGE, inner)), each((EDGE, double)),
+            each((length, inner)), each((length, 128)), each((length, model)), whole(gate_w.shape),
+            whole(value_w.shape), whole(state_w.shape), whole(step_w.shape),
+        ],
+        [blocks, blocks, each((length, inner)), each((length, double)), whole((8, model))],
+        [
+            bf16(half, count * rows, model), bf16(half, count * rows, model), bf16(count, length, inner),
+            bf16(count, length, double), f32(8, model),
+        ],
+        [pltpu.VMEM((length, model), jnp.bfloat16)],
+        1,
+    )(
+        order, value_local, state_local, edge_value, edge_state, gate_grad, step_grad, x,
+        gate_w, value_w, state_w, step_w,
+    )
 
 
 def body(
@@ -285,8 +754,8 @@
             conv_state_bias,
         ]
     )
-    route_rows = route_weight.reshape(row_count, -1)
-    chosen = routes.reshape(row_count, -1, 1) == jnp.arange(expert_count, dtype=jnp.int32)
+    route_rows = route_weight.transpose(1, 0, 2).reshape(row_count, -1)
+    chosen = routes.transpose(1, 0, 2).reshape(row_count, -1, 1) == jnp.arange(expert_count, dtype=jnp.int32)
     coefficient = jnp.sum(jnp.where(chosen, route_rows[..., None], 0.0), axis=1)
     coefficient_high = rounded(coefficient)
     coefficient_low = coefficient - coefficient_high
@@ -328,77 +797,67 @@
     down_shared = seq_gather(shared_down).reshape(hidden_own, model_width)
     gate_weight, up_weight, down_weight = expert_gate[0], routed_up_weights[0], expert_down[0]
 
-    inputs = tokens.astype(jnp.float32)
-    normed = rms_scale(inputs, gain_first.astype(jnp.float32)).astype(jnp.bfloat16)
-    gate_raw = jnp.dot(normed, gate_proj, preferred_element_type=jnp.float32)
-    value_raw = jnp.dot(normed, value_proj, preferred_element_type=jnp.float32)
-    state_raw = jnp.dot(normed, state_whole, preferred_element_type=jnp.float32)
-    step_raw = jnp.dot(normed, step_proj, preferred_element_type=jnp.float32)
-    conv_input = jnp.concatenate([value_raw, state_raw], axis=-1)
-    edge_rows = shifted(conv_input[slot_count - window + 1 :], "seq", 1)
-    extended = jnp.concatenate([edge_rows, conv_input], axis=0)
-    conv_weight = jnp.concatenate([conv_value, conv_state_whole.astype(jnp.float32).T], axis=1)
-    conv_bias = jnp.concatenate([conv_value_bias, conv_bias_whole.astype(jnp.float32)])
-
-    def first_piece(ext_values, weight_values, bias_values, step_values, bias_step, decay_values):
-        return conv_decay(
-            ext_values,
-            weight_values,
-            bias_values,
-            step_values,
-            bias_step,
-            decay_values,
-            inner_width,
-            STATE,
-        )
-
-    mixer_inputs, first_back = jax.vjp(
-        first_piece, extended, conv_weight, conv_bias, step_raw, step_bias, decay_log
-    )
-    values, input_matrix_b, c_matrix, step_size, log_decay = mixer_inputs
-    local_out, state_back = jax.vjp(state_update, values, input_matrix_b, step_size, log_decay)
-    decay_total, local_state = local_out
-    entering = seq_entering(decay_total, local_state, False)
-
-    def second_piece(
-        in_values,
-        in_bmatrix,
-        in_cmatrix,
-        in_step,
-        in_decay,
-        in_state,
-        in_skip,
-        in_gate,
-        in_gain_mix,
-    ):
-        result = ssd_output(in_values, in_bmatrix, in_cmatrix, in_step, in_decay, in_state, in_skip)
-        gated_part = result.reshape(in_gate.shape) * jax.nn.silu(in_gate)
-        return (gated_part, gated_part * in_gain_mix)
-
-    gated_pair, second_back = jax.vjp(
-        second_piece,
-        values,
-        input_matrix_b,
-        c_matrix,
-        step_size,
-        log_decay,
+    order = relative_owner().reshape(-1).astype(jnp.int32)
+    head_count = step_proj.shape[1]
+    start_row = lax.axis_index("mp") * shared_expert_rows
+    sequences = tokens.transpose(1, 0, 2)
+    own_inputs = wide(
+        lax.dynamic_slice_in_dim(sequences, start_row, shared_expert_rows, 1)
+    ).reshape(row_count, model_width)
+    edge_rows = shifted(tokens[slot_count - window + 1 :].transpose(1, 0, 2), "seq", 1)
+    edge_rows = jnp.pad(edge_rows, ((0, 0), (EDGE - window + 1, 0), (0, 0)))
+    lane_pad = ((0, 0), (0, 128 - head_count))
+    step_weight = jnp.pad(step_proj, lane_pad)
+    step_shift = jnp.pad(step_bias[None], lane_pad)
+    decay_rate = jnp.pad(decay_log[None], lane_pad)
+    skip_row = jnp.pad(skip_gain[None], lane_pad)
+    state_taps = wide(conv_state_whole).T
+    mixer = mixer_input(
+        sequences,
+        edge_rows,
+        wide(gain_first)[None],
+        gate_proj,
+        value_proj,
+        state_whole,
+        step_weight,
+        conv_value,
+        state_taps,
+        conv_value_bias[None],
+        wide(conv_bias_whole)[None],
+        step_shift,
+        decay_rate,
+        head_count,
+    )
+    normed, gate_raw, ext_value, ext_state, pre_value, pre_state, step_raw, decay_sum, local_state = mixer
+    decay_total = jnp.exp(decay_sum[:, slot_count - 1, :head_count])
+    state_shape = (seq_count, head_count, inner_width // head_count, STATE)
+
+    def entering_of(state, backward):
+        moved = seq_entering(decay_total, state.reshape(state_shape), backward)
+        return moved.reshape(state.shape)
+
+    entering = entering_of(local_state, False)
+    within = mixer_within(pre_value, pre_state, step_raw, decay_sum, step_shift, skip_row, head_count)
+    ssm, scaled_low, squares, mix_own, mix_partner = mixer_output(
+        order,
+        within,
+        pre_state,
+        decay_sum,
         entering,
-        skip_gain,
         gate_raw,
-        mixer_gain,
-    )
-    gated_out, scaled = gated_pair
-    scaled_low = scaled.astype(jnp.bfloat16)
-    mix_part = jnp.dot(scaled_low, out_proj, preferred_element_type=jnp.float32)
-    squares = jnp.sum(gated_out * gated_out, axis=-1)
+        mixer_gain[None],
+        out_proj,
+        head_count,
+        mp_count,
+    )
+    squares = squares[:, 0].reshape(seq_count, mp_count, shared_expert_rows).transpose(1, 0, 2)
     square_sum = jnp.sum(mp_exchange(squares.reshape(mp_count, row_count)), axis=0)
-    mix_send = bits(mix_part).reshape(mp_count, row_count, model_width)
-    pre_mix = scatter_relative(*to_relative(mix_send))
+    ring = mp_count // 4
+    pre_mix = scatter_relative(
+        mix_own.reshape(ring, 2, row_count, model_width),
+        mix_partner.reshape(ring, 2, row_count, model_width),
+    )
     inv_norm = lax.rsqrt(square_sum / INNER + epsilon)[:, None]
-    start_row = lax.axis_index("mp") * shared_expert_rows
-    own_inputs = lax.dynamic_slice_in_dim(inputs, start_row, shared_expert_rows, 0).reshape(
-        row_count, model_width
-    )
     hidden = own_inputs + pre_mix * inv_norm
     ffn_input = rms_scale(hidden, wide(gain_second)).astype(jnp.bfloat16)
 
@@ -431,14 +890,18 @@
         return cut_value[0], cut_value[1]
 
     output = hidden + scatter_relative(*halves(partial_out))
-    block_out = output.astype(jnp.bfloat16).reshape(shared_expert_rows, seq_count, model_width)
+
+    def slots_first(value):
+        return value.reshape(seq_count, shared_expert_rows, model_width).transpose(1, 0, 2)
+
+    block_out = slots_first(output.astype(jnp.bfloat16))
     position = (
         lax.axis_index("seq") * slot_count
         + start_row
         + jnp.arange(shared_expert_rows, dtype=jnp.int32)
     )
-    valid_mask = (position[:, None] < lengths[None, :]).astype(jnp.float32).reshape(row_count, 1)
-    grad_out = (output - target.astype(jnp.float32).reshape(row_count, model_width)) * valid_mask
+    valid_mask = (position[None, :] < lengths[:, None]).astype(jnp.float32).reshape(row_count, 1)
+    grad_out = (output - wide(target).transpose(1, 0, 2).reshape(row_count, model_width)) * valid_mask
     grad_own, grad_partner = gather_relative(bits(grad_out))
     all_grads = jnp.stack([grad_own, grad_partner]).reshape(-1, model_width)
     route_grads = bits(shares * wide(all_grads))
@@ -490,83 +953,78 @@
         ],
         axis=-1,
     )
-    mix_all = from_relative(*gather_relative(mix_grad_send))
-    mix_all = mix_all.reshape(slot_count, seq_count, -1)
-    mix_grad_all = mix_all[..., :model_width]
-    sum_grad = wide(mix_all[..., model_width]) + wide(mix_all[..., model_width + 1])
-    out_proj_grad = jnp.einsum(
-        "sbc,sbd->cd", scaled_low, mix_grad_all, preferred_element_type=jnp.float32
-    )
-    scaled_grad = jnp.einsum(
-        "sbd,cd->sbc", mix_grad_all, out_proj, preferred_element_type=jnp.float32
-    )
-    gated_grad = 2.0 * gated_out * sum_grad[..., None]
-    (
-        out_values_grad,
-        out_bmatrix_grad,
-        out_cmatrix_grad,
-        out_step_grad,
-        out_decay_grad,
-        entering_grad,
-        skip_gain_grad,
-        gate_raw_grad,
-        mixer_gain_grad,
-    ) = second_back((gated_grad, scaled_grad))
-    exit_grad = seq_entering(decay_total, entering_grad, True)
-    total_grad = jnp.sum(entering * exit_grad, axis=(-2, -1))
-    tail_values_grad, tail_bmatrix_grad, tail_step_grad, tail_decay_grad = state_back(
-        (total_grad, exit_grad)
-    )
-    ext_grad, conv_weight_grad, conv_bias_grad, step_raw_grad, step_bias_grad, decay_log_grad = (
-        first_back(
-            (
-                out_values_grad + tail_values_grad,
-                out_bmatrix_grad + tail_bmatrix_grad,
-                out_cmatrix_grad,
-                out_step_grad + tail_step_grad,
-                out_decay_grad + tail_decay_grad,
-            )
+    mix_blocks = jnp.stack(gather_relative(mix_grad_send)).reshape(mp_count, row_count, -1)
+    mix_grad_all, ssm_grad, gate_grad, entering_grad, mixer_gain_grad = mixer_output_back(
+        order,
+        mix_blocks,
+        gate_raw,
+        ssm,
+        pre_state,
+        decay_sum,
+        mixer_gain[None],
+        out_proj,
+        head_count,
+    )
+    exit_grad = entering_of(entering_grad, True)
+    scaled_value_grad, state_part_grad = mixer_within_back(
+        pre_value, pre_state, step_raw, decay_sum, step_shift, ssm_grad, entering, head_count
+    )
+    value_local, state_local, edge_value, edge_state, step_grad, taps_value, taps_state, head_grads = (
+        mixer_input_back(
+            pre_value,
+            pre_state,
+            ext_value,
+            ext_state,
+            step_raw,
+            decay_sum,
+            ssm,
+            ssm_grad,
+            scaled_value_grad,
+            state_part_grad,
+            entering,
+            exit_grad,
+            conv_value,
+            state_taps,
+            step_shift,
+            decay_rate,
+            skip_row,
+            head_count,
         )
     )
-    edge_grad = shifted(ext_grad[: window - 1], "seq", -1)
-    conv_grad = ext_grad[window - 1 :] + jnp.concatenate(
-        [jnp.zeros((slot_count - window + 1,) + ext_grad.shape[1:], jnp.float32), edge_grad], axis=0
-    )
-    conv_grad_low = conv_grad.astype(jnp.bfloat16)
-    value_grad = conv_grad_low[..., :inner_width]
-    state_grad = conv_grad_low[..., inner_width:]
-    gate_grad = gate_raw_grad.astype(jnp.bfloat16)
-    step_grad = step_raw_grad.astype(jnp.bfloat16)
-    partial_value = jnp.einsum(
-        "sbc,dc->sbd", gate_grad, gate_proj, preferred_element_type=jnp.float32
-    )
-    partial_value = partial_value + jnp.einsum(
-        "sbc,dc->sbd", value_grad, value_proj, preferred_element_type=jnp.float32
-    )
-    partial_value = partial_value + jnp.einsum(
-        "sbc,dc->sbd", state_grad, state_whole, preferred_element_type=jnp.float32
-    )
-    partial_value = partial_value + jnp.einsum(
-        "sbh,dh->sbd", step_grad, step_proj, preferred_element_type=jnp.float32
-    )
-    gate_proj_grad = jnp.einsum(
-        "sbd,sbc->dc", normed, gate_grad, preferred_element_type=jnp.float32
-    )
-    value_proj_grad = jnp.einsum(
-        "sbd,sbc->dc", normed, value_grad, preferred_element_type=jnp.float32
-    )
-    state_proj_grad = jnp.einsum(
-        "sbd,sbc->dc", normed, state_grad, preferred_element_type=jnp.float32
-    )
-    step_proj_grad = jnp.einsum(
-        "sbd,sbh->dh", normed, step_grad, preferred_element_type=jnp.float32
-    )
-    conv_value_grad = conv_weight_grad[:, :inner_width]
-    conv_state_grad = conv_weight_grad[:, inner_width:].T
-    conv_value_bias_grad = conv_bias_grad[:inner_width]
-    conv_state_bias_grad = conv_bias_grad[inner_width:]
-    whole_width = lax.rsqrt(jnp.mean(inputs * inputs, axis=-1, keepdims=True) + epsilon)
-    in_gain_grad = jnp.sum(partial_value * inputs * whole_width, axis=(0, 1))
+    edges = shifted(jnp.concatenate([edge_value, edge_state], axis=-1), "seq", -1)
+    last_own, last_partner, value_grad, state_grad, in_gain_grad = mixer_project_back(
+        order,
+        value_local,
+        state_local,
+        edges[..., :inner_width],
+        edges[..., inner_width:],
+        gate_grad,
+        step_grad,
+        sequences,
+        gate_proj,
+        value_proj,
+        state_whole,
+        step_weight,
+        mp_count,
+    )
+
+    def by_rows(value):
+        return value.reshape(slot_count * seq_count, -1)
+
+    out_proj_grad = t_dot(by_rows(scaled_low), by_rows(mix_grad_all))
+    gate_proj_grad = t_dot(by_rows(normed), by_rows(gate_grad))
+    value_proj_grad = t_dot(by_rows(normed), by_rows(value_grad))
+    state_proj_grad = t_dot(by_rows(normed), by_rows(state_grad))
+    step_proj_grad = t_dot(by_rows(normed), by_rows(step_grad))[:, :head_count]
+    conv_value_grad = taps_value[:window]
+    conv_state_grad = taps_state[:window].T
+    conv_value_bias_grad = taps_value[window]
+    conv_state_bias_grad = taps_state[window]
+    step_bias_grad = head_grads[0, :head_count]
+    decay_log_grad = head_grads[1, :head_count]
+    skip_gain_grad = head_grads[2, :head_count]
+    mixer_gain_grad = mixer_gain_grad[0]
+    in_gain_grad = in_gain_grad[0]
 
     def by_owner(value):
         parts = value.reshape((seq_devices, mp_count, -1))
@@ -583,20 +1041,14 @@
     extra_rows = -(-extra.shape[1] // (8 * model_width)) * 8
     extra_size = extra.shape[1]
     extra = jnp.pad(extra, ((0, 0), (0, extra_rows * model_width - extra_size)))
-    last_send = jnp.concatenate(
-        [
-            bits(partial_value).reshape(mp_count, row_count, model_width),
-            bits(extra).reshape(mp_count, extra_rows, model_width),
-        ],
-        axis=1,
-    )
-    last_sum = scatter_relative(*to_relative(last_send))
-    normed_grad = last_sum[:row_count]
-    extra_sum = last_sum[row_count:].reshape(-1)[:extra_size]
+    extra_own, extra_partner = to_relative(bits(extra).reshape(mp_count, extra_rows, model_width))
+    normed_grad = scatter_relative(
+        last_own.reshape(ring, 2, row_count, model_width),
+        last_partner.reshape(ring, 2, row_count, model_width),
+    )
+    extra_sum = scatter_relative(extra_own, extra_partner).reshape(-1)[:extra_size]
     _, first_norm_back = jax.vjp(rms_scale, own_inputs, wide(gain_first))
-    tokens_grad = (first_norm_back(normed_grad)[0] + hidden_grad_share).reshape(
-        shared_expert_rows, seq_count, model_width
-    )
+    tokens_grad = slots_first(first_norm_back(normed_grad)[0] + hidden_grad_share)
     sizes = [gain_rows * state_width, gain_rows, gain_rows]
     parts, at = [], 0
     for size in sizes:

time: 743 us -> 602 us (0.81)
  local copies, waits for them, and re-layouts: 168 us -> 81.6 us
  other arithmetic: 156 us -> 77.4 us
  matrix products: 112 us -> 43.5 us
  Pallas kernels: 0 us -> 65.6 us
  waiting for transfers between devices: 197 us -> 225 us
    dot_general x27 -> x0, matrix products: 75.3 us -> none  [the longest x3 13.8 us: ssd_output(): within = jnp.einsum('tsbh,sbhp->tbhp', weighted, scaled, precision=highest)]
    pallas_call x0 -> x7, Pallas kernels: none -> 65.6 us  [the longest x1 13.1 us: mixer_input_back(): call(kernel, (count,), [each((length, inner)), each((length, double)), ea...]
    another operation x10 -> x2, other arithmetic: 40.2 us -> 5.04 us  [body(): jnp.stack(gather_relative(mix_grad_send)).reshape(mp_count, row_count, -1)]
    reshape x10 -> x0, local copies, waits for them, and re-layouts: 23.7 us -> none  [the longest x1 6.81 us: body(): mix_all = mix_all.reshape(slot_count, seq_count, -1)]
    ppermute x61 -> x69, waiting for transfers between devices: 155 us -> 170 us  [mp_permute(): return lax.ppermute(value, 'mp', [(i, target(i)) for i in range(count)])]
    dot_general x6 -> x11, matrix products: 12.1 us -> 22.7 us  [t_dot(): lax.dot_general(left, right, (((0,), (0,)), ((), ())), preferred_element_...]
    concatenate x5 -> x1, other arithmetic: 9.71 us -> 0.09 us  [body(): jnp.concatenate([edge_value, edge_state], axis=-1)]
    gather x3 -> x2, local copies, waits for them, and re-layouts: 10.3 us -> 1.43 us  [to_relative(): both = value[order.reshape(-1)].reshape((2, ring, 2) + value.shape[1:])]
  transfers between devices with their start and end apart: 82 -> 90, of which waited for: 43 -> 48; matrix products, arithmetic and copies ran while one was open for 31% -> 23% of each run, Pallas kernels for 0% -> 7%
where the time goes in v2:
time: 602 us; the launch traced here: 591 us
  waiting for transfers between devices  225 us (37%)
  starting transfers between devices  94.5 us (16%)
  local copies, waits for them, and re-layouts  81.6 us (14%)
  other arithmetic  77.4 us (13%)
  Pallas kernels  65.6 us (11%)
  matrix products  43.5 us (7%)
    ppermute x69, waiting for transfers between devices, mp_permute(): return lax.ppermute(value, 'mp', [(i, target(i)) for i in range(count)])  170 us
    ppermute x69, starting transfers between devices, mp_permute(): return lax.ppermute(value, 'mp', [(i, target(i)) for i in range(count)])  47.9 us
    ppermute x6, waiting for transfers between devices, seq_sum(): return wide(low) + wide(lax.ppermute(low, 'seq', [(0, 1), (1, 0)]))  30.5 us
    dot_general x11, matrix products, t_dot(): lax.dot_general(left, right, (((0,), (0,)), ((), ())), preferred_element_...  22.7 us
    unnamed x185, local copies, waits for them, and re-layouts  22.6 us
    all_to_all x4, starting transfers between devices, mp_exchange(): return lax.all_to_all(value, 'mp', split_axis=0, concat_axis=0, tiled=True)  21.8 us
    all_to_all x4, waiting for transfers between devices, mp_exchange(): return lax.all_to_all(value, 'mp', split_axis=0, concat_axis=0, tiled=True)  13.9 us
    pallas_call x1, Pallas kernels, mixer_input_back(): call(kernel, (count,), [each((length, inner)), each((length, double)), ea...  13.1 us
  transfers between devices with their start and end apart: 90, of which 48 were waited for; matrix products, arithmetic and copies ran while one was open for 23% of the time, Pallas kernels for 7%

profile of v2, /device:TPU:0, one launch (start us, length us, event | category | flops | bytes accessed | tf_op | source)
XLA Modules:
  0.0 590.7 jit_solution(7805170885471487362)
XLA Ops:
  5.1 5.0 collective-permute-start
  22.3 3.6 collective-permute-done.3
  26.3 3.7 collective-permute-start.6
  31.2 4.5 collective-permute-done.6
  35.7 12.4 %collective-permute-done.5 = bf16[2,2,26896]{2,1,0:T(2,128)(2,1)S(1)} collective-permute-done((bf16[2,2,26896]{2,1,0:T(2,128)(2,1)S(1)}, bf16[2,2,26896]{2,1,0:T(2,128)(2,1)S(1)}, u32[]{:S(2)}, u32[]{:S(2)}) %collective-permute-start.5) | collective-permute-done | bytes 215200 | tf_op jit(solution)/shard_map/ppermute | solution.py:66
  58.8 11.0 %shard_map.425 = (bf16[4,256,1536]{2,1,0:T(8,128)(2,1)}, f32[4,256,192]{2,1,0:T(8,128)}, f32[4,272,192]{2,1,0:T(8,128)}, f32[4,272,256]{2,1,0:T(8,128)}, f32[4,2...) custom-call(bf16[4,256,1536]{2,1,0:T(8,128)(2,1)} %bitcast.514, ...), custom_call_target="tpu_custom_call" | custom-call | tf_op jit(solution)/shard_map/pallas_call | solution.py:343
  73.3 5.9 shard_map.426.within_ref
  80.3 7.8 %shard_map.427 = (f32[4,256,192]{2,1,0:T(8,128)}, bf16[4,256,192]{2,1,0:T(8,128)(2,1)}, f32[4,8,256]{2,1,0:T(8,128)}, bf16[8,64,1536]{2,1,0:T(8,128)(2,1)}, bf16[8,64,1536]{2,1,0:T(8,128)(2,1)}) custom-call(s32[16]{0:T(128)} %add.501.order_ref, f32[4,256,192]{2,1,0:T(8,128)} %shard_map.426.within_ref, f32[4,256,256]{2,1,0:T(8,128)} %get-tuple-element.58.ps_ref, ...), custom_call_target="tpu_custom_call" | custom-call | tf_op jit(solution)/shard_map/pallas_call | solution.py:430
  94.8 5.6 all-to-all-start.1
  119.8 5.4 collective-permute-done.12
  127.7 6.0 %collective-permute-done.13 = bf16[64,1536]{1,0:T(8,128)(2,1)S(1)} collective-permute-done((bf16[64,1536]{1,0:T(8,128)(2,1)S(1)}, bf16[64,1536]{1,0:T(8,128)(2,1)S(1)}, u32[]{:S(2)}, u32[]{:S(2)}) %collective-permute-start.13) | collective-permute-done | bytes 196640 | tf_op jit(solution)/shard_map/ppermute | solution.py:66
  136.0 5.2 all-to-all-start
  142.8 4.7 all-to-all-done
  149.9 4.3 collective-permute-done.9
  160.6 5.8 collective-permute-done.17
  167.9 6.0 %collective-permute-done.19 = bf16[64,1536]{1,0:T(8,128)(2,1)S(1)} collective-permute-done((bf16[64,1536]{1,0:T(8,128)(2,1)S(1)}, bf16[64,1536]{1,0:T(8,128)(2,1)S(1)}, u32[]{:S(2)}, u32[]{:S(2)}) %collective-permute-start.19) | collective-permute-done | bytes 196640 | tf_op jit(solution)/shard_map/ppermute | solution.py:66
  175.7 5.9 collective-permute-done.21
  183.1 4.2 collective-permute-done.22
  217.9 5.7 collective-permute-done.30
  234.3 5.5 collective-permute-done.32
  241.8 7.6 %collective-permute-done.33 = bf16[64,1536]{1,0:T(8,128)(2,1)} collective-permute-done((bf16[64,1536]{1,0:T(8,128)(2,1)}, bf16[64,1536]{1,0:T(8,128)(2,1)}, u32[]{:S(2)}, u32[]{:S(2)}) %collective-permute-start.33) | collective-permute-done | bytes 196640 | tf_op jit(solution)/shard_map/ppermute | solution.py:66
  252.2 6.9 %collective-permute-done.35 = bf16[64,1536]{1,0:T(8,128)(2,1)S(1)} collective-permute-done((bf16[64,1536]{1,0:T(8,128)(2,1)S(1)}, bf16[64,1536]{1,0:T(8,128)(2,1)S(1)}, u32[]{:S(2)}, u32[]{:S(2)}) %collective-permute-start.35) | collective-permute-done | bytes 196640 | tf_op jit(solution)/shard_map/ppermute | solution.py:66
  260.6 8.1 %collective-permute-done.37 = bf16[64,1536]{1,0:T(8,128)(2,1)S(1)} collective-permute-done((bf16[64,1536]{1,0:T(8,128)(2,1)S(1)}, bf16[64,1536]{1,0:T(8,128)(2,1)S(1)}, u32[]{:S(2)}, u32[]{:S(2)}) %collective-permute-start.37) | collective-permute-done | bytes 196640 | tf_op jit(solution)/shard_map/ppermute | solution.py:66
  270.2 6.0 %collective-permute-done.39 = bf16[64,1536]{1,0:T(8,128)(2,1)S(1)} collective-permute-done((bf16[64,1536]{1,0:T(8,128)(2,1)S(1)}, bf16[64,1536]{1,0:T(8,128)(2,1)S(1)}, u32[]{:S(2)}, u32[]{:S(2)}) %collective-permute-start.39) | collective-permute-done | bytes 196640 | tf_op jit(solution)/shard_map/ppermute | solution.py:66
  277.7 4.2 collective-permute-done.40
  285.8 5.0 copy.278
  324.7 4.9 collective-permute-done.46
  342.8 5.2 all-to-all-start.3
  371.6 4.8 collective-permute-done.51
  378.5 7.0 %collective-permute-done.53 = bf16[64,1664]{1,0:T(8,128)(2,1)S(1)} collective-permute-done((bf16[64,1664]{1,0:T(8,128)(2,1)}, bf16[64,1664]{1,0:T(8,128)(2,1)S(1)}, u32[]{:S(2)}, u32[]{:S(2)}) %collective-permute-start.53) | collective-permute-done | bytes 213024 | tf_op jit(solution)/shard_map/ppermute | solution.py:66
  387.4 5.8 collective-permute-done.55
  394.4 4.8 collective-permute-done.56
  400.6 4.0 add_bitcast_fusion.2
  404.7 4.1 add_bitcast_fusion.1
  408.8 26.3 %collective-permute-done.85 = bf16[512,1536]{1,0:T(8,128)(2,1)} collective-permute-done((bf16[512,1536]{1,0:T(8,128)(2,1)}, bf16[512,1536]{1,0:T(8,128)(2,1)}, u32[]{:S(2)}, u32[]{:S(2)}) %collective-permute-start.85) | collective-permute-done | bytes 1572896 | tf_op jit(solution)/shard_map/ppermute | solution.py:176
  435.1 3.5 add_bitcast_fusion
  439.7 3.6 pad_maximum_fusion
  443.2 8.0 %shard_map.428 = (bf16[4,256,1536]{2,1,0:T(8,128)(2,1)}, f32[4,256,192]{2,1,0:T(8,128)}, bf16[4,256,192]{2,1,0:T(8,128)(2,1)}, f32[4,192,128]{2,1,0:T(8,128)}, f32[8,192]{1,0:T(8,128)}) custom-call(s32[16]{0:T(128)} %add.501.order_ref, bf16[16,64,1664]{2,1,0:T(8,128)(2,1)} %bitcast.521, f32[4,256,192]{2,1,0:T(8,128)} %get-tuple-element.62.gate_ref, ...), custom_call_target="tpu_custom_call" | custom-call | tf_op jit(solution)/shard_map/pallas_call | solution.py:480
  455.2 9.1 %shard_map.429 = (f32[4,256,192]{2,1,0:T(8,128)}, f32[4,256,256]{2,1,0:T(8,128)}) custom-call(f32[4,256,192]{2,1,0:T(8,128)} %get-tuple-element.57.pv_ref, f32[4,256,256]{2,1,0:T(8,128)} %get-tuple-element.58.ps_ref, f32[4,256,128]{2,1,0:T(8,128)} %get-tuple-element.59.step_ref, f32[4,256,128]{2,1,0:T(8,128)} %get-tuple-element.60.decay_ref, ...), custom_call_target="tpu_custom_call" | custom-call | tf_op jit(solution)/shard_map/pallas_call | solution.py:524
  470.1 13.1 %shard_map.430 = (f32[4,256,192]{2,1,0:T(8,128)}, f32[4,256,256]{2,1,0:T(8,128)}, f32[4,16,192]{2,1,0:T(8,128)}, f32[4,16,256]{2,1,0:T(8,128)}, bf16[4,256,128]{...) custom-call(f32[4,256,192]{2,1,0:T(8,128)} %get-tuple-element.57.pv_ref, ...), custom_call_target="tpu_custom_call" | custom-call | tf_op jit(solution)/shard_map/pallas_call | solution.py:622
  487.4 5.8 all-to-all-start.2
  494.8 4.7 all-to-all-done.2
  504.8 3.8 collective-permute-done.59
  509.9 10.7 %shard_map.431 = (bf16[8,64,1536]{2,1,0:T(8,128)(2,1)}, bf16[8,64,1536]{2,1,0:T(8,128)(2,1)}, bf16[4,256,192]{2,1,0:T(8,128)(2,1)}, bf16[4,256,256]{2,1,0:T(8,128)(2,1)}, f32[8,1536]{1,0:T(8,128)}) custom-call(s32[16]{0:T(128)} %add.501.order_ref, f32[4,256,192]{2,1,0:T(8,128)} %get-tuple-element.73.value_ref, f32[4,256,256]{2,1,0:T(8,128)} %get-tuple-element.74.state_ref, ...), custom_call_target="tpu_custom_call" | custom-call | tf_op jit(solution)/shard_map/pallas_call | solution.py:687
  545.7 4.2 collective-permute-done.78
  553.7 4.4 collective-permute-done.75
  571.7 6.0 %collective-permute-done.66 = bf16[64,1536]{1,0:T(8,128)(2,1)} collective-permute-done((bf16[64,1536]{1,0:T(8,128)(2,1)}, bf16[64,1536]{1,0:T(8,128)(2,1)}, u32[]{:S(2)}, u32[]{:S(2)}) %collective-permute-start.66) | collective-permute-done | bytes 196640 | tf_op jit(solution)/shard_map/ppermute | solution.py:66
  580.2 6.1 %collective-permute-done.67 = bf16[64,1536]{1,0:T(8,128)(2,1)S(1)} collective-permute-done((bf16[64,1536]{1,0:T(8,128)(2,1)S(1)}, bf16[64,1536]{1,0:T(8,128)(2,1)S(1)}, u32[]{:S(2)}, u32[]{:S(2)}) %collective-permute-start.67) | collective-permute-done | bytes 196640 | tf_op jit(solution)/shard_map/ppermute | solution.py:66
  (580 shorter events, 281.9 us)
Async XLA Ops:
  5.1 14.3 %collective-permute-start = (bf16[4,3,1536]{2,1,0:T(4,128)(2,1)S(1)}, bf16[4,3,1536]{2,1,0:T(4,128)(2,1)S(1)}, u32[]{:S(2)}, u32[]{:S(2)}) collective-permute-start(bf16[4,3,1536]{2,1,0:T(4,128)(2,1)S(1)} %slice_bitcast_fusion.40), channel_id=1, source_target_pairs={{0,16},{1,17},{2,18},{3,19},{4,20},{5,21},{6,22},{7,23},{8,24},{9,... | collective-permute-start | bytes 110600 | tf_op jit(solution)/shard_map/ppermute | solution.py:19
  26.3 9.4 %collective-permute-start.6 = (bf16[2,2,26896]{2,1,0:T(2,128)(2,1)S(1)}, bf16[2,2,26896]{2,1,0:T(2,128)(2,1)S(1)}, u32[]{:S(2)}, u32[]{:S(2)}) collective-permute-start(bf16[2,2,26896]{2,1,0:T(2,128)(2,1)S(1)} %pad_maximum_fusion.7), channel_id=1, source_target_pairs={{0,12},{1,13},{2,14},{3,15},{4,0},{5,1},{6,2},{7,3},{8,4},{9,5},{1... | collective-permute-start | bytes 645512 | tf_op jit(solution)/shard_map/ppermute | solution.py:66
  29.9 18.2 %collective-permute-start.5 = (bf16[2,2,26896]{2,1,0:T(2,128)(2,1)S(1)}, bf16[2,2,26896]{2,1,0:T(2,128)(2,1)S(1)}, u32[]{:S(2)}, u32[]{:S(2)}) collective-permute-start(bf16[2,2,26896]{2,1,0:T(2,128)(2,1)S(1)} %pad_maximum_fusion.7), channel_id=1, source_target_pairs={{0,8},{1,9},{2,10},{3,11},{4,12},{5,13},{6,14},{7,15},{8,0},{9,1},... | collective-permute-start | bytes 645512 | tf_op jit(solution)/shard_map/ppermute | solution.py:66
  29.9 18.2 %collective-permute-start.4 = (bf16[2,2,26896]{2,1,0:T(2,128)(2,1)S(1)}, bf16[2,2,26896]{2,1,0:T(2,128)(2,1)S(1)}, u32[]{:S(2)}, u32[]{:S(2)}) collective-permute-start(bf16[2,2,26896]{2,1,0:T(2,128)(2,1)S(1)} %pad_maximum_fusion.7), channel_id=1, source_target_pairs={{0,4},{1,5},{2,6},{3,7},{4,8},{5,9},{6,10},{7,11},{8,12},{9,13},{1... | collective-permute-start | bytes 645512 | tf_op jit(solution)/shard_map/ppermute | solution.py:66
  69.8 9.7 %collective-permute-start.7 = (f32[4,3,64,128]{3,2,1,0:T(8,128)}, f32[4,3,64,128]{3,2,1,0:T(8,128)S(1)}, u32[]{:S(2)}, u32[]{:S(2)}) collective-permute-start(f32[4,3,64,128]{3,2,1,0:T(8,128)} %bitcast.599), channel_id=1, source_target_pairs={{0,16},{1,17},{2,18},{3,19},{4,20},{5,21},{6,22},{7,23},{8,24},{9,... | collective-permute-start | bytes 1179656 | tf_op jit(solution)/shard_map/ppermute | solution.py:182
  88.1 25.7 %collective-permute-start.8 = (bf16[4,2,64,1536]{3,2,1,0:T(8,128)(2,1)}, bf16[4,2,64,1536]{3,2,1,0:T(8,128)(2,1)}, u32[]{:S(2)}, u32[]{:S(2)}) collective-permute-start(bf16[4,2,64,1536]{3,2,1,0:T(8,128)(2,1)} %bitcast.597), channel_id=1, source_target_pairs={{0,1},{1,0},{2,3},{3,2},{4,5},{5,4},{6,7},{7,6},{8,9},{9,8},{10,11... | collective-permute-start | bytes 4718600 | tf_op jit(solution)/shard_map/ppermute | solution.py:66
  94.8 14.6 %all-to-all-start.1 = ((bf16[16,2,3072]{2,1,0:T(2,128)(2,1)}), bf16[16,2,3072]{2,1,0:T(2,128)(2,1)S(1)}, u32[]{:S(2)}, u32[]{:S(2)}) async-start(bf16[16,2,3072]{2,1,0:T(2,128)(2,1)} %reshape.924), calls=%async_computation.1 | async-start | bytes 393216 | tf_op jit(solution)/shard_map/all_to_all | solution.py:193
  110.4 78.3 %collective-permute-start.24 = (bf16[16,6144]{1,0:T(8,128)(2,1)}, bf16[16,6144]{1,0:T(8,128)(2,1)}, u32[]{:S(2)}, u32[]{:S(2)}) collective-permute-start(bf16[16,6144]{1,0:T(8,128)(2,1)} %bitcast.504), channel_id=1, source_target_pairs={{0,16},{16,0},{1,17},{17,1},{2,18},{18,2},{3,19},{19,3},{4,20},{20... | collective-permute-start | bytes 589832 | tf_op jit(solution)/shard_map/ppermute | solution.py:159
  117.7 10.0 %collective-permute-start.11 = (bf16[64,1536]{1,0:T(8,128)(2,1)S(1)}, bf16[64,1536]{1,0:T(8,128)(2,1)S(1)}, u32[]{:S(2)}, u32[]{:S(2)}) collective-permute-start(bf16[64,1536]{1,0:T(8,128)(2,1)S(1)} %get-tuple-element.266), channel_id=1, source_target_pairs={{0,2},{1,3},{2,0},{3,1},{4,6},{5,7},{6,4},{7,5},{8,10},{9,11},{10,... | collective-permute-start | bytes 589832 | tf_op jit(solution)/shard_map/ppermute | solution.py:66
  126.8 21.3 %collective-permute-start.10 = (bf16[64,1536]{1,0:T(8,128)(2,1)}, bf16[64,1536]{1,0:T(8,128)(2,1)}, u32[]{:S(2)}, u32[]{:S(2)}) collective-permute-start(bf16[64,1536]{1,0:T(8,128)(2,1)} %get-tuple-element.267), channel_id=1, source_target_pairs={{0,2},{1,3},{2,0},{3,1},{4,6},{5,7},{6,4},{7,5},{8,10},{9,11},{10,... | collective-permute-start | bytes 589832 | tf_op jit(solution)/shard_map/ppermute | solution.py:66
  134.4 13.7 %collective-permute-start.14 = (bf16[64,1536]{1,0:T(8,128)(2,1)}, bf16[64,1536]{1,0:T(8,128)(2,1)}, u32[]{:S(2)}, u32[]{:S(2)}) collective-permute-start(bf16[64,1536]{1,0:T(8,128)(2,1)} %fusion.56), channel_id=1, source_target_pairs={{0,4},{1,5},{2,6},{3,7},{4,8},{5,9},{6,10},{7,11},{8,12},{9,13},{1... | collective-permute-start | bytes 589832 | tf_op jit(solution)/shard_map/ppermute | solution.py:66
  136.0 11.5 %all-to-all-start = ((f32[16,1,64]{2,1,0:T(1,128)}), f32[16,1,64]{2,1,0:T(1,128)S(1)}, u32[]{:S(2)}, u32[]{:S(2)}) async-start(f32[16,1,64]{2,1,0:T(1,128)} %bitcast.34), calls=%async_computation | async-start | bytes 16384 | tf_op jit(solution)/shard_map/all_to_all | solution.py:193
  159.0 8.9 %collective-permute-start.16 = (bf16[64,1536]{1,0:T(8,128)(2,1)S(1)}, bf16[64,1536]{1,0:T(8,128)(2,1)S(1)}, u32[]{:S(2)}, u32[]{:S(2)}) collective-permute-start(bf16[64,1536]{1,0:T(8,128)(2,1)S(1)} %multiply_convert_fusion.9), channel_id=1, source_target_pairs={{0,2},{1,3},{2,0},{3,1},{4,6},{5,7},{6,4},{7,5},{8,10},{9,11},{10,... | collective-permute-start | bytes 589832 | tf_op jit(solution)/shard_map/ppermute | solution.py:66
  166.5 9.2 %collective-permute-start.18 = (bf16[64,1536]{1,0:T(8,128)(2,1)S(1)}, bf16[64,1536]{1,0:T(8,128)(2,1)S(1)}, u32[]{:S(2)}, u32[]{:S(2)}) collective-permute-start(bf16[64,1536]{1,0:T(8,128)(2,1)S(1)} %collective-permute-done.17), channel_id=1, source_target_pairs={{0,2},{1,3},{2,0},{3,1},{4,6},{5,7},{6,4},{7,5},{8,10},{9,11},{10,... | collective-permute-start | bytes 589832 | tf_op jit(solution)/shard_map/ppermute | solution.py:66
  174.1 8.9 %collective-permute-start.20 = (bf16[64,1536]{1,0:T(8,128)(2,1)S(1)}, bf16[64,1536]{1,0:T(8,128)(2,1)S(1)}, u32[]{:S(2)}, u32[]{:S(2)}) collective-permute-start(bf16[64,1536]{1,0:T(8,128)(2,1)S(1)} %collective-permute-done.19), channel_id=1, source_target_pairs={{0,2},{1,3},{2,0},{3,1},{4,6},{5,7},{6,4},{7,5},{8,10},{9,11},{10,... | collective-permute-start | bytes 589832 | tf_op jit(solution)/shard_map/ppermute | solution.py:66
  217.3 10.5 %collective-permute-start.29 = (bf16[64,1536]{1,0:T(8,128)(2,1)S(1)}, bf16[64,1536]{1,0:T(8,128)(2,1)S(1)}, u32[]{:S(2)}, u32[]{:S(2)}) collective-permute-start(bf16[64,1536]{1,0:T(8,128)(2,1)S(1)} %get-tuple-element.260), channel_id=1, source_target_pairs={{0,2},{1,3},{2,0},{3,1},{4,6},{5,7},{6,4},{7,5},{8,10},{9,11},{10,... | collective-permute-start | bytes 589832 | tf_op jit(solution)/shard_map/ppermute | solution.py:66
  223.7 10.6 %collective-permute-start.28 = (bf16[64,1536]{1,0:T(8,128)(2,1)}, bf16[64,1536]{1,0:T(8,128)(2,1)}, u32[]{:S(2)}, u32[]{:S(2)}) collective-permute-start(bf16[64,1536]{1,0:T(8,128)(2,1)} %get-tuple-element.261), channel_id=1, source_target_pairs={{0,2},{1,3},{2,0},{3,1},{4,6},{5,7},{6,4},{7,5},{8,10},{9,11},{10,... | collective-permute-start | bytes 589832 | tf_op jit(solution)/shard_map/ppermute | solution.py:66
  232.9 8.9 %collective-permute-start.27 = (bf16[64,1536]{1,0:T(8,128)(2,1)}, bf16[64,1536]{1,0:T(8,128)(2,1)}, u32[]{:S(2)}, u32[]{:S(2)}) collective-permute-start(bf16[64,1536]{1,0:T(8,128)(2,1)} %get-tuple-element.258), channel_id=1, source_target_pairs={{0,2},{1,3},{2,0},{3,1},{4,6},{5,7},{6,4},{7,5},{8,10},{9,11},{10,... | collective-permute-start | bytes 589832 | tf_op jit(solution)/shard_map/ppermute | solution.py:66
  250.7 9.9 %collective-permute-start.34 = (bf16[64,1536]{1,0:T(8,128)(2,1)S(1)}, bf16[64,1536]{1,0:T(8,128)(2,1)S(1)}, u32[]{:S(2)}, u32[]{:S(2)}) collective-permute-start(bf16[64,1536]{1,0:T(8,128)(2,1)S(1)} %fusion.77), channel_id=1, source_target_pairs={{0,2},{1,3},{2,0},{3,1},{4,6},{5,7},{6,4},{7,5},{8,10},{9,11},{10,... | collective-permute-start | bytes 589832 | tf_op jit(solution)/shard_map/ppermute | solution.py:66
  259.1 9.6 %collective-permute-start.37 = (bf16[64,1536]{1,0:T(8,128)(2,1)S(1)}, bf16[64,1536]{1,0:T(8,128)(2,1)S(1)}, u32[]{:S(2)}, u32[]{:S(2)}) collective-permute-start(bf16[64,1536]{1,0:T(8,128)(2,1)S(1)} %collective-permute-done.35), channel_id=1, source_target_pairs={{0,4},{1,5},{2,6},{3,7},{4,8},{5,9},{6,10},{7,11},{8,12},{9,13},{1... | collective-permute-start | bytes 589832 | tf_op jit(solution)/shard_map/ppermute | solution.py:66
  259.1 11.0 %collective-permute-start.36 = (bf16[64,1536]{1,0:T(8,128)(2,1)S(1)}, bf16[64,1536]{1,0:T(8,128)(2,1)S(1)}, u32[]{:S(2)}, u32[]{:S(2)}) collective-permute-start(bf16[64,1536]{1,0:T(8,128)(2,1)S(1)} %collective-permute-done.35), channel_id=1, source_target_pairs={{0,2},{1,3},{2,0},{3,1},{4,6},{5,7},{6,4},{7,5},{8,10},{9,11},{10,... | collective-permute-start | bytes 589832 | tf_op jit(solution)/shard_map/ppermute | solution.py:66
  268.7 8.9 %collective-permute-start.38 = (bf16[64,1536]{1,0:T(8,128)(2,1)S(1)}, bf16[64,1536]{1,0:T(8,128)(2,1)S(1)}, u32[]{:S(2)}, u32[]{:S(2)}) collective-permute-start(bf16[64,1536]{1,0:T(8,128)(2,1)S(1)} %collective-permute-done.37), channel_id=1, source_target_pairs={{0,2},{1,3},{2,0},{3,1},{4,6},{5,7},{6,4},{7,5},{8,10},{9,11},{10,... | collective-permute-start | bytes 589832 | tf_op jit(solution)/shard_map/ppermute | solution.py:66
  306.6 14.1 %collective-permute-start.42 = (bf16[4,2,64,1536]{3,2,1,0:T(8,128)(2,1)S(1)}, bf16[4,2,64,1536]{3,2,1,0:T(8,128)(2,1)S(1)}, u32[]{:S(2)}, u32[]{:S(2)}) collective-permute-start(bf16[4,2,64,1536]{3,2,1,0:T(8,128)(2,1)S(1)} %bitcast.546), channel_id=1, source_target_pairs={{0,1},{1,0},{2,3},{3,2},{4,5},{5,4},{6,7},{7,6},{8,9},{9,8},{10,11... | collective-permute-start | bytes 4718600 | tf_op jit(solution)/shard_map/ppermute | solution.py:66
  310.3 29.5 %collective-permute-start.81 = (bf16[16,2,48,64]{3,2,0,1:T(8,128)(2,1)S(1)}, bf16[16,2,48,64]{3,2,0,1:T(8,128)(2,1)S(1)}, u32[]{:S(2)}, u32[]{:S(2)}) collective-permute-start(bf16[16,2,48,64]{3,2,0,1:T(8,128)(2,1)S(1)} %fusion.32), channel_id=1, source_target_pairs={{0,16},{16,0},{1,17},{17,1},{2,18},{18,2},{3,19},{19,3},{4,20},{20... | collective-permute-start | bytes 589832 | tf_op jit(solution)/shard_map/ppermute | solution.py:168
  324.0 9.4 %collective-permute-start.45 = (bf16[64,1536]{1,0:T(8,128)(2,1)S(1)}, bf16[64,1536]{1,0:T(8,128)(2,1)S(1)}, u32[]{:S(2)}, u32[]{:S(2)}) collective-permute-start(bf16[64,1536]{1,0:T(8,128)(2,1)S(1)} %get-tuple-element.254), channel_id=1, source_target_pairs={{0,2},{1,3},{2,0},{3,1},{4,6},{5,7},{6,4},{7,5},{8,10},{9,11},{10,... | collective-permute-start | bytes 589832 | tf_op jit(solution)/shard_map/ppermute | solution.py:66
  329.8 22.6 %collective-permute-start.82 = (bf16[32,1536]{1,0:T(8,128)(2,1)S(1)}, bf16[32,1536]{1,0:T(8,128)(2,1)}, u32[]{:S(2)}, u32[]{:S(2)}) collective-permute-start(bf16[32,1536]{1,0:T(8,128)(2,1)S(1)} %fusion.76), channel_id=1, source_target_pairs={{0,16},{16,0},{1,17},{17,1},{2,18},{18,2},{3,19},{19,3},{4,20},{20... | collective-permute-start | bytes 294920 | tf_op jit(solution)/shard_map/ppermute | solution.py:168
  330.9 69.8 %collective-permute-start.83 = (bf16[1536,512]{1,0:T(8,128)(2,1)}, bf16[1536,512]{1,0:T(8,128)(2,1)}, u32[]{:S(2)}, u32[]{:S(2)}) collective-permute-start(bf16[1536,512]{1,0:T(8,128)(2,1)} %convolution_convert_fusion.2), channel_id=1, source_target_pairs={{0,16},{16,0},{1,17},{17,1},{2,18},{18,2},{3,19},{19,3},{4,20},{20... | collective-permute-start | bytes 4718600 | tf_op jit(solution)/shard_map/ppermute | solution.py:176
  333.5 71.2 %collective-permute-start.84 = (bf16[1536,512]{1,0:T(8,128)(2,1)}, bf16[1536,512]{1,0:T(8,128)(2,1)}, u32[]{:S(2)}, u32[]{:S(2)}) collective-permute-start(bf16[1536,512]{1,0:T(8,128)(2,1)} %convolution_convert_fusion.1), channel_id=1, source_target_pairs={{0,16},{16,0},{1,17},{17,1},{2,18},{18,2},{3,19},{19,3},{4,20},{20... | collective-permute-start | bytes 4718600 | tf_op jit(solution)/shard_map/ppermute | solution.py:176
  337.7 10.4 %collective-permute-start.44 = (bf16[64,1536]{1,0:T(8,128)(2,1)S(1)}, bf16[64,1536]{1,0:T(8,128)(2,1)}, u32[]{:S(2)}, u32[]{:S(2)}) collective-permute-start(bf16[64,1536]{1,0:T(8,128)(2,1)S(1)} %get-tuple-element.255), channel_id=1, source_target_pairs={{0,2},{1,3},{2,0},{3,1},{4,6},{5,7},{6,4},{7,5},{8,10},{9,11},{10,... | collective-permute-start | bytes 589832 | tf_op jit(solution)/shard_map/ppermute | solution.py:66
  339.9 8.8 %collective-permute-start.48 = (bf16[64,1536]{1,0:T(8,128)(2,1)}, bf16[64,1536]{1,0:T(8,128)(2,1)}, u32[]{:S(2)}, u32[]{:S(2)}) collective-permute-start(bf16[64,1536]{1,0:T(8,128)(2,1)} %fusion.42), channel_id=1, source_target_pairs={{0,4},{1,5},{2,6},{3,7},{4,8},{5,9},{6,10},{7,11},{8,12},{9,13},{1... | collective-permute-start | bytes 589832 | tf_op jit(solution)/shard_map/ppermute | solution.py:66
  342.8 14.7 %all-to-all-start.3 = ((bf16[16,2,3072]{2,1,0:T(2,128)(2,1)}), bf16[16,2,3072]{2,1,0:T(2,128)(2,1)S(1)}, u32[]{:S(2)}, u32[]{:S(2)}) async-start(bf16[16,2,3072]{2,1,0:T(2,128)(2,1)} %reshape.926), calls=%async_computation.3 | async-start | bytes 393216 | tf_op jit(solution)/shard_map/all_to_all | solution.py:193
  348.1 87.1 %collective-permute-start.85 = (bf16[512,1536]{1,0:T(8,128)(2,1)}, bf16[512,1536]{1,0:T(8,128)(2,1)}, u32[]{:S(2)}, u32[]{:S(2)}) collective-permute-start(bf16[512,1536]{1,0:T(8,128)(2,1)} %fusion.6), channel_id=1, source_target_pairs={{0,16},{16,0},{1,17},{17,1},{2,18},{18,2},{3,19},{19,3},{4,20},{20... | collective-permute-start | bytes 4718600 | tf_op jit(solution)/shard_map/ppermute | solution.py:176
  348.7 13.2 %collective-permute-start.43 = (bf16[64,1536]{1,0:T(8,128)(2,1)}, bf16[64,1536]{1,0:T(8,128)(2,1)}, u32[]{:S(2)}, u32[]{:S(2)}) collective-permute-start(bf16[64,1536]{1,0:T(8,128)(2,1)} %get-tuple-element.252), channel_id=1, source_target_pairs={{0,2},{1,3},{2,0},{3,1},{4,6},{5,7},{6,4},{7,5},{8,10},{9,11},{10,... | collective-permute-start | bytes 589832 | tf_op jit(solution)/shard_map/ppermute | solution.py:66
  352.4 9.5 %collective-permute-start.49 = (bf16[64,1536]{1,0:T(8,128)(2,1)}, bf16[64,1536]{1,0:T(8,128)(2,1)}, u32[]{:S(2)}, u32[]{:S(2)}) collective-permute-start(bf16[64,1536]{1,0:T(8,128)(2,1)} %fusion.44), channel_id=1, source_target_pairs={{0,4},{1,5},{2,6},{3,7},{4,8},{5,9},{6,10},{7,11},{8,12},{9,13},{1... | collective-permute-start | bytes 589832 | tf_op jit(solution)/shard_map/ppermute | solution.py:66
  376.4 9.1 %collective-permute-start.53 = (bf16[64,1664]{1,0:T(8,128)(2,1)}, bf16[64,1664]{1,0:T(8,128)(2,1)S(1)}, u32[]{:S(2)}, u32[]{:S(2)}) collective-permute-start(bf16[64,1664]{1,0:T(8,128)(2,1)} %collective-permute-done.51), channel_id=1, source_target_pairs={{0,4},{1,5},{2,6},{3,7},{4,8},{5,9},{6,10},{7,11},{8,12},{9,13},{1... | collective-permute-start | bytes 638984 | tf_op jit(solution)/shard_map/ppermute | solution.py:66
  376.7 8.8 %collective-permute-start.52 = (bf16[64,1664]{1,0:T(8,128)(2,1)}, bf16[64,1664]{1,0:T(8,128)(2,1)S(1)}, u32[]{:S(2)}, u32[]{:S(2)}) collective-permute-start(bf16[64,1664]{1,0:T(8,128)(2,1)} %collective-permute-done.51), channel_id=1, source_target_pairs={{0,2},{1,3},{2,0},{3,1},{4,6},{5,7},{6,4},{7,5},{8,10},{9,11},{10,... | collective-permute-start | bytes 638984 | tf_op jit(solution)/shard_map/ppermute | solution.py:66
  385.5 8.8 %collective-permute-start.54 = (bf16[64,1664]{1,0:T(8,128)(2,1)S(1)}, bf16[64,1664]{1,0:T(8,128)(2,1)S(1)}, u32[]{:S(2)}, u32[]{:S(2)}) collective-permute-start(bf16[64,1664]{1,0:T(8,128)(2,1)S(1)} %collective-permute-done.53), channel_id=1, source_target_pairs={{0,2},{1,3},{2,0},{3,1},{4,6},{5,7},{6,4},{7,5},{8,10},{9,11},{10,... | collective-permute-start | bytes 638984 | tf_op jit(solution)/shard_map/ppermute | solution.py:66
  400.6 39.0 %collective-permute-start.57 = (bf16[4,2,64,1664]{3,2,1,0:T(8,128)(2,1)}, bf16[4,2,64,1664]{3,2,1,0:T(8,128)(2,1)}, u32[]{:S(2)}, u32[]{:S(2)}) collective-permute-start(bf16[4,2,64,1664]{3,2,1,0:T(8,128)(2,1)} %get-tuple-element.245), channel_id=1, source_target_pairs={{0,1},{1,0},{2,3},{3,2},{4,5},{5,4},{6,7},{7,6},{8,9},{9,8},{10,11... | collective-permute-start | bytes 5111816 | tf_op jit(solution)/shard_map/ppermute | solution.py:66
  451.2 18.1 %collective-permute-start.58 = (f32[4,3,64,128]{3,2,1,0:T(8,128)}, f32[4,3,64,128]{3,2,1,0:T(8,128)S(1)}, u32[]{:S(2)}, u32[]{:S(2)}) collective-permute-start(f32[4,3,64,128]{3,2,1,0:T(8,128)} %bitcast.598), channel_id=1, source_target_pairs={{16,0},{17,1},{18,2},{19,3},{20,4},{21,5},{22,6},{23,7},{24,8},{25... | collective-permute-start | bytes 1179656 | tf_op jit(solution)/shard_map/ppermute | solution.py:182
  464.3 71.1 %collective-permute-start.77 = (bf16[1536,192]{0,1:T(8,128)(2,1)}, bf16[1536,192]{0,1:T(8,128)(2,1)}, u32[]{:S(2)}, u32[]{:S(2)}) collective-permute-start(bf16[1536,192]{0,1:T(8,128)(2,1)} %fusion.8), channel_id=1, source_target_pairs={{0,16},{16,0},{1,17},{17,1},{2,18},{18,2},{3,19},{19,3},{4,20},{20... | collective-permute-start | bytes 1769480 | tf_op jit(solution)/shard_map/ppermute | solution.py:176
  469.3 70.6 %collective-permute-start.80 = (bf16[192,1536]{1,0:T(8,128)(2,1)}, bf16[192,1536]{1,0:T(8,128)(2,1)S(1)}, u32[]{:S(2)}, u32[]{:S(2)}) collective-permute-start(bf16[192,1536]{1,0:T(8,128)(2,1)} %fusion.10), channel_id=1, source_target_pairs={{0,16},{16,0},{1,17},{17,1},{2,18},{18,2},{3,19},{19,3},{4,20},{20... | collective-permute-start | bytes 1769480 | tf_op jit(solution)/shard_map/ppermute | solution.py:176
  487.4 12.1 %all-to-all-start.2 = ((f32[16,1,80]{2,1,0:T(1,128)}), f32[16,1,80]{2,1,0:T(1,128)S(1)}, u32[]{:S(2)}, u32[]{:S(2)}) async-start(f32[16,1,80]{2,1,0:T(1,128)} %bitcast.161), calls=%async_computation.2 | async-start | bytes 16384 | tf_op jit(solution)/shard_map/all_to_all | solution.py:193
  531.2 20.7 %collective-permute-start.60 = (bf16[4,2,64,1536]{3,2,1,0:T(8,128)(2,1)}, bf16[4,2,64,1536]{3,2,1,0:T(8,128)(2,1)S(1)}, u32[]{:S(2)}, u32[]{:S(2)}) collective-permute-start(bf16[4,2,64,1536]{3,2,1,0:T(8,128)(2,1)} %bitcast.596), channel_id=1, source_target_pairs={{0,1},{1,0},{2,3},{3,2},{4,5},{5,4},{6,7},{7,6},{8,9},{9,8},{10,11... | collective-permute-start | bytes 4718600 | tf_op jit(solution)/shard_map/ppermute | solution.py:66
  534.6 15.3 %collective-permute-start.78 = (bf16[1536,192]{0,1:T(8,128)(2,1)S(1)}, bf16[1536,192]{0,1:T(8,128)(2,1)S(1)}, u32[]{:S(2)}, u32[]{:S(2)}) collective-permute-start(bf16[1536,192]{0,1:T(8,128)(2,1)S(1)} %fusion.9), channel_id=1, source_target_pairs={{0,16},{16,0},{1,17},{17,1},{2,18},{18,2},{3,19},{19,3},{4,20},{20... | collective-permute-start | bytes 1769480 | tf_op jit(solution)/shard_map/ppermute | solution.py:176
  542.2 8.9 %collective-permute-start.70 = (bf16[24,1536]{1,0:T(8,128)(2,1)S(1)}, bf16[24,1536]{1,0:T(8,128)(2,1)S(1)}, u32[]{:S(2)}, u32[]{:S(2)}) collective-permute-start(bf16[24,1536]{1,0:T(8,128)(2,1)S(1)} %get-tuple-element.277), channel_id=1, source_target_pairs={{0,2},{1,3},{2,0},{3,1},{4,6},{5,7},{6,4},{7,5},{8,10},{9,11},{10,... | collective-permute-start | bytes 221192 | tf_op jit(solution)/shard_map/ppermute | solution.py:66
  542.8 10.9 %collective-permute-start.69 = (bf16[24,1536]{1,0:T(8,128)(2,1)S(1)}, bf16[24,1536]{1,0:T(8,128)(2,1)S(1)}, u32[]{:S(2)}, u32[]{:S(2)}) collective-permute-start(bf16[24,1536]{1,0:T(8,128)(2,1)S(1)} %get-tuple-element.274), channel_id=1, source_target_pairs={{0,2},{1,3},{2,0},{3,1},{4,6},{5,7},{6,4},{7,5},{8,10},{9,11},{10,... | collective-permute-start | bytes 221192 | tf_op jit(solution)/shard_map/ppermute | solution.py:66
  568.7 8.9 %collective-permute-start.66 = (bf16[64,1536]{1,0:T(8,128)(2,1)}, bf16[64,1536]{1,0:T(8,128)(2,1)}, u32[]{:S(2)}, u32[]{:S(2)}) collective-permute-start(bf16[64,1536]{1,0:T(8,128)(2,1)} %fusion.35), channel_id=1, source_target_pairs={{0,4},{1,5},{2,6},{3,7},{4,8},{5,9},{6,10},{7,11},{8,12},{9,13},{1... | collective-permute-start | bytes 589832 | tf_op jit(solution)/shard_map/ppermute | solution.py:66
  571.5 8.7 %collective-permute-start.61 = (bf16[64,1536]{1,0:T(8,128)(2,1)}, bf16[64,1536]{1,0:T(8,128)(2,1)S(1)}, u32[]{:S(2)}, u32[]{:S(2)}) collective-permute-start(bf16[64,1536]{1,0:T(8,128)(2,1)} %get-tuple-element.248), channel_id=1, source_target_pairs={{0,2},{1,3},{2,0},{3,1},{4,6},{5,7},{6,4},{7,5},{8,10},{9,11},{10,... | collective-permute-start | bytes 589832 | tf_op jit(solution)/shard_map/ppermute | solution.py:66
  (126 other events, 1316.2 us)

commit v3 on v2

--- a/solution.py
+++ b/solution.py
@@ -88,69 +88,23 @@
     return lax.dynamic_index_in_dim(value, index, axis, keepdims=False)
 
 
-def gather_relative(block):
-    ring = lax.axis_size("mp") // 4
-    held, pairs = block, []
-    for step in range(ring):
-        pairs.append(jnp.stack([held, across_pair(held)]))
-        if step < ring - 1:
-            held = ring_step(held)
-    own = jnp.stack(pairs)
-    return own, across_core(own)
-
-
 def relative_owner():
     ring = lax.axis_size("mp") // 4
     deep, pair, core = coordinates()
     cores = jnp.arange(2)[:, None, None]
-    steps = jnp.arange(ring)[None, :, None]
+    steps = jnp.array(distances())[None, :, None]
     pairs = jnp.arange(2)[None, None, :]
     return ((deep - steps) % ring) * 4 + (pair ^ pairs) * 2 + (core ^ cores)
 
 
-def scatter_relative(own, partner, kept=jnp.bfloat16):
-    ring = lax.axis_size("mp") // 4
-    half = (wide(own) + wide(across_core(partner))).astype(kept)
-    order = list(range(1, ring)) + [0]
-    received = {step: across_pair(half[step, 1]) for step in order}
-    moving = None
-    for step in range(1, ring):
-        total = wide(half[step, 0]) + wide(received[step])
-        if moving is not None:
-            total = total + wide(moving)
-        moving = ring_step(total.astype(kept))
-    return wide(half[0, 0]) + wide(received[0]) + wide(moving)
-
-
-def to_relative(value):
-    ring = lax.axis_size("mp") // 4
-    order = relative_owner()
-    both = value[order.reshape(-1)].reshape((2, ring, 2) + value.shape[1:])
-    return both[0], both[1]
-
-
-def from_relative(own, partner):
+def gather_small(block):
     count = lax.axis_size("mp")
+    every = jnp.stack([block] + [ring_step(block, step) for step in distances()[1:]])
+    every = jnp.stack([every, across_pair(every)], axis=1)
+    every = jnp.stack([every, across_core(every)])
     order = relative_owner().reshape(-1)
     place = jnp.zeros((count,), jnp.int32).at[order].set(jnp.arange(count, dtype=jnp.int32))
-    both = jnp.stack([own, partner])
-    return both.reshape((count,) + both.shape[3:])[place]
-
-
-def gather_small(block):
-    ring = lax.axis_size("mp") // 4
-    deep, pair, core = coordinates()
-    both = [block, across_core(block)]
-    rows = jnp.stack(both)
-    rows = jnp.stack([rows, across_pair(rows)])
-    turned = [rows] + [ring_step(rows, step) for step in range(1, ring)]
-    every = jnp.stack(turned)
-    count = lax.axis_size("mp")
-    flat = every.reshape((count,) + block.shape)
-    position = jnp.arange(count)
-    steps = (deep - position // 4) % ring
-    place = steps * 4 + (pair ^ ((position // 2) % 2)) * 2 + (core ^ (position % 2))
-    return flat[place]
+    return every.reshape((count,) + block.shape)[place]
 
 
 def seq_gather(value):
@@ -281,7 +235,7 @@
     return jax.ShapeDtypeStruct(shape, jnp.bfloat16)
 
 
-def call(kernel, grid, in_specs, out_specs, out_shape, scratch=(), prefetch=0):
+def call(kernel, grid, in_specs, out_specs, out_shape, scratch=(), prefetch=0, micros=2):
     return pl.pallas_call(
         kernel,
         grid_spec=pltpu.PrefetchScalarGridSpec(
@@ -293,6 +247,9 @@
         ),
         out_shape=out_shape,
         compiler_params=pltpu.CompilerParams(vmem_limit_bytes=56 * 1024 * 1024),
+        cost_estimate=pl.CostEstimate(
+            flops=int(micros * 9e+07), bytes_accessed=int(micros * 2.5e+05), transcendentals=0
+        ),
     )
 
 
@@ -359,6 +316,7 @@
             f32(count, length + EDGE, double), f32(count, length, inner), f32(count, length, double),
             f32(count, length, 128), f32(count, length, 128), f32(count, inner, double // 2),
         ],
+        micros=11,
     )(
         x, edge, gain, gate_w, value_w, state_w, step_w, value_taps, state_taps,
         value_bias, state_bias, step_shift, decay_rate,
@@ -399,6 +357,7 @@
         ],
         each((length, inner)),
         f32(count, length, inner),
+        micros=6,
     )(pre_value, pre_state, step_raw, decay_sum, step_shift, skip)
 
 
@@ -410,8 +369,9 @@
 
     def kernel(
         order_ref, within_ref, ps_ref, decay_ref, state_ref, gate_ref, gain_ref, out_ref,
-        ssm_out, scaled_out, square_out, own_out, partner_out, mixed,
+        ssm_out, scaled_out, *outs,
     ):
+        part_outs, mixed = outs[:-1], outs[-1]
         c_matrix = jax.nn.silu(ps_ref[0, :, double // 2 :])
         carried = fine(c_matrix, state_ref[0], TRANSPOSED)
         ssm = within_ref[0] + spread(jnp.exp(decay_ref[0]), heads, inner) * carried
@@ -419,14 +379,15 @@
         gated = ssm * jax.nn.silu(gate_ref[0])
         scaled = (gated * gain_ref[...]).astype(jnp.bfloat16)
         scaled_out[0] = scaled
-        square_out[0] = exact_left(jnp.ones((8, inner), jnp.bfloat16), gated * gated, TRANSPOSED)
-        mixed[...] = product(scaled, out_ref[...]).astype(jnp.bfloat16)
+        squares = jnp.sum(gated * gated, axis=-1, keepdims=True)
+        mixed[:, :model] = product(scaled, out_ref[...]).astype(jnp.bfloat16)
+        tail = jnp.zeros((length, 128), jnp.float32)
+        mixed[:, model:] = two_parts(squares, tail).astype(jnp.bfloat16)
         for place in range(owners):
             start = pl.multiple_of(order_ref[place] * rows, rows)
-            target = own_out if place < half else partner_out
-            target[place % half] = mixed[pl.ds(start, rows)]
-
-    blocks = pl.BlockSpec((half, rows, model), lambda b, *_: (0, b, 0))
+            part_outs[place // half][place % half // 2, place % 2] = mixed[pl.ds(start, rows)]
+
+    blocks = pl.BlockSpec((half // 2, 2, rows, model + 128), lambda b, *_: (0, 0, b, 0))
     return call(
         kernel,
         (count,),
@@ -434,30 +395,29 @@
             each((length, inner)), each((length, double)), each((length, 128)),
             each((inner, double // 2)), each((length, inner)), whole(gain.shape), whole(out_w.shape),
         ],
-        [each((length, inner)), each((length, inner)), each((8, length)), blocks, blocks],
-        [
-            f32(count, length, inner), bf16(count, length, inner), f32(count, 8, length),
-            bf16(half, count * rows, model), bf16(half, count * rows, model),
-        ],
-        [pltpu.VMEM((length, model), jnp.bfloat16)],
+        [each((length, inner)), each((length, inner))] + [blocks] * 2,
+        [f32(count, length, inner), bf16(count, length, inner)]
+        + [bf16(half // 2, 2, count * rows, model + 128)] * 2,
+        [pltpu.VMEM((length, model + 128), jnp.bfloat16)],
         1,
+        micros=7,
     )(order, within, pre_state, decay_sum, entering, gate_raw, gain, out_w)
 
 
 def mixer_output_back(order, blocks, gate_raw, ssm, pre_state, decay_sum, gain, out_w, heads):
     count, length, inner = ssm.shape
     double, model = pre_state.shape[2], out_w.shape[1]
-    owners, _, wide_model = blocks.shape
+    owners, wide_model = len(blocks), blocks[0].shape[1]
     rows = length // owners
 
-    def kernel(
-        order_ref, blocks_ref, gate_ref, ssm_ref, ps_ref, decay_ref, gain_ref, out_ref,
-        mix_out, ssm_grad_out, gate_grad_out, state_out, gain_out, sums,
-    ):
+    def kernel(order_ref, *refs):
+        blocks_ref = refs[:owners]
+        gate_ref, ssm_ref, ps_ref, decay_ref, gain_ref, out_ref = refs[owners : owners + 6]
+        mix_out, ssm_grad_out, gate_grad_out, state_out, gain_out, sums = refs[owners + 6 :]
         for place in range(owners):
             start = pl.multiple_of(order_ref[place] * rows, rows)
-            mix_out[0, pl.ds(start, rows)] = blocks_ref[place, :, :model]
-            sums[pl.ds(start, rows)] = blocks_ref[place, :, model:].astype(jnp.float32)
+            mix_out[0, pl.ds(start, rows)] = blocks_ref[place][:, :model]
+            sums[pl.ds(start, rows)] = blocks_ref[place][:, model:].astype(jnp.float32)
         sum_grad = sums[:, 0:1] + sums[:, 1:2]
         scaled_grad = product(mix_out[0], out_ref[...], TRANSPOSED)
         gate, value = gate_ref[0], ssm_ref[0]
@@ -480,8 +440,8 @@
     return call(
         kernel,
         (count,),
-        [
-            pl.BlockSpec((owners, rows, wide_model), lambda b, *_: (0, b, 0)),
+        [pl.BlockSpec((rows, wide_model), lambda b, *_: (b, 0))] * owners
+        + [
             each((length, inner)), each((length, inner)), each((length, double)), each((length, 128)),
             whole(gain.shape), whole(out_w.shape),
         ],
@@ -495,7 +455,8 @@
         ],
         [pltpu.VMEM((length, wide_model - model), jnp.float32)],
         1,
-    )(order, blocks, gate_raw, ssm, pre_state, decay_sum, gain, out_w)
+        micros=8,
+    )(order, *blocks, gate_raw, ssm, pre_state, decay_sum, gain, out_w)
 
 
 def mixer_within_back(pre_value, pre_state, step_raw, decay_sum, step_shift, ssm_grad, entering, heads):
@@ -530,6 +491,7 @@
         ],
         [each((length, inner)), each((length, double))],
         [f32(count, length, inner), f32(count, length, double)],
+        micros=9,
     )(pre_value, pre_state, step_raw, decay_sum, step_shift, ssm_grad, entering)
 
 
@@ -641,6 +603,7 @@
             pltpu.VMEM((length + 2 * EDGE, inner), jnp.float32),
             pltpu.VMEM((length + 2 * EDGE, double), jnp.float32),
         ],
+        micros=13,
     )(
         pre_value, pre_state, ext_value, ext_state, step_raw, decay_sum, ssm, ssm_grad, scaled_grad,
         state_part, entering, exit_grad, value_taps, state_taps, step_shift, decay_rate, skip,
@@ -659,8 +622,9 @@
     def kernel(
         order_ref, value_ref, state_ref, ev_ref, es_ref, gate_grad_ref, step_grad_ref, x_ref,
         gate_ref, vw_ref, sw_ref, step_ref,
-        own_out, partner_out, value_out, state_out, gain_out, mixed,
+        value_out, state_out, gain_out, *outs,
     ):
+        part_outs, mixed = outs[:-1], outs[-1]
         body_rows = length - EDGE
         for part, edge, out in ((value_ref, ev_ref, value_out), (state_ref, es_ref, state_out)):
             out[0, :body_rows] = part[0, :body_rows].astype(jnp.bfloat16)
@@ -680,10 +644,9 @@
         mixed[...] = grad.astype(jnp.bfloat16)
         for place in range(owners):
             start = pl.multiple_of(order_ref[place] * rows, rows)
-            target = own_out if place < half else partner_out
-            target[place % half] = mixed[pl.ds(start, rows)]
-
-    blocks = pl.BlockSpec((half, rows, model), lambda b, *_: (0, b, 0))
+            part_outs[place // half][place % half // 2, place % 2] = mixed[pl.ds(start, rows)]
+
+    blocks = pl.BlockSpec((half // 2, 2, rows, model), lambda b, *_: (0, 0, b, 0))
     return call(
         kernel,
         (count,),
@@ -692,17 +655,399 @@
             each((length, inner)), each((length, 128)), each((length, model)), whole(gate_w.shape),
             whole(value_w.shape), whole(state_w.shape), whole(step_w.shape),
         ],
-        [blocks, blocks, each((length, inner)), each((length, double)), whole((8, model))],
-        [
-            bf16(half, count * rows, model), bf16(half, count * rows, model), bf16(count, length, inner),
-            bf16(count, length, double), f32(8, model),
-        ],
+        [each((length, inner)), each((length, double)), whole((8, model))] + [blocks] * 2,
+        [bf16(count, length, inner), bf16(count, length, double), f32(8, model)]
+        + [bf16(half // 2, 2, count * rows, model)] * 2,
         [pltpu.VMEM((length, model), jnp.bfloat16)],
         1,
+        micros=10,
     )(
         order, value_local, state_local, edge_value, edge_state, gate_grad, step_grad, x,
         gate_w, value_w, state_w, step_w,
     )
+
+
+def total_of(refs):
+    result = refs[0][...].astype(jnp.float32)
+    for ref in refs[1:]:
+        result = result + ref[...].astype(jnp.float32)
+    return result
+
+
+def two_parts(value, like):
+    lane = lax.broadcasted_iota(jnp.int32, like.shape, len(like.shape) - 1)
+    high = value.astype(jnp.bfloat16).astype(jnp.float32)
+    return jnp.where(lane == 0, high, jnp.where(lane == 1, value - high, 0.0))
+
+
+def store_sum(total, tail, out_refs):
+    model = total.shape[-1] - tail
+    for place, out in enumerate(out_refs):
+        part = total[place] if len(out_refs) > 1 else total
+        out[:, :model] = part[:, :model].astype(jnp.bfloat16)
+        if tail:
+            column = part[:, model : model + 1] + part[:, model + 1 : model + 2]
+            out[:, model:] = two_parts(column, part[:, model:]).astype(jnp.bfloat16)
+
+
+def add_pairs(left, right, tail):
+    steps, _, rows, width = left.shape
+
+    def kernel(left_ref, right_ref, *out_refs):
+        for step in range(steps):
+            total = left_ref[step].astype(jnp.float32) + right_ref[step].astype(jnp.float32)
+            store_sum(total, tail, out_refs[2 * step : 2 * step + 2])
+
+    sums = call(
+        kernel,
+        (1,),
+        [whole(left.shape)] * 2,
+        [whole((rows, width))] * (2 * steps),
+        [bf16(rows, width)] * (2 * steps),
+        micros=3,
+    )(left, right)
+    return list(sums[0::2]), list(sums[1::2])
+
+
+def add_blocks(left, right, tail):
+    def kernel(left_ref, right_ref, out_ref):
+        store_sum(total_of((left_ref, right_ref)), tail, [out_ref])
+
+    return call(
+        kernel, (1,), [whole(left.shape)] * 2, whole(left.shape), bf16(*left.shape)
+    )(left, right)
+
+
+def after(value, *others):
+    return lax.optimization_barrier((value, others))[0]
+
+
+def distances():
+    ring = lax.axis_size("mp") // 4
+    return sorted(range(ring), key=lambda step: min(step, ring - step))
+
+
+def gather_blocks(block, early=None, ties=()):
+    ring = lax.axis_size("mp") // 4
+    own, partner, result = [], [], None
+    arrived = [block] + [ring_step(block, step) for step in distances()[1:]]
+    for step, tie in enumerate(ties):
+        arrived[step] = after(arrived[step], tie)
+    for step, held in enumerate(arrived):
+        both = [held, across_pair(held)]
+        if early is not None and step == ring // 2:
+            result = early(own + partner)
+        if early is not None and step == ring - 1:
+            partner += [across_core(value) for value in after(both, result[-1])]
+        else:
+            partner += [across_core(value) for value in both]
+        own += both
+    return own + partner, result
+
+
+def scatter_core(own, partner, tail=0):
+    return add_pairs(own, across_core(partner), tail)
+
+
+def scatter_deep(kept, sent, tail=0):
+    ring = len(kept)
+    received = [across_pair(block) for block in sent]
+    moving = [add_blocks(kept[step], received[step], tail) for step in range(1, ring)]
+    result = [kept[0], received[0]]
+    for step in range(1, ring):
+        result.append(ring_step(moving[step - 1], ring - distances()[step]))
+    return result, moving
+
+
+def hidden_rows(parts, own_inputs, gain):
+    rows, model = own_inputs.shape
+
+    def kernel(*refs):
+        part_refs, (x_ref, gain_ref, hidden_out, mix_out, inv_out, low_out) = refs[:-6], refs[-6:]
+        total = total_of(part_refs)
+        mixed = total[:, :model]
+        squares = total[:, model : model + 1] + total[:, model + 1 : model + 2]
+        inv_norm = lax.rsqrt(squares / INNER + epsilon)
+        hidden = x_ref[...].astype(jnp.float32) + mixed * inv_norm
+        hidden_out[...] = hidden
+        mix_out[...] = mixed
+        inv_out[...] = jnp.broadcast_to(inv_norm, inv_out.shape)
+        low_out[...] = rms_scale(hidden, gain_ref[...]).astype(jnp.bfloat16)
+
+    return call(
+        kernel,
+        (1,),
+        [whole(part.shape) for part in parts] + [whole(own_inputs.shape), whole(gain.shape)],
+        [whole((rows, model)), whole((rows, model)), whole((rows, 128)), whole((rows, model))],
+        [f32(rows, model), f32(rows, model), f32(rows, 128), bf16(rows, model)],
+    )(*parts, own_inputs, gain)
+
+
+def output_rows(parts, hidden, target, valid):
+    rows, model = hidden.shape
+
+    def kernel(*refs):
+        part_refs, (hidden_ref, target_ref, valid_ref, block_out, grad_out, low_out) = refs[:-6], refs[-6:]
+        output = hidden_ref[...] + total_of(part_refs)
+        block_out[...] = output.astype(jnp.bfloat16)
+        grad = (output - target_ref[...].astype(jnp.float32)) * valid_ref[...]
+        grad_out[...] = grad
+        low_out[...] = grad.astype(jnp.bfloat16)
+
+    return call(
+        kernel,
+        (1,),
+        [whole(part.shape) for part in parts]
+        + [whole(hidden.shape), whole(target.shape), whole(valid.shape)],
+        [whole((rows, model))] * 3,
+        [bf16(rows, model), f32(rows, model), bf16(rows, model)],
+    )(*parts, hidden, target, valid)
+
+
+def hidden_rows_back(parts, grad_out, hidden, mixed, inv_norm, gain):
+    rows, model = hidden.shape
+
+    def kernel(*refs):
+        part_refs = refs[:-8]
+        grad_ref, hidden_ref, mix_ref, inv_ref, gain_ref, hidden_out, send_out, gain_out = refs[-8:]
+        input_grad = total_of(part_refs)
+        value = hidden_ref[...]
+        scale = lax.rsqrt(jnp.mean(value * value, axis=-1, keepdims=True) + epsilon)
+        gained = input_grad * gain_ref[...]
+        dot_sum = jnp.sum(gained * value, axis=-1, keepdims=True)
+        grad = grad_ref[...] + scale * gained - value * (scale * scale * scale * dot_sum / model)
+        hidden_out[...] = grad
+        gain_out[...] = jnp.broadcast_to(
+            jnp.sum(input_grad * value * scale, axis=0, keepdims=True), gain_out.shape
+        )
+        inv = inv_ref[:, 0:1]
+        send_out[:, :model] = (grad * inv).astype(jnp.bfloat16)
+        sum_grad = jnp.sum(grad * mix_ref[...], axis=-1, keepdims=True) * (-0.5 / INNER) * inv * inv * inv
+        send_out[:, model:] = two_parts(sum_grad, inv_ref[...]).astype(jnp.bfloat16)
+
+    return call(
+        kernel,
+        (1,),
+        [whole(part.shape) for part in parts]
+        + [whole(grad_out.shape), whole(hidden.shape), whole(mixed.shape), whole(inv_norm.shape), whole(gain.shape)],
+        [whole((rows, model)), whole((rows, model + 128)), whole((8, model))],
+        [f32(rows, model), bf16(rows, model + 128), f32(8, model)],
+    )(*parts, grad_out, hidden, mixed, inv_norm, gain)
+
+
+def token_rows_back(parts, hidden_grad, own_inputs, gain):
+    rows, model = hidden_grad.shape
+
+    def kernel(*refs):
+        part_refs, (grad_ref, x_ref, gain_ref, out) = refs[:-4], refs[-4:]
+        normed_grad = total_of(part_refs)
+        value = x_ref[...].astype(jnp.float32)
+        scale = lax.rsqrt(jnp.mean(value * value, axis=-1, keepdims=True) + epsilon)
+        gained = normed_grad * gain_ref[...]
+        dot_sum = jnp.sum(gained * value, axis=-1, keepdims=True)
+        out[...] = grad_ref[...] + scale * gained - value * (scale * scale * scale * dot_sum / model)
+
+    return call(
+        kernel,
+        (1,),
+        [whole(part.shape) for part in parts]
+        + [whole(hidden_grad.shape), whole(own_inputs.shape), whole(gain.shape)],
+        whole((rows, model)),
+        f32(rows, model),
+    )(*parts, hidden_grad, own_inputs, gain)
+
+
+def store_parts(value, out_refs):
+    for place, out in enumerate(out_refs):
+        size = value.shape[0] // len(out_refs)
+        out[...] = value[place * size : (place + 1) * size].reshape(out.shape).astype(jnp.bfloat16)
+
+
+def experts_forward(blocks, share, gate_w, up_w, down_w, pair_w, pair_down):
+    rows, model = blocks[0].shape
+    count, hidden = len(blocks), gate_w.shape[1]
+    total, double = rows * count, pair_w.shape[1]
+
+    def kernel(*refs):
+        block_refs = refs[:count]
+        share_ref, gate_ref, up_ref, down_ref, pair_ref, pd_ref = refs[count : count + 6]
+        rows_out, gate_out, up_out, both_out, act_out, shared_out = refs[count + 6 : count + 12]
+        part_refs = refs[count + 12 :]
+        for place, block in enumerate(block_refs):
+            rows_out[place * rows : (place + 1) * rows] = block[...]
+        value = rows_out[...]
+        gate = product(value, gate_ref[...])
+        up = product(value, up_ref[...])
+        gate_out[...] = gate
+        up_out[...] = up
+        act = (jax.nn.silu(gate) * up).astype(jnp.bfloat16)
+        act_out[...] = act
+        both = product(value, pair_ref[...])
+        both_out[...] = both
+        lane = lax.broadcasted_iota(jnp.int32, both.shape, 1)
+        shared = jax.nn.silu(both) * pltpu.roll(both, double // 2, 1)
+        shared = jnp.where(lane < double // 2, shared, 0.0).astype(jnp.bfloat16)
+        shared_out[...] = shared
+        result = product(act, down_ref[...]).astype(jnp.bfloat16).astype(jnp.float32)
+        store_parts(share_ref[...] * result + product(shared, pd_ref[...]), part_refs)
+
+    parts, steps = 2, count // 4
+    return call(
+        kernel,
+        (1,),
+        [whole(block.shape) for block in blocks]
+        + [whole(w.shape) for w in (share, gate_w, up_w, down_w, pair_w, pair_down)],
+        [whole((total, model)), whole((total, hidden)), whole((total, hidden)), whole((total, double))]
+        + [whole((total, hidden)), whole((total, double))]
+        + [whole((steps, 2, rows, model))] * parts,
+        [bf16(total, model), f32(total, hidden), f32(total, hidden), f32(total, double)]
+        + [bf16(total, hidden), bf16(total, double)]
+        + [bf16(steps, 2, rows, model)] * parts,
+        micros=8,
+    )(*blocks, share, gate_w, up_w, down_w, pair_w, pair_down)
+
+
+def experts_backward(blocks, share, gate, up, both, gate_w, up_w, down_w, pair_w, pair_down):
+    rows, model = blocks[0].shape
+    count, hidden = len(blocks), gate_w.shape[1]
+    total, double = rows * count, pair_w.shape[1]
+
+    def kernel(*refs):
+        block_refs = refs[:count]
+        share_ref, g_ref, u_ref, both_ref, gate_ref, up_ref, down_ref, pair_ref, pd_ref = refs[count : count + 9]
+        grads_out, gate_out, up_out, shared_out = refs[count + 9 : count + 13]
+        part_refs = refs[count + 13 :]
+        for place, block in enumerate(block_refs):
+            grads_out[place * rows : (place + 1) * rows] = block[...]
+        grad = grads_out[...]
+        routed = (share_ref[...] * grad.astype(jnp.float32)).astype(jnp.bfloat16)
+        act_grad = product(routed, down_ref[...], TRANSPOSED)
+        gate = g_ref[...]
+        gate_out[...] = (act_grad * u_ref[...] * silu_slope(gate)).astype(jnp.bfloat16)
+        up_out[...] = (act_grad * jax.nn.silu(gate)).astype(jnp.bfloat16)
+        pair_value = both_ref[...]
+        turned = pltpu.roll(pair_value, double // 2, 1)
+        lane = lax.broadcasted_iota(jnp.int32, pair_value.shape, 1)
+        factor = jnp.where(lane < double // 2, turned * silu_slope(pair_value), jax.nn.silu(turned))
+        shared_out[...] = (product(grad, pd_ref[...], TRANSPOSED) * factor).astype(jnp.bfloat16)
+        result = product(gate_out[...], gate_ref[...], TRANSPOSED)
+        result = result + product(up_out[...], up_ref[...], TRANSPOSED)
+        store_parts(result + product(shared_out[...], pair_ref[...], TRANSPOSED), part_refs)
+
+    parts, steps = 2, count // 4
+    return call(
+        kernel,
+        (1,),
+        [whole(block.shape) for block in blocks]
+        + [whole(w.shape) for w in (share, gate, up, both, gate_w, up_w, down_w, pair_w, pair_down)],
+        [whole((total, model)), whole((total, hidden)), whole((total, hidden)), whole((total, double))]
+        + [whole((steps, 2, rows, model))] * parts,
+        [bf16(total, model), bf16(total, hidden), bf16(total, hidden), bf16(total, double)]
+        + [bf16(steps, 2, rows, model)] * parts,
+        micros=9,
+    )(*blocks, share, gate, up, both, gate_w, up_w, down_w, pair_w, pair_down)
+
+
+def experts_weights(groups):
+    rows, grads, share, act, shared, gate_grad, up_grad, pair_grad = groups[0]
+    model, hidden, double = rows.shape[1], act.shape[1], shared.shape[1]
+    width = 256 if model % 256 == 0 else model
+    each_group = len(groups[0])
+
+    steps = model // width
+    runs = [(2, 2, 2), (2, 2, 2), (2, 2, 2)] if steps == 6 else [(steps,)] * 3
+
+    def kernel(*refs):
+        *piece_outs, pair_out, pair_down_out = refs[len(groups) * each_group :]
+        sums = [0.0] * 5
+        for group in range(len(groups)):
+            x, g, s, a, sa, gg, ug, pg = refs[group * each_group : (group + 1) * each_group]
+            routed = (s[...] * g[...].astype(jnp.float32)).astype(jnp.bfloat16)
+            sums[0] = sums[0] + product(a[...], routed, ROWS_SUMMED)
+            sums[1] = sums[1] + product(x[...], gg[...], ROWS_SUMMED)
+            sums[2] = sums[2] + product(x[...], ug[...], ROWS_SUMMED)
+            sums[3] = sums[3] + product(x[...], pg[...], ROWS_SUMMED)
+            sums[4] = sums[4] + product(sa[...], g[...], ROWS_SUMMED)
+        pair_out[...] = sums[3].astype(jnp.bfloat16)
+        pair_down_out[...] = sums[4].astype(jnp.bfloat16)
+        number = 0
+        for kind in range(3):
+            first = 0
+            for run in runs[kind]:
+                store_piece(piece_outs[number], sums[kind], first, run)
+                number, first = number + 1, first + run
+
+    def store_piece(out, value, first, run):
+        @pl.when((pl.program_id(0) >= first) & (pl.program_id(0) < first + run))
+        def _():
+            out[...] = value.astype(jnp.bfloat16)
+
+    in_specs = []
+    for group in groups:
+        total = group[0].shape[0]
+        columns = pl.BlockSpec((total, width), lambda d: (0, d))
+        in_specs += [columns, columns] + [whole(value.shape) for value in group[2:]]
+
+    def piece_spec(kind, first, run):
+        if kind < 2:
+            return pl.BlockSpec((width, hidden), lambda d: (jnp.clip(d - first, 0, run - 1), 0))
+        return pl.BlockSpec((hidden, width), lambda d: (0, jnp.clip(d - first, 0, run - 1)))
+
+    out_specs, shapes = [], []
+    for place, kind in enumerate((2, 0, 1)):
+        first = 0
+        for run in runs[place]:
+            out_specs.append(piece_spec(kind, first, run))
+            shapes.append(bf16(width * run, hidden) if kind < 2 else bf16(hidden, width * run))
+            first += run
+    outs = call(
+        kernel,
+        (steps,),
+        in_specs,
+        out_specs
+        + [
+            pl.BlockSpec((width, double), lambda d: (d, 0)),
+            pl.BlockSpec((double, width), lambda d: (0, d)),
+        ],
+        shapes + [bf16(model, double), bf16(double, model)],
+        micros=11,
+    )(*[value for group in groups for value in group])
+    return outs[:-2], [len(run) for run in runs], outs[-2], outs[-1]
+
+
+def mixer_weights(normed, gate_grad, value_grad, state_grad):
+    count, length, model = normed.shape
+    width = 256 if model % 256 == 0 else model
+    inner = gate_grad.shape[2]
+
+    def kernel(normed_ref, gate_ref, value_ref, state_ref, both_out, state_out):
+        def summed(grad):
+            total = 0.0
+            for place in range(count):
+                total = total + product(normed_ref[place], grad[place], ROWS_SUMMED)
+            return total.astype(jnp.bfloat16)
+
+        def shift(start):
+            row = lax.broadcasted_iota(jnp.int32, (inner, 2 * inner), 0)
+            lane = lax.broadcasted_iota(jnp.int32, (inner, 2 * inner), 1)
+            return ones_of(row + start == lane)
+
+        both = product(summed(gate_ref), shift(0)) + product(summed(value_ref), shift(inner))
+        both_out[...] = both.astype(jnp.bfloat16)
+        state_out[...] = summed(state_ref)
+
+    grads = (gate_grad, value_grad, state_grad)
+    return call(
+        kernel,
+        (model // width,),
+        [pl.BlockSpec((count, length, width), lambda d: (0, 0, d))] + [whole(grad.shape) for grad in grads],
+        [
+            pl.BlockSpec((width, 2 * inner), lambda d: (d, 0)),
+            pl.BlockSpec((width, state_grad.shape[2]), lambda d: (d, 0)),
+        ],
+        [bf16(model, 2 * inner), bf16(model, state_grad.shape[2])],
+        micros=8,
+    )(normed, *grads)
 
 
 def body(
@@ -759,6 +1104,10 @@
     coefficient = jnp.sum(jnp.where(chosen, route_rows[..., None], 0.0), axis=1)
     coefficient_high = rounded(coefficient)
     coefficient_low = coefficient - coefficient_high
+    columns = shared_gate.shape[1] // (seq_devices * mp_count)
+    hidden_own = seq_devices * columns
+    pair_cut = jnp.stack([shared_gate, shared_up]).reshape(2, gain_rows, seq_devices, mp_count, columns)
+    pair_cut = pair_cut.transpose(3, 1, 0, 2, 4).reshape(mp_count, -1)
     both_packed = seq_gather(packed)
     small = gather_small(
         jnp.concatenate(
@@ -783,27 +1132,19 @@
     share = small[:, seq_devices * width :].reshape(mp_count, 2, row_count, expert_count)
     share = lax.dynamic_index_in_dim(share, lax.axis_index("mp"), 3, keepdims=False)
     share = wide(share[:, 0]) + wide(share[:, 1])
-    share_own, share_partner = to_relative(share)
-
-    columns = shared_gate.shape[1] // (seq_devices * mp_count)
-    hidden_own = seq_devices * columns
-    pair_cut = jnp.stack([shared_gate, shared_up]).reshape(2, gain_rows, seq_devices, mp_count, columns)
-    pair_moved = mp_exchange(pair_cut.transpose(3, 0, 1, 2, 4).reshape(mp_count, -1))
-    pair_all = seq_gather(pair_moved).reshape(
-        seq_devices, mp_count, 2, gain_rows, hidden_own
-    )
-    pair_all = pair_all.transpose(2, 0, 1, 3, 4).reshape(2, model_width, hidden_own)
-    gate_shared, up_shared = pair_all[0], pair_all[1]
-    down_shared = seq_gather(shared_down).reshape(hidden_own, model_width)
+    ring = mp_count // 4
+    order = relative_owner().reshape(-1).astype(jnp.int32)
+    share = share[order].reshape(2, ring, 2 * row_count)
+    ring_groups = [tuple(range(ring // 2)), tuple(range(ring // 2, ring))]
+    shares = [share[:, group[0] : group[-1] + 1].reshape(-1, 1) for group in ring_groups]
+
     gate_weight, up_weight, down_weight = expert_gate[0], routed_up_weights[0], expert_down[0]
 
-    order = relative_owner().reshape(-1).astype(jnp.int32)
     head_count = step_proj.shape[1]
     start_row = lax.axis_index("mp") * shared_expert_rows
     sequences = tokens.transpose(1, 0, 2)
-    own_inputs = wide(
-        lax.dynamic_slice_in_dim(sequences, start_row, shared_expert_rows, 1)
-    ).reshape(row_count, model_width)
+    own_inputs = lax.dynamic_slice_in_dim(sequences, start_row, shared_expert_rows, 1)
+    own_inputs = own_inputs.reshape(row_count, model_width)
     edge_rows = shifted(tokens[slot_count - window + 1 :].transpose(1, 0, 2), "seq", 1)
     edge_rows = jnp.pad(edge_rows, ((0, 0), (EDGE - window + 1, 0), (0, 0)))
     lane_pad = ((0, 0), (0, 128 - head_count))
@@ -838,7 +1179,7 @@
 
     entering = entering_of(local_state, False)
     within = mixer_within(pre_value, pre_state, step_raw, decay_sum, step_shift, skip_row, head_count)
-    ssm, scaled_low, squares, mix_own, mix_partner = mixer_output(
+    ssm, scaled_low, *mix_parts = mixer_output(
         order,
         within,
         pre_state,
@@ -850,110 +1191,93 @@
         head_count,
         mp_count,
     )
-    squares = squares[:, 0].reshape(seq_count, mp_count, shared_expert_rows).transpose(1, 0, 2)
-    square_sum = jnp.sum(mp_exchange(squares.reshape(mp_count, row_count)), axis=0)
-    ring = mp_count // 4
-    pre_mix = scatter_relative(
-        mix_own.reshape(ring, 2, row_count, model_width),
-        mix_partner.reshape(ring, 2, row_count, model_width),
-    )
-    inv_norm = lax.rsqrt(square_sum / INNER + epsilon)[:, None]
-    hidden = own_inputs + pre_mix * inv_norm
-    ffn_input = rms_scale(hidden, wide(gain_second)).astype(jnp.bfloat16)
-
-    def dot(left, right):
-        return jnp.dot(left, right, preferred_element_type=jnp.float32)
-
-    def dot_t(left, right):
-        return lax.dot_general(
-            left, right, (((1,), (1,)), ((), ())), preferred_element_type=jnp.float32
-        )
-
-    def t_dot(left, right):
-        return lax.dot_general(
-            left, right, (((0,), (0,)), ((), ())), preferred_element_type=jnp.float32
-        )
-
-    rows_own, rows_partner = gather_relative(ffn_input)
-    all_rows = jnp.stack([rows_own, rows_partner]).reshape(-1, model_width)
-    shares = jnp.stack([share_own, share_partner]).reshape(-1, 1)
-    gate_activation = dot(all_rows, gate_weight)
-    up_val = dot(all_rows, up_weight)
-    act_val = bits(jax.nn.silu(gate_activation) * up_val)
-    shared_gate_val = dot(all_rows, gate_shared)
-    shared_up_val = dot(all_rows, up_shared)
-    shared_act = bits(jax.nn.silu(shared_gate_val) * shared_up_val)
-    partial_out = shares * wide(bits(dot(act_val, down_weight))) + dot(shared_act, down_shared)
-
-    def halves(value):
-        cut_value = bits(value).reshape((2,) + rows_own.shape)
-        return cut_value[0], cut_value[1]
-
-    output = hidden + scatter_relative(*halves(partial_out))
-
-    def slots_first(value):
-        return value.reshape(seq_count, shared_expert_rows, model_width).transpose(1, 0, 2)
-
-    block_out = slots_first(output.astype(jnp.bfloat16))
+    first_gain, second_gain = wide(gain_first)[None], wide(gain_second)[None]
+    kept, sent = scatter_core(*mix_parts, 128)
+    pair_moved = mp_exchange(after(pair_cut, sent))
+    pair_weight = seq_gather(pair_moved).reshape(model_width, 2 * hidden_own)
+    down_shared = seq_gather(after(shared_down, sent)).reshape(hidden_own, model_width)
+    pair_down = jnp.concatenate([down_shared, down_shared])
+    mix_sums, _ = scatter_deep(kept, sent, 128)
+    hidden, pre_mix, inv_norm, ffn_input = hidden_rows(
+        after(mix_sums, pair_moved), own_inputs, second_gain
+    )
+
+    def of_group(blocks, group):
+        half = 2 * ring
+        picked = [2 * step + side for step in group for side in (0, 1)]
+        return [blocks[core * half + place] for core in (0, 1) for place in picked]
+
+    def of_groups(parts_of_groups):
+        both = [scatter_core(*parts) for parts in parts_of_groups]
+        return sum([kept for kept, _ in both], []), sum([sent for _, sent in both], [])
+
+    expert_weights = (gate_weight, up_weight, down_weight, pair_weight, pair_down)
+    row_blocks, first_forward = gather_blocks(
+        ffn_input, lambda blocks: experts_forward(blocks, shares[0], *expert_weights)
+    )
+    forwards = [
+        first_forward,
+        experts_forward(of_group(row_blocks, ring_groups[1]), shares[1], *expert_weights),
+    ]
     position = (
         lax.axis_index("seq") * slot_count
         + start_row
         + jnp.arange(shared_expert_rows, dtype=jnp.int32)
     )
     valid_mask = (position[None, :] < lengths[:, None]).astype(jnp.float32).reshape(row_count, 1)
-    grad_out = (output - wide(target).transpose(1, 0, 2).reshape(row_count, model_width)) * valid_mask
-    grad_own, grad_partner = gather_relative(bits(grad_out))
-    all_grads = jnp.stack([grad_own, grad_partner]).reshape(-1, model_width)
-    route_grads = bits(shares * wide(all_grads))
-    activation_gradient = dot_t(route_grads, down_weight)
-    egate_grad = bits(activation_gradient * up_val * silu_slope(gate_activation))
-    expert_up_gradient = bits(activation_gradient * jax.nn.silu(gate_activation))
-    shact_grad = dot_t(all_grads, down_shared)
-    sgate_grad = bits(shact_grad * shared_up_val * silu_slope(shared_gate_val))
-    sup_grad = bits(shact_grad * jax.nn.silu(shared_gate_val))
-    partial_rows = (
-        dot_t(egate_grad, gate_weight)
-        + dot_t(expert_up_gradient, up_weight)
-        + dot_t(sgate_grad, gate_shared)
-        + dot_t(sup_grad, up_shared)
-    )
-    ffn_input_grad = scatter_relative(*halves(partial_rows))
-    expert_down_grad = seq_sum(t_dot(act_val, route_grads))[None]
-    expert_gate_grad = seq_sum(t_dot(all_rows, egate_grad))[None]
-    expert_up_grad = seq_sum(t_dot(all_rows, expert_up_gradient))[None]
-    shared_down_grad = seq_scatter(
-        t_dot(shared_act, all_grads).reshape(seq_devices, columns, model_width)
-    )
-    pair_grad = jnp.stack([t_dot(all_rows, sgate_grad), t_dot(all_rows, sup_grad)])
-    pair_grad = pair_grad.reshape(2, seq_devices, mp_count, gain_rows, hidden_own)
-    pair_grad = seq_scatter(pair_grad.transpose(1, 2, 0, 3, 4))
-    pair_grad = wide(mp_exchange(bits(pair_grad).reshape(mp_count, -1)))
-    pair_grad = pair_grad.reshape(mp_count, 2, gain_rows, seq_devices, columns)
-    pair_grad = pair_grad.transpose(1, 2, 3, 0, 4).reshape(2, gain_rows, -1)
-    shared_gate_grad, shared_up_grad = pair_grad[0], pair_grad[1]
-
-    _, second_norm_back = jax.vjp(rms_scale, hidden, wide(gain_second))
-    hidden_part, ffn_gain_grad = second_norm_back(ffn_input_grad)
-    hidden_grad_share = grad_out + hidden_part
-    sum_grad_share = (
-        jnp.sum(hidden_grad_share * pre_mix, axis=-1, keepdims=True)
-        * (-0.5 / INNER)
-        * inv_norm
-        * inv_norm
-        * inv_norm
-    )
-    sum_high = rounded(sum_grad_share)
-    sum_low = sum_grad_share - sum_high
-    mix_grad_send = jnp.concatenate(
-        [
-            bits(hidden_grad_share * inv_norm),
-            bits(sum_high),
-            bits(sum_low),
-            jnp.zeros((row_count, 126), jnp.bfloat16),
-        ],
-        axis=-1,
-    )
-    mix_blocks = jnp.stack(gather_relative(mix_grad_send)).reshape(mp_count, row_count, -1)
+    block_rows, grad_out, grad_low = output_rows(
+        scatter_deep(*of_groups([result[6:] for result in forwards]))[0],
+        hidden,
+        target.transpose(1, 0, 2).reshape(row_count, model_width),
+        valid_mask,
+    )
+
+    def slots_first(value):
+        return value.reshape(seq_count, shared_expert_rows, model_width).transpose(1, 0, 2)
+
+    block_out = slots_first(block_rows)
+    grad_blocks, first_backward = gather_blocks(
+        grad_low,
+        lambda blocks: experts_backward(blocks, shares[0], *forwards[0][1:4], *expert_weights),
+    )
+    backwards = [
+        first_backward,
+        experts_backward(
+            of_group(grad_blocks, ring_groups[1]), shares[1], *forwards[1][1:4], *expert_weights
+        ),
+    ]
+    kept, sent = of_groups([result[4:] for result in backwards])
+    expert_parts, part_counts, pair_grad, pair_down_grad = experts_weights(
+        [
+            (after(ahead[0], sent), back[0], share_rows, ahead[4], ahead[5], back[1], back[2], back[3])
+            for ahead, back, share_rows in zip(forwards, backwards, shares)
+        ]
+    )
+    row_sums, _ = scatter_deep(after(kept, pair_down_grad), sent)
+
+    def seq_moved(value):
+        return lax.ppermute(value, "seq", [(0, 1), (1, 0)])
+
+    paired = seq_devices == 2
+    chunks = len(expert_parts)
+    expert_moved = [None] * chunks
+    early_chunks, mix_ties = 5 if chunks == 9 else 0, ()
+    if paired:
+        for place in range(early_chunks):
+            expert_moved[place] = seq_moved(expert_parts[place])
+        row_sums = after(row_sums, expert_moved[: min(early_chunks, 1)])
+        mix_ties = [(), *expert_moved[1 : max(early_chunks - 2, 1)]]
+    hidden_grad, mix_grad_send, ffn_gain_grad = hidden_rows_back(
+        row_sums,
+        grad_out,
+        hidden,
+        pre_mix,
+        inv_norm,
+        second_gain,
+    )
+    mix_blocks, _ = gather_blocks(mix_grad_send, None, mix_ties)
+    if paired and early_chunks:
+        mix_blocks = after(mix_blocks, expert_moved[early_chunks - 2])
     mix_grad_all, ssm_grad, gate_grad, entering_grad, mixer_gain_grad = mixer_output_back(
         order,
         mix_blocks,
@@ -966,8 +1290,31 @@
         head_count,
     )
     exit_grad = entering_of(entering_grad, True)
+    within_grad = ssm_grad
+    if paired and early_chunks:
+        within_grad = after(ssm_grad, expert_moved[early_chunks - 1])
     scaled_value_grad, state_part_grad = mixer_within_back(
-        pre_value, pre_state, step_raw, decay_sum, step_shift, ssm_grad, entering, head_count
+        pre_value, pre_state, step_raw, decay_sum, step_shift, within_grad, entering, head_count
+    )
+    def by_rows(value):
+        return value.reshape(slot_count * seq_count, -1)
+
+    out_proj_grad = lax.dot_general(
+        by_rows(scaled_low),
+        by_rows(after(mix_grad_all, scaled_value_grad)),
+        ROWS_SUMMED,
+        preferred_element_type=jnp.float32,
+    )
+    out_proj_part = bits(out_proj_grad)
+    scaled_value_grad = after(scaled_value_grad, out_proj_part)
+    if paired:
+        out_proj_moved = seq_moved(after(out_proj_part, scaled_value_grad))
+    if paired and early_chunks:
+        expert_moved[6] = seq_moved(expert_parts[6])
+        expert_moved[5] = seq_moved(after(expert_parts[5], scaled_value_grad))
+        exit_grad = after(exit_grad, expert_moved[6])
+    shared_down_grad = seq_scatter(
+        after(pair_down_grad, scaled_value_grad)[:hidden_own].reshape(seq_devices, columns, model_width)
     )
     value_local, state_local, edge_value, edge_state, step_grad, taps_value, taps_state, head_grads = (
         mixer_input_back(
@@ -991,8 +1338,28 @@
             head_count,
         )
     )
+    exact = (
+        taps_value[:window],
+        taps_value[window],
+        head_grads[0, :head_count],
+        head_grads[1, :head_count],
+        head_grads[2, :head_count],
+        mixer_gain_grad[0],
+        taps_state[:window].T,
+        taps_state[window],
+    )
+    flat = jnp.concatenate([part.reshape(-1) for part in exact])
+    step_proj_grad = lax.dot_general(
+        by_rows(normed), by_rows(step_grad), ROWS_SUMMED, preferred_element_type=jnp.float32
+    )[:, :head_count]
+    step_flat = step_proj_grad.reshape(-1)
     edges = shifted(jnp.concatenate([edge_value, edge_state], axis=-1), "seq", -1)
-    last_own, last_partner, value_grad, state_grad, in_gain_grad = mixer_project_back(
+    if paired:
+        flat = flat + seq_moved(flat)
+        edges = after(edges, flat, out_proj_moved, shared_down_grad, expert_moved[5:6] if early_chunks else ())
+    else:
+        flat = lax.psum(flat, "seq")
+    value_grad, state_grad, in_gain_grad, *last_parts = mixer_project_back(
         order,
         value_local,
         state_local,
@@ -1008,106 +1375,110 @@
         mp_count,
     )
 
-    def by_rows(value):
-        return value.reshape(slot_count * seq_count, -1)
-
-    out_proj_grad = t_dot(by_rows(scaled_low), by_rows(mix_grad_all))
-    gate_proj_grad = t_dot(by_rows(normed), by_rows(gate_grad))
-    value_proj_grad = t_dot(by_rows(normed), by_rows(value_grad))
-    state_proj_grad = t_dot(by_rows(normed), by_rows(state_grad))
-    step_proj_grad = t_dot(by_rows(normed), by_rows(step_grad))[:, :head_count]
-    conv_value_grad = taps_value[:window]
-    conv_state_grad = taps_state[:window].T
-    conv_value_bias_grad = taps_value[window]
-    conv_state_bias_grad = taps_state[window]
-    step_bias_grad = head_grads[0, :head_count]
-    decay_log_grad = head_grads[1, :head_count]
-    skip_gain_grad = head_grads[2, :head_count]
-    mixer_gain_grad = mixer_gain_grad[0]
+    if paired:
+        step_flat = step_flat + seq_moved(step_flat)
+        last_parts[0] = after(last_parts[0], step_flat)
+        if early_chunks:
+            expert_moved[7] = seq_moved(after(expert_parts[7], edges))
+            last_parts[0] = after(last_parts[0], expert_moved[7])
+    else:
+        step_flat = lax.psum(step_flat, "seq")
+    kept, sent = scatter_core(*last_parts)
+    if paired and early_chunks == 0:
+        expert_moved = [seq_moved(after(part, value_grad)) for part in expert_parts]
+    both_proj_grad, state_proj_grad = mixer_weights(
+        after(normed, sent), gate_grad, value_grad, state_grad
+    )
+    in_gain_grad, pair_grad = after((in_gain_grad, pair_grad), sent)
     in_gain_grad = in_gain_grad[0]
+    pair_extra = pair_grad.reshape(seq_devices, mp_count, -1)
 
     def by_owner(value):
-        parts = value.reshape((seq_devices, mp_count, -1))
-        return jnp.moveaxis(parts, 1, 0).reshape(mp_count, -1)
-
-    extra = jnp.concatenate(
-        [
-            by_owner(state_proj_grad),
-            by_owner(in_gain_grad),
-            by_owner(ffn_gain_grad),
-        ],
-        axis=-1,
-    )
-    extra_rows = -(-extra.shape[1] // (8 * model_width)) * 8
-    extra_size = extra.shape[1]
-    extra = jnp.pad(extra, ((0, 0), (0, extra_rows * model_width - extra_size)))
-    extra_own, extra_partner = to_relative(bits(extra).reshape(mp_count, extra_rows, model_width))
-    normed_grad = scatter_relative(
-        last_own.reshape(ring, 2, row_count, model_width),
-        last_partner.reshape(ring, 2, row_count, model_width),
-    )
-    extra_sum = scatter_relative(extra_own, extra_partner).reshape(-1)[:extra_size]
-    _, first_norm_back = jax.vjp(rms_scale, own_inputs, wide(gain_first))
-    tokens_grad = slots_first(first_norm_back(normed_grad)[0] + hidden_grad_share)
-    sizes = [gain_rows * state_width, gain_rows, gain_rows]
-    parts, at = [], 0
-    for size in sizes:
-        parts.append(extra_sum[at : at + seq_devices * size].reshape(seq_devices, size))
-        at += seq_devices * size
-    extra_own = seq_scatter(jnp.concatenate(parts, axis=-1))
-    state_proj_out = extra_own[: sizes[0]].reshape(gain_rows, state_width)
-    at = sizes[0]
-    in_gain_out = extra_own[at : at + gain_rows]
-    at += gain_rows
-    ffn_gain_out = extra_own[at : at + gain_rows]
-    conv_small = jnp.concatenate(
-        [
-            conv_state_grad.reshape(seq_devices, mp_count, -1),
-            conv_state_bias_grad.reshape(seq_devices, mp_count, -1),
-        ],
-        axis=-1,
-    )
-    conv_small = jnp.moveaxis(conv_small, 1, 0).reshape(mp_count, -1)
-    conv_small = jnp.sum(mp_exchange(conv_small), axis=0)
-    exact = (
-        step_proj_grad,
-        conv_value_grad,
-        conv_value_bias_grad,
-        step_bias_grad,
-        decay_log_grad,
-        skip_gain_grad,
-        mixer_gain_grad,
-        conv_small.reshape(seq_devices, -1),
-    )
-    flat = jnp.concatenate([part.reshape(-1) for part in exact])
-    if seq_devices == 2:
-        flat = flat + lax.ppermute(flat, "seq", [(0, 1), (1, 0)])
-    else:
-        flat = lax.psum(flat, "seq")
+        return value.reshape(seq_devices, mp_count, -1)
+
     exact_out, at = [], 0
     for part in exact:
         exact_out.append(flat[at : at + part.size].reshape(part.shape))
         at += part.size
-    conv_own = pick(exact_out[7], lax.axis_index("seq"))
+    mine = lax.axis_index("seq")
+    conv_small = jnp.concatenate(
+        [pick(by_owner(exact_out[6]), mine), pick(by_owner(exact_out[7]), mine)], axis=-1
+    )
+    conv_high = rounded(conv_small)
+    extra = jnp.concatenate(
+        [
+            by_owner(state_proj_grad),
+            bits(by_owner(in_gain_grad)),
+            bits(by_owner(ffn_gain_grad[0])),
+            pair_extra,
+        ],
+        axis=-1,
+    )
+    local_extra = extra
+    if paired and early_chunks:
+        expert_moved[-1] = seq_moved(after(expert_parts[-1], local_extra))
+    last_sums, moving = scatter_deep(after(kept, extra), sent)
+    extra_low = bits(seq_scatter(extra))
+    extra = jnp.concatenate(
+        [extra_low, bits(conv_high), bits(conv_small - conv_high)], axis=-1
+    )
+    extra = mp_exchange(after(extra, last_sums))
+    tokens_grad = slots_first(
+        token_rows_back(last_sums, hidden_grad, own_inputs, first_gain)
+    )
+    cuts = [gain_rows * state_width]
+    for size in (gain_rows, gain_rows, pair_extra.shape[2], conv_small.shape[1]):
+        cuts.append(cuts[-1] + size)
+    pair_grad = wide(extra[:, cuts[2] : cuts[3]])
+    extra_own = jnp.sum(wide(jnp.concatenate([extra[:, : cuts[2]], extra[:, cuts[3] :]], axis=1)), axis=0)
+    cuts = cuts[:3] + [cuts[4] - cuts[3] + cuts[2]]
+    state_proj_out = extra_own[: cuts[0]].reshape(gain_rows, state_width)
+    in_gain_out = extra_own[cuts[0] : cuts[1]]
+    ffn_gain_out = extra_own[cuts[1] : cuts[2]]
+    conv_own = extra_own[cuts[2] : cuts[3]] + extra_own[cuts[3] :]
     conv_state_out = conv_own[: state_rows * window].reshape(state_rows, window)
     conv_state_bias_out = conv_own[state_rows * window :]
+    pair_grad = pair_grad.reshape(mp_count, gain_rows, 2, seq_devices, columns)
+    pair_grad = pair_grad.transpose(2, 1, 3, 0, 4).reshape(2, gain_rows, -1)
+    shared_gate_grad, shared_up_grad = pair_grad[0], pair_grad[1]
+    if paired:
+        early_sums = sum(part_counts[:2])
+        expert_moved[:early_sums] = after(expert_moved[:early_sums], last_sums[2:3])
+        both_part = after(both_proj_grad, local_extra)
+        both_moved = seq_moved(both_part)
+        expert_moved[early_sums:], out_proj_moved, both_moved = after(
+            (expert_moved[early_sums:], out_proj_moved, both_moved), tokens_grad
+        )
+        both_proj_grad = wide(both_part) + wide(both_moved)
+        out_proj_grad = wide(out_proj_part) + wide(out_proj_moved)
+        expert_sums = [wide(part) + wide(other) for part, other in zip(expert_parts, expert_moved)]
+    else:
+        both_proj_grad = seq_sum(both_proj_grad)
+        out_proj_grad = seq_sum(out_proj_grad)
+        expert_sums = [seq_sum(part) for part in expert_parts]
+    gate_proj_grad, value_proj_grad = both_proj_grad[:, :inner_width], both_proj_grad[:, inner_width:]
+    step_proj_grad = step_flat.reshape(step_proj_grad.shape)
+    one, two = part_counts[0], part_counts[0] + part_counts[1]
+    expert_down_grad = jnp.concatenate(expert_sums[:one], axis=1)[None]
+    expert_gate_grad = jnp.concatenate(expert_sums[one:two])[None]
+    expert_up_grad = jnp.concatenate(expert_sums[two:])[None]
     return (
         block_out,
         tokens_grad,
         in_gain_out,
-        seq_sum(gate_proj_grad),
-        seq_sum(value_proj_grad),
+        gate_proj_grad,
+        value_proj_grad,
         state_proj_out,
+        step_proj_grad,
         exact_out[0],
         exact_out[1],
-        exact_out[2],
         conv_state_out,
         conv_state_bias_out,
+        exact_out[2],
         exact_out[3],
         exact_out[4],
         exact_out[5],
-        exact_out[6],
-        seq_sum(out_proj_grad),
+        out_proj_grad,
         ffn_gain_out,
         shared_gate_grad,
         shared_up_grad,

time: 602 us -> 546 us (0.907)
  Pallas kernels: 65.6 us -> 170 us
  waiting for transfers between devices: 225 us -> 149 us
  other arithmetic: 77.4 us -> 18.6 us
  matrix products: 43.5 us -> 1.45 us
  starting transfers between devices: 94.5 us -> 107 us
    pallas_call x1 -> x29, Pallas kernels: 8 us -> 112 us  [the longest x12 21.5 us: add_blocks(): call(kernel, (1,), [whole(left.shape)] * 2, whole(left.shape), bf16(*left...]
    ppermute x69 -> x84, waiting for transfers between devices: 170 us -> 100 us  [mp_permute(): return lax.ppermute(value, 'mp', [(i, target(i)) for i in range(count)])]
    dot_general x23 -> x2, matrix products: 43.5 us -> 1.45 us  [the longest x1 0.81 us: body(): lax.dot_general(by_rows(scaled_low), by_rows(after(mix_grad_all, scaled_v...]
    ppermute x69 -> x84, starting transfers between devices: 47.9 us -> 66.4 us  [mp_permute(): return lax.ppermute(value, 'mp', [(i, target(i)) for i in range(count)])]
    unnamed x185 -> x290, local copies, waits for them, and re-layouts: 22.6 us -> 39.2 us
    another operation x25 -> x4, other arithmetic: 17.4 us -> 2 us  [the longest x2 0.98 us: gather_small(): every = jnp.stack([every, across_core(every)])]
    all_to_all x4 -> x2, waiting for transfers between devices: 13.9 us -> 0.01 us  [mp_exchange(): return lax.all_to_all(value, 'mp', split_axis=0, concat_axis=0, tiled=True)]
    all_to_all x4 -> x2, starting transfers between devices: 21.8 us -> 7.95 us  [mp_exchange(): return lax.all_to_all(value, 'mp', split_axis=0, concat_axis=0, tiled=True)]
  transfers between devices with their start and end apart: 90 -> 108, of which waited for: 48 -> 39; matrix products, arithmetic and copies ran while one was open for 23% -> 11% of each run, Pallas kernels for 7% -> 24%
where the time goes in v3:
time: 546 us; the launch traced here: 536 us
  Pallas kernels  170 us (31%)
  waiting for transfers between devices  149 us (27%)
  starting transfers between devices  107 us (20%)
  local copies, waits for them, and re-layouts  87.3 us (16%)
  other arithmetic  18.6 us (3%)
    ppermute x84, waiting for transfers between devices, mp_permute(): return lax.ppermute(value, 'mp', [(i, target(i)) for i in range(count)])  100 us
    ppermute x84, starting transfers between devices, mp_permute(): return lax.ppermute(value, 'mp', [(i, target(i)) for i in range(count)])  66.4 us
    unnamed x290, local copies, waits for them, and re-layouts  39.2 us
    ppermute x13, waiting for transfers between devices, seq_moved(): return lax.ppermute(value, 'seq', [(0, 1), (1, 0)])  37.7 us
    pallas_call x12, Pallas kernels, add_blocks(): call(kernel, (1,), [whole(left.shape)] * 2, whole(left.shape), bf16(*left...  21.5 us
    ppermute x13, starting transfers between devices, seq_moved(): return lax.ppermute(value, 'seq', [(0, 1), (1, 0)])  17.9 us
    pallas_call x2, Pallas kernels, experts_backward(): call(kernel, (1,), [whole(block.shape) for block in blocks] + [whole(w.sh...  17.9 us
    pallas_call x2, Pallas kernels, experts_forward(): call(kernel, (1,), [whole(block.shape) for block in blocks] + [whole(w.sh...  16.2 us
  transfers between devices with their start and end apart: 108, of which 39 were waited for; matrix products, arithmetic and copies ran while one was open for 11% of the time, Pallas kernels for 24%

profile of v3, /device:TPU:0, one launch (start us, length us, event | category | flops | bytes accessed | tf_op | source)
XLA Modules:
  0.0 536.0 jit_solution(12558201014841302157)
XLA Ops:
  5.0 4.8 collective-permute-start
  10.7 3.3 collective-permute-done.1
  14.5 2.7 collective-permute-start.4
  27.1 3.8 collective-permute-done.5
  45.1 11.0 %shard_map.443 = (bf16[4,256,1536]{2,1,0:T(8,128)(2,1)}, f32[4,256,192]{2,1,0:T(8,128)}, f32[4,272,192]{2,1,0:T(8,128)}, f32[4,272,256]{2,1,0:T(8,128)}, f32[4,2...) custom-call(bf16[4,256,1536]{2,1,0:T(8,128)(2,1)} %bitcast.122, ...), custom_call_target="tpu_custom_call" | custom-call | flops 990000000 | bytes 2750000 | tf_op jit(solution)/shard_map/pallas_call | solution.py:300
  59.6 5.9 %shard_map.444.within_ref = f32[4,256,192]{2,1,0:T(8,128)} custom-call(f32[4,256,192]{2,1,0:T(8,128)} %get-tuple-element.211.pv_ref, f32[4,256,256]{2,1,0:T(8,128)} %get-tuple-element.212.ps_ref.refs_18_, f32[4,256,128]{2,1,0:T(8,128)} %get-tuple-element.213.step_ref, f32[4,256,128]{2,1,0:T(8,128)} %get-tuple-element.214.decay_ref.refs_19_, ...), custom_call_target="tpu_custom_call" | custom-call | flops 540000000 | bytes 1500000 | tf_op jit(solution)/shard_map/pallas_call | solution.py:351
  68.3 7.5 %shard_map.445 = (f32[4,256,192]{2,1,0:T(8,128)}, bf16[4,256,192]{2,1,0:T(8,128)(2,1)}, bf16[4,2,64,1664]{3,2,1,0:T(8,128)(2,1)}, bf16[4,2,64,1664]{3,2,1,0:T(8,128)(2,1)}) custom-call(s32[16]{0:T(128)} %add.239.order_ref, f32[4,256,192]{2,1,0:T(8,128)} %shard_map.444.within_ref, f32[4,256,256]{2,1,0:T(8,128)} %get-tuple-element.212.ps_ref.refs_18_, ...), custom_call_target="tpu_custom_call" | custom-call | flops 630000000 | bytes 1750000 | tf_op jit(solution)/shard_map/pallas_call | solution.py:391
  83.4 3.7 shard_map.446
  97.1 3.5 all-to-all-start
  100.7 3.2 collective-permute-done.10.right_ref
  106.9 3.1 collective-permute-done.12.right_ref
  117.4 5.2 collective-permute-done.13.refs_3_
  122.5 6.7 %collective-permute-done.15.refs_4_ = bf16[64,1664]{1,0:T(8,128)(2,1)S(1)} collective-permute-done((bf16[64,1664]{1,0:T(8,128)(2,1)}, bf16[64,1664]{1,0:T(8,128)(2,1)S(1)}, u32[]{:S(2)}, u32[]{:S(2)}) %collective-permute-start.15) | collective-permute-done | bytes 213024 | tf_op jit(solution)/shard_map/ppermute | solution.py:66
  135.1 4.3 collective-permute-start.29
  147.5 6.6 %collective-permute-done.31.refs_2_ = bf16[64,1536]{1,0:T(8,128)(2,1)S(1)} collective-permute-done((bf16[64,1536]{1,0:T(8,128)(2,1)}, bf16[64,1536]{1,0:T(8,128)(2,1)S(1)}, u32[]{:S(2)}, u32[]{:S(2)}) %collective-permute-start.31) | collective-permute-done | bytes 196640 | tf_op jit(solution)/shard_map/ppermute | solution.py:66
  158.1 8.1 %shard_map.451 = (bf16[512,1536]{1,0:T(8,128)(2,1)}, f32[512,512]{1,0:T(8,128)}, f32[512,512]{1,0:T(8,128)}, f32[512,128]{1,0:T(8,128)}, bf16[512,512]{1,0:T(8,1...) custom-call(bf16[64,1536]{1,0:T(8,128)(2,1)} %get-tuple-element.233.refs_0_, ...), custom_call_target="tpu_custom_call" | custom-call | flops 720000000 | bytes 2000000 | tf_op jit(solution)/shard_map/pallas_call | solution.py:895
  169.6 8.1 %shard_map.454 = (bf16[512,1536]{1,0:T(8,128)(2,1)}, f32[512,512]{1,0:T(8,128)}, f32[512,512]{1,0:T(8,128)}, f32[512,128]{1,0:T(8,128)}, bf16[512,512]{1,0:T(8,1...) custom-call(bf16[64,1536]{1,0:T(8,128)(2,1)} %copy-done.77, ...), custom_call_target="tpu_custom_call" | custom-call | flops 720000000 | bytes 2000000 | tf_op jit(solution)/shard_map/pallas_call | solution.py:895
  201.2 4.3 collective-permute-done.39.refs_3_
  205.5 6.5 %collective-permute-done.41.refs_4_ = bf16[64,1536]{1,0:T(8,128)(2,1)S(1)} collective-permute-done((bf16[64,1536]{1,0:T(8,128)(2,1)}, bf16[64,1536]{1,0:T(8,128)(2,1)S(1)}, u32[]{:S(2)}, u32[]{:S(2)}) %collective-permute-start.41) | collective-permute-done | bytes 196640 | tf_op jit(solution)/shard_map/ppermute | solution.py:66
  212.7 2.6 shard_map.458
  216.3 4.0 collective-permute-start.50
  220.2 4.9 collective-permute-done.43.refs_2_
  228.5 3.9 collective-permute-done.44.refs_3_
  232.4 3.9 collective-permute-done.52.refs_2_
  238.3 8.9 %shard_map.459 = (bf16[512,1536]{1,0:T(8,128)(2,1)}, bf16[512,512]{1,0:T(8,128)(2,1)}, bf16[512,512]{1,0:T(8,128)(2,1)}, bf16[512,128]{1,0:T(8,128)(2,1)}, bf16[...) custom-call(bf16[64,1536]{1,0:T(8,128)(2,1)} %get-tuple-element.254.refs_0_, bf16[64,1536]{1,0:T(8,128)(2,1)} %copy-done.88, ...), custom_call_target="tpu_custom_call" | custom-call | flops 810000000 | bytes 2250000 | tf_op jit(solution)/shard_map/pallas_call | solution.py:938
  249.8 8.9 %shard_map.461 = (bf16[512,1536]{1,0:T(8,128)(2,1)}, bf16[512,512]{1,0:T(8,128)(2,1)}, bf16[512,512]{1,0:T(8,128)(2,1)}, bf16[512,128]{1,0:T(8,128)(2,1)}, bf16[...) custom-call(bf16[64,1536]{1,0:T(8,128)(2,1)} %copy-done.79, bf16[64,1536]{1,0:T(8,128)(2,1)} %copy-done.83, ...), custom_call_target="tpu_custom_call" | custom-call | flops 810000000 | bytes 2250000 | tf_op jit(solution)/shard_map/pallas_call | solution.py:938
  267.4 13.6 %shard_map.463 = (bf16[512,512]{1,0:T(8,128)(2,1)}, bf16[512,512]{1,0:T(8,128)(2,1)}, bf16[512,512]{1,0:T(8,128)(2,1)}, bf16[512,512]{1,0:T(8,128)(2,1)}, bf16[5...) custom-call(bf16[512,1536]{1,0:T(8,128)(2,1)} %get-tuple-element.276, ...), custom_call_target="tpu_custom_call" | custom-call | flops 990000000 | bytes 2750000 | tf_op jit(solution)/shard_map/pallas_call | solution.py:1003
  297.5 9.4 %collective-permute-done.65.refs_4_ = bf16[64,1536]{1,0:T(8,128)(2,1)S(1)} collective-permute-done((bf16[64,1536]{1,0:T(8,128)(2,1)}, bf16[64,1536]{1,0:T(8,128)(2,1)S(1)}, u32[]{:S(2)}, u32[]{:S(2)}) %collective-permute-start.65) | collective-permute-done | bytes 196640 | tf_op jit(solution)/shard_map/ppermute | solution.py:66
  307.5 2.8 shard_map.467
  310.7 3.7 collective-permute-start.71
  315.5 5.1 collective-permute-done.68.refs_2_
  320.6 2.8 collective-permute-start.74
  324.0 4.6 collective-permute-done.84
  336.1 4.3 collective-permute-done.75.refs_7_
  344.1 7.9 %shard_map.468 = (bf16[4,256,1536]{2,1,0:T(8,128)(2,1)}, f32[4,256,192]{2,1,0:T(8,128)}, bf16[4,256,192]{2,1,0:T(8,128)(2,1)}, f32[4,192,128]{2,1,0:T(8,128)}, f32[8,192]{1,0:T(8,128)}) custom-call(s32[16]{0:T(128)} %add.239.order_ref, bf16[64,1664]{1,0:T(8,128)(2,1)} %get-tuple-element.311.refs_0_, bf16[64,1664]{1,0:T(8,128)(2,1)} %copy-done.57, ...), custom_call_target="tpu_custom_call" | custom-call | flops 720000000 | bytes 2000000 | tf_op jit(solution)/shard_map/pallas_call | solution.py:440
  352.1 9.2 %shard_map.469 = (f32[4,256,192]{2,1,0:T(8,128)}, f32[4,256,256]{2,1,0:T(8,128)}) custom-call(f32[4,256,192]{2,1,0:T(8,128)} %get-tuple-element.211.pv_ref, f32[4,256,256]{2,1,0:T(8,128)} %get-tuple-element.212.ps_ref.refs_18_, f32[4,256,128]{2,1,0:T(8,128)} %get-tuple-element.213.step_ref, f32[4,256,128]{2,1,0:T(8,128)} %get-tuple-element.214.decay_ref.refs_19_, ...), custom_call_target="tpu_custom_call" | custom-call | flops 810000000 | bytes 2250000 | tf_op jit(solution)/shard_map/pallas_call | solution.py:485
  364.1 2.7 collective-permute-start.90
  368.9 6.2 %collective-permute-done.86 = f32[4,3,64,128]{3,2,1,0:T(8,128)S(1)} collective-permute-done((f32[4,3,64,128]{3,2,1,0:T(8,128)S(1)}, f32[4,3,64,128]{3,2,1,0:T(8,128)S(1)}, u32[]{:S(2)}, u32[]{:S(2)}) %collective-permute-start.86) | collective-permute-done | bytes 393248 | tf_op jit(solution)/shard_map/ppermute | solution.py:136
  375.8 13.2 %shard_map.470 = (f32[4,256,192]{2,1,0:T(8,128)}, f32[4,256,256]{2,1,0:T(8,128)}, f32[4,16,192]{2,1,0:T(8,128)}, f32[4,16,256]{2,1,0:T(8,128)}, bf16[4,256,128]{...) custom-call(f32[4,256,192]{2,1,0:T(8,128)} %get-tuple-element.211.pv_ref, ...), custom_call_target="tpu_custom_call" | custom-call | flops 1170000000 | bytes 3250000 | tf_op jit(solution)/shard_map/pallas_call | solution.py:584
  395.8 2.7 collective-permute-start.89
  399.2 4.2 collective-permute-done.89
  404.8 10.6 %shard_map.471 = (bf16[4,256,192]{2,1,0:T(8,128)(2,1)}, bf16[4,256,256]{2,1,0:T(8,128)(2,1)}, f32[8,1536]{1,0:T(8,128)}, bf16[4,2,64,1536]{3,2,1,0:T(8,128)(2,1)}, bf16[4,2,64,1536]{3,2,1,0:T(8,128)(2,1)}) custom-call(s32[16]{0:T(128)} %add.239.order_ref, f32[4,256,192]{2,1,0:T(8,128)} %get-tuple-element.339.value_ref, ...), custom_call_target="tpu_custom_call" | custom-call | flops 900000000 | bytes 2500000 | tf_op jit(solution)/shard_map/pallas_call | solution.py:650
  422.8 10.9 %collective-permute-done.94 = bf16[512,512]{1,0:T(8,128)(2,1)S(1)} collective-permute-done((bf16[512,512]{1,0:T(8,128)(2,1)S(1)}, bf16[512,512]{1,0:T(8,128)(2,1)S(1)}, u32[]{:S(2)}, u32[]{:S(2)}) %collective-permute-start.94) | collective-permute-done | bytes 524320 | tf_op jit(solution)/shard_map/ppermute | solution.py:1259
  434.4 3.1 shard_map.472
  443.8 8.7 %shard_map.473 = (bf16[1536,384]{1,0:T(8,128)(2,1)}, bf16[1536,256]{1,0:T(8,128)(2,1)}) custom-call(bf16[4,256,1536]{2,1,0:T(8,128)(2,1)} %get-tuple-element.369.normed_ref, bf16[4,256,192]{2,1,0:T(8,128)(2,1)} %get-tuple-element.352.gate_grad_ref.gate_ref, bf16[4,256,192]{2,1,0:T(8,128)(2,1)} %get-tuple-element.370.value_ref, ...), custom_call_target="tpu_custom_call" | custom-call | flops 720000000 | bytes 2000000 | tf_op jit(solution)/shard_map/pallas_call | solution.py:1040
  471.3 6.9 %collective-permute-done.102.refs_4_ = bf16[64,1536]{1,0:T(8,128)(2,1)S(1)} collective-permute-done((bf16[64,1536]{1,0:T(8,128)(2,1)}, bf16[64,1536]{1,0:T(8,128)(2,1)S(1)}, u32[]{:S(2)}, u32[]{:S(2)}) %collective-permute-start.102) | collective-permute-done | bytes 196640 | tf_op jit(solution)/shard_map/ppermute | solution.py:66
  493.4 4.4 all-to-all-start.1
  497.8 17.7 %collective-permute-done.105 = bf16[1536,384]{1,0:T(8,128)(2,1)} collective-permute-done((bf16[1536,384]{1,0:T(8,128)(2,1)S(1)}, bf16[1536,384]{1,0:T(8,128)(2,1)}, u32[]{:S(2)}, u32[]{:S(2)}) %collective-permute-start.105) | collective-permute-done | bytes 1179680 | tf_op jit(solution)/shard_map/ppermute | solution.py:1259
  (654 shorter events, 239.3 us)
Async XLA Ops:
  5.0 31.7 %collective-permute-start = (bf16[4,3,1536]{2,1,0:T(4,128)(2,1)S(1)}, bf16[4,3,1536]{2,1,0:T(4,128)(2,1)S(1)}, u32[]{:S(2)}, u32[]{:S(2)}) collective-permute-start(bf16[4,3,1536]{2,1,0:T(4,128)(2,1)S(1)} %slice_bitcast_fusion), channel_id=1, source_target_pairs={{0,16},{1,17},{2,18},{3,19},{4,20},{5,21},{6,22},{7,23},{8,24},{9,... | collective-permute-start | bytes 110600 | tf_op jit(solution)/shard_map/ppermute | solution.py:19
  56.1 11.4 %collective-permute-start.7 = (f32[4,3,64,128]{3,2,1,0:T(8,128)}, f32[4,3,64,128]{3,2,1,0:T(8,128)S(1)}, u32[]{:S(2)}, u32[]{:S(2)}) collective-permute-start(f32[4,3,64,128]{3,2,1,0:T(8,128)} %bitcast.182), channel_id=1, source_target_pairs={{0,16},{1,17},{2,18},{3,19},{4,20},{5,21},{6,22},{7,23},{8,24},{9,... | collective-permute-start | bytes 1179656 | tf_op jit(solution)/shard_map/ppermute | solution.py:136
  87.1 13.6 %collective-permute-start.24 = (bf16[32,1536]{1,0:T(8,128)(2,1)S(1)}, bf16[32,1536]{1,0:T(8,128)(2,1)S(1)}, u32[]{:S(2)}, u32[]{:S(2)}) collective-permute-start(bf16[32,1536]{1,0:T(8,128)(2,1)S(1)} %copy-done.108), channel_id=1, source_target_pairs={{0,16},{16,0},{1,17},{17,1},{2,18},{18,2},{3,19},{19,3},{4,20},{20... | collective-permute-start | bytes 294920 | tf_op jit(solution)/shard_map/ppermute | solution.py:113
  91.0 26.4 %collective-permute-start.9 = (bf16[64,1664]{1,0:T(8,128)(2,1)}, bf16[64,1664]{1,0:T(8,128)(2,1)S(1)}, u32[]{:S(2)}, u32[]{:S(2)}) collective-permute-start(bf16[64,1664]{1,0:T(8,128)(2,1)} %get-tuple-element.220), channel_id=1, source_target_pairs={{0,2},{1,3},{2,0},{3,1},{4,6},{5,7},{6,4},{7,5},{8,10},{9,11},{10,... | collective-permute-start | bytes 638984 | tf_op jit(solution)/shard_map/ppermute | solution.py:66
  92.5 11.3 %collective-permute-start.10 = (bf16[64,1664]{1,0:T(8,128)(2,1)}, bf16[64,1664]{1,0:T(8,128)(2,1)S(1)}, u32[]{:S(2)}, u32[]{:S(2)}) collective-permute-start(bf16[64,1664]{1,0:T(8,128)(2,1)} %get-tuple-element.222), channel_id=1, source_target_pairs={{0,2},{1,3},{2,0},{3,1},{4,6},{5,7},{6,4},{7,5},{8,10},{9,11},{10,... | collective-permute-start | bytes 638984 | tf_op jit(solution)/shard_map/ppermute | solution.py:66
  93.0 17.0 %collective-permute-start.12 = (bf16[64,1664]{1,0:T(8,128)(2,1)}, bf16[64,1664]{1,0:T(8,128)(2,1)S(1)}, u32[]{:S(2)}, u32[]{:S(2)}) collective-permute-start(bf16[64,1664]{1,0:T(8,128)(2,1)} %get-tuple-element.224), channel_id=1, source_target_pairs={{0,2},{1,3},{2,0},{3,1},{4,6},{5,7},{6,4},{7,5},{8,10},{9,11},{10,... | collective-permute-start | bytes 638984 | tf_op jit(solution)/shard_map/ppermute | solution.py:66
  94.5 19.6 %collective-permute-start.14 = (bf16[64,1664]{1,0:T(8,128)(2,1)}, bf16[64,1664]{1,0:T(8,128)(2,1)S(1)}, u32[]{:S(2)}, u32[]{:S(2)}) collective-permute-start(bf16[64,1664]{1,0:T(8,128)(2,1)} %get-tuple-element.226), channel_id=1, source_target_pairs={{0,2},{1,3},{2,0},{3,1},{4,6},{5,7},{6,4},{7,5},{8,10},{9,11},{10,... | collective-permute-start | bytes 638984 | tf_op jit(solution)/shard_map/ppermute | solution.py:66
  97.1 19.6 %all-to-all-start = ((bf16[16,2,3072]{2,1,0:T(2,128)(2,1)}), bf16[16,2,3072]{2,1,0:T(2,128)(2,1)S(1)}, u32[]{:S(2)}, u32[]{:S(2)}) async-start(bf16[16,2,3072]{2,1,0:T(2,128)(2,1)} %reshape.497), calls=%async_computation | async-start | bytes 393216 | tf_op jit(solution)/shard_map/all_to_all | solution.py:147
  116.7 12.6 %collective-permute-start.15 = (bf16[64,1664]{1,0:T(8,128)(2,1)}, bf16[64,1664]{1,0:T(8,128)(2,1)S(1)}, u32[]{:S(2)}, u32[]{:S(2)}) collective-permute-start(bf16[64,1664]{1,0:T(8,128)(2,1)} %shard_map.449), channel_id=1, source_target_pairs={{0,8},{1,9},{2,10},{3,11},{4,12},{5,13},{6,14},{7,15},{8,0},{9,1},... | collective-permute-start | bytes 638984 | tf_op jit(solution)/shard_map/ppermute | solution.py:66
  117.0 22.5 %collective-permute-start.23 = (bf16[16,6144]{1,0:T(8,128)(2,1)S(1)}, bf16[16,6144]{1,0:T(8,128)(2,1)S(1)}, u32[]{:S(2)}, u32[]{:S(2)}) collective-permute-start(bf16[16,6144]{1,0:T(8,128)(2,1)S(1)} %bitcast.164), channel_id=1, source_target_pairs={{0,16},{16,0},{1,17},{17,1},{2,18},{18,2},{3,19},{19,3},{4,20},{20... | collective-permute-start | bytes 589832 | tf_op jit(solution)/shard_map/ppermute | solution.py:113
  139.4 14.6 %collective-permute-start.31 = (bf16[64,1536]{1,0:T(8,128)(2,1)}, bf16[64,1536]{1,0:T(8,128)(2,1)S(1)}, u32[]{:S(2)}, u32[]{:S(2)}) collective-permute-start(bf16[64,1536]{1,0:T(8,128)(2,1)} %get-tuple-element.233.refs_0_), channel_id=1, source_target_pairs={{0,8},{1,9},{2,10},{3,11},{4,12},{5,13},{6,14},{7,15},{8,0},{9,1},... | collective-permute-start | bytes 589832 | tf_op jit(solution)/shard_map/ppermute | solution.py:66
  141.7 13.9 %collective-permute-start.18 = (bf16[64,1536]{1,0:T(8,128)(2,1)S(1)}, bf16[64,1536]{1,0:T(8,128)(2,1)S(1)}, u32[]{:S(2)}, u32[]{:S(2)}) collective-permute-start(bf16[64,1536]{1,0:T(8,128)(2,1)S(1)} %collective-permute-done.17.refs_2_), channel_id=1, source_target_pairs={{0,2},{1,3},{2,0},{3,1},{4,6},{5,7},{6,4},{7,5},{8,10},{9,11},{10,... | collective-permute-start | bytes 589832 | tf_op jit(solution)/shard_map/ppermute | solution.py:66
  144.3 13.0 %collective-permute-start.21 = (bf16[64,1536]{1,0:T(8,128)(2,1)S(1)}, bf16[64,1536]{1,0:T(8,128)(2,1)S(1)}, u32[]{:S(2)}, u32[]{:S(2)}) collective-permute-start(bf16[64,1536]{1,0:T(8,128)(2,1)S(1)} %collective-permute-done.17.refs_2_), channel_id=1, source_target_pairs={{0,1},{1,0},{2,3},{3,2},{4,5},{5,4},{6,7},{7,6},{8,9},{9,8},{10,11... | collective-permute-start | bytes 589832 | tf_op jit(solution)/shard_map/ppermute | solution.py:66
  144.4 12.3 %collective-permute-start.20 = (bf16[64,1536]{1,0:T(8,128)(2,1)S(1)}, bf16[64,1536]{1,0:T(8,128)(2,1)S(1)}, u32[]{:S(2)}, u32[]{:S(2)}) collective-permute-start(bf16[64,1536]{1,0:T(8,128)(2,1)S(1)} %collective-permute-done.16.refs_1_), channel_id=1, source_target_pairs={{0,1},{1,0},{2,3},{3,2},{4,5},{5,4},{6,7},{7,6},{8,9},{9,8},{10,11... | collective-permute-start | bytes 589832 | tf_op jit(solution)/shard_map/ppermute | solution.py:66
  145.6 11.6 %collective-permute-start.30 = (bf16[64,1536]{1,0:T(8,128)(2,1)S(1)}, bf16[64,1536]{1,0:T(8,128)(2,1)S(1)}, u32[]{:S(2)}, u32[]{:S(2)}) collective-permute-start(bf16[64,1536]{1,0:T(8,128)(2,1)S(1)} %collective-permute-done.29.refs_0_), channel_id=1, source_target_pairs={{0,2},{1,3},{2,0},{3,1},{4,6},{5,7},{6,4},{7,5},{8,10},{9,11},{10,... | collective-permute-start | bytes 589832 | tf_op jit(solution)/shard_map/ppermute | solution.py:66
  154.0 12.2 %collective-permute-start.32 = (bf16[64,1536]{1,0:T(8,128)(2,1)S(1)}, bf16[64,1536]{1,0:T(8,128)(2,1)S(1)}, u32[]{:S(2)}, u32[]{:S(2)}) collective-permute-start(bf16[64,1536]{1,0:T(8,128)(2,1)S(1)} %collective-permute-done.31.refs_2_), channel_id=1, source_target_pairs={{0,2},{1,3},{2,0},{3,1},{4,6},{5,7},{6,4},{7,5},{8,10},{9,11},{10,... | collective-permute-start | bytes 589832 | tf_op jit(solution)/shard_map/ppermute | solution.py:66
  156.7 11.4 %collective-permute-start.33 = (bf16[64,1536]{1,0:T(8,128)(2,1)S(1)}, bf16[64,1536]{1,0:T(8,128)(2,1)S(1)}, u32[]{:S(2)}, u32[]{:S(2)}) collective-permute-start(bf16[64,1536]{1,0:T(8,128)(2,1)S(1)} %collective-permute-done.29.refs_0_), channel_id=1, source_target_pairs={{0,1},{1,0},{2,3},{3,2},{4,5},{5,4},{6,7},{7,6},{8,9},{9,8},{10,11... | collective-permute-start | bytes 589832 | tf_op jit(solution)/shard_map/ppermute | solution.py:66
  187.4 13.8 %collective-permute-start.26 = (bf16[64,1536]{1,0:T(8,128)(2,1)S(1)}, bf16[64,1536]{1,0:T(8,128)(2,1)S(1)}, u32[]{:S(2)}, u32[]{:S(2)}) collective-permute-start(bf16[64,1536]{1,0:T(8,128)(2,1)S(1)} %copy-done.126), channel_id=1, source_target_pairs={{0,2},{1,3},{2,0},{3,1},{4,6},{5,7},{6,4},{7,5},{8,10},{9,11},{10,... | collective-permute-start | bytes 589832 | tf_op jit(solution)/shard_map/ppermute | solution.py:66
  199.8 12.2 %collective-permute-start.41 = (bf16[64,1536]{1,0:T(8,128)(2,1)}, bf16[64,1536]{1,0:T(8,128)(2,1)S(1)}, u32[]{:S(2)}, u32[]{:S(2)}) collective-permute-start(bf16[64,1536]{1,0:T(8,128)(2,1)} %shard_map.457), channel_id=1, source_target_pairs={{0,8},{1,9},{2,10},{3,11},{4,12},{5,13},{6,14},{7,15},{8,0},{9,1},... | collective-permute-start | bytes 589832 | tf_op jit(solution)/shard_map/ppermute | solution.py:66
  216.3 11.1 %collective-permute-start.50 = (bf16[64,1536]{1,0:T(8,128)(2,1)}, bf16[64,1536]{1,0:T(8,128)(2,1)S(1)}, u32[]{:S(2)}, u32[]{:S(2)}) collective-permute-start(bf16[64,1536]{1,0:T(8,128)(2,1)} %get-tuple-element.254.refs_0_), channel_id=1, source_target_pairs={{0,12},{1,13},{2,14},{3,15},{4,0},{5,1},{6,2},{7,3},{8,4},{9,5},{1... | collective-permute-start | bytes 589832 | tf_op jit(solution)/shard_map/ppermute | solution.py:66
  247.9 11.1 %collective-permute-start.49 = (bf16[2,2,64,1536]{3,2,1,0:T(8,128)(2,1)}, bf16[2,2,64,1536]{3,2,1,0:T(8,128)(2,1)S(1)}, u32[]{:S(2)}, u32[]{:S(2)}) collective-permute-start(bf16[2,2,64,1536]{3,2,1,0:T(8,128)(2,1)} %get-tuple-element.259), channel_id=1, source_target_pairs={{0,1},{1,0},{2,3},{3,2},{4,5},{5,4},{6,7},{7,6},{8,9},{9,8},{10,11... | collective-permute-start | bytes 2359304 | tf_op jit(solution)/shard_map/ppermute | solution.py:66
  262.2 20.9 %collective-permute-start.60 = (bf16[64,1536]{1,0:T(8,128)(2,1)}, bf16[64,1536]{1,0:T(8,128)(2,1)S(1)}, u32[]{:S(2)}, u32[]{:S(2)}) collective-permute-start(bf16[64,1536]{1,0:T(8,128)(2,1)} %get-tuple-element.273), channel_id=1, source_target_pairs={{0,2},{1,3},{2,0},{3,1},{4,6},{5,7},{6,4},{7,5},{8,10},{9,11},{10,... | collective-permute-start | bytes 589832 | tf_op jit(solution)/shard_map/ppermute | solution.py:66
  266.7 20.4 %collective-permute-start.62 = (bf16[64,1536]{1,0:T(8,128)(2,1)}, bf16[64,1536]{1,0:T(8,128)(2,1)S(1)}, u32[]{:S(2)}, u32[]{:S(2)}) collective-permute-start(bf16[64,1536]{1,0:T(8,128)(2,1)} %get-tuple-element.274), channel_id=1, source_target_pairs={{0,2},{1,3},{2,0},{3,1},{4,6},{5,7},{6,4},{7,5},{8,10},{9,11},{10,... | collective-permute-start | bytes 589832 | tf_op jit(solution)/shard_map/ppermute | solution.py:66
  281.0 25.8 %collective-permute-start.66 = (bf16[512,512]{1,0:T(8,128)(2,1)}, bf16[512,512]{1,0:T(8,128)(2,1)S(1)}, u32[]{:S(2)}, u32[]{:S(2)}) collective-permute-start(bf16[512,512]{1,0:T(8,128)(2,1)} %get-tuple-element.296), channel_id=1, source_target_pairs={{0,16},{16,0},{1,17},{17,1},{2,18},{18,2},{3,19},{19,3},{4,20},{20... | collective-permute-start | bytes 1572872 | tf_op jit(solution)/shard_map/ppermute | solution.py:1259
  290.6 23.8 %collective-permute-start.69 = (bf16[512,512]{1,0:T(8,128)(2,1)}, bf16[512,512]{1,0:T(8,128)(2,1)S(1)}, u32[]{:S(2)}, u32[]{:S(2)}) collective-permute-start(bf16[512,512]{1,0:T(8,128)(2,1)} %get-tuple-element.306), channel_id=1, source_target_pairs={{0,16},{16,0},{1,17},{17,1},{2,18},{18,2},{3,19},{19,3},{4,20},{20... | collective-permute-start | bytes 1572872 | tf_op jit(solution)/shard_map/ppermute | solution.py:1259
  292.1 31.3 %collective-permute-start.72 = (bf16[512,512]{1,0:T(8,128)(2,1)}, bf16[512,512]{1,0:T(8,128)(2,1)S(1)}, u32[]{:S(2)}, u32[]{:S(2)}) collective-permute-start(bf16[512,512]{1,0:T(8,128)(2,1)} %get-tuple-element.308), channel_id=1, source_target_pairs={{0,16},{16,0},{1,17},{17,1},{2,18},{18,2},{3,19},{19,3},{4,20},{20... | collective-permute-start | bytes 1572872 | tf_op jit(solution)/shard_map/ppermute | solution.py:1259
  293.0 35.5 %collective-permute-start.84 = (bf16[512,512]{1,0:T(8,128)(2,1)}, bf16[512,512]{1,0:T(8,128)(2,1)S(1)}, u32[]{:S(2)}, u32[]{:S(2)}) collective-permute-start(bf16[512,512]{1,0:T(8,128)(2,1)} %get-tuple-element.310), channel_id=1, source_target_pairs={{0,16},{16,0},{1,17},{17,1},{2,18},{18,2},{3,19},{19,3},{4,20},{20... | collective-permute-start | bytes 1572872 | tf_op jit(solution)/shard_map/ppermute | solution.py:1259
  310.7 12.7 %collective-permute-start.71 = (bf16[64,1664]{1,0:T(8,128)(2,1)}, bf16[64,1664]{1,0:T(8,128)(2,1)S(1)}, u32[]{:S(2)}, u32[]{:S(2)}) collective-permute-start(bf16[64,1664]{1,0:T(8,128)(2,1)} %get-tuple-element.311.refs_0_), channel_id=1, source_target_pairs={{0,12},{1,13},{2,14},{3,15},{4,0},{5,1},{6,2},{7,3},{8,4},{9,5},{1... | collective-permute-start | bytes 638984 | tf_op jit(solution)/shard_map/ppermute | solution.py:66
  314.4 15.5 %collective-permute-start.67 = (bf16[64,1664]{1,0:T(8,128)(2,1)}, bf16[64,1664]{1,0:T(8,128)(2,1)S(1)}, u32[]{:S(2)}, u32[]{:S(2)}) collective-permute-start(bf16[64,1664]{1,0:T(8,128)(2,1)} %get-tuple-element.311.refs_0_), channel_id=1, source_target_pairs={{0,2},{1,3},{2,0},{3,1},{4,6},{5,7},{6,4},{7,5},{8,10},{9,11},{10,... | collective-permute-start | bytes 638984 | tf_op jit(solution)/shard_map/ppermute | solution.py:66
  320.6 12.2 %collective-permute-start.74 = (bf16[64,1664]{1,0:T(8,128)(2,1)}, bf16[64,1664]{1,0:T(8,128)(2,1)S(1)}, u32[]{:S(2)}, u32[]{:S(2)}) collective-permute-start(bf16[64,1664]{1,0:T(8,128)(2,1)} %get-tuple-element.311.refs_0_), channel_id=1, source_target_pairs={{0,8},{1,9},{2,10},{3,11},{4,12},{5,13},{6,14},{7,15},{8,0},{9,1},... | collective-permute-start | bytes 638984 | tf_op jit(solution)/shard_map/ppermute | solution.py:66
  329.9 22.2 %collective-permute-start.85 = (bf16[512,512]{1,0:T(8,128)(2,1)S(1)}, bf16[512,512]{1,0:T(8,128)(2,1)S(1)}, u32[]{:S(2)}, u32[]{:S(2)}) collective-permute-start(bf16[512,512]{1,0:T(8,128)(2,1)S(1)} %copy-done.30), channel_id=1, source_target_pairs={{0,16},{16,0},{1,17},{17,1},{2,18},{18,2},{3,19},{19,3},{4,20},{20... | collective-permute-start | bytes 1572872 | tf_op jit(solution)/shard_map/ppermute | solution.py:1259
  342.3 26.6 %collective-permute-start.87 = (bf16[512,512]{1,0:T(8,128)(2,1)S(1)}, bf16[512,512]{1,0:T(8,128)(2,1)S(1)}, u32[]{:S(2)}, u32[]{:S(2)}) collective-permute-start(bf16[512,512]{1,0:T(8,128)(2,1)S(1)} %copy-done.18), channel_id=1, source_target_pairs={{0,16},{16,0},{1,17},{17,1},{2,18},{18,2},{3,19},{19,3},{4,20},{20... | collective-permute-start | bytes 1572872 | tf_op jit(solution)/shard_map/ppermute | solution.py:1259
  361.2 13.9 %collective-permute-start.86 = (f32[4,3,64,128]{3,2,1,0:T(8,128)S(1)}, f32[4,3,64,128]{3,2,1,0:T(8,128)S(1)}, u32[]{:S(2)}, u32[]{:S(2)}) collective-permute-start(f32[4,3,64,128]{3,2,1,0:T(8,128)S(1)} %bitcast.181), channel_id=1, source_target_pairs={{16,0},{17,1},{18,2},{19,3},{20,4},{21,5},{22,6},{23,7},{24,8},{25... | collective-permute-start | bytes 1179656 | tf_op jit(solution)/shard_map/ppermute | solution.py:136
  364.1 39.2 %collective-permute-start.90 = (bf16[192,1536]{1,0:T(8,128)(2,1)S(1)}, bf16[192,1536]{1,0:T(8,128)(2,1)S(1)}, u32[]{:S(2)}, u32[]{:S(2)}) collective-permute-start(bf16[192,1536]{1,0:T(8,128)(2,1)S(1)} %fusion), channel_id=1, source_target_pairs={{0,16},{16,0},{1,17},{17,1},{2,18},{18,2},{3,19},{19,3},{4,20},{20... | collective-permute-start | bytes 1769480 | tf_op jit(solution)/shard_map/ppermute | solution.py:1259
  366.8 31.6 %collective-permute-start.91 = (bf16[32,1536]{1,0:T(8,128)(2,1)S(1)}, bf16[32,1536]{1,0:T(8,128)(2,1)S(1)}, u32[]{:S(2)}, u32[]{:S(2)}) collective-permute-start(bf16[32,1536]{1,0:T(8,128)(2,1)S(1)} %dynamic-slice_bitcast_fusion.2), channel_id=1, source_target_pairs={{0,16},{16,0},{1,17},{17,1},{2,18},{18,2},{3,19},{19,3},{4,20},{20... | collective-permute-start | bytes 294920 | tf_op jit(solution)/shard_map/ppermute | solution.py:122
  366.9 36.4 %collective-permute-start.92 = (bf16[512,512]{1,0:T(8,128)(2,1)S(1)}, bf16[512,512]{1,0:T(8,128)(2,1)S(1)}, u32[]{:S(2)}, u32[]{:S(2)}) collective-permute-start(bf16[512,512]{1,0:T(8,128)(2,1)S(1)} %copy-done.33), channel_id=1, source_target_pairs={{0,16},{16,0},{1,17},{17,1},{2,18},{18,2},{3,19},{19,3},{4,20},{20... | collective-permute-start | bytes 1572872 | tf_op jit(solution)/shard_map/ppermute | solution.py:1259
  390.0 13.3 %collective-permute-start.88 = (f32[4,16,448]{2,1,0:T(8,128)S(1)}, f32[4,16,448]{2,1,0:T(8,128)S(1)}, u32[]{:S(2)}, u32[]{:S(2)}) collective-permute-start(f32[4,16,448]{2,1,0:T(8,128)S(1)} %pad_maximum_fusion.6), channel_id=1, source_target_pairs={{16,0},{17,1},{18,2},{19,3},{20,4},{21,5},{22,6},{23,7},{24,8},{25... | collective-permute-start | bytes 344072 | tf_op jit(solution)/shard_map/ppermute | solution.py:19
  415.4 19.0 %collective-permute-start.95 = (bf16[4,2,64,1536]{3,2,1,0:T(8,128)(2,1)}, bf16[4,2,64,1536]{3,2,1,0:T(8,128)(2,1)}, u32[]{:S(2)}, u32[]{:S(2)}) collective-permute-start(bf16[4,2,64,1536]{3,2,1,0:T(8,128)(2,1)} %get-tuple-element.360), channel_id=1, source_target_pairs={{0,1},{1,0},{2,3},{3,2},{4,5},{5,4},{6,7},{7,6},{8,9},{9,8},{10,11... | collective-permute-start | bytes 4718600 | tf_op jit(solution)/shard_map/ppermute | solution.py:66
  419.1 14.6 %collective-permute-start.94 = (bf16[512,512]{1,0:T(8,128)(2,1)S(1)}, bf16[512,512]{1,0:T(8,128)(2,1)S(1)}, u32[]{:S(2)}, u32[]{:S(2)}) collective-permute-start(bf16[512,512]{1,0:T(8,128)(2,1)S(1)} %copy-done.23), channel_id=1, source_target_pairs={{0,16},{16,0},{1,17},{17,1},{2,18},{18,2},{3,19},{19,3},{4,20},{20... | collective-permute-start | bytes 1572872 | tf_op jit(solution)/shard_map/ppermute | solution.py:1259
  437.5 18.4 %collective-permute-start.97 = (bf16[64,1536]{1,0:T(8,128)(2,1)}, bf16[64,1536]{1,0:T(8,128)(2,1)}, u32[]{:S(2)}, u32[]{:S(2)}) collective-permute-start(bf16[64,1536]{1,0:T(8,128)(2,1)} %get-tuple-element.366), channel_id=1, source_target_pairs={{0,2},{1,3},{2,0},{3,1},{4,6},{5,7},{6,4},{7,5},{8,10},{9,11},{10,... | collective-permute-start | bytes 589832 | tf_op jit(solution)/shard_map/ppermute | solution.py:66
  440.2 26.7 %collective-permute-start.96 = (bf16[64,1536]{1,0:T(8,128)(2,1)}, bf16[64,1536]{1,0:T(8,128)(2,1)}, u32[]{:S(2)}, u32[]{:S(2)}) collective-permute-start(bf16[64,1536]{1,0:T(8,128)(2,1)} %get-tuple-element.365), channel_id=1, source_target_pairs={{0,2},{1,3},{2,0},{3,1},{4,6},{5,7},{6,4},{7,5},{8,10},{9,11},{10,... | collective-permute-start | bytes 589832 | tf_op jit(solution)/shard_map/ppermute | solution.py:66
  441.8 18.0 %collective-permute-start.99 = (bf16[64,1536]{1,0:T(8,128)(2,1)}, bf16[64,1536]{1,0:T(8,128)(2,1)}, u32[]{:S(2)}, u32[]{:S(2)}) collective-permute-start(bf16[64,1536]{1,0:T(8,128)(2,1)} %get-tuple-element.367), channel_id=1, source_target_pairs={{0,2},{1,3},{2,0},{3,1},{4,6},{5,7},{6,4},{7,5},{8,10},{9,11},{10,... | collective-permute-start | bytes 589832 | tf_op jit(solution)/shard_map/ppermute | solution.py:66
  442.3 19.8 %collective-permute-start.101 = (bf16[64,1536]{1,0:T(8,128)(2,1)}, bf16[64,1536]{1,0:T(8,128)(2,1)}, u32[]{:S(2)}, u32[]{:S(2)}) collective-permute-start(bf16[64,1536]{1,0:T(8,128)(2,1)} %get-tuple-element.368), channel_id=1, source_target_pairs={{0,2},{1,3},{2,0},{3,1},{4,6},{5,7},{6,4},{7,5},{8,10},{9,11},{10,... | collective-permute-start | bytes 589832 | tf_op jit(solution)/shard_map/ppermute | solution.py:66
  463.8 14.4 %collective-permute-start.102 = (bf16[64,1536]{1,0:T(8,128)(2,1)}, bf16[64,1536]{1,0:T(8,128)(2,1)S(1)}, u32[]{:S(2)}, u32[]{:S(2)}) collective-permute-start(bf16[64,1536]{1,0:T(8,128)(2,1)} %shard_map.476), channel_id=1, source_target_pairs={{0,8},{1,9},{2,10},{3,11},{4,12},{5,13},{6,14},{7,15},{8,0},{9,1},... | collective-permute-start | bytes 589832 | tf_op jit(solution)/shard_map/ppermute | solution.py:66
  465.4 25.2 %collective-permute-start.103 = (bf16[16,18528]{1,0:T(8,128)(2,1)S(1)}, bf16[16,18528]{1,0:T(8,128)(2,1)S(1)}, u32[]{:S(2)}, u32[]{:S(2)}) collective-permute-start(bf16[16,18528]{1,0:T(8,128)(2,1)S(1)} %dynamic-slice_bitcast_fusion), channel_id=1, source_target_pairs={{0,16},{16,0},{1,17},{17,1},{2,18},{18,2},{3,19},{19,3},{4,20},{20... | collective-permute-start | bytes 1778696 | tf_op jit(solution)/shard_map/ppermute | solution.py:122
  467.0 30.8 %collective-permute-start.104 = (bf16[512,512]{1,0:T(8,128)(2,1)S(1)}, bf16[512,512]{1,0:T(8,128)(2,1)}, u32[]{:S(2)}, u32[]{:S(2)}) collective-permute-start(bf16[512,512]{1,0:T(8,128)(2,1)S(1)} %copy-done.25), channel_id=1, source_target_pairs={{0,16},{16,0},{1,17},{17,1},{2,18},{18,2},{3,19},{19,3},{4,20},{20... | collective-permute-start | bytes 1572872 | tf_op jit(solution)/shard_map/ppermute | solution.py:1259
  467.5 48.0 %collective-permute-start.105 = (bf16[1536,384]{1,0:T(8,128)(2,1)S(1)}, bf16[1536,384]{1,0:T(8,128)(2,1)}, u32[]{:S(2)}, u32[]{:S(2)}) collective-permute-start(bf16[1536,384]{1,0:T(8,128)(2,1)S(1)} %copy-done.7), channel_id=1, source_target_pairs={{0,16},{16,0},{1,17},{17,1},{2,18},{18,2},{3,19},{19,3},{4,20},{20... | collective-permute-start | bytes 3538952 | tf_op jit(solution)/shard_map/ppermute | solution.py:1259
  493.4 31.9 %all-to-all-start.1 = ((bf16[16,2,9304]{2,1,0:T(2,128)(2,1)}), bf16[16,2,9304]{2,1,0:T(2,128)(2,1)}, u32[]{:S(2)}, u32[]{:S(2)}) async-start(bf16[16,2,9304]{2,1,0:T(2,128)(2,1)} %reshape.499), calls=%async_computation.1 | async-start | bytes 1196032 | tf_op jit(solution)/shard_map/all_to_all | solution.py:147
  (197 other events, 1509.1 us)

commit v4 on v3

--- a/solution.py
+++ b/solution.py
@@ -258,7 +258,7 @@
     value_bias, state_bias, step_shift, decay_rate, heads,
 ):
     count, length, model = x.shape
-    inner, double = value_w.shape[1], state_w.shape[1]
+    inner, double = value_w.shape[0], state_w.shape[1]
     window = value_taps.shape[0]
 
     def kernel(
@@ -273,13 +273,13 @@
 
         normed = norm(x_ref[0])
         normed_out[0] = normed
-        ev_out[0, EDGE:] = product(normed, value_ref[...])
+        ev_out[0, EDGE:] = product(normed, value_ref[...], TRANSPOSED)
         es_out[0, EDGE:] = product(normed, state_ref[...])
         step_raw = product(normed, step_ref[...])
         step_out[0] = step_raw
-        gate_out[0] = product(normed, gate_ref[...])
+        gate_out[0] = product(normed, gate_ref[...], TRANSPOSED)
         edge_normed = norm(edge_ref[0])
-        ev_out[0, :EDGE] = product(edge_normed, value_ref[...])
+        ev_out[0, :EDGE] = product(edge_normed, value_ref[...], TRANSPOSED)
         es_out[0, :EDGE] = product(edge_normed, state_ref[...])
         first = EDGE - window + 1
         pre_value = jnp.broadcast_to(vb_ref[...], (length, inner))
@@ -629,8 +629,8 @@
         for part, edge, out in ((value_ref, ev_ref, value_out), (state_ref, es_ref, state_out)):
             out[0, :body_rows] = part[0, :body_rows].astype(jnp.bfloat16)
             out[0, body_rows:] = (part[0, body_rows:] + edge[0]).astype(jnp.bfloat16)
-        grad = product(gate_grad_ref[0], gate_ref[...], TRANSPOSED)
-        grad = grad + product(value_out[0], vw_ref[...], TRANSPOSED)
+        grad = product(gate_grad_ref[0], gate_ref[...])
+        grad = grad + product(value_out[0], vw_ref[...])
         grad = grad + product(state_out[0], sw_ref[...], TRANSPOSED)
         grad = grad + product(step_grad_ref[0], step_ref[...], TRANSPOSED)
         value = x_ref[0].astype(jnp.float32)
@@ -907,16 +907,20 @@
     )(*blocks, share, gate_w, up_w, down_w, pair_w, pair_down)
 
 
-def experts_backward(blocks, share, gate, up, both, gate_w, up_w, down_w, pair_w, pair_down):
+def experts_backward(blocks, share, gate, up, both, act, before, last, gate_w, up_w, down_w, pair_w, pair_down):
     rows, model = blocks[0].shape
     count, hidden = len(blocks), gate_w.shape[1]
     total, double = rows * count, pair_w.shape[1]
+    others = [share, gate, up, both, act, gate_w, up_w, down_w, pair_w, pair_down]
+    others += [] if before is None else [before]
 
     def kernel(*refs):
         block_refs = refs[:count]
-        share_ref, g_ref, u_ref, both_ref, gate_ref, up_ref, down_ref, pair_ref, pd_ref = refs[count : count + 9]
-        grads_out, gate_out, up_out, shared_out = refs[count + 9 : count + 13]
-        part_refs = refs[count + 13 :]
+        share_ref, g_ref, u_ref, both_ref, act_ref, gate_ref, up_ref, down_ref, pair_ref, pd_ref = refs[
+            count : count + 10
+        ]
+        before_ref = None if before is None else refs[count + 10]
+        grads_out, gate_out, up_out, shared_out, *outs = refs[count + len(others) :]
         for place, block in enumerate(block_refs):
             grads_out[place * rows : (place + 1) * rows] = block[...]
         grad = grads_out[...]
@@ -932,46 +936,48 @@
         shared_out[...] = (product(grad, pd_ref[...], TRANSPOSED) * factor).astype(jnp.bfloat16)
         result = product(gate_out[...], gate_ref[...], TRANSPOSED)
         result = result + product(up_out[...], up_ref[...], TRANSPOSED)
-        store_parts(result + product(shared_out[...], pair_ref[...], TRANSPOSED), part_refs)
-
-    parts, steps = 2, count // 4
+        store_parts(result + product(shared_out[...], pair_ref[...], TRANSPOSED), outs[:2])
+        down_grad = product(act_ref[...], routed, ROWS_SUMMED)
+        if before_ref is not None:
+            down_grad = down_grad + before_ref[...]
+        outs[2][...] = down_grad.astype(outs[2].dtype)
+
+    steps = count // 4
     return call(
         kernel,
         (1,),
-        [whole(block.shape) for block in blocks]
-        + [whole(w.shape) for w in (share, gate, up, both, gate_w, up_w, down_w, pair_w, pair_down)],
+        [whole(block.shape) for block in blocks] + [whole(value.shape) for value in others],
         [whole((total, model)), whole((total, hidden)), whole((total, hidden)), whole((total, double))]
-        + [whole((steps, 2, rows, model))] * parts,
+        + [whole((steps, 2, rows, model))] * 2
+        + [whole((hidden, model))],
         [bf16(total, model), bf16(total, hidden), bf16(total, hidden), bf16(total, double)]
-        + [bf16(steps, 2, rows, model)] * parts,
-        micros=9,
-    )(*blocks, share, gate, up, both, gate_w, up_w, down_w, pair_w, pair_down)
+        + [bf16(steps, 2, rows, model)] * 2
+        + [(bf16 if last else f32)(hidden, model)],
+        micros=10,
+    )(*blocks, *others)
 
 
 def experts_weights(groups):
-    rows, grads, share, act, shared, gate_grad, up_grad, pair_grad = groups[0]
-    model, hidden, double = rows.shape[1], act.shape[1], shared.shape[1]
+    rows, grads, shared, gate_grad, up_grad, pair_grad = groups[0]
+    model, hidden, double = rows.shape[1], gate_grad.shape[1], shared.shape[1]
     width = 256 if model % 256 == 0 else model
     each_group = len(groups[0])
-
     steps = model // width
-    runs = [(2, 2, 2), (2, 2, 2), (2, 2, 2)] if steps == 6 else [(steps,)] * 3
+    runs = ((4, 2), (2, 2, 2)) if steps == 6 else ((steps,), (steps,))
 
     def kernel(*refs):
         *piece_outs, pair_out, pair_down_out = refs[len(groups) * each_group :]
-        sums = [0.0] * 5
+        sums = [0.0] * 4
         for group in range(len(groups)):
-            x, g, s, a, sa, gg, ug, pg = refs[group * each_group : (group + 1) * each_group]
-            routed = (s[...] * g[...].astype(jnp.float32)).astype(jnp.bfloat16)
-            sums[0] = sums[0] + product(a[...], routed, ROWS_SUMMED)
-            sums[1] = sums[1] + product(x[...], gg[...], ROWS_SUMMED)
-            sums[2] = sums[2] + product(x[...], ug[...], ROWS_SUMMED)
-            sums[3] = sums[3] + product(x[...], pg[...], ROWS_SUMMED)
-            sums[4] = sums[4] + product(sa[...], g[...], ROWS_SUMMED)
-        pair_out[...] = sums[3].astype(jnp.bfloat16)
-        pair_down_out[...] = sums[4].astype(jnp.bfloat16)
+            x, g, sa, gg, ug, pg = refs[group * each_group : (group + 1) * each_group]
+            sums[0] = sums[0] + product(x[...], gg[...], ROWS_SUMMED)
+            sums[1] = sums[1] + product(x[...], ug[...], ROWS_SUMMED)
+            sums[2] = sums[2] + product(x[...], pg[...], ROWS_SUMMED)
+            sums[3] = sums[3] + product(sa[...], g[...], ROWS_SUMMED)
+        pair_out[...] = sums[2].astype(jnp.bfloat16)
+        pair_down_out[...] = sums[3].astype(jnp.bfloat16)
         number = 0
-        for kind in range(3):
+        for kind in range(2):
             first = 0
             for run in runs[kind]:
                 store_piece(piece_outs[number], sums[kind], first, run)
@@ -981,24 +987,21 @@
         @pl.when((pl.program_id(0) >= first) & (pl.program_id(0) < first + run))
         def _():
             out[...] = value.astype(jnp.bfloat16)
+
+    def piece_spec(first, run):
+        return pl.BlockSpec((width, hidden), lambda d: (jnp.clip(d - first, 0, run - 1), 0))
 
     in_specs = []
     for group in groups:
         total = group[0].shape[0]
         columns = pl.BlockSpec((total, width), lambda d: (0, d))
         in_specs += [columns, columns] + [whole(value.shape) for value in group[2:]]
-
-    def piece_spec(kind, first, run):
-        if kind < 2:
-            return pl.BlockSpec((width, hidden), lambda d: (jnp.clip(d - first, 0, run - 1), 0))
-        return pl.BlockSpec((hidden, width), lambda d: (0, jnp.clip(d - first, 0, run - 1)))
-
     out_specs, shapes = [], []
-    for place, kind in enumerate((2, 0, 1)):
+    for kind in range(2):
         first = 0
-        for run in runs[place]:
-            out_specs.append(piece_spec(kind, first, run))
-            shapes.append(bf16(width * run, hidden) if kind < 2 else bf16(hidden, width * run))
+        for run in runs[kind]:
+            out_specs.append(piece_spec(first, run))
+            shapes.append(bf16(width * run, hidden))
             first += run
     outs = call(
         kernel,
@@ -1012,7 +1015,7 @@
         shapes + [bf16(model, double), bf16(double, model)],
         micros=11,
     )(*[value for group in groups for value in group])
-    return outs[:-2], [len(run) for run in runs], outs[-2], outs[-1]
+    return outs[: len(runs[0])], outs[len(runs[0]) : -2], outs[-2], outs[-1]
 
 
 def mixer_weights(normed, gate_grad, value_grad, state_grad):
@@ -1108,7 +1111,13 @@
     hidden_own = seq_devices * columns
     pair_cut = jnp.stack([shared_gate, shared_up]).reshape(2, gain_rows, seq_devices, mp_count, columns)
     pair_cut = pair_cut.transpose(3, 1, 0, 2, 4).reshape(mp_count, -1)
-    both_packed = seq_gather(packed)
+    head_count = step_proj.shape[1]
+    lane_pad = ((0, 0), (0, 128 - head_count))
+    step_weight = jnp.pad(step_proj, lane_pad)
+    step_shift = jnp.pad(step_bias[None], lane_pad)
+    decay_rate = jnp.pad(decay_log[None], lane_pad)
+    skip_row = jnp.pad(skip_gain[None], lane_pad)
+    both_packed = after(seq_gather(packed), step_weight, step_shift, decay_rate, skip_row)
     small = gather_small(
         jnp.concatenate(
             [
@@ -1147,18 +1156,13 @@
     own_inputs = own_inputs.reshape(row_count, model_width)
     edge_rows = shifted(tokens[slot_count - window + 1 :].transpose(1, 0, 2), "seq", 1)
     edge_rows = jnp.pad(edge_rows, ((0, 0), (EDGE - window + 1, 0), (0, 0)))
-    lane_pad = ((0, 0), (0, 128 - head_count))
-    step_weight = jnp.pad(step_proj, lane_pad)
-    step_shift = jnp.pad(step_bias[None], lane_pad)
-    decay_rate = jnp.pad(decay_log[None], lane_pad)
-    skip_row = jnp.pad(skip_gain[None], lane_pad)
     state_taps = wide(conv_state_whole).T
     mixer = mixer_input(
         sequences,
         edge_rows,
         wide(gain_first)[None],
-        gate_proj,
-        value_proj,
+        gate_proj.T,
+        value_proj.T,
         state_whole,
         step_weight,
         conv_value,
@@ -1238,35 +1242,44 @@
     block_out = slots_first(block_rows)
     grad_blocks, first_backward = gather_blocks(
         grad_low,
-        lambda blocks: experts_backward(blocks, shares[0], *forwards[0][1:4], *expert_weights),
+        lambda blocks: experts_backward(
+            blocks, shares[0], *forwards[0][1:5], None, False, *expert_weights
+        ),
     )
     backwards = [
         first_backward,
         experts_backward(
-            of_group(grad_blocks, ring_groups[1]), shares[1], *forwards[1][1:4], *expert_weights
+            of_group(grad_blocks, ring_groups[1]),
+            shares[1],
+            *forwards[1][1:5],
+            first_backward[6],
+            True,
+            *expert_weights,
         ),
     ]
-    kept, sent = of_groups([result[4:] for result in backwards])
-    expert_parts, part_counts, pair_grad, pair_down_grad = experts_weights(
-        [
-            (after(ahead[0], sent), back[0], share_rows, ahead[4], ahead[5], back[1], back[2], back[3])
-            for ahead, back, share_rows in zip(forwards, backwards, shares)
-        ]
-    )
-    row_sums, _ = scatter_deep(after(kept, pair_down_grad), sent)
-
     def seq_moved(value):
         return lax.ppermute(value, "seq", [(0, 1), (1, 0)])
 
     paired = seq_devices == 2
-    chunks = len(expert_parts)
-    expert_moved = [None] * chunks
-    early_chunks, mix_ties = 5 if chunks == 9 else 0, ()
-    if paired:
-        for place in range(early_chunks):
-            expert_moved[place] = seq_moved(expert_parts[place])
-        row_sums = after(row_sums, expert_moved[: min(early_chunks, 1)])
-        mix_ties = [(), *expert_moved[1 : max(early_chunks - 2, 1)]]
+    kept, sent = of_groups([result[4:6] for result in backwards])
+    down_part = backwards[1][6]
+    first_row = after(forwards[0][0], sent)
+    gate_parts, up_parts, pair_grad, pair_down_grad = experts_weights(
+        [
+            (ahead_rows, back[0], ahead[5], back[1], back[2], back[3])
+            for ahead_rows, ahead, back in zip((first_row, forwards[1][0]), forwards, backwards)
+        ]
+    )
+    expert_parts = [down_part, *gate_parts, *up_parts]
+    part_counts = [1, len(gate_parts)]
+    ordered = paired and len(expert_parts) == 6
+    expert_moved = [None] * len(expert_parts)
+    row_sums, _ = scatter_deep(after(kept, pair_down_grad), sent)
+    mix_ties = ()
+    if ordered:
+        expert_moved[:4] = [seq_moved(part) for part in expert_parts[:4]]
+        row_sums = after(row_sums, expert_moved[0])
+        mix_ties = [(), (), expert_moved[1]]
     hidden_grad, mix_grad_send, ffn_gain_grad = hidden_rows_back(
         row_sums,
         grad_out,
@@ -1276,8 +1289,8 @@
         second_gain,
     )
     mix_blocks, _ = gather_blocks(mix_grad_send, None, mix_ties)
-    if paired and early_chunks:
-        mix_blocks = after(mix_blocks, expert_moved[early_chunks - 2])
+    if ordered:
+        mix_blocks = after(mix_blocks, expert_moved[2])
     mix_grad_all, ssm_grad, gate_grad, entering_grad, mixer_gain_grad = mixer_output_back(
         order,
         mix_blocks,
@@ -1291,8 +1304,8 @@
     )
     exit_grad = entering_of(entering_grad, True)
     within_grad = ssm_grad
-    if paired and early_chunks:
-        within_grad = after(ssm_grad, expert_moved[early_chunks - 1])
+    if ordered:
+        within_grad = after(ssm_grad, expert_moved[3])
     scaled_value_grad, state_part_grad = mixer_within_back(
         pre_value, pre_state, step_raw, decay_sum, step_shift, within_grad, entering, head_count
     )
@@ -1309,13 +1322,8 @@
     scaled_value_grad = after(scaled_value_grad, out_proj_part)
     if paired:
         out_proj_moved = seq_moved(after(out_proj_part, scaled_value_grad))
-    if paired and early_chunks:
-        expert_moved[6] = seq_moved(expert_parts[6])
-        expert_moved[5] = seq_moved(after(expert_parts[5], scaled_value_grad))
-        exit_grad = after(exit_grad, expert_moved[6])
-    shared_down_grad = seq_scatter(
-        after(pair_down_grad, scaled_value_grad)[:hidden_own].reshape(seq_devices, columns, model_width)
-    )
+    if ordered:
+        expert_moved[4] = seq_moved(after(expert_parts[4], scaled_value_grad))
     value_local, state_local, edge_value, edge_state, step_grad, taps_value, taps_state, head_grads = (
         mixer_input_back(
             pre_value,
@@ -1356,7 +1364,9 @@
     edges = shifted(jnp.concatenate([edge_value, edge_state], axis=-1), "seq", -1)
     if paired:
         flat = flat + seq_moved(flat)
-        edges = after(edges, flat, out_proj_moved, shared_down_grad, expert_moved[5:6] if early_chunks else ())
+        edges = after(edges, flat, out_proj_moved)
+        if ordered:
+            edges = after(edges, expert_moved[4])
     else:
         flat = lax.psum(flat, "seq")
     value_grad, state_grad, in_gain_grad, *last_parts = mixer_project_back(
@@ -1368,8 +1378,8 @@
         gate_grad,
         step_grad,
         sequences,
-        gate_proj,
-        value_proj,
+        gate_proj.T,
+        value_proj.T,
         state_whole,
         step_weight,
         mp_count,
@@ -1378,13 +1388,13 @@
     if paired:
         step_flat = step_flat + seq_moved(step_flat)
         last_parts[0] = after(last_parts[0], step_flat)
-        if early_chunks:
-            expert_moved[7] = seq_moved(after(expert_parts[7], edges))
-            last_parts[0] = after(last_parts[0], expert_moved[7])
     else:
         step_flat = lax.psum(step_flat, "seq")
     kept, sent = scatter_core(*last_parts)
-    if paired and early_chunks == 0:
+    if ordered:
+        expert_moved[5] = seq_moved(after(expert_parts[5], value_grad))
+        kept = after(kept, expert_moved[5])
+    elif paired:
         expert_moved = [seq_moved(after(part, value_grad)) for part in expert_parts]
     both_proj_grad, state_proj_grad = mixer_weights(
         after(normed, sent), gate_grad, value_grad, state_grad
@@ -1415,16 +1425,15 @@
         axis=-1,
     )
     local_extra = extra
-    if paired and early_chunks:
-        expert_moved[-1] = seq_moved(after(expert_parts[-1], local_extra))
     last_sums, moving = scatter_deep(after(kept, extra), sent)
     extra_low = bits(seq_scatter(extra))
     extra = jnp.concatenate(
         [extra_low, bits(conv_high), bits(conv_small - conv_high)], axis=-1
     )
-    extra = mp_exchange(after(extra, last_sums))
+    extra_sent = after(extra, last_sums)
+    extra = mp_exchange(extra_sent)
     tokens_grad = slots_first(
-        token_rows_back(last_sums, hidden_grad, own_inputs, first_gain)
+        token_rows_back(last_sums, after(hidden_grad, extra_low), own_inputs, first_gain)
     )
     cuts = [gain_rows * state_width]
     for size in (gain_rows, gain_rows, pair_extra.shape[2], conv_small.shape[1]):
@@ -1442,8 +1451,8 @@
     pair_grad = pair_grad.transpose(2, 1, 3, 0, 4).reshape(2, gain_rows, -1)
     shared_gate_grad, shared_up_grad = pair_grad[0], pair_grad[1]
     if paired:
-        early_sums = sum(part_counts[:2])
-        expert_moved[:early_sums] = after(expert_moved[:early_sums], last_sums[2:3])
+        early_sums = part_counts[0] + part_counts[1]
+        expert_moved[:early_sums] = after(expert_moved[:early_sums], extra_sent)
         both_part = after(both_proj_grad, local_extra)
         both_moved = seq_moved(both_part)
         expert_moved[early_sums:], out_proj_moved, both_moved = after(
@@ -1458,6 +1467,12 @@
         expert_sums = [seq_sum(part) for part in expert_parts]
     gate_proj_grad, value_proj_grad = both_proj_grad[:, :inner_width], both_proj_grad[:, inner_width:]
     step_proj_grad = step_flat.reshape(step_proj_grad.shape)
+    down_low = pair_down_grad[:hidden_own].reshape(seq_devices, columns, model_width)
+    if paired:
+        own_down, other_down = pick(down_low, mine), pick(down_low, 1 - mine)
+        shared_down_grad = wide(own_down) + wide(after(seq_moved(after(other_down, tokens_grad)), both_moved))
+    else:
+        shared_down_grad = seq_scatter(down_low)
     one, two = part_counts[0], part_counts[0] + part_counts[1]
     expert_down_grad = jnp.concatenate(expert_sums[:one], axis=1)[None]
     expert_gate_grad = jnp.concatenate(expert_sums[one:two])[None]

time: 546 us -> 525 us (0.962)
  waiting for transfers between devices: 149 us -> 137 us
  starting transfers between devices: 107 us -> 99.1 us
    ppermute x13 -> x11, waiting for transfers between devices: 37.7 us -> 7.27 us  [seq_moved(): return lax.ppermute(value, 'seq', [(0, 1), (1, 0)])]
    ppermute x84, waiting for transfers between devices: 100 us -> 127 us  [mp_permute(): return lax.ppermute(value, 'mp', [(i, target(i)) for i in range(count)])]
    ppermute x13 -> x11, starting transfers between devices: 17.9 us -> 9.81 us  [seq_moved(): return lax.ppermute(value, 'seq', [(0, 1), (1, 0)])]
    ppermute x2, waiting for transfers between devices: 8.17 us -> 2.19 us  [seq_entering(): return lax.ppermute(state, 'seq', route)]
    unnamed x290 -> x278, local copies, waits for them, and re-layouts: 39.2 us -> 34.9 us
  transfers between devices with their start and end apart: 108 -> 105, of which waited for: 39 -> 46; matrix products, arithmetic and copies ran while one was open for 11% -> 12% of each run, Pallas kernels for 24% -> 24%
where the time goes in v4:
time: 525 us; the launch traced here: 515 us
  Pallas kernels  169 us (32%)
  waiting for transfers between devices  137 us (26%)
  starting transfers between devices  99.1 us (19%)
  local copies, waits for them, and re-layouts  85.1 us (16%)
  other arithmetic  21.2 us (4%)
    ppermute x84, waiting for transfers between devices, mp_permute(): return lax.ppermute(value, 'mp', [(i, target(i)) for i in range(count)])  127 us
    ppermute x84, starting transfers between devices, mp_permute(): return lax.ppermute(value, 'mp', [(i, target(i)) for i in range(count)])  64.9 us
    unnamed x278, local copies, waits for them, and re-layouts  34.9 us
    pallas_call x12, Pallas kernels, add_blocks(): call(kernel, (1,), [whole(left.shape)] * 2, whole(left.shape), bf16(*left...  21.3 us
    pallas_call x2, Pallas kernels, experts_backward(): call(kernel, (1,), [whole(block.shape) for block in blocks] + [whole(valu...  21 us
    pallas_call x2, Pallas kernels, experts_forward(): call(kernel, (1,), [whole(block.shape) for block in blocks] + [whole(w.sh...  16.2 us
    pallas_call x6, Pallas kernels, add_pairs(): call(kernel, (1,), [whole(left.shape)] * 2, [whole((rows, width))] * (2 *...  15.9 us
    pallas_call x1, Pallas kernels, mixer_input_back(): call(kernel, (count,), [each((length, inner)), each((length, double)), ea...  13.1 us
  transfers between devices with their start and end apart: 105, of which 46 were waited for; matrix products, arithmetic and copies ran while one was open for 12% of the time, Pallas kernels for 24%

profile of v4, /device:TPU:0, one launch (start us, length us, event | category | flops | bytes accessed | tf_op | source)
XLA Modules:
  0.0 515.0 jit_solution(1120833940685436076)
XLA Ops:
  5.0 4.8 collective-permute-start
  21.4 3.1 collective-permute-done.2
  27.1 3.8 collective-permute-done.5
  41.5 11.0 %shard_map.443 = (bf16[4,256,1536]{2,1,0:T(8,128)(2,1)}, f32[4,256,192]{2,1,0:T(8,128)}, f32[4,272,192]{2,1,0:T(8,128)}, f32[4,272,256]{2,1,0:T(8,128)}, f32[4,2...) custom-call(bf16[4,256,1536]{2,1,0:T(8,128)(2,1)} %bitcast.124, ...), custom_call_target="tpu_custom_call" | custom-call | flops 990000000 | bytes 2750000 | tf_op jit(solution)/shard_map/pallas_call | solution.py:300
  52.5 3.5 collective-permute-start.7
  56.6 5.9 %shard_map.444.within_ref = f32[4,256,192]{2,1,0:T(8,128)} custom-call(f32[4,256,192]{2,1,0:T(8,128)} %get-tuple-element.210.pv_ref, f32[4,256,256]{2,1,0:T(8,128)} %get-tuple-element.211.ps_ref.refs_18_, f32[4,256,128]{2,1,0:T(8,128)} %get-tuple-element.212.step_ref, f32[4,256,128]{2,1,0:T(8,128)} %get-tuple-element.213.decay_ref.refs_19_, ...), custom_call_target="tpu_custom_call" | custom-call | flops 540000000 | bytes 1500000 | tf_op jit(solution)/shard_map/pallas_call | solution.py:351
  65.5 7.5 %shard_map.445 = (f32[4,256,192]{2,1,0:T(8,128)}, bf16[4,256,192]{2,1,0:T(8,128)(2,1)}, bf16[4,2,64,1664]{3,2,1,0:T(8,128)(2,1)}, bf16[4,2,64,1664]{3,2,1,0:T(8,128)(2,1)}) custom-call(s32[16]{0:T(128)} %add.230.order_ref, f32[4,256,192]{2,1,0:T(8,128)} %shard_map.444.within_ref, f32[4,256,256]{2,1,0:T(8,128)} %get-tuple-element.211.ps_ref.refs_18_, ...), custom_call_target="tpu_custom_call" | custom-call | flops 630000000 | bytes 1750000 | tf_op jit(solution)/shard_map/pallas_call | solution.py:391
  79.9 3.7 shard_map.446
  93.7 3.5 all-to-all-start
  97.2 3.2 collective-permute-done.10.right_ref
  103.6 2.9 collective-permute-done.12.right_ref
  115.1 4.2 collective-permute-done.13.refs_3_
  119.3 6.7 %collective-permute-done.15.refs_4_ = bf16[64,1664]{1,0:T(8,128)(2,1)S(1)} collective-permute-done((bf16[64,1664]{1,0:T(8,128)(2,1)}, bf16[64,1664]{1,0:T(8,128)(2,1)S(1)}, u32[]{:S(2)}, u32[]{:S(2)}) %collective-permute-start.15) | collective-permute-done | bytes 213024 | tf_op jit(solution)/shard_map/ppermute | solution.py:66
  131.7 4.3 collective-permute-start.29
  144.0 6.8 %collective-permute-done.31.refs_2_ = bf16[64,1536]{1,0:T(8,128)(2,1)S(1)} collective-permute-done((bf16[64,1536]{1,0:T(8,128)(2,1)}, bf16[64,1536]{1,0:T(8,128)(2,1)S(1)}, u32[]{:S(2)}, u32[]{:S(2)}) %collective-permute-start.31) | collective-permute-done | bytes 196640 | tf_op jit(solution)/shard_map/ppermute | solution.py:66
  154.7 8.1 %shard_map.451 = (bf16[512,1536]{1,0:T(8,128)(2,1)}, f32[512,512]{1,0:T(8,128)}, f32[512,512]{1,0:T(8,128)}, f32[512,128]{1,0:T(8,128)}, bf16[512,512]{1,0:T(8,1...) custom-call(bf16[64,1536]{1,0:T(8,128)(2,1)} %get-tuple-element.232.refs_0_, ...), custom_call_target="tpu_custom_call" | custom-call | flops 720000000 | bytes 2000000 | tf_op jit(solution)/shard_map/pallas_call | solution.py:895
  166.3 8.1 %shard_map.454 = (bf16[512,1536]{1,0:T(8,128)(2,1)}, f32[512,512]{1,0:T(8,128)}, f32[512,512]{1,0:T(8,128)}, f32[512,128]{1,0:T(8,128)}, bf16[512,512]{1,0:T(8,1...) custom-call(bf16[64,1536]{1,0:T(8,128)(2,1)} %copy-done.69, ...), custom_call_target="tpu_custom_call" | custom-call | flops 720000000 | bytes 2000000 | tf_op jit(solution)/shard_map/pallas_call | solution.py:895
  197.8 4.3 collective-permute-done.39.refs_3_
  202.1 6.5 %collective-permute-done.41.refs_4_ = bf16[64,1536]{1,0:T(8,128)(2,1)S(1)} collective-permute-done((bf16[64,1536]{1,0:T(8,128)(2,1)}, bf16[64,1536]{1,0:T(8,128)(2,1)S(1)}, u32[]{:S(2)}, u32[]{:S(2)}) %collective-permute-start.41) | collective-permute-done | bytes 196640 | tf_op jit(solution)/shard_map/ppermute | solution.py:66
  212.7 4.0 collective-permute-start.50
  216.6 5.1 collective-permute-done.43.refs_2_
  225.1 4.2 collective-permute-done.44.refs_3_
  229.3 3.4 collective-permute-done.52.refs_2_
  234.8 10.2 %shard_map.459 = (bf16[512,1536]{1,0:T(8,128)(2,1)}, bf16[512,512]{1,0:T(8,128)(2,1)}, bf16[512,512]{1,0:T(8,128)(2,1)}, bf16[512,128]{1,0:T(8,128)(2,1)}, bf16[...) custom-call(bf16[64,1536]{1,0:T(8,128)(2,1)} %get-tuple-element.253.refs_0_, ...), custom_call_target="tpu_custom_call" | custom-call | flops 900000000 | bytes 2500000 | tf_op jit(solution)/shard_map/pallas_call | solution.py:946
  247.6 10.8 %shard_map.461 = (bf16[512,1536]{1,0:T(8,128)(2,1)}, bf16[512,512]{1,0:T(8,128)(2,1)}, bf16[512,512]{1,0:T(8,128)(2,1)}, bf16[512,128]{1,0:T(8,128)(2,1)}, bf16[...) custom-call(bf16[64,1536]{1,0:T(8,128)(2,1)} %copy-done.71, ...), custom_call_target="tpu_custom_call" | custom-call | flops 900000000 | bytes 2500000 | tf_op jit(solution)/shard_map/pallas_call | solution.py:946
  259.5 2.9 collective-permute-done.49.right_ref
  268.7 10.5 %shard_map.463 = (bf16[1024,512]{1,0:T(8,128)(2,1)}, bf16[512,512]{1,0:T(8,128)(2,1)}, bf16[512,512]{1,0:T(8,128)(2,1)}, bf16[512,512]{1,0:T(8,128)(2,1)}, bf16[...) custom-call(bf16[512,1536]{1,0:T(8,128)(2,1)} %get-tuple-element.278.refs_0_, ...), custom_call_target="tpu_custom_call" | custom-call | flops 990000000 | bytes 2750000 | tf_op jit(solution)/shard_map/pallas_call | solution.py:1006
  283.9 4.6 collective-permute-done.60.right_ref
  293.8 3.1 collective-permute-done.64.right_ref
  302.8 7.4 %collective-permute-done.63.refs_3_ = bf16[64,1536]{1,0:T(8,128)(2,1)S(1)} collective-permute-done((bf16[64,1536]{1,0:T(8,128)(2,1)}, bf16[64,1536]{1,0:T(8,128)(2,1)S(1)}, u32[]{:S(2)}, u32[]{:S(2)}) %collective-permute-start.63) | collective-permute-done | bytes 196640 | tf_op jit(solution)/shard_map/ppermute | solution.py:66
  310.2 5.4 %collective-permute-done.65.refs_4_ = bf16[64,1536]{1,0:T(8,128)(2,1)S(1)} collective-permute-done((bf16[64,1536]{1,0:T(8,128)(2,1)}, bf16[64,1536]{1,0:T(8,128)(2,1)S(1)}, u32[]{:S(2)}, u32[]{:S(2)}) %collective-permute-start.65) | collective-permute-done | bytes 196640 | tf_op jit(solution)/shard_map/ppermute | solution.py:66
  316.3 2.8 shard_map.467
  319.1 3.8 collective-permute-start.70
  323.0 6.4 %collective-permute-done.68.refs_2_ = bf16[64,1664]{1,0:T(8,128)(2,1)S(1)} collective-permute-done((bf16[64,1664]{1,0:T(8,128)(2,1)}, bf16[64,1664]{1,0:T(8,128)(2,1)S(1)}, u32[]{:S(2)}, u32[]{:S(2)}) %collective-permute-start.68) | collective-permute-done | bytes 213024 | tf_op jit(solution)/shard_map/ppermute | solution.py:66
  333.2 5.6 %collective-permute-done.73.refs_6_ = bf16[64,1664]{1,0:T(8,128)(2,1)S(1)} collective-permute-done((bf16[64,1664]{1,0:T(8,128)(2,1)}, bf16[64,1664]{1,0:T(8,128)(2,1)S(1)}, u32[]{:S(2)}, u32[]{:S(2)}) %collective-permute-start.73) | collective-permute-done | bytes 213024 | tf_op jit(solution)/shard_map/ppermute | solution.py:66
  341.8 2.7 collective-permute-done.74.refs_7_
  346.3 4.1 collective-permute-done.72.refs_5_
  352.6 7.9 %shard_map.468 = (bf16[4,256,1536]{2,1,0:T(8,128)(2,1)}, f32[4,256,192]{2,1,0:T(8,128)}, bf16[4,256,192]{2,1,0:T(8,128)(2,1)}, f32[4,192,128]{2,1,0:T(8,128)}, f32[8,192]{1,0:T(8,128)}) custom-call(s32[16]{0:T(128)} %add.230.order_ref, bf16[64,1664]{1,0:T(8,128)(2,1)} %get-tuple-element.308.refs_0_, bf16[64,1664]{1,0:T(8,128)(2,1)} %copy-done.44, ...), custom_call_target="tpu_custom_call" | custom-call | flops 720000000 | bytes 2000000 | tf_op jit(solution)/shard_map/pallas_call | solution.py:440
  362.1 8.9 %shard_map.469 = (f32[4,256,192]{2,1,0:T(8,128)}, f32[4,256,256]{2,1,0:T(8,128)}) custom-call(f32[4,256,192]{2,1,0:T(8,128)} %get-tuple-element.210.pv_ref, f32[4,256,256]{2,1,0:T(8,128)} %get-tuple-element.211.ps_ref.refs_18_, f32[4,256,128]{2,1,0:T(8,128)} %get-tuple-element.212.step_ref, f32[4,256,128]{2,1,0:T(8,128)} %get-tuple-element.213.decay_ref.refs_19_, ...), custom_call_target="tpu_custom_call" | custom-call | flops 810000000 | bytes 2250000 | tf_op jit(solution)/shard_map/pallas_call | solution.py:485
  376.1 13.1 %shard_map.470 = (f32[4,256,192]{2,1,0:T(8,128)}, f32[4,256,256]{2,1,0:T(8,128)}, f32[4,16,192]{2,1,0:T(8,128)}, f32[4,16,256]{2,1,0:T(8,128)}, bf16[4,256,128]{...) custom-call(f32[4,256,192]{2,1,0:T(8,128)} %get-tuple-element.210.pv_ref, ...), custom_call_target="tpu_custom_call" | custom-call | flops 1170000000 | bytes 3250000 | tf_op jit(solution)/shard_map/pallas_call | solution.py:584
  398.6 4.4 collective-permute-done.87
  404.5 10.3 %shard_map.471 = (bf16[4,256,192]{2,1,0:T(8,128)(2,1)}, bf16[4,256,256]{2,1,0:T(8,128)(2,1)}, f32[8,1536]{1,0:T(8,128)}, bf16[4,2,64,1536]{3,2,1,0:T(8,128)(2,1)}, bf16[4,2,64,1536]{3,2,1,0:T(8,128)(2,1)}) custom-call(s32[16]{0:T(128)} %add.230.order_ref, f32[4,256,192]{2,1,0:T(8,128)} %get-tuple-element.334.value_ref, ...), custom_call_target="tpu_custom_call" | custom-call | flops 900000000 | bytes 2500000 | tf_op jit(solution)/shard_map/pallas_call | solution.py:650
  421.5 2.9 collective-permute-done.90
  424.5 3.1 shard_map.472
  427.5 8.7 %shard_map.473 = (bf16[1536,384]{1,0:T(8,128)(2,1)}, bf16[1536,256]{1,0:T(8,128)(2,1)}) custom-call(bf16[4,256,1536]{2,1,0:T(8,128)(2,1)} %get-tuple-element.368.normed_ref, bf16[4,256,192]{2,1,0:T(8,128)(2,1)} %get-tuple-element.347.gate_grad_ref.gate_ref, bf16[4,256,192]{2,1,0:T(8,128)(2,1)} %get-tuple-element.358.value_ref, ...), custom_call_target="tpu_custom_call" | custom-call | flops 720000000 | bytes 2000000 | tf_op jit(solution)/shard_map/pallas_call | solution.py:1043
  464.7 2.8 collective-permute-done.97.refs_3_
  467.5 5.9 %collective-permute-done.99.refs_4_ = bf16[64,1536]{1,0:T(8,128)(2,1)S(1)} collective-permute-done((bf16[64,1536]{1,0:T(8,128)(2,1)}, bf16[64,1536]{1,0:T(8,128)(2,1)S(1)}, u32[]{:S(2)}, u32[]{:S(2)}) %collective-permute-start.99) | collective-permute-done | bytes 196640 | tf_op jit(solution)/shard_map/ppermute | solution.py:66
  481.1 4.6 all-to-all-start.1
  (634 shorter events, 240.7 us)
Async XLA Ops:
  5.0 27.1 %collective-permute-start = (bf16[4,3,1536]{2,1,0:T(4,128)(2,1)S(1)}, bf16[4,3,1536]{2,1,0:T(4,128)(2,1)S(1)}, u32[]{:S(2)}, u32[]{:S(2)}) collective-permute-start(bf16[4,3,1536]{2,1,0:T(4,128)(2,1)S(1)} %slice_bitcast_fusion), channel_id=1, source_target_pairs={{0,16},{1,17},{2,18},{3,19},{4,20},{5,21},{6,22},{7,23},{8,24},{9,... | collective-permute-start | bytes 110600 | tf_op jit(solution)/shard_map/ppermute | solution.py:19
  52.5 12.2 %collective-permute-start.7 = (f32[4,3,64,128]{3,2,1,0:T(8,128)}, f32[4,3,64,128]{3,2,1,0:T(8,128)S(1)}, u32[]{:S(2)}, u32[]{:S(2)}) collective-permute-start(f32[4,3,64,128]{3,2,1,0:T(8,128)} %bitcast.188), channel_id=1, source_target_pairs={{0,16},{1,17},{2,18},{3,19},{4,20},{5,21},{6,22},{7,23},{8,24},{9,... | collective-permute-start | bytes 1179656 | tf_op jit(solution)/shard_map/ppermute | solution.py:136
  83.6 13.6 %collective-permute-start.24 = (bf16[32,1536]{1,0:T(8,128)(2,1)S(1)}, bf16[32,1536]{1,0:T(8,128)(2,1)S(1)}, u32[]{:S(2)}, u32[]{:S(2)}) collective-permute-start(bf16[32,1536]{1,0:T(8,128)(2,1)S(1)} %copy-done.99), channel_id=1, source_target_pairs={{0,16},{16,0},{1,17},{17,1},{2,18},{18,2},{3,19},{19,3},{4,20},{20... | collective-permute-start | bytes 294920 | tf_op jit(solution)/shard_map/ppermute | solution.py:113
  87.6 27.5 %collective-permute-start.9 = (bf16[64,1664]{1,0:T(8,128)(2,1)}, bf16[64,1664]{1,0:T(8,128)(2,1)S(1)}, u32[]{:S(2)}, u32[]{:S(2)}) collective-permute-start(bf16[64,1664]{1,0:T(8,128)(2,1)} %get-tuple-element.219), channel_id=1, source_target_pairs={{0,2},{1,3},{2,0},{3,1},{4,6},{5,7},{6,4},{7,5},{8,10},{9,11},{10,... | collective-permute-start | bytes 638984 | tf_op jit(solution)/shard_map/ppermute | solution.py:66
  89.1 11.3 %collective-permute-start.10 = (bf16[64,1664]{1,0:T(8,128)(2,1)}, bf16[64,1664]{1,0:T(8,128)(2,1)S(1)}, u32[]{:S(2)}, u32[]{:S(2)}) collective-permute-start(bf16[64,1664]{1,0:T(8,128)(2,1)} %get-tuple-element.221), channel_id=1, source_target_pairs={{0,2},{1,3},{2,0},{3,1},{4,6},{5,7},{6,4},{7,5},{8,10},{9,11},{10,... | collective-permute-start | bytes 638984 | tf_op jit(solution)/shard_map/ppermute | solution.py:66
  89.6 17.0 %collective-permute-start.12 = (bf16[64,1664]{1,0:T(8,128)(2,1)}, bf16[64,1664]{1,0:T(8,128)(2,1)S(1)}, u32[]{:S(2)}, u32[]{:S(2)}) collective-permute-start(bf16[64,1664]{1,0:T(8,128)(2,1)} %get-tuple-element.223), channel_id=1, source_target_pairs={{0,2},{1,3},{2,0},{3,1},{4,6},{5,7},{6,4},{7,5},{8,10},{9,11},{10,... | collective-permute-start | bytes 638984 | tf_op jit(solution)/shard_map/ppermute | solution.py:66
  91.1 19.6 %collective-permute-start.14 = (bf16[64,1664]{1,0:T(8,128)(2,1)}, bf16[64,1664]{1,0:T(8,128)(2,1)S(1)}, u32[]{:S(2)}, u32[]{:S(2)}) collective-permute-start(bf16[64,1664]{1,0:T(8,128)(2,1)} %get-tuple-element.225), channel_id=1, source_target_pairs={{0,2},{1,3},{2,0},{3,1},{4,6},{5,7},{6,4},{7,5},{8,10},{9,11},{10,... | collective-permute-start | bytes 638984 | tf_op jit(solution)/shard_map/ppermute | solution.py:66
  93.7 20.8 %all-to-all-start = ((bf16[16,2,3072]{2,1,0:T(2,128)(2,1)}), bf16[16,2,3072]{2,1,0:T(2,128)(2,1)S(1)}, u32[]{:S(2)}, u32[]{:S(2)}) async-start(bf16[16,2,3072]{2,1,0:T(2,128)(2,1)} %reshape.497), calls=%async_computation | async-start | bytes 393216 | tf_op jit(solution)/shard_map/all_to_all | solution.py:147
  103.0 12.1 %collective-permute-start.11 = (bf16[64,1664]{1,0:T(8,128)(2,1)}, bf16[64,1664]{1,0:T(8,128)(2,1)S(1)}, u32[]{:S(2)}, u32[]{:S(2)}) collective-permute-start(bf16[64,1664]{1,0:T(8,128)(2,1)} %shard_map.447), channel_id=1, source_target_pairs={{0,12},{1,13},{2,14},{3,15},{4,0},{5,1},{6,2},{7,3},{8,4},{9,5},{1... | collective-permute-start | bytes 638984 | tf_op jit(solution)/shard_map/ppermute | solution.py:66
  113.3 12.8 %collective-permute-start.15 = (bf16[64,1664]{1,0:T(8,128)(2,1)}, bf16[64,1664]{1,0:T(8,128)(2,1)S(1)}, u32[]{:S(2)}, u32[]{:S(2)}) collective-permute-start(bf16[64,1664]{1,0:T(8,128)(2,1)} %shard_map.449), channel_id=1, source_target_pairs={{0,8},{1,9},{2,10},{3,11},{4,12},{5,13},{6,14},{7,15},{8,0},{9,1},... | collective-permute-start | bytes 638984 | tf_op jit(solution)/shard_map/ppermute | solution.py:66
  114.7 21.3 %collective-permute-start.23 = (bf16[16,6144]{1,0:T(8,128)(2,1)S(1)}, bf16[16,6144]{1,0:T(8,128)(2,1)S(1)}, u32[]{:S(2)}, u32[]{:S(2)}) collective-permute-start(bf16[16,6144]{1,0:T(8,128)(2,1)S(1)} %bitcast.170), channel_id=1, source_target_pairs={{0,16},{16,0},{1,17},{17,1},{2,18},{18,2},{3,19},{19,3},{4,20},{20... | collective-permute-start | bytes 589832 | tf_op jit(solution)/shard_map/ppermute | solution.py:113
  136.0 14.7 %collective-permute-start.31 = (bf16[64,1536]{1,0:T(8,128)(2,1)}, bf16[64,1536]{1,0:T(8,128)(2,1)S(1)}, u32[]{:S(2)}, u32[]{:S(2)}) collective-permute-start(bf16[64,1536]{1,0:T(8,128)(2,1)} %get-tuple-element.232.refs_0_), channel_id=1, source_target_pairs={{0,8},{1,9},{2,10},{3,11},{4,12},{5,13},{6,14},{7,15},{8,0},{9,1},... | collective-permute-start | bytes 589832 | tf_op jit(solution)/shard_map/ppermute | solution.py:66
  138.7 13.7 %collective-permute-start.18 = (bf16[64,1536]{1,0:T(8,128)(2,1)S(1)}, bf16[64,1536]{1,0:T(8,128)(2,1)S(1)}, u32[]{:S(2)}, u32[]{:S(2)}) collective-permute-start(bf16[64,1536]{1,0:T(8,128)(2,1)S(1)} %collective-permute-done.17.refs_2_), channel_id=1, source_target_pairs={{0,2},{1,3},{2,0},{3,1},{4,6},{5,7},{6,4},{7,5},{8,10},{9,11},{10,... | collective-permute-start | bytes 589832 | tf_op jit(solution)/shard_map/ppermute | solution.py:66
  140.8 13.1 %collective-permute-start.21 = (bf16[64,1536]{1,0:T(8,128)(2,1)S(1)}, bf16[64,1536]{1,0:T(8,128)(2,1)S(1)}, u32[]{:S(2)}, u32[]{:S(2)}) collective-permute-start(bf16[64,1536]{1,0:T(8,128)(2,1)S(1)} %collective-permute-done.17.refs_2_), channel_id=1, source_target_pairs={{0,1},{1,0},{2,3},{3,2},{4,5},{5,4},{6,7},{7,6},{8,9},{9,8},{10,11... | collective-permute-start | bytes 589832 | tf_op jit(solution)/shard_map/ppermute | solution.py:66
  140.9 12.4 %collective-permute-start.20 = (bf16[64,1536]{1,0:T(8,128)(2,1)S(1)}, bf16[64,1536]{1,0:T(8,128)(2,1)S(1)}, u32[]{:S(2)}, u32[]{:S(2)}) collective-permute-start(bf16[64,1536]{1,0:T(8,128)(2,1)S(1)} %collective-permute-done.16.refs_1_), channel_id=1, source_target_pairs={{0,1},{1,0},{2,3},{3,2},{4,5},{5,4},{6,7},{7,6},{8,9},{9,8},{10,11... | collective-permute-start | bytes 589832 | tf_op jit(solution)/shard_map/ppermute | solution.py:66
  142.4 11.5 %collective-permute-start.30 = (bf16[64,1536]{1,0:T(8,128)(2,1)S(1)}, bf16[64,1536]{1,0:T(8,128)(2,1)S(1)}, u32[]{:S(2)}, u32[]{:S(2)}) collective-permute-start(bf16[64,1536]{1,0:T(8,128)(2,1)S(1)} %collective-permute-done.29.refs_0_), channel_id=1, source_target_pairs={{0,2},{1,3},{2,0},{3,1},{4,6},{5,7},{6,4},{7,5},{8,10},{9,11},{10,... | collective-permute-start | bytes 589832 | tf_op jit(solution)/shard_map/ppermute | solution.py:66
  150.8 12.1 %collective-permute-start.32 = (bf16[64,1536]{1,0:T(8,128)(2,1)S(1)}, bf16[64,1536]{1,0:T(8,128)(2,1)S(1)}, u32[]{:S(2)}, u32[]{:S(2)}) collective-permute-start(bf16[64,1536]{1,0:T(8,128)(2,1)S(1)} %collective-permute-done.31.refs_2_), channel_id=1, source_target_pairs={{0,2},{1,3},{2,0},{3,1},{4,6},{5,7},{6,4},{7,5},{8,10},{9,11},{10,... | collective-permute-start | bytes 589832 | tf_op jit(solution)/shard_map/ppermute | solution.py:66
  153.4 11.4 %collective-permute-start.33 = (bf16[64,1536]{1,0:T(8,128)(2,1)S(1)}, bf16[64,1536]{1,0:T(8,128)(2,1)S(1)}, u32[]{:S(2)}, u32[]{:S(2)}) collective-permute-start(bf16[64,1536]{1,0:T(8,128)(2,1)S(1)} %collective-permute-done.29.refs_0_), channel_id=1, source_target_pairs={{0,1},{1,0},{2,3},{3,2},{4,5},{5,4},{6,7},{7,6},{8,9},{9,8},{10,11... | collective-permute-start | bytes 589832 | tf_op jit(solution)/shard_map/ppermute | solution.py:66
  182.9 11.1 %collective-permute-start.40 = (bf16[64,1536]{1,0:T(8,128)(2,1)}, bf16[64,1536]{1,0:T(8,128)(2,1)S(1)}, u32[]{:S(2)}, u32[]{:S(2)}) collective-permute-start(bf16[64,1536]{1,0:T(8,128)(2,1)} %get-tuple-element.247), channel_id=1, source_target_pairs={{0,2},{1,3},{2,0},{3,1},{4,6},{5,7},{6,4},{7,5},{8,10},{9,11},{10,... | collective-permute-start | bytes 589832 | tf_op jit(solution)/shard_map/ppermute | solution.py:66
  184.1 13.7 %collective-permute-start.26 = (bf16[64,1536]{1,0:T(8,128)(2,1)S(1)}, bf16[64,1536]{1,0:T(8,128)(2,1)S(1)}, u32[]{:S(2)}, u32[]{:S(2)}) collective-permute-start(bf16[64,1536]{1,0:T(8,128)(2,1)S(1)} %copy-done.117), channel_id=1, source_target_pairs={{0,2},{1,3},{2,0},{3,1},{4,6},{5,7},{6,4},{7,5},{8,10},{9,11},{10,... | collective-permute-start | bytes 589832 | tf_op jit(solution)/shard_map/ppermute | solution.py:66
  196.4 12.2 %collective-permute-start.41 = (bf16[64,1536]{1,0:T(8,128)(2,1)}, bf16[64,1536]{1,0:T(8,128)(2,1)S(1)}, u32[]{:S(2)}, u32[]{:S(2)}) collective-permute-start(bf16[64,1536]{1,0:T(8,128)(2,1)} %shard_map.457), channel_id=1, source_target_pairs={{0,8},{1,9},{2,10},{3,11},{4,12},{5,13},{6,14},{7,15},{8,0},{9,1},... | collective-permute-start | bytes 589832 | tf_op jit(solution)/shard_map/ppermute | solution.py:66
  212.7 11.1 %collective-permute-start.50 = (bf16[64,1536]{1,0:T(8,128)(2,1)}, bf16[64,1536]{1,0:T(8,128)(2,1)S(1)}, u32[]{:S(2)}, u32[]{:S(2)}) collective-permute-start(bf16[64,1536]{1,0:T(8,128)(2,1)} %get-tuple-element.253.refs_0_), channel_id=1, source_target_pairs={{0,12},{1,13},{2,14},{3,15},{4,0},{5,1},{6,2},{7,3},{8,4},{9,5},{1... | collective-permute-start | bytes 589832 | tf_op jit(solution)/shard_map/ppermute | solution.py:66
  232.7 12.4 %collective-permute-start.53 = (bf16[64,1536]{1,0:T(8,128)(2,1)S(1)}, bf16[64,1536]{1,0:T(8,128)(2,1)S(1)}, u32[]{:S(2)}, u32[]{:S(2)}) collective-permute-start(bf16[64,1536]{1,0:T(8,128)(2,1)S(1)} %collective-permute-done.52.refs_2_), channel_id=1, source_target_pairs={{0,2},{1,3},{2,0},{3,1},{4,6},{5,7},{6,4},{7,5},{8,10},{9,11},{10,... | collective-permute-start | bytes 589832 | tf_op jit(solution)/shard_map/ppermute | solution.py:66
  233.6 12.1 %collective-permute-start.54 = (bf16[64,1536]{1,0:T(8,128)(2,1)S(1)}, bf16[64,1536]{1,0:T(8,128)(2,1)S(1)}, u32[]{:S(2)}, u32[]{:S(2)}) collective-permute-start(bf16[64,1536]{1,0:T(8,128)(2,1)S(1)} %collective-permute-done.50.refs_0_), channel_id=1, source_target_pairs={{0,1},{1,0},{2,3},{3,2},{4,5},{5,4},{6,7},{7,6},{8,9},{9,8},{10,11... | collective-permute-start | bytes 589832 | tf_op jit(solution)/shard_map/ppermute | solution.py:66
  233.6 12.1 %collective-permute-start.55 = (bf16[64,1536]{1,0:T(8,128)(2,1)S(1)}, bf16[64,1536]{1,0:T(8,128)(2,1)S(1)}, u32[]{:S(2)}, u32[]{:S(2)}) collective-permute-start(bf16[64,1536]{1,0:T(8,128)(2,1)S(1)} %collective-permute-done.51.refs_1_), channel_id=1, source_target_pairs={{0,1},{1,0},{2,3},{3,2},{4,5},{5,4},{6,7},{7,6},{8,9},{9,8},{10,11... | collective-permute-start | bytes 589832 | tf_op jit(solution)/shard_map/ppermute | solution.py:66
  258.4 57.3 %collective-permute-start.66 = (bf16[512,1536]{1,0:T(8,128)(2,1)}, bf16[512,1536]{1,0:T(8,128)(2,1)S(1)}, u32[]{:S(2)}, u32[]{:S(2)}) collective-permute-start(bf16[512,1536]{1,0:T(8,128)(2,1)} %get-tuple-element.295), channel_id=1, source_target_pairs={{0,16},{16,0},{1,17},{17,1},{2,18},{18,2},{3,19},{19,3},{4,20},{20... | collective-permute-start | bytes 4718600 | tf_op jit(solution)/shard_map/ppermute | solution.py:1261
  279.2 60.7 %collective-permute-start.71 = (bf16[1024,512]{1,0:T(8,128)(2,1)}, bf16[1024,512]{1,0:T(8,128)(2,1)S(1)}, u32[]{:S(2)}, u32[]{:S(2)}) collective-permute-start(bf16[1024,512]{1,0:T(8,128)(2,1)} %get-tuple-element.305), channel_id=1, source_target_pairs={{0,16},{16,0},{1,17},{17,1},{2,18},{18,2},{3,19},{19,3},{4,20},{20... | collective-permute-start | bytes 3145736 | tf_op jit(solution)/shard_map/ppermute | solution.py:1261
  282.7 14.2 %collective-permute-start.64 = (bf16[64,1536]{1,0:T(8,128)(2,1)S(1)}, bf16[64,1536]{1,0:T(8,128)(2,1)S(1)}, u32[]{:S(2)}, u32[]{:S(2)}) collective-permute-start(bf16[64,1536]{1,0:T(8,128)(2,1)S(1)} %copy-done.118), channel_id=1, source_target_pairs={{0,2},{1,3},{2,0},{3,1},{4,6},{5,7},{6,4},{7,5},{8,10},{9,11},{10,... | collective-permute-start | bytes 589832 | tf_op jit(solution)/shard_map/ppermute | solution.py:66
  288.5 12.5 %collective-permute-start.59 = (bf16[64,1536]{1,0:T(8,128)(2,1)S(1)}, bf16[64,1536]{1,0:T(8,128)(2,1)S(1)}, u32[]{:S(2)}, u32[]{:S(2)}) collective-permute-start(bf16[64,1536]{1,0:T(8,128)(2,1)S(1)} %copy-done.116), channel_id=1, source_target_pairs={{0,2},{1,3},{2,0},{3,1},{4,6},{5,7},{6,4},{7,5},{8,10},{9,11},{10,... | collective-permute-start | bytes 589832 | tf_op jit(solution)/shard_map/ppermute | solution.py:66
  296.9 33.6 %collective-permute-start.83 = (bf16[512,512]{1,0:T(8,128)(2,1)}, bf16[512,512]{1,0:T(8,128)(2,1)S(1)}, u32[]{:S(2)}, u32[]{:S(2)}) collective-permute-start(bf16[512,512]{1,0:T(8,128)(2,1)} %get-tuple-element.307), channel_id=1, source_target_pairs={{0,16},{16,0},{1,17},{17,1},{2,18},{18,2},{3,19},{19,3},{4,20},{20... | collective-permute-start | bytes 1572872 | tf_op jit(solution)/shard_map/ppermute | solution.py:1261
  301.2 14.4 %collective-permute-start.65 = (bf16[64,1536]{1,0:T(8,128)(2,1)}, bf16[64,1536]{1,0:T(8,128)(2,1)S(1)}, u32[]{:S(2)}, u32[]{:S(2)}) collective-permute-start(bf16[64,1536]{1,0:T(8,128)(2,1)} %shard_map.466), channel_id=1, source_target_pairs={{0,8},{1,9},{2,10},{3,11},{4,12},{5,13},{6,14},{7,15},{8,0},{9,1},... | collective-permute-start | bytes 589832 | tf_op jit(solution)/shard_map/ppermute | solution.py:66
  319.1 12.9 %collective-permute-start.70 = (bf16[64,1664]{1,0:T(8,128)(2,1)}, bf16[64,1664]{1,0:T(8,128)(2,1)S(1)}, u32[]{:S(2)}, u32[]{:S(2)}) collective-permute-start(bf16[64,1664]{1,0:T(8,128)(2,1)} %get-tuple-element.308.refs_0_), channel_id=1, source_target_pairs={{0,12},{1,13},{2,14},{3,15},{4,0},{5,1},{6,2},{7,3},{8,4},{9,5},{1... | collective-permute-start | bytes 638984 | tf_op jit(solution)/shard_map/ppermute | solution.py:66
  323.0 15.8 %collective-permute-start.73 = (bf16[64,1664]{1,0:T(8,128)(2,1)}, bf16[64,1664]{1,0:T(8,128)(2,1)S(1)}, u32[]{:S(2)}, u32[]{:S(2)}) collective-permute-start(bf16[64,1664]{1,0:T(8,128)(2,1)} %get-tuple-element.308.refs_0_), channel_id=1, source_target_pairs={{0,8},{1,9},{2,10},{3,11},{4,12},{5,13},{6,14},{7,15},{8,0},{9,1},... | collective-permute-start | bytes 638984 | tf_op jit(solution)/shard_map/ppermute | solution.py:66
  329.3 11.6 %collective-permute-start.67 = (bf16[64,1664]{1,0:T(8,128)(2,1)}, bf16[64,1664]{1,0:T(8,128)(2,1)S(1)}, u32[]{:S(2)}, u32[]{:S(2)}) collective-permute-start(bf16[64,1664]{1,0:T(8,128)(2,1)} %get-tuple-element.308.refs_0_), channel_id=1, source_target_pairs={{0,2},{1,3},{2,0},{3,1},{4,6},{5,7},{6,4},{7,5},{8,10},{9,11},{10,... | collective-permute-start | bytes 638984 | tf_op jit(solution)/shard_map/ppermute | solution.py:66
  339.9 20.6 %collective-permute-start.84 = (bf16[512,512]{1,0:T(8,128)(2,1)S(1)}, bf16[512,512]{1,0:T(8,128)(2,1)S(1)}, u32[]{:S(2)}, u32[]{:S(2)}) collective-permute-start(bf16[512,512]{1,0:T(8,128)(2,1)S(1)} %copy-done.27), channel_id=1, source_target_pairs={{0,16},{16,0},{1,17},{17,1},{2,18},{18,2},{3,19},{19,3},{4,20},{20... | collective-permute-start | bytes 1572872 | tf_op jit(solution)/shard_map/ppermute | solution.py:1261
  360.6 14.8 %collective-permute-start.85 = (f32[4,3,64,128]{3,2,1,0:T(8,128)}, f32[4,3,64,128]{3,2,1,0:T(8,128)S(1)}, u32[]{:S(2)}, u32[]{:S(2)}) collective-permute-start(f32[4,3,64,128]{3,2,1,0:T(8,128)} %bitcast.187), channel_id=1, source_target_pairs={{16,0},{17,1},{18,2},{19,3},{20,4},{21,5},{22,6},{23,7},{24,8},{25... | collective-permute-start | bytes 1179656 | tf_op jit(solution)/shard_map/ppermute | solution.py:136
  372.7 30.3 %collective-permute-start.88 = (bf16[192,1536]{1,0:T(8,128)(2,1)S(1)}, bf16[192,1536]{1,0:T(8,128)(2,1)S(1)}, u32[]{:S(2)}, u32[]{:S(2)}) collective-permute-start(bf16[192,1536]{1,0:T(8,128)(2,1)S(1)} %fusion), channel_id=1, source_target_pairs={{0,16},{16,0},{1,17},{17,1},{2,18},{18,2},{3,19},{19,3},{4,20},{20... | collective-permute-start | bytes 1769480 | tf_op jit(solution)/shard_map/ppermute | solution.py:1261
  375.3 27.7 %collective-permute-start.89 = (bf16[512,512]{1,0:T(8,128)(2,1)S(1)}, bf16[512,512]{1,0:T(8,128)(2,1)S(1)}, u32[]{:S(2)}, u32[]{:S(2)}) collective-permute-start(bf16[512,512]{1,0:T(8,128)(2,1)S(1)} %copy-done.24), channel_id=1, source_target_pairs={{0,16},{16,0},{1,17},{17,1},{2,18},{18,2},{3,19},{19,3},{4,20},{20... | collective-permute-start | bytes 1572872 | tf_op jit(solution)/shard_map/ppermute | solution.py:1261
  390.2 12.8 %collective-permute-start.86 = (f32[4,16,448]{2,1,0:T(8,128)S(1)}, f32[4,16,448]{2,1,0:T(8,128)S(1)}, u32[]{:S(2)}, u32[]{:S(2)}) collective-permute-start(f32[4,16,448]{2,1,0:T(8,128)S(1)} %pad_maximum_fusion.6), channel_id=1, source_target_pairs={{16,0},{17,1},{18,2},{19,3},{20,4},{21,5},{22,6},{23,7},{24,8},{25... | collective-permute-start | bytes 344072 | tf_op jit(solution)/shard_map/ppermute | solution.py:19
  424.4 24.1 %collective-permute-start.92 = (bf16[512,512]{1,0:T(8,128)(2,1)}, bf16[512,512]{1,0:T(8,128)(2,1)}, u32[]{:S(2)}, u32[]{:S(2)}) collective-permute-start(bf16[512,512]{1,0:T(8,128)(2,1)} %get-tuple-element.359), channel_id=1, source_target_pairs={{0,16},{16,0},{1,17},{17,1},{2,18},{18,2},{3,19},{19,3},{4,20},{20... | collective-permute-start | bytes 1572872 | tf_op jit(solution)/shard_map/ppermute | solution.py:1261
  440.4 21.4 %collective-permute-start.100 = (bf16[16,18528]{1,0:T(8,128)(2,1)}, bf16[16,18528]{1,0:T(8,128)(2,1)}, u32[]{:S(2)}, u32[]{:S(2)}) collective-permute-start(bf16[16,18528]{1,0:T(8,128)(2,1)} %dynamic-slice_bitcast_fusion), channel_id=1, source_target_pairs={{0,16},{16,0},{1,17},{17,1},{2,18},{18,2},{3,19},{19,3},{4,20},{20... | collective-permute-start | bytes 1778696 | tf_op jit(solution)/shard_map/ppermute | solution.py:122
  444.2 11.2 %collective-permute-start.96 = (bf16[64,1536]{1,0:T(8,128)(2,1)}, bf16[64,1536]{1,0:T(8,128)(2,1)}, u32[]{:S(2)}, u32[]{:S(2)}) collective-permute-start(bf16[64,1536]{1,0:T(8,128)(2,1)} %get-tuple-element.366), channel_id=1, source_target_pairs={{0,2},{1,3},{2,0},{3,1},{4,6},{5,7},{6,4},{7,5},{8,10},{9,11},{10,... | collective-permute-start | bytes 589832 | tf_op jit(solution)/shard_map/ppermute | solution.py:66
  445.1 14.3 %collective-permute-start.98 = (bf16[64,1536]{1,0:T(8,128)(2,1)}, bf16[64,1536]{1,0:T(8,128)(2,1)S(1)}, u32[]{:S(2)}, u32[]{:S(2)}) collective-permute-start(bf16[64,1536]{1,0:T(8,128)(2,1)} %get-tuple-element.367), channel_id=1, source_target_pairs={{0,2},{1,3},{2,0},{3,1},{4,6},{5,7},{6,4},{7,5},{8,10},{9,11},{10,... | collective-permute-start | bytes 589832 | tf_op jit(solution)/shard_map/ppermute | solution.py:66
  448.5 16.1 %collective-permute-start.93 = (bf16[64,1536]{1,0:T(8,128)(2,1)}, bf16[64,1536]{1,0:T(8,128)(2,1)S(1)}, u32[]{:S(2)}, u32[]{:S(2)}) collective-permute-start(bf16[64,1536]{1,0:T(8,128)(2,1)} %get-tuple-element.364), channel_id=1, source_target_pairs={{0,2},{1,3},{2,0},{3,1},{4,6},{5,7},{6,4},{7,5},{8,10},{9,11},{10,... | collective-permute-start | bytes 589832 | tf_op jit(solution)/shard_map/ppermute | solution.py:66
  451.2 38.5 %collective-permute-start.101 = (bf16[1536,384]{1,0:T(8,128)(2,1)S(1)}, bf16[1536,384]{1,0:T(8,128)(2,1)}, u32[]{:S(2)}, u32[]{:S(2)}) collective-permute-start(bf16[1536,384]{1,0:T(8,128)(2,1)S(1)} %copy-done.10), channel_id=1, source_target_pairs={{0,16},{16,0},{1,17},{17,1},{2,18},{18,2},{3,19},{19,3},{4,20},{20... | collective-permute-start | bytes 3538952 | tf_op jit(solution)/shard_map/ppermute | solution.py:1261
  461.8 11.5 %collective-permute-start.99 = (bf16[64,1536]{1,0:T(8,128)(2,1)}, bf16[64,1536]{1,0:T(8,128)(2,1)S(1)}, u32[]{:S(2)}, u32[]{:S(2)}) collective-permute-start(bf16[64,1536]{1,0:T(8,128)(2,1)} %shard_map.476), channel_id=1, source_target_pairs={{0,8},{1,9},{2,10},{3,11},{4,12},{5,13},{6,14},{7,15},{8,0},{9,1},... | collective-permute-start | bytes 589832 | tf_op jit(solution)/shard_map/ppermute | solution.py:66
  481.1 23.1 %all-to-all-start.1 = ((bf16[16,2,9304]{2,1,0:T(2,128)(2,1)}), bf16[16,2,9304]{2,1,0:T(2,128)(2,1)}, u32[]{:S(2)}, u32[]{:S(2)}) async-start(bf16[16,2,9304]{2,1,0:T(2,128)(2,1)} %reshape.499), calls=%async_computation.1 | async-start | bytes 1196032 | tf_op jit(solution)/shard_map/all_to_all | solution.py:147
  485.7 15.8 %collective-permute-start.102 = (bf16[32,1536]{1,0:T(8,128)(2,1)S(1)}, bf16[32,1536]{1,0:T(8,128)(2,1)}, u32[]{:S(2)}, u32[]{:S(2)}) collective-permute-start(bf16[32,1536]{1,0:T(8,128)(2,1)S(1)} %dynamic-slice_bitcast_fusion.2), channel_id=1, source_target_pairs={{0,16},{16,0},{1,17},{17,1},{2,18},{18,2},{3,19},{19,3},{4,20},{20... | collective-permute-start | bytes 294920 | tf_op jit(solution)/shard_map/ppermute | solution.py:1261
  (189 other events, 1355.5 us)

commit v5 on v4

--- a/solution.py
+++ b/solution.py
@@ -248,7 +248,7 @@
         out_shape=out_shape,
         compiler_params=pltpu.CompilerParams(vmem_limit_bytes=56 * 1024 * 1024),
         cost_estimate=pl.CostEstimate(
-            flops=int(micros * 9e+07), bytes_accessed=int(micros * 2.5e+05), transcendentals=0
+            flops=int(micros * 3e+08), bytes_accessed=int(micros * 8e+05), transcendentals=0
         ),
     )
 
@@ -1274,10 +1274,11 @@
     part_counts = [1, len(gate_parts)]
     ordered = paired and len(expert_parts) == 6
     expert_moved = [None] * len(expert_parts)
-    row_sums, _ = scatter_deep(after(kept, pair_down_grad), sent)
+    row_sums, row_moving = scatter_deep(after(kept, pair_down_grad), sent)
     mix_ties = ()
     if ordered:
-        expert_moved[:4] = [seq_moved(part) for part in expert_parts[:4]]
+        expert_moved[0] = seq_moved(expert_parts[0])
+        expert_moved[1:4] = [seq_moved(after(part, row_moving)) for part in expert_parts[1:4]]
         row_sums = after(row_sums, expert_moved[0])
         mix_ties = [(), (), expert_moved[1]]
     hidden_grad, mix_grad_send, ffn_gain_grad = hidden_rows_back(

time: 525 us -> 516 us (0.983)
  waiting for transfers between devices: 137 us -> 129 us
    ppermute x84, waiting for transfers between devices: 127 us -> 119 us  [mp_permute(): return lax.ppermute(value, 'mp', [(i, target(i)) for i in range(count)])]
  transfers between devices with their start and end apart: 105 -> 105, of which waited for: 46 -> 43; matrix products, arithmetic and copies ran while one was open for 12% -> 12% of each run, Pallas kernels for 24% -> 26%
where the time goes in v5:
time: 516 us; the launch traced here: 507 us
  Pallas kernels  169 us (33%)
  waiting for transfers between devices  129 us (25%)
  starting transfers between devices  96.8 us (19%)
  local copies, waits for them, and re-layouts  86.9 us (17%)
  other arithmetic  21.2 us (4%)
    ppermute x84, waiting for transfers between devices, mp_permute(): return lax.ppermute(value, 'mp', [(i, target(i)) for i in range(count)])  119 us
    ppermute x84, starting transfers between devices, mp_permute(): return lax.ppermute(value, 'mp', [(i, target(i)) for i in range(count)])  63.2 us
    unnamed x278, local copies, waits for them, and re-layouts  36.7 us
    pallas_call x12, Pallas kernels, add_blocks(): call(kernel, (1,), [whole(left.shape)] * 2, whole(left.shape), bf16(*left...  21.3 us
    pallas_call x2, Pallas kernels, experts_backward(): call(kernel, (1,), [whole(block.shape) for block in blocks] + [whole(valu...  21 us
    pallas_call x2, Pallas kernels, experts_forward(): call(kernel, (1,), [whole(block.shape) for block in blocks] + [whole(w.sh...  16.2 us
    pallas_call x6, Pallas kernels, add_pairs(): call(kernel, (1,), [whole(left.shape)] * 2, [whole((rows, width))] * (2 *...  16 us
    pallas_call x1, Pallas kernels, mixer_input_back(): call(kernel, (count,), [each((length, inner)), each((length, double)), ea...  13.1 us
  transfers between devices with their start and end apart: 105, of which 43 were waited for; matrix products, arithmetic and copies ran while one was open for 12% of the time, Pallas kernels for 26%

profile of v5, /device:TPU:0, one launch (start us, length us, event | category | flops | bytes accessed | tf_op | source)
XLA Modules:
  0.0 506.8 jit_solution(16746896676751473526)
XLA Ops:
  5.0 4.8 collective-permute-start
  21.4 3.1 collective-permute-done.2
  27.1 3.8 collective-permute-done.5
  41.5 11.0 %shard_map.443 = (bf16[4,256,1536]{2,1,0:T(8,128)(2,1)}, f32[4,256,192]{2,1,0:T(8,128)}, f32[4,272,192]{2,1,0:T(8,128)}, f32[4,272,256]{2,1,0:T(8,128)}, f32[4,2...) custom-call(bf16[4,256,1536]{2,1,0:T(8,128)(2,1)} %bitcast.129, ...), custom_call_target="tpu_custom_call" | custom-call | flops 3300000000 | bytes 8800000 | tf_op jit(solution)/shard_map/pallas_call | solution.py:300
  52.5 3.5 collective-permute-start.7
  56.6 5.9 %shard_map.444.within_ref = f32[4,256,192]{2,1,0:T(8,128)} custom-call(f32[4,256,192]{2,1,0:T(8,128)} %get-tuple-element.213.pv_ref, f32[4,256,256]{2,1,0:T(8,128)} %get-tuple-element.214.ps_ref.refs_18_, f32[4,256,128]{2,1,0:T(8,128)} %get-tuple-element.215.step_ref, f32[4,256,128]{2,1,0:T(8,128)} %get-tuple-element.216.decay_ref.refs_19_, ...), custom_call_target="tpu_custom_call" | custom-call | flops 1800000000 | bytes 4800000 | tf_op jit(solution)/shard_map/pallas_call | solution.py:351
  65.5 7.5 %shard_map.445 = (f32[4,256,192]{2,1,0:T(8,128)}, bf16[4,256,192]{2,1,0:T(8,128)(2,1)}, bf16[4,2,64,1664]{3,2,1,0:T(8,128)(2,1)}, bf16[4,2,64,1664]{3,2,1,0:T(8,128)(2,1)}) custom-call(s32[16]{0:T(128)} %add.230.order_ref, f32[4,256,192]{2,1,0:T(8,128)} %shard_map.444.within_ref, f32[4,256,256]{2,1,0:T(8,128)} %get-tuple-element.214.ps_ref.refs_18_, ...), custom_call_target="tpu_custom_call" | custom-call | flops 2100000000 | bytes 5600000 | tf_op jit(solution)/shard_map/pallas_call | solution.py:391
  79.9 3.7 shard_map.446
  93.7 3.5 all-to-all-start
  97.2 3.2 collective-permute-done.10.right_ref
  103.6 2.9 collective-permute-done.12.right_ref
  115.1 4.2 collective-permute-done.13.refs_3_
  119.3 6.7 %collective-permute-done.15.refs_4_ = bf16[64,1664]{1,0:T(8,128)(2,1)S(1)} collective-permute-done((bf16[64,1664]{1,0:T(8,128)(2,1)}, bf16[64,1664]{1,0:T(8,128)(2,1)S(1)}, u32[]{:S(2)}, u32[]{:S(2)}) %collective-permute-start.15) | collective-permute-done | bytes 213024 | tf_op jit(solution)/shard_map/ppermute | solution.py:66
  131.7 4.3 collective-permute-start.29
  136.0 2.7 collective-permute-done.17.refs_2_
  145.4 5.4 %collective-permute-done.31.refs_2_ = bf16[64,1536]{1,0:T(8,128)(2,1)S(1)} collective-permute-done((bf16[64,1536]{1,0:T(8,128)(2,1)}, bf16[64,1536]{1,0:T(8,128)(2,1)S(1)}, u32[]{:S(2)}, u32[]{:S(2)}) %collective-permute-start.31) | collective-permute-done | bytes 196640 | tf_op jit(solution)/shard_map/ppermute | solution.py:66
  153.4 8.1 %shard_map.451 = (bf16[512,1536]{1,0:T(8,128)(2,1)}, f32[512,512]{1,0:T(8,128)}, f32[512,512]{1,0:T(8,128)}, f32[512,128]{1,0:T(8,128)}, bf16[512,512]{1,0:T(8,1...) custom-call(bf16[64,1536]{1,0:T(8,128)(2,1)} %get-tuple-element.235.refs_0_, ...), custom_call_target="tpu_custom_call" | custom-call | flops 2400000000 | bytes 6400000 | tf_op jit(solution)/shard_map/pallas_call | solution.py:895
  164.8 8.1 %shard_map.454 = (bf16[512,1536]{1,0:T(8,128)(2,1)}, f32[512,512]{1,0:T(8,128)}, f32[512,512]{1,0:T(8,128)}, f32[512,128]{1,0:T(8,128)}, bf16[512,512]{1,0:T(8,1...) custom-call(bf16[64,1536]{1,0:T(8,128)(2,1)} %copy-done.83, ...), custom_call_target="tpu_custom_call" | custom-call | flops 2400000000 | bytes 6400000 | tf_op jit(solution)/shard_map/pallas_call | solution.py:895
  196.3 4.2 collective-permute-done.39.refs_3_
  200.5 6.5 %collective-permute-done.41.refs_4_ = bf16[64,1536]{1,0:T(8,128)(2,1)S(1)} collective-permute-done((bf16[64,1536]{1,0:T(8,128)(2,1)}, bf16[64,1536]{1,0:T(8,128)(2,1)S(1)}, u32[]{:S(2)}, u32[]{:S(2)}) %collective-permute-start.41) | collective-permute-done | bytes 196640 | tf_op jit(solution)/shard_map/ppermute | solution.py:66
  211.3 4.0 collective-permute-start.50
  215.3 4.9 collective-permute-done.43.refs_2_
  223.5 3.9 collective-permute-done.44.refs_3_
  227.4 3.7 collective-permute-done.52.refs_2_
  233.1 10.2 %shard_map.459 = (bf16[512,1536]{1,0:T(8,128)(2,1)}, bf16[512,512]{1,0:T(8,128)(2,1)}, bf16[512,512]{1,0:T(8,128)(2,1)}, bf16[512,128]{1,0:T(8,128)(2,1)}, bf16[...) custom-call(bf16[64,1536]{1,0:T(8,128)(2,1)} %get-tuple-element.256.refs_0_, ...), custom_call_target="tpu_custom_call" | custom-call | flops 3000000000 | bytes 8000000 | tf_op jit(solution)/shard_map/pallas_call | solution.py:946
  245.9 10.8 %shard_map.461 = (bf16[512,1536]{1,0:T(8,128)(2,1)}, bf16[512,512]{1,0:T(8,128)(2,1)}, bf16[512,512]{1,0:T(8,128)(2,1)}, bf16[512,128]{1,0:T(8,128)(2,1)}, bf16[...) custom-call(bf16[64,1536]{1,0:T(8,128)(2,1)} %copy-done.34, ...), custom_call_target="tpu_custom_call" | custom-call | flops 3000000000 | bytes 8000000 | tf_op jit(solution)/shard_map/pallas_call | solution.py:946
  267.0 10.3 %shard_map.463 = (bf16[1024,512]{1,0:T(8,128)(2,1)}, bf16[512,512]{1,0:T(8,128)(2,1)}, bf16[512,512]{1,0:T(8,128)(2,1)}, bf16[512,512]{1,0:T(8,128)(2,1)}, bf16[...) custom-call(bf16[512,1536]{1,0:T(8,128)(2,1)} %get-tuple-element.281.refs_0_, ...), custom_call_target="tpu_custom_call" | custom-call | flops 3300000000 | bytes 8800000 | tf_op jit(solution)/shard_map/pallas_call | solution.py:1006
  291.7 4.3 collective-permute-done.61.refs_2_
  298.0 6.5 %collective-permute-done.65.refs_4_ = bf16[64,1536]{1,0:T(8,128)(2,1)S(1)} collective-permute-done((bf16[64,1536]{1,0:T(8,128)(2,1)}, bf16[64,1536]{1,0:T(8,128)(2,1)S(1)}, u32[]{:S(2)}, u32[]{:S(2)}) %collective-permute-start.65) | collective-permute-done | bytes 196640 | tf_op jit(solution)/shard_map/ppermute | solution.py:66
  305.1 2.8 shard_map.467
  309.4 3.4 collective-permute-start.70
  312.8 5.3 %collective-permute-done.68.refs_2_ = bf16[64,1664]{1,0:T(8,128)(2,1)S(1)} collective-permute-done((bf16[64,1664]{1,0:T(8,128)(2,1)}, bf16[64,1664]{1,0:T(8,128)(2,1)S(1)}, u32[]{:S(2)}, u32[]{:S(2)}) %collective-permute-start.68) | collective-permute-done | bytes 213024 | tf_op jit(solution)/shard_map/ppermute | solution.py:66
  318.1 2.9 collective-permute-start.73
  322.2 8.6 %collective-permute-done.73.refs_6_ = bf16[64,1664]{1,0:T(8,128)(2,1)S(1)} collective-permute-done((bf16[64,1664]{1,0:T(8,128)(2,1)}, bf16[64,1664]{1,0:T(8,128)(2,1)S(1)}, u32[]{:S(2)}, u32[]{:S(2)}) %collective-permute-start.73) | collective-permute-done | bytes 213024 | tf_op jit(solution)/shard_map/ppermute | solution.py:66
  333.5 5.5 %collective-permute-done.74.refs_7_ = bf16[64,1664]{1,0:T(8,128)(2,1)S(1)} collective-permute-done((bf16[64,1664]{1,0:T(8,128)(2,1)S(1)}, bf16[64,1664]{1,0:T(8,128)(2,1)S(1)}, u32[]{:S(2)}, u32[]{:S(2)}) %collective-permute-start.74) | collective-permute-done | bytes 213024 | tf_op jit(solution)/shard_map/ppermute | solution.py:66
  344.6 7.9 %shard_map.468 = (bf16[4,256,1536]{2,1,0:T(8,128)(2,1)}, f32[4,256,192]{2,1,0:T(8,128)}, bf16[4,256,192]{2,1,0:T(8,128)(2,1)}, f32[4,192,128]{2,1,0:T(8,128)}, f32[8,192]{1,0:T(8,128)}) custom-call(s32[16]{0:T(128)} %add.230.order_ref, bf16[64,1664]{1,0:T(8,128)(2,1)} %get-tuple-element.313.refs_0_, bf16[64,1664]{1,0:T(8,128)(2,1)} %copy-done.62, ...), custom_call_target="tpu_custom_call" | custom-call | flops 2400000000 | bytes 6400000 | tf_op jit(solution)/shard_map/pallas_call | solution.py:440
  354.2 8.9 %shard_map.469 = (f32[4,256,192]{2,1,0:T(8,128)}, f32[4,256,256]{2,1,0:T(8,128)}) custom-call(f32[4,256,192]{2,1,0:T(8,128)} %get-tuple-element.213.pv_ref, f32[4,256,256]{2,1,0:T(8,128)} %get-tuple-element.214.ps_ref.refs_18_, f32[4,256,128]{2,1,0:T(8,128)} %get-tuple-element.215.step_ref, f32[4,256,128]{2,1,0:T(8,128)} %get-tuple-element.216.decay_ref.refs_19_, ...), custom_call_target="tpu_custom_call" | custom-call | flops 2700000000 | bytes 7200000 | tf_op jit(solution)/shard_map/pallas_call | solution.py:485
  364.7 2.7 collective-permute-start.88
  368.1 13.1 %shard_map.470 = (f32[4,256,192]{2,1,0:T(8,128)}, f32[4,256,256]{2,1,0:T(8,128)}, f32[4,16,192]{2,1,0:T(8,128)}, f32[4,16,256]{2,1,0:T(8,128)}, bf16[4,256,128]{...) custom-call(f32[4,256,192]{2,1,0:T(8,128)} %get-tuple-element.213.pv_ref, ...), custom_call_target="tpu_custom_call" | custom-call | flops 3900000000 | bytes 10400000 | tf_op jit(solution)/shard_map/pallas_call | solution.py:584
  387.9 2.7 collective-permute-start.87
  390.6 4.4 collective-permute-done.87
  396.5 10.3 %shard_map.471 = (bf16[4,256,192]{2,1,0:T(8,128)(2,1)}, bf16[4,256,256]{2,1,0:T(8,128)(2,1)}, f32[8,1536]{1,0:T(8,128)}, bf16[4,2,64,1536]{3,2,1,0:T(8,128)(2,1)}, bf16[4,2,64,1536]{3,2,1,0:T(8,128)(2,1)}) custom-call(s32[16]{0:T(128)} %add.230.order_ref, f32[4,256,192]{2,1,0:T(8,128)} %get-tuple-element.340.value_ref, ...), custom_call_target="tpu_custom_call" | custom-call | flops 3000000000 | bytes 8000000 | tf_op jit(solution)/shard_map/pallas_call | solution.py:650
  413.7 2.8 collective-permute-done.90
  416.5 3.1 shard_map.472
  419.6 8.7 %shard_map.473 = (bf16[1536,384]{1,0:T(8,128)(2,1)}, bf16[1536,256]{1,0:T(8,128)(2,1)}) custom-call(bf16[4,256,1536]{2,1,0:T(8,128)(2,1)} %get-tuple-element.374.normed_ref, bf16[4,256,192]{2,1,0:T(8,128)(2,1)} %get-tuple-element.353.gate_grad_ref.gate_ref, bf16[4,256,192]{2,1,0:T(8,128)(2,1)} %get-tuple-element.364.value_ref, ...), custom_call_target="tpu_custom_call" | custom-call | flops 2400000000 | bytes 6400000 | tf_op jit(solution)/shard_map/pallas_call | solution.py:1043
  455.5 3.6 collective-permute-done.97.refs_3_
  459.1 6.0 %collective-permute-done.99.refs_4_ = bf16[64,1536]{1,0:T(8,128)(2,1)S(1)} collective-permute-done((bf16[64,1536]{1,0:T(8,128)(2,1)}, bf16[64,1536]{1,0:T(8,128)(2,1)S(1)}, u32[]{:S(2)}, u32[]{:S(2)}) %collective-permute-start.99) | collective-permute-done | bytes 196640 | tf_op jit(solution)/shard_map/ppermute | solution.py:66
  472.9 4.6 all-to-all-start.1
  (634 shorter events, 235.1 us)
Async XLA Ops:
  5.0 27.1 %collective-permute-start = (bf16[4,3,1536]{2,1,0:T(4,128)(2,1)S(1)}, bf16[4,3,1536]{2,1,0:T(4,128)(2,1)S(1)}, u32[]{:S(2)}, u32[]{:S(2)}) collective-permute-start(bf16[4,3,1536]{2,1,0:T(4,128)(2,1)S(1)} %slice_bitcast_fusion), channel_id=1, source_target_pairs={{0,16},{1,17},{2,18},{3,19},{4,20},{5,21},{6,22},{7,23},{8,24},{9,... | collective-permute-start | bytes 110600 | tf_op jit(solution)/shard_map/ppermute | solution.py:19
  52.5 12.2 %collective-permute-start.7 = (f32[4,3,64,128]{3,2,1,0:T(8,128)}, f32[4,3,64,128]{3,2,1,0:T(8,128)S(1)}, u32[]{:S(2)}, u32[]{:S(2)}) collective-permute-start(f32[4,3,64,128]{3,2,1,0:T(8,128)} %bitcast.185), channel_id=1, source_target_pairs={{0,16},{1,17},{2,18},{3,19},{4,20},{5,21},{6,22},{7,23},{8,24},{9,... | collective-permute-start | bytes 1179656 | tf_op jit(solution)/shard_map/ppermute | solution.py:136
  83.6 13.6 %collective-permute-start.24 = (bf16[32,1536]{1,0:T(8,128)(2,1)S(1)}, bf16[32,1536]{1,0:T(8,128)(2,1)S(1)}, u32[]{:S(2)}, u32[]{:S(2)}) collective-permute-start(bf16[32,1536]{1,0:T(8,128)(2,1)S(1)} %copy-done.42), channel_id=1, source_target_pairs={{0,16},{16,0},{1,17},{17,1},{2,18},{18,2},{3,19},{19,3},{4,20},{20... | collective-permute-start | bytes 294920 | tf_op jit(solution)/shard_map/ppermute | solution.py:113
  87.6 27.5 %collective-permute-start.9 = (bf16[64,1664]{1,0:T(8,128)(2,1)}, bf16[64,1664]{1,0:T(8,128)(2,1)S(1)}, u32[]{:S(2)}, u32[]{:S(2)}) collective-permute-start(bf16[64,1664]{1,0:T(8,128)(2,1)} %get-tuple-element.222), channel_id=1, source_target_pairs={{0,2},{1,3},{2,0},{3,1},{4,6},{5,7},{6,4},{7,5},{8,10},{9,11},{10,... | collective-permute-start | bytes 638984 | tf_op jit(solution)/shard_map/ppermute | solution.py:66
  89.1 11.3 %collective-permute-start.10 = (bf16[64,1664]{1,0:T(8,128)(2,1)}, bf16[64,1664]{1,0:T(8,128)(2,1)S(1)}, u32[]{:S(2)}, u32[]{:S(2)}) collective-permute-start(bf16[64,1664]{1,0:T(8,128)(2,1)} %get-tuple-element.224), channel_id=1, source_target_pairs={{0,2},{1,3},{2,0},{3,1},{4,6},{5,7},{6,4},{7,5},{8,10},{9,11},{10,... | collective-permute-start | bytes 638984 | tf_op jit(solution)/shard_map/ppermute | solution.py:66
  89.6 17.0 %collective-permute-start.12 = (bf16[64,1664]{1,0:T(8,128)(2,1)}, bf16[64,1664]{1,0:T(8,128)(2,1)S(1)}, u32[]{:S(2)}, u32[]{:S(2)}) collective-permute-start(bf16[64,1664]{1,0:T(8,128)(2,1)} %get-tuple-element.226), channel_id=1, source_target_pairs={{0,2},{1,3},{2,0},{3,1},{4,6},{5,7},{6,4},{7,5},{8,10},{9,11},{10,... | collective-permute-start | bytes 638984 | tf_op jit(solution)/shard_map/ppermute | solution.py:66
  91.1 19.6 %collective-permute-start.14 = (bf16[64,1664]{1,0:T(8,128)(2,1)}, bf16[64,1664]{1,0:T(8,128)(2,1)S(1)}, u32[]{:S(2)}, u32[]{:S(2)}) collective-permute-start(bf16[64,1664]{1,0:T(8,128)(2,1)} %get-tuple-element.228), channel_id=1, source_target_pairs={{0,2},{1,3},{2,0},{3,1},{4,6},{5,7},{6,4},{7,5},{8,10},{9,11},{10,... | collective-permute-start | bytes 638984 | tf_op jit(solution)/shard_map/ppermute | solution.py:66
  93.7 20.8 %all-to-all-start = ((bf16[16,2,3072]{2,1,0:T(2,128)(2,1)}), bf16[16,2,3072]{2,1,0:T(2,128)(2,1)S(1)}, u32[]{:S(2)}, u32[]{:S(2)}) async-start(bf16[16,2,3072]{2,1,0:T(2,128)(2,1)} %reshape.497), calls=%async_computation | async-start | bytes 393216 | tf_op jit(solution)/shard_map/all_to_all | solution.py:147
  103.0 12.1 %collective-permute-start.11 = (bf16[64,1664]{1,0:T(8,128)(2,1)}, bf16[64,1664]{1,0:T(8,128)(2,1)S(1)}, u32[]{:S(2)}, u32[]{:S(2)}) collective-permute-start(bf16[64,1664]{1,0:T(8,128)(2,1)} %shard_map.447), channel_id=1, source_target_pairs={{0,12},{1,13},{2,14},{3,15},{4,0},{5,1},{6,2},{7,3},{8,4},{9,5},{1... | collective-permute-start | bytes 638984 | tf_op jit(solution)/shard_map/ppermute | solution.py:66
  113.3 12.8 %collective-permute-start.15 = (bf16[64,1664]{1,0:T(8,128)(2,1)}, bf16[64,1664]{1,0:T(8,128)(2,1)S(1)}, u32[]{:S(2)}, u32[]{:S(2)}) collective-permute-start(bf16[64,1664]{1,0:T(8,128)(2,1)} %shard_map.449), channel_id=1, source_target_pairs={{0,8},{1,9},{2,10},{3,11},{4,12},{5,13},{6,14},{7,15},{8,0},{9,1},... | collective-permute-start | bytes 638984 | tf_op jit(solution)/shard_map/ppermute | solution.py:66
  114.7 21.3 %collective-permute-start.23 = (bf16[16,6144]{1,0:T(8,128)(2,1)S(1)}, bf16[16,6144]{1,0:T(8,128)(2,1)S(1)}, u32[]{:S(2)}, u32[]{:S(2)}) collective-permute-start(bf16[16,6144]{1,0:T(8,128)(2,1)S(1)} %bitcast.162), channel_id=1, source_target_pairs={{0,16},{16,0},{1,17},{17,1},{2,18},{18,2},{3,19},{19,3},{4,20},{20... | collective-permute-start | bytes 589832 | tf_op jit(solution)/shard_map/ppermute | solution.py:113
  136.0 14.7 %collective-permute-start.31 = (bf16[64,1536]{1,0:T(8,128)(2,1)}, bf16[64,1536]{1,0:T(8,128)(2,1)S(1)}, u32[]{:S(2)}, u32[]{:S(2)}) collective-permute-start(bf16[64,1536]{1,0:T(8,128)(2,1)} %get-tuple-element.235.refs_0_), channel_id=1, source_target_pairs={{0,8},{1,9},{2,10},{3,11},{4,12},{5,13},{6,14},{7,15},{8,0},{9,1},... | collective-permute-start | bytes 589832 | tf_op jit(solution)/shard_map/ppermute | solution.py:66
  140.8 11.8 %collective-permute-start.21 = (bf16[64,1536]{1,0:T(8,128)(2,1)S(1)}, bf16[64,1536]{1,0:T(8,128)(2,1)S(1)}, u32[]{:S(2)}, u32[]{:S(2)}) collective-permute-start(bf16[64,1536]{1,0:T(8,128)(2,1)S(1)} %collective-permute-done.17.refs_2_), channel_id=1, source_target_pairs={{0,1},{1,0},{2,3},{3,2},{4,5},{5,4},{6,7},{7,6},{8,9},{9,8},{10,11... | collective-permute-start | bytes 589832 | tf_op jit(solution)/shard_map/ppermute | solution.py:66
  150.8 12.6 %collective-permute-start.33 = (bf16[64,1536]{1,0:T(8,128)(2,1)S(1)}, bf16[64,1536]{1,0:T(8,128)(2,1)S(1)}, u32[]{:S(2)}, u32[]{:S(2)}) collective-permute-start(bf16[64,1536]{1,0:T(8,128)(2,1)S(1)} %collective-permute-done.29.refs_0_), channel_id=1, source_target_pairs={{0,1},{1,0},{2,3},{3,2},{4,5},{5,4},{6,7},{7,6},{8,9},{9,8},{10,11... | collective-permute-start | bytes 589832 | tf_op jit(solution)/shard_map/ppermute | solution.py:66
  152.4 10.9 %collective-permute-start.34 = (bf16[64,1536]{1,0:T(8,128)(2,1)S(1)}, bf16[64,1536]{1,0:T(8,128)(2,1)S(1)}, u32[]{:S(2)}, u32[]{:S(2)}) collective-permute-start(bf16[64,1536]{1,0:T(8,128)(2,1)S(1)} %collective-permute-done.30.refs_1_), channel_id=1, source_target_pairs={{0,1},{1,0},{2,3},{3,2},{4,5},{5,4},{6,7},{7,6},{8,9},{9,8},{10,11... | collective-permute-start | bytes 589832 | tf_op jit(solution)/shard_map/ppermute | solution.py:66
  182.7 13.6 %collective-permute-start.26 = (bf16[64,1536]{1,0:T(8,128)(2,1)S(1)}, bf16[64,1536]{1,0:T(8,128)(2,1)S(1)}, u32[]{:S(2)}, u32[]{:S(2)}) collective-permute-start(bf16[64,1536]{1,0:T(8,128)(2,1)S(1)} %copy-done.95), channel_id=1, source_target_pairs={{0,2},{1,3},{2,0},{3,1},{4,6},{5,7},{6,4},{7,5},{8,10},{9,11},{10,... | collective-permute-start | bytes 589832 | tf_op jit(solution)/shard_map/ppermute | solution.py:66
  195.0 12.0 %collective-permute-start.41 = (bf16[64,1536]{1,0:T(8,128)(2,1)}, bf16[64,1536]{1,0:T(8,128)(2,1)S(1)}, u32[]{:S(2)}, u32[]{:S(2)}) collective-permute-start(bf16[64,1536]{1,0:T(8,128)(2,1)} %shard_map.457), channel_id=1, source_target_pairs={{0,8},{1,9},{2,10},{3,11},{4,12},{5,13},{6,14},{7,15},{8,0},{9,1},... | collective-permute-start | bytes 589832 | tf_op jit(solution)/shard_map/ppermute | solution.py:66
  211.3 11.1 %collective-permute-start.50 = (bf16[64,1536]{1,0:T(8,128)(2,1)}, bf16[64,1536]{1,0:T(8,128)(2,1)S(1)}, u32[]{:S(2)}, u32[]{:S(2)}) collective-permute-start(bf16[64,1536]{1,0:T(8,128)(2,1)} %get-tuple-element.256.refs_0_), channel_id=1, source_target_pairs={{0,12},{1,13},{2,14},{3,15},{4,0},{5,1},{6,2},{7,3},{8,4},{9,5},{1... | collective-permute-start | bytes 589832 | tf_op jit(solution)/shard_map/ppermute | solution.py:66
  231.1 13.2 %collective-permute-start.54 = (bf16[64,1536]{1,0:T(8,128)(2,1)S(1)}, bf16[64,1536]{1,0:T(8,128)(2,1)S(1)}, u32[]{:S(2)}, u32[]{:S(2)}) collective-permute-start(bf16[64,1536]{1,0:T(8,128)(2,1)S(1)} %collective-permute-done.50.refs_0_), channel_id=1, source_target_pairs={{0,1},{1,0},{2,3},{3,2},{4,5},{5,4},{6,7},{7,6},{8,9},{9,8},{10,11... | collective-permute-start | bytes 589832 | tf_op jit(solution)/shard_map/ppermute | solution.py:66
  231.1 12.2 %collective-permute-start.53 = (bf16[64,1536]{1,0:T(8,128)(2,1)S(1)}, bf16[64,1536]{1,0:T(8,128)(2,1)S(1)}, u32[]{:S(2)}, u32[]{:S(2)}) collective-permute-start(bf16[64,1536]{1,0:T(8,128)(2,1)S(1)} %collective-permute-done.52.refs_2_), channel_id=1, source_target_pairs={{0,2},{1,3},{2,0},{3,1},{4,6},{5,7},{6,4},{7,5},{8,10},{9,11},{10,... | collective-permute-start | bytes 589832 | tf_op jit(solution)/shard_map/ppermute | solution.py:66
  232.2 12.1 %collective-permute-start.55 = (bf16[64,1536]{1,0:T(8,128)(2,1)S(1)}, bf16[64,1536]{1,0:T(8,128)(2,1)S(1)}, u32[]{:S(2)}, u32[]{:S(2)}) collective-permute-start(bf16[64,1536]{1,0:T(8,128)(2,1)S(1)} %collective-permute-done.51.refs_1_), channel_id=1, source_target_pairs={{0,1},{1,0},{2,3},{3,2},{4,5},{5,4},{6,7},{7,6},{8,9},{9,8},{10,11... | collective-permute-start | bytes 589832 | tf_op jit(solution)/shard_map/ppermute | solution.py:66
  243.9 13.5 %collective-permute-start.49 = (bf16[2,2,64,1536]{3,2,1,0:T(8,128)(2,1)}, bf16[2,2,64,1536]{3,2,1,0:T(8,128)(2,1)S(1)}, u32[]{:S(2)}, u32[]{:S(2)}) collective-permute-start(bf16[2,2,64,1536]{3,2,1,0:T(8,128)(2,1)} %get-tuple-element.262), channel_id=1, source_target_pairs={{0,1},{1,0},{2,3},{3,2},{4,5},{5,4},{6,7},{7,6},{8,9},{9,8},{10,11... | collective-permute-start | bytes 2359304 | tf_op jit(solution)/shard_map/ppermute | solution.py:66
  256.9 47.5 %collective-permute-start.66 = (bf16[512,1536]{1,0:T(8,128)(2,1)}, bf16[512,1536]{1,0:T(8,128)(2,1)S(1)}, u32[]{:S(2)}, u32[]{:S(2)}) collective-permute-start(bf16[512,1536]{1,0:T(8,128)(2,1)} %get-tuple-element.298), channel_id=1, source_target_pairs={{0,16},{16,0},{1,17},{17,1},{2,18},{18,2},{3,19},{19,3},{4,20},{20... | collective-permute-start | bytes 4718600 | tf_op jit(solution)/shard_map/ppermute | solution.py:1261
  260.6 16.8 %collective-permute-start.60 = (bf16[64,1536]{1,0:T(8,128)(2,1)}, bf16[64,1536]{1,0:T(8,128)(2,1)S(1)}, u32[]{:S(2)}, u32[]{:S(2)}) collective-permute-start(bf16[64,1536]{1,0:T(8,128)(2,1)} %get-tuple-element.278), channel_id=1, source_target_pairs={{0,2},{1,3},{2,0},{3,1},{4,6},{5,7},{6,4},{7,5},{8,10},{9,11},{10,... | collective-permute-start | bytes 589832 | tf_op jit(solution)/shard_map/ppermute | solution.py:66
  265.0 14.8 %collective-permute-start.62 = (bf16[64,1536]{1,0:T(8,128)(2,1)}, bf16[64,1536]{1,0:T(8,128)(2,1)S(1)}, u32[]{:S(2)}, u32[]{:S(2)}) collective-permute-start(bf16[64,1536]{1,0:T(8,128)(2,1)} %get-tuple-element.279), channel_id=1, source_target_pairs={{0,2},{1,3},{2,0},{3,1},{4,6},{5,7},{6,4},{7,5},{8,10},{9,11},{10,... | collective-permute-start | bytes 589832 | tf_op jit(solution)/shard_map/ppermute | solution.py:66
  265.8 16.5 %collective-permute-start.64 = (bf16[64,1536]{1,0:T(8,128)(2,1)}, bf16[64,1536]{1,0:T(8,128)(2,1)S(1)}, u32[]{:S(2)}, u32[]{:S(2)}) collective-permute-start(bf16[64,1536]{1,0:T(8,128)(2,1)} %get-tuple-element.280), channel_id=1, source_target_pairs={{0,2},{1,3},{2,0},{3,1},{4,6},{5,7},{6,4},{7,5},{8,10},{9,11},{10,... | collective-permute-start | bytes 589832 | tf_op jit(solution)/shard_map/ppermute | solution.py:66
  284.7 47.2 %collective-permute-start.71 = (bf16[1024,512]{1,0:T(8,128)(2,1)S(1)}, bf16[1024,512]{1,0:T(8,128)(2,1)S(1)}, u32[]{:S(2)}, u32[]{:S(2)}) collective-permute-start(bf16[1024,512]{1,0:T(8,128)(2,1)S(1)} %copy-done.10), channel_id=1, source_target_pairs={{0,16},{16,0},{1,17},{17,1},{2,18},{18,2},{3,19},{19,3},{4,20},{20... | collective-permute-start | bytes 3145736 | tf_op jit(solution)/shard_map/ppermute | solution.py:1261
  291.7 12.7 %collective-permute-start.65 = (bf16[64,1536]{1,0:T(8,128)(2,1)}, bf16[64,1536]{1,0:T(8,128)(2,1)S(1)}, u32[]{:S(2)}, u32[]{:S(2)}) collective-permute-start(bf16[64,1536]{1,0:T(8,128)(2,1)} %shard_map.466), channel_id=1, source_target_pairs={{0,8},{1,9},{2,10},{3,11},{4,12},{5,13},{6,14},{7,15},{8,0},{9,1},... | collective-permute-start | bytes 589832 | tf_op jit(solution)/shard_map/ppermute | solution.py:66
  296.0 35.9 %collective-permute-start.83 = (bf16[512,512]{1,0:T(8,128)(2,1)S(1)}, bf16[512,512]{1,0:T(8,128)(2,1)S(1)}, u32[]{:S(2)}, u32[]{:S(2)}) collective-permute-start(bf16[512,512]{1,0:T(8,128)(2,1)S(1)} %copy-done.21), channel_id=1, source_target_pairs={{0,16},{16,0},{1,17},{17,1},{2,18},{18,2},{3,19},{19,3},{4,20},{20... | collective-permute-start | bytes 1572872 | tf_op jit(solution)/shard_map/ppermute | solution.py:1261
  308.4 12.7 %collective-permute-start.67 = (bf16[64,1664]{1,0:T(8,128)(2,1)}, bf16[64,1664]{1,0:T(8,128)(2,1)S(1)}, u32[]{:S(2)}, u32[]{:S(2)}) collective-permute-start(bf16[64,1664]{1,0:T(8,128)(2,1)} %get-tuple-element.313.refs_0_), channel_id=1, source_target_pairs={{0,2},{1,3},{2,0},{3,1},{4,6},{5,7},{6,4},{7,5},{8,10},{9,11},{10,... | collective-permute-start | bytes 638984 | tf_op jit(solution)/shard_map/ppermute | solution.py:66
  309.4 11.6 %collective-permute-start.70 = (bf16[64,1664]{1,0:T(8,128)(2,1)}, bf16[64,1664]{1,0:T(8,128)(2,1)S(1)}, u32[]{:S(2)}, u32[]{:S(2)}) collective-permute-start(bf16[64,1664]{1,0:T(8,128)(2,1)} %get-tuple-element.313.refs_0_), channel_id=1, source_target_pairs={{0,12},{1,13},{2,14},{3,15},{4,0},{5,1},{6,2},{7,3},{8,4},{9,5},{1... | collective-permute-start | bytes 638984 | tf_op jit(solution)/shard_map/ppermute | solution.py:66
  318.1 12.7 %collective-permute-start.73 = (bf16[64,1664]{1,0:T(8,128)(2,1)}, bf16[64,1664]{1,0:T(8,128)(2,1)S(1)}, u32[]{:S(2)}, u32[]{:S(2)}) collective-permute-start(bf16[64,1664]{1,0:T(8,128)(2,1)} %get-tuple-element.313.refs_0_), channel_id=1, source_target_pairs={{0,8},{1,9},{2,10},{3,11},{4,12},{5,13},{6,14},{7,15},{8,0},{9,1},... | collective-permute-start | bytes 638984 | tf_op jit(solution)/shard_map/ppermute | solution.py:66
  321.0 11.4 %collective-permute-start.75 = (bf16[64,1664]{1,0:T(8,128)(2,1)}, bf16[64,1664]{1,0:T(8,128)(2,1)S(1)}, u32[]{:S(2)}, u32[]{:S(2)}) collective-permute-start(bf16[64,1664]{1,0:T(8,128)(2,1)} %get-tuple-element.313.refs_0_), channel_id=1, source_target_pairs={{0,1},{1,0},{2,3},{3,2},{4,5},{5,4},{6,7},{7,6},{8,9},{9,8},{10,11... | collective-permute-start | bytes 638984 | tf_op jit(solution)/shard_map/ppermute | solution.py:66
  321.0 11.5 %collective-permute-start.69 = (bf16[64,1664]{1,0:T(8,128)(2,1)S(1)}, bf16[64,1664]{1,0:T(8,128)(2,1)S(1)}, u32[]{:S(2)}, u32[]{:S(2)}) collective-permute-start(bf16[64,1664]{1,0:T(8,128)(2,1)S(1)} %collective-permute-done.68.refs_2_), channel_id=1, source_target_pairs={{0,2},{1,3},{2,0},{3,1},{4,6},{5,7},{6,4},{7,5},{8,10},{9,11},{10,... | collective-permute-start | bytes 638984 | tf_op jit(solution)/shard_map/ppermute | solution.py:66
  339.0 13.6 %collective-permute-start.84 = (bf16[512,512]{1,0:T(8,128)(2,1)S(1)}, bf16[512,512]{1,0:T(8,128)(2,1)S(1)}, u32[]{:S(2)}, u32[]{:S(2)}) collective-permute-start(bf16[512,512]{1,0:T(8,128)(2,1)S(1)} %copy-done.23), channel_id=1, source_target_pairs={{0,16},{16,0},{1,17},{17,1},{2,18},{18,2},{3,19},{19,3},{4,20},{20... | collective-permute-start | bytes 1572872 | tf_op jit(solution)/shard_map/ppermute | solution.py:1261
  352.6 14.8 %collective-permute-start.85 = (f32[4,3,64,128]{3,2,1,0:T(8,128)}, f32[4,3,64,128]{3,2,1,0:T(8,128)S(1)}, u32[]{:S(2)}, u32[]{:S(2)}) collective-permute-start(f32[4,3,64,128]{3,2,1,0:T(8,128)} %bitcast.183), channel_id=1, source_target_pairs={{16,0},{17,1},{18,2},{19,3},{20,4},{21,5},{22,6},{23,7},{24,8},{25... | collective-permute-start | bytes 1179656 | tf_op jit(solution)/shard_map/ppermute | solution.py:136
  364.7 30.3 %collective-permute-start.88 = (bf16[192,1536]{1,0:T(8,128)(2,1)S(1)}, bf16[192,1536]{1,0:T(8,128)(2,1)S(1)}, u32[]{:S(2)}, u32[]{:S(2)}) collective-permute-start(bf16[192,1536]{1,0:T(8,128)(2,1)S(1)} %fusion), channel_id=1, source_target_pairs={{0,16},{16,0},{1,17},{17,1},{2,18},{18,2},{3,19},{19,3},{4,20},{20... | collective-permute-start | bytes 1769480 | tf_op jit(solution)/shard_map/ppermute | solution.py:1261
  367.4 27.7 %collective-permute-start.89 = (bf16[512,512]{1,0:T(8,128)(2,1)S(1)}, bf16[512,512]{1,0:T(8,128)(2,1)S(1)}, u32[]{:S(2)}, u32[]{:S(2)}) collective-permute-start(bf16[512,512]{1,0:T(8,128)(2,1)S(1)} %copy-done.19), channel_id=1, source_target_pairs={{0,16},{16,0},{1,17},{17,1},{2,18},{18,2},{3,19},{19,3},{4,20},{20... | collective-permute-start | bytes 1572872 | tf_op jit(solution)/shard_map/ppermute | solution.py:1261
  382.2 12.8 %collective-permute-start.86 = (f32[4,16,448]{2,1,0:T(8,128)S(1)}, f32[4,16,448]{2,1,0:T(8,128)S(1)}, u32[]{:S(2)}, u32[]{:S(2)}) collective-permute-start(f32[4,16,448]{2,1,0:T(8,128)S(1)} %pad_maximum_fusion.6), channel_id=1, source_target_pairs={{16,0},{17,1},{18,2},{19,3},{20,4},{21,5},{22,6},{23,7},{24,8},{25... | collective-permute-start | bytes 344072 | tf_op jit(solution)/shard_map/ppermute | solution.py:19
  416.5 24.0 %collective-permute-start.92 = (bf16[512,512]{1,0:T(8,128)(2,1)}, bf16[512,512]{1,0:T(8,128)(2,1)}, u32[]{:S(2)}, u32[]{:S(2)}) collective-permute-start(bf16[512,512]{1,0:T(8,128)(2,1)} %get-tuple-element.365), channel_id=1, source_target_pairs={{0,16},{16,0},{1,17},{17,1},{2,18},{18,2},{3,19},{19,3},{4,20},{20... | collective-permute-start | bytes 1572872 | tf_op jit(solution)/shard_map/ppermute | solution.py:1261
  432.5 21.4 %collective-permute-start.100 = (bf16[16,18528]{1,0:T(8,128)(2,1)}, bf16[16,18528]{1,0:T(8,128)(2,1)}, u32[]{:S(2)}, u32[]{:S(2)}) collective-permute-start(bf16[16,18528]{1,0:T(8,128)(2,1)} %dynamic-slice_bitcast_fusion), channel_id=1, source_target_pairs={{0,16},{16,0},{1,17},{17,1},{2,18},{18,2},{3,19},{19,3},{4,20},{20... | collective-permute-start | bytes 1778696 | tf_op jit(solution)/shard_map/ppermute | solution.py:122
  436.2 11.3 %collective-permute-start.96 = (bf16[64,1536]{1,0:T(8,128)(2,1)}, bf16[64,1536]{1,0:T(8,128)(2,1)}, u32[]{:S(2)}, u32[]{:S(2)}) collective-permute-start(bf16[64,1536]{1,0:T(8,128)(2,1)} %get-tuple-element.372), channel_id=1, source_target_pairs={{0,2},{1,3},{2,0},{3,1},{4,6},{5,7},{6,4},{7,5},{8,10},{9,11},{10,... | collective-permute-start | bytes 589832 | tf_op jit(solution)/shard_map/ppermute | solution.py:66
  437.8 13.6 %collective-permute-start.98 = (bf16[64,1536]{1,0:T(8,128)(2,1)}, bf16[64,1536]{1,0:T(8,128)(2,1)S(1)}, u32[]{:S(2)}, u32[]{:S(2)}) collective-permute-start(bf16[64,1536]{1,0:T(8,128)(2,1)} %get-tuple-element.373), channel_id=1, source_target_pairs={{0,2},{1,3},{2,0},{3,1},{4,6},{5,7},{6,4},{7,5},{8,10},{9,11},{10,... | collective-permute-start | bytes 589832 | tf_op jit(solution)/shard_map/ppermute | solution.py:66
  440.5 14.6 %collective-permute-start.93 = (bf16[64,1536]{1,0:T(8,128)(2,1)}, bf16[64,1536]{1,0:T(8,128)(2,1)S(1)}, u32[]{:S(2)}, u32[]{:S(2)}) collective-permute-start(bf16[64,1536]{1,0:T(8,128)(2,1)} %get-tuple-element.370), channel_id=1, source_target_pairs={{0,2},{1,3},{2,0},{3,1},{4,6},{5,7},{6,4},{7,5},{8,10},{9,11},{10,... | collective-permute-start | bytes 589832 | tf_op jit(solution)/shard_map/ppermute | solution.py:66
  443.2 38.3 %collective-permute-start.101 = (bf16[1536,384]{1,0:T(8,128)(2,1)S(1)}, bf16[1536,384]{1,0:T(8,128)(2,1)}, u32[]{:S(2)}, u32[]{:S(2)}) collective-permute-start(bf16[1536,384]{1,0:T(8,128)(2,1)S(1)} %copy-done.9), channel_id=1, source_target_pairs={{0,16},{16,0},{1,17},{17,1},{2,18},{18,2},{3,19},{19,3},{4,20},{20... | collective-permute-start | bytes 3538952 | tf_op jit(solution)/shard_map/ppermute | solution.py:1261
  453.8 11.3 %collective-permute-start.99 = (bf16[64,1536]{1,0:T(8,128)(2,1)}, bf16[64,1536]{1,0:T(8,128)(2,1)S(1)}, u32[]{:S(2)}, u32[]{:S(2)}) collective-permute-start(bf16[64,1536]{1,0:T(8,128)(2,1)} %shard_map.476), channel_id=1, source_target_pairs={{0,8},{1,9},{2,10},{3,11},{4,12},{5,13},{6,14},{7,15},{8,0},{9,1},... | collective-permute-start | bytes 589832 | tf_op jit(solution)/shard_map/ppermute | solution.py:66
  472.9 23.1 %all-to-all-start.1 = ((bf16[16,2,9304]{2,1,0:T(2,128)(2,1)}), bf16[16,2,9304]{2,1,0:T(2,128)(2,1)}, u32[]{:S(2)}, u32[]{:S(2)}) async-start(bf16[16,2,9304]{2,1,0:T(2,128)(2,1)} %reshape.499), calls=%async_computation.1 | async-start | bytes 1196032 | tf_op jit(solution)/shard_map/all_to_all | solution.py:147
  477.5 15.8 %collective-permute-start.102 = (bf16[32,1536]{1,0:T(8,128)(2,1)S(1)}, bf16[32,1536]{1,0:T(8,128)(2,1)}, u32[]{:S(2)}, u32[]{:S(2)}) collective-permute-start(bf16[32,1536]{1,0:T(8,128)(2,1)S(1)} %dynamic-slice_bitcast_fusion.2), channel_id=1, source_target_pairs={{0,16},{16,0},{1,17},{17,1},{2,18},{18,2},{3,19},{19,3},{4,20},{20... | collective-permute-start | bytes 294920 | tf_op jit(solution)/shard_map/ppermute | solution.py:1261
  (189 other events, 1330.0 us)
